TPU v7x, 128 devices: a whole 4x4x4 slice. The times are simulated.
128 devices in a mesh: req: 8 (over y, core), hist: 16 (over x, z).
Axes of the slice: x: 4, y: 4, z: 4, core: 2. Of those that a mesh axis runs over, the one named last changes fastest.
Arguments:
- cand_x: bfloat16 [16, 2048, 1024], P('req', 'hist'), may hold values from -6 to 6
- kv_cache: bfloat16 [1024, 128, 2048], P(('req', 'hist')), may hold values from -6 to 6
- w_uvqk: bfloat16 [1024, 4096], replicated, may hold values from -0.1875 to 0.1875
- w_out: bfloat16 [1024, 1024], replicated, may hold values from -0.1875 to 0.1875
- self_bias: float32 [8], replicated, may hold values from 1 to 5
- user_rank: int32 [16], replicated, may hold values from 0 to 15, each once
- hist_len: int32 [16], replicated, may hold values from 1 to 8192, 32768 in all
- cand_count: int32 [16], replicated, may hold values from 1 to 2048, 24576 in all
- tile_slot: int32 [16, 64], replicated, may hold values from 0 to 63, as said below
Outputs:
- ranked: bfloat16 [16, 2048, 1024], P('req', 'hist')
Inputs may be any that keep to these rules, and one draw needn't show every extreme that they name: Ranking slot g holds the candidates of user user_rank[g]. `tile_slot`: value o * 8 + s: the tile is slot s of the cache block of the device with req index o and hist index j mod 16; every slot of every block holds exactly one tile; one block holds at most 2 tiles of the slots of one req index, exactly 2 for some.
All inputs are finite; a program needn't handle non-finite values.
Results may differ from a plain program's by a relative error of at most 0.014.
Values may be sent and summed in bfloat16 or wider, within the bound.
A program may use at most 128 MiB of HBM per device.

v0:
```python
import math

import jax
import jax.numpy as jnp
from jax import lax
from jax.sharding import PartitionSpec as P


def layer_norm(values):
    mean_value = jnp.mean(values, axis=-1, keepdims=True)
    centred = values - mean_value
    spread = jnp.mean(centred * centred, axis=-1, keepdims=True)
    return centred * lax.rsqrt(spread + 1e-05)


def class_term(query_block, keyvals, live_part, score_scale):
    scores = (
        jnp.einsum(
            "nhd,khd->hnk", query_block, keyvals[:, :, 0, :], preferred_element_type=jnp.float32
        )
        * score_scale
    )
    weights = jnp.where(live_part[None, None, :], jax.nn.silu(scores), 0.0).astype(jnp.bfloat16)
    return jnp.einsum(
        "hnk,khd->nhd", weights, keyvals[:, :, 1, :], preferred_element_type=jnp.float32
    )


def local(cand_x, kv_cache, w_uvqk, w_out, self_bias, user_rank, hist_len, cand_count, tile_slot):
    users_here, cand_rows, width = cand_x.shape
    heads = self_bias.shape[0]
    head_dim = width // heads
    score_scale = 1.0 / math.sqrt(head_dim)
    slots_own, tile_len, _ = kv_cache.shape
    user_total, tiles_max = tile_slot.shape
    req_count = lax.axis_size("req")
    hist_count = lax.axis_size("hist")
    req_index = lax.axis_index("req")
    hist_index = lax.axis_index("hist")
    per_hist = tiles_max // hist_count
    capacity = slots_own // req_count + 1
    first_slot = req_index * users_here
    user_ids = lax.dynamic_slice_in_dim(user_rank, first_slot, users_here)
    match_user = user_ids[:, None] == jnp.arange(user_total)[None, :]
    lengths = jnp.sum(jnp.where(match_user, hist_len[None, :], 0), axis=1)
    live_counts = jnp.sum(jnp.where(match_user, cand_count[None, :], 0), axis=1)
    column = lax.dynamic_index_in_dim(
        tile_slot.reshape(user_total, per_hist, hist_count), hist_index, axis=2, keepdims=False
    )
    codes = column.reshape(-1)
    owners = codes // slots_own
    local_slot = codes % slots_own
    dests = jnp.repeat(jnp.arange(user_total) // users_here, per_hist)
    entry_ids = jnp.arange(codes.shape[0])
    same_pair = (
        (owners[:, None] == owners[None, :])
        & (dests[:, None] == dests[None, :])
        & (entry_ids[:, None] > entry_ids[None, :])
    )
    places = jnp.sum(jnp.where(same_pair, 1, 0), axis=1)
    picked = (
        (owners[None, None, :] == req_index)
        & (dests[None, None, :] == jnp.arange(req_count)[:, None, None])
        & (places[None, None, :] == jnp.arange(capacity)[None, :, None])
    )
    source_slot = jnp.sum(jnp.where(picked, local_slot[None, None, :], 0), axis=2).reshape(-1)
    filled = jnp.any(picked, axis=2).reshape(-1)
    outgoing = jnp.take(kv_cache, source_slot, axis=0)
    outgoing = jnp.where(filled[:, None, None], outgoing, jnp.zeros((), kv_cache.dtype))
    outgoing = outgoing.reshape(req_count, capacity, tile_len, 2 * width)
    incoming = lax.all_to_all(outgoing, "req", split_axis=0, concat_axis=0, tiled=True)
    first_entry = first_slot * per_hist
    my_owner = lax.dynamic_slice_in_dim(owners, first_entry, users_here * per_hist)
    my_place = lax.dynamic_slice_in_dim(places, first_entry, users_here * per_hist)
    tiles = jnp.take(
        incoming.reshape(req_count * capacity, tile_len, 2 * width),
        my_owner * capacity + my_place,
        axis=0,
    )
    tiles = tiles.reshape(users_here, per_hist * tile_len, heads, 2, head_dim)
    normed = layer_norm(cand_x.astype(jnp.float32)).astype(jnp.bfloat16)
    mixed_in = jnp.dot(normed.reshape(-1, width), w_uvqk, preferred_element_type=jnp.float32)
    projected = jax.nn.silu(mixed_in).astype(jnp.bfloat16).reshape(users_here, cand_rows, 4, width)
    u_gate = projected[:, :, 0]
    v_self = projected[:, :, 1]
    queries = projected[:, :, 2]
    k_self = projected[:, :, 3]
    class_len = per_hist * tile_len
    key_local = jnp.arange(class_len)
    key_pos = (hist_index + hist_count * (key_local // tile_len)) * tile_len + key_local % tile_len
    live = key_pos[None, :] < lengths[:, None]
    piece = lax.all_gather(queries, "hist", axis=1, tiled=True)
    results = []
    for user_slot in range(users_here):
        query_block = piece[user_slot].reshape(-1, heads, head_dim)
        class_sum = class_term(query_block, tiles[user_slot], live[user_slot], score_scale)
        results.append(class_sum.reshape(query_block.shape[0], width))
    terms = jnp.stack(results)
    combined = lax.psum_scatter(
        terms.astype(jnp.bfloat16), "hist", scatter_dimension=1, tiled=True
    ).astype(jnp.float32)
    query_wide = queries.astype(jnp.float32).reshape(users_here, cand_rows, heads, head_dim)
    key_wide = k_self.astype(jnp.float32).reshape(users_here, cand_rows, heads, head_dim)
    value_wide = v_self.astype(jnp.float32).reshape(users_here, cand_rows, heads, head_dim)
    self_scores = jnp.sum(query_wide * key_wide, axis=-1) * score_scale + self_bias
    own_term = jax.nn.silu(self_scores)[..., None] * value_wide
    divisor = (lengths + 1).astype(jnp.float32)[:, None, None, None]
    attended = (combined.reshape(users_here, cand_rows, heads, head_dim) + own_term) / divisor
    gated = (
        layer_norm(attended.reshape(users_here, cand_rows, width)) * u_gate.astype(jnp.float32)
    ).astype(jnp.bfloat16)
    update = jnp.dot(gated.reshape(-1, width), w_out, preferred_element_type=jnp.float32)
    result = cand_x.astype(jnp.float32) + update.reshape(users_here, cand_rows, width)
    cand_index = hist_index * cand_rows + jnp.arange(cand_rows)
    live_rows = cand_index[None, :] < live_counts[:, None]
    return jnp.where(live_rows[:, :, None], result, 0.0).astype(jnp.bfloat16)


def solution(mesh):
    return jax.shard_map(
        local,
        mesh=mesh,
        in_specs=(
            P("req", "hist", None),
            P(("req", "hist"), None, None),
            P(),
            P(),
            P(),
            P(),
            P(),
            P(),
            P(),
        ),
        out_specs=P("req", "hist", None),
        check_vma=False,
    )
```

profile of v0, /device:TPU:8, one launch (start us, length us, event | category | flops | bytes accessed | tf_op | source)
XLA Modules:
  0.0 351.2 jit_solution(13322362282158327677)
XLA Ops:
  6.5 0.0 copy-start
  6.5 0.0 all-gather.3.cloned.1.call-start
  6.5 1.3 convert_reduce_fusion
  7.9 1.3 fusion.12
  9.2 1.3 fusion.13
  10.5 7.1 %multiply_convert_fusion = bf16[256,4096]{1,0:T(8,128)(2,1)} fusion(bf16[256,1024]{1,0:T(8,128)(2,1)S(1)} %bitcast.61, bf16[1024,4096]{1,0:T(8,128)(2,1)} %param.11), kind=kOutput, calls=%fused_computation.6 | convolution fusion | flops 2152726528 | bytes 11010048 | tf_op jit(solution)/shard_map/dot_general | solution.py:82
  17.6 4.5 %reshape.369 = bf16[2,128,4,1024]{3,2,1,0:T(4,128)(2,1)} reshape(bf16[256,4096]{1,0:T(8,128)(2,1)} %multiply_convert_fusion) | data formatting | bytes 4194304 | tf_op jit(solution)/shard_map/reshape | solution.py:83
  22.2 8.9 %fusion.47 = (bf16[2,128,1,1024]{3,2,1,0:T(2,128)(2,1)}, bf16[2,128,1,1024]{3,2,1,0:T(2,128)(2,1)}, bf16[2,128,1,1024]{3,2,1,0:T(2,128)(2,1)S(1)}, bf16[2,128,1,1024]{3,2,1,0:T(2,128)(2,1)}) fusion(bf16[2,128,4,1024]{3,2,1,0:T(4,128)(2,1)} %reshape.369), kind=kLoop, calls=%fused_computation.102 | loop fusion | bytes 4194304 | tf_op jit(solution)/shard_map/slice | solution.py:84
  31.0 1.9 copy.65
  32.9 0.0 all-gather.3.cloned.1.call-update
  33.0 0.0 copy-done.4
  33.0 0.1 reshape.364
  33.1 0.4 dynamic-slice_reduce_fusion
  33.5 0.1 reshape.365
  33.6 0.1 broadcast_in_dim.139
  33.7 0.1 eq.100
  33.8 0.2 select_reduce_fusion
  34.0 0.1 fusion.23
  34.1 0.1 copy.47
  34.2 0.1 reshape.366
  34.3 0.1 copy.46
  34.4 0.1 and_reduce_fusion
  34.6 0.1 copy.45
  34.7 6.8 %gather_fusion = bf16[16,128,2048]{2,1,0:T(8,128)(2,1)} fusion(bf16[8,128,2048]{2,1,0:T(8,128)(2,1)} %param.10, s32[1024]{0:T(1024)S(1)} %pad_clamp_fusion.1), kind=kCustom, calls=%fused_computation | custom fusion | bytes 16777280 | tf_op jit(solution)/shard_map/jit(_take)/gather | solution.py:68
  41.5 7.6 %select_select_fusion = bf16[8,2,128,2048]{3,2,1,0:T(8,128)(2,1)} fusion(bf16[8,2,128,2048]{3,2,1,0:T(8,128)(2,1)} %bitcast.55, pred[8,2]{1,0:T(8,128)(4,1)S(1)} %copy.46, pred[8,2]{1,0:T(8,128)(4,1)S(1)} %copy.45), kind=kLoop, calls=%fused_computation.5 | loop fusion | flops 8388608 | bytes 16777248 | tf_op jit(solution)/shard_map/jit(_where)/select_n | solution.py:69
  49.1 5.4 %all-to-all-start = ((bf16[8,2,128,2048]{3,2,1,0:T(8,128)(2,1)}), bf16[8,2,128,2048]{3,2,1,0:T(8,128)(2,1)}, u32[]{:S(2)}, u32[]{:S(2)}) async-start(bf16[8,2,128,2048]{3,2,1,0:T(8,128)(2,1)} %select_select_fusion), calls=%async_computation | async-start | bytes 16777216 | tf_op jit(solution)/shard_map/all_to_all | solution.py:71
  54.6 0.0 reduce-scatter.2.cloned.1.call-start
  54.6 0.1 dynamic_slice.13
  54.6 0.1 compare_and_fusion.1
  54.8 0.8 select_reduce_fusion.2
  55.5 0.1 broadcast_compare_fusion
  55.6 0.5 copy-done.5
  56.1 91.8 %all-to-all-done = bf16[8,2,128,2048]{3,2,1,0:T(8,128)(2,1)} async-done(((bf16[8,2,128,2048]{3,2,1,0:T(8,128)(2,1)}), bf16[8,2,128,2048]{3,2,1,0:T(8,128)(2,1)}, u32[]{:S(2)}, u32[]{:S(2)}) %all-to-all-start) | async-done | bytes 8388640 | tf_op jit(solution)/shard_map/all_to_all | solution.py:71
  147.8 6.1 %gather_fusion.1 = bf16[8,128,2048]{2,1,0:T(8,128)(2,1)} fusion(bf16[16,128,2048]{2,1,0:T(8,128)(2,1)} %bitcast.2, s32[1024]{0:T(1024)S(1)} %pad_clamp_fusion), kind=kCustom, calls=%fused_computation.1 | custom fusion | bytes 8388640 | tf_op jit(solution)/shard_map/jit(_take)/gather | solution.py:75
  154.0 2.7 broadcast_select_fusion
  156.6 2.3 fusion.46
  159.0 4.5 %squeeze.26 = bf16[512,8,2,128]{3,2,1,0:T(2,128)(2,1)} reshape(bf16[4,128,2048]{2,1,0:T(8,128)(2,1)} %get-tuple-element.17) | data formatting | bytes 4194304 | tf_op jit(solution)/shard_map/squeeze | solution.py:96
  163.4 6.9 %fusion.48 = (bf16[512,8,1,128]{3,2,1,0:T(2,128)(2,1)}, bf16[512,8,1,128]{3,2,1,0:T(2,128)(2,1)}) fusion(bf16[512,8,2,128]{3,2,1,0:T(2,128)(2,1)} %squeeze.26), kind=kLoop, calls=%fused_computation.103 | loop fusion | bytes 4194304 | tf_op jit(solution)/shard_map/slice | solution.py:25
  170.3 5.8 %copy.64 = bf16[512,8,1,128]{0,3,1,2:T(8,128)(2,1)} copy(bf16[512,8,1,128]{3,2,1,0:T(2,128)(2,1)} %get-tuple-element.23) | data formatting | bytes 2097152
  176.1 4.5 %squeeze.30 = bf16[512,8,2,128]{3,2,1,0:T(2,128)(2,1)} reshape(bf16[4,128,2048]{2,1,0:T(8,128)(2,1)} %get-tuple-element.18) | data formatting | bytes 4194304 | tf_op jit(solution)/shard_map/squeeze | solution.py:96
  180.6 6.9 %fusion.49 = (bf16[512,8,1,128]{3,2,1,0:T(2,128)(2,1)}, bf16[512,8,1,128]{3,2,1,0:T(2,128)(2,1)}) fusion(bf16[512,8,2,128]{3,2,1,0:T(2,128)(2,1)} %squeeze.30), kind=kLoop, calls=%fused_computation.104 | loop fusion | bytes 4194304 | tf_op jit(solution)/shard_map/slice | solution.py:25
  187.5 4.6 %copy.67 = bf16[512,8,1,128]{0,3,1,2:T(8,128)(2,1)S(1)} copy(bf16[512,8,1,128]{3,2,1,0:T(2,128)(2,1)} %get-tuple-element.25) | data formatting | bytes 2097152
  192.1 0.0 all-gather.3.cloned.1.call-done
  192.1 6.0 %fusion.45 = (bf16[1,2048,1,1024]{1,3,2,0:T(8,128)(2,1)}, bf16[1,2048,1,1024]{1,3,2,0:T(8,128)(2,1)}) fusion(bf16[2,2048,1,1024]{1,3,2,0:T(8,128)(2,1)} %all-gather.3.cloned.1.call-done), kind=kLoop, calls=%fused_computation.100 | loop fusion | bytes 16777216 | tf_op jit(solution)/shard_map/slice | solution.py:95
  198.1 17.8 %convolution_convert_fusion.1 = bf16[8,128,2048]{2,1,0:T(8,128)(2,1)} fusion(bf16[2048,8,128]{0,2,1:T(8,128)(2,1)} %bitcast.60, pred[512]{0:T(512)(128)(4,1)S(1)} %get-tuple-element.5, bf16[512,8,1,128]{3,2,1,0:T(2,128)(2,1)} %get-tuple-element.24, bf16[512,8,1,128]{0,3,1,2:T(8,128)(2,1)} %copy.64), kind=kOutput, calls=%fused_computation.9 | convolution fusion | flops 4355784704 | bytes 10486272 | tf_op jit(solution)/shard_map/hnk,khd->nhd/dot_general | solution.py:24
  215.9 6.4 %copy.55 = bf16[1,2048,1024]{2,1,0:T(8,128)(2,1)} copy(bf16[1,2048,1024]{1,2,0:T(8,128)(2,1)} %bitcast.56) | data formatting | bytes 8388608 | tf_op jit(solution)/shard_map/stack;reshape | solution.py:98
  222.3 17.3 %convolution_convert_fusion = bf16[8,128,2048]{2,1,0:T(8,128)(2,1)} fusion(bf16[2048,8,128]{0,2,1:T(8,128)(2,1)} %bitcast.59, pred[512]{0:T(512)(128)(4,1)S(1)} %get-tuple-element.6, bf16[512,8,1,128]{3,2,1,0:T(2,128)(2,1)} %get-tuple-element.26, bf16[512,8,1,128]{0,3,1,2:T(8,128)(2,1)S(1)} %copy.67), kind=kOutput, calls=%fused_computation.8 | convolution fusion | flops 4355784704 | bytes 10486272 | tf_op jit(solution)/shard_map/hnk,khd->nhd/dot_general | solution.py:24
  239.6 6.4 %copy.56 = bf16[1,2048,1024]{2,1,0:T(8,128)(2,1)} copy(bf16[1,2048,1024]{1,2,0:T(8,128)(2,1)} %bitcast.57) | data formatting | bytes 8388608 | tf_op jit(solution)/shard_map/stack;reshape | solution.py:98
  246.0 7.5 %pad_maximum_fusion = bf16[2,2048,1024]{2,1,0:T(8,128)(2,1)} fusion(bf16[1,2048,1024]{2,1,0:T(8,128)(2,1)} %copy.56, bf16[1,2048,1024]{2,1,0:T(8,128)(2,1)} %copy.55), kind=kLoop, calls=%fused_computation.4 | loop fusion | flops 4194304 | bytes 16777216 | tf_op jit(solution)/shard_map/stack | solution.py:98
  253.5 0.0 reduce-scatter.2.cloned.1.call-update
  253.5 0.0 copy-start.9
  253.5 2.5 copy.69
  256.0 1.2 convert_multiply_fusion.2
  257.2 1.3 reduce_sum.87
  258.5 0.0 copy-start.1
  258.5 0.1 divide_multiply_fusion
  258.6 0.1 copy.58
  258.7 1.3 mul.131
  260.0 2.5 mul.132
  262.5 0.1 broadcast_compare_fusion.1
  262.6 77.7 %reduce-scatter.2.cloned.1.call-done = bf16[2,128,1024]{2,1,0:T(8,128)(2,1)} async-done(((bf16[2,2048,1024]{2,1,0:T(8,128)(2,1)}), bf16[2,128,1024]{2,1,0:T(8,128)(2,1)}) %reduce-scatter.2.cloned.1.call-update) | async-done | bytes 524304 | tf_op jit(solution)/shard_map/reduce_scatter | solution.py:99
  340.3 2.1 fusion.43
  342.4 0.3 multiply_reduce_fusion
  342.7 1.7 fusion.7
  (36 shorter events, 0.2 us)
Async XLA Ops:
  6.5 336.1 %copy-start = (bf16[1024,1024]{1,0:T(8,128)(2,1)S(1)}, bf16[1024,1024]{1,0:T(8,128)(2,1)}, u32[]{:S(2)}) copy-start(bf16[1024,1024]{1,0:T(8,128)(2,1)} %param.12) | copy-start | bytes 6291460
  6.5 185.5 %all-gather.3.cloned.1.call-start = ((), (), s32[]{:S(2)}) async-start(), calls=%async_computation.3 | async-start | bytes 8912896 | tf_op jit(solution)/shard_map/all_gather | solution.py:92
  22.1 10.8 %copy-start.4 = (s32[16,64]{1,0:T(8,128)S(1)}, s32[16,64]{1,0:T(8,128)}, u32[]{:S(2)}) copy-start(s32[16,64]{1,0:T(8,128)} %param.17) | copy-start | bytes 12292
  49.1 5.5 %copy-start.11 = (s32[16]{0:T(128)S(1)}, s32[16]{0:T(128)}, u32[]{:S(2)}) copy-start(s32[16]{0:T(128)} %param.14) | copy-start | bytes 196
  49.1 5.6 %copy-start.7 = (s32[16]{0:T(128)S(1)}, s32[16]{0:T(128)}, u32[]{:S(2)}) copy-start(s32[16]{0:T(128)} %param.16) | copy-start | bytes 196
  49.1 5.7 %copy-start.8 = (s32[16]{0:T(128)S(1)}, s32[16]{0:T(128)}, u32[]{:S(2)}) copy-start(s32[16]{0:T(128)} %param.15) | copy-start | bytes 196
  49.1 98.7 %all-to-all-start = ((bf16[8,2,128,2048]{3,2,1,0:T(8,128)(2,1)}), bf16[8,2,128,2048]{3,2,1,0:T(8,128)(2,1)}, u32[]{:S(2)}, u32[]{:S(2)}) async-start(bf16[8,2,128,2048]{3,2,1,0:T(8,128)(2,1)} %select_select_fusion), calls=%async_computation | async-start | bytes 16777216 | tf_op jit(solution)/shard_map/all_to_all | solution.py:71
  54.6 285.7 %reduce-scatter.2.cloned.1.call-start = ((), (), s32[]{:S(2)}) async-start(), calls=%async_computation.2 | async-start | bytes 8912896 | tf_op jit(solution)/shard_map/reduce_scatter | solution.py:99
  55.5 0.5 copy-start.5
  253.5 2.5 copy-start.2
  253.5 5.0 %copy-start.9 = (f32[8]{0:T(128)S(1)}, f32[8]{0:T(128)}, u32[]{:S(2)}) copy-start(f32[8]{0:T(128)} %param.13) | copy-start | bytes 100
  253.5 9.0 %copy-start.6 = (s32[2]{0:T(128)S(1)}, s32[2]{0:T(128)}, u32[]{:S(2)}) copy-start(s32[2]{0:T(128)} %copy-done.5) | copy-start | bytes 28
  253.5 9.0 %copy-start.10 = (s32[2]{0:T(128)S(1)}, s32[2]{0:T(128)}, u32[]{:S(2)}) copy-start(s32[2]{0:T(128)} %get-tuple-element.7) | copy-start | bytes 28
  258.5 84.2 %copy-start.1 = (bf16[2,128,1024]{2,1,0:T(8,128)(2,1)S(1)}, bf16[2,128,1024]{2,1,0:T(8,128)(2,1)}, u32[]{:S(2)}) copy-start(bf16[2,128,1024]{2,1,0:T(8,128)(2,1)} %param.9) | copy-start | bytes 1572868
  340.3 2.4 copy-start.3
Sparse Core Ops, SparseCore 0:
  33.1 80.8 all-gather.2
  253.6 86.6 reduce-scatter.1
where the time goes:
time: 353 us; the launch traced here: 351 us
  waiting for transfers between devices  169 us (48%)
  local copies, waits for them, and re-layouts  90.6 us (26%)
  matrix products  43.9 us (12%)
  other arithmetic  28.1 us (8%)
  between operations  13.7 us (4%)
  starting transfers between devices  5.45 us (2%)
    all_to_all x1, waiting for transfers between devices, local(): lax.all_to_all(outgoing, 'req', split_axis=0, concat_axis=0, tiled=True)  91.8 us
    reduce_scatter x1, waiting for transfers between devices, local(): lax.psum_scatter(terms.astype(jnp.bfloat16), 'hist', scatter_dimension=1,...  77.7 us
    dot_general x2, matrix products, class_term(): jnp.einsum('hnk,khd->nhd', weights, keyvals[:, :, 1, :], preferred_elemen...  35.1 us
    unnamed x28, local copies, waits for them, and re-layouts  15.2 us
    slice x2, local copies, waits for them, and re-layouts, class_term(): keyvals[:, :, 1, :]  13.8 us
    another operation x2, local copies, waits for them, and re-layouts, local(): terms = jnp.stack(results)  12.8 us
    squeeze x2, local copies, waits for them, and re-layouts, local(): tiles[user_slot]  8.94 us
    slice x1, local copies, waits for them, and re-layouts, local(): u_gate = projected[:, :, 0]  8.89 us
  transfers between devices with their start and end apart: 3, of which 2 were waited for; matrix products, arithmetic and copies ran while one was open for 20% of the time, Pallas kernels for 0%

commit v1 on v0

--- a/solution.py
+++ b/solution.py
@@ -1,8 +1,11 @@
+import functools
 import math
 
 import jax
 import jax.numpy as jnp
 from jax import lax
+from jax.experimental import pallas as pl
+from jax.experimental.pallas import tpu as pltpu
 from jax.sharding import PartitionSpec as P
 
 
@@ -13,17 +16,55 @@
     return centred * lax.rsqrt(spread + 1e-05)
 
 
-def class_term(query_block, keyvals, live_part, score_scale):
-    scores = (
-        jnp.einsum(
-            "nhd,khd->hnk", query_block, keyvals[:, :, 0, :], preferred_element_type=jnp.float32
-        )
-        * score_scale
-    )
-    weights = jnp.where(live_part[None, None, :], jax.nn.silu(scores), 0.0).astype(jnp.bfloat16)
-    return jnp.einsum(
-        "hnk,khd->nhd", weights, keyvals[:, :, 1, :], preferred_element_type=jnp.float32
-    )
+def silu_tanh(values):
+    return values * (0.5 + 0.5 * jnp.tanh(0.5 * values))
+
+
+def attend_kernel(len_ref, q_ref, kv_ref, o_ref, acc_ref, *, score_scale, chunk):
+    length = len_ref[0]
+    n_cls, n_tiles, tile_len, _ = kv_ref.shape
+    head_dim = q_ref.shape[1]
+    o_ref[...] = jnp.zeros_like(o_ref)
+
+    def one_class(c, carry):
+        for ci in range(q_ref.shape[0] // chunk):
+            rows = pl.ds(ci * chunk, chunk)
+            acc_ref[...] = jnp.zeros_like(acc_ref)
+            q_chunk = q_ref[rows, :]
+            for t in range(n_tiles):
+                remaining = length - (c + n_cls * t) * tile_len
+
+                @pl.when(remaining > 0)
+                def _():
+                    keys = kv_ref[c, t, :, pl.ds(0, head_dim)]
+                    values = kv_ref[c, t, :, pl.ds(head_dim, head_dim)]
+                    scores = lax.dot_general(
+                        q_chunk, keys, (((1,), (1,)), ((), ())), preferred_element_type=jnp.float32
+                    ) * score_scale
+                    token = lax.broadcasted_iota(jnp.int32, scores.shape, 1)
+                    weights = jnp.where(token < remaining, silu_tanh(scores), 0.0).astype(jnp.bfloat16)
+                    acc_ref[...] += jnp.dot(weights, values, preferred_element_type=jnp.float32)
+
+            o_ref[rows, :] += acc_ref[...].astype(jnp.bfloat16).astype(jnp.float32)
+        return carry
+
+    lax.fori_loop(0, n_cls, one_class, 0)
+
+
+def attend(length, q_all, head_tiles, score_scale):
+    rows, head_dim = q_all.shape
+    chunk = 512
+    return pl.pallas_call(
+        functools.partial(attend_kernel, score_scale=score_scale, chunk=chunk),
+        out_shape=jax.ShapeDtypeStruct((rows, head_dim), jnp.float32),
+        in_specs=[
+            pl.BlockSpec(memory_space=pltpu.SMEM),
+            pl.BlockSpec(memory_space=pltpu.VMEM),
+            pl.BlockSpec(memory_space=pltpu.VMEM),
+        ],
+        out_specs=pl.BlockSpec(memory_space=pltpu.VMEM),
+        scratch_shapes=[pltpu.VMEM((chunk, head_dim), jnp.float32)],
+    )(length, q_all, head_tiles)
 
 
 def local(cand_x, kv_cache, w_uvqk, w_out, self_bias, user_rank, hist_len, cand_count, tile_slot):
@@ -77,7 +118,9 @@
         my_owner * capacity + my_place,
         axis=0,
     )
-    tiles = tiles.reshape(users_here, per_hist * tile_len, heads, 2, head_dim)
+    tiles = tiles.reshape(users_here, per_hist, tile_len, heads, 2 * head_dim)
+    by_head = tiles.transpose(0, 3, 1, 2, 4).reshape(users_here * heads, per_hist, tile_len, 2 * head_dim)
+    head_tiles = lax.all_to_all(by_head, "hist", split_axis=0, concat_axis=0, tiled=True)
     normed = layer_norm(cand_x.astype(jnp.float32)).astype(jnp.bfloat16)
     mixed_in = jnp.dot(normed.reshape(-1, width), w_uvqk, preferred_element_type=jnp.float32)
     projected = jax.nn.silu(mixed_in).astype(jnp.bfloat16).reshape(users_here, cand_rows, 4, width)
@@ -85,27 +128,24 @@
     v_self = projected[:, :, 1]
     queries = projected[:, :, 2]
     k_self = projected[:, :, 3]
-    class_len = per_hist * tile_len
-    key_local = jnp.arange(class_len)
-    key_pos = (hist_index + hist_count * (key_local // tile_len)) * tile_len + key_local % tile_len
-    live = key_pos[None, :] < lengths[:, None]
-    piece = lax.all_gather(queries, "hist", axis=1, tiled=True)
-    results = []
-    for user_slot in range(users_here):
-        query_block = piece[user_slot].reshape(-1, heads, head_dim)
-        class_sum = class_term(query_block, tiles[user_slot], live[user_slot], score_scale)
-        results.append(class_sum.reshape(query_block.shape[0], width))
-    terms = jnp.stack(results)
-    combined = lax.psum_scatter(
-        terms.astype(jnp.bfloat16), "hist", scatter_dimension=1, tiled=True
-    ).astype(jnp.float32)
+    q_by_head = queries.reshape(users_here, cand_rows, heads, head_dim).transpose(0, 2, 1, 3)
+    q_by_head = q_by_head.reshape(users_here * heads, cand_rows, head_dim)
+    q_all = lax.all_to_all(q_by_head, "hist", split_axis=0, concat_axis=0, tiled=True)
+    q_all = q_all.reshape(hist_count * cand_rows, head_dim)
+    my_user = hist_index // heads
+    my_length = lax.dynamic_slice_in_dim(lengths, my_user, 1)
+    history_mine = attend(my_length, q_all, head_tiles, score_scale)
+    history_back = lax.all_to_all(
+        history_mine.reshape(hist_count, cand_rows, head_dim), "hist", split_axis=0, concat_axis=0, tiled=True
+    )
+    combined = history_back.reshape(users_here, heads, cand_rows, head_dim).transpose(0, 2, 1, 3)
     query_wide = queries.astype(jnp.float32).reshape(users_here, cand_rows, heads, head_dim)
     key_wide = k_self.astype(jnp.float32).reshape(users_here, cand_rows, heads, head_dim)
     value_wide = v_self.astype(jnp.float32).reshape(users_here, cand_rows, heads, head_dim)
     self_scores = jnp.sum(query_wide * key_wide, axis=-1) * score_scale + self_bias
     own_term = jax.nn.silu(self_scores)[..., None] * value_wide
     divisor = (lengths + 1).astype(jnp.float32)[:, None, None, None]
-    attended = (combined.reshape(users_here, cand_rows, heads, head_dim) + own_term) / divisor
+    attended = (combined + own_term) / divisor
     gated = (
         layer_norm(attended.reshape(users_here, cand_rows, width)) * u_gate.astype(jnp.float32)
     ).astype(jnp.bfloat16)

time: 353 us -> 335 us (0.949)
  the two profiles are of different devices: /device:TPU:8 before, /device:TPU:9 now
where the time goes in v1:
time: 335 us; the launch traced here: 334 us
  waiting for transfers between devices  124 us (37%)
  Pallas kernels  95.7 us (29%)
  local copies, waits for them, and re-layouts  40.9 us (12%)
  other arithmetic  35.3 us (11%)
  starting transfers between devices  27.5 us (8%)
  matrix products  10.5 us (3%)
    pallas_call x1, Pallas kernels, attend(): pl.pallas_call(functools.partial(attend_kernel, score_scale=score_scale,...  95.7 us
    all_to_all x1, waiting for transfers between devices, local(): lax.all_to_all(outgoing, 'req', split_axis=0, concat_axis=0, tiled=True)  67.9 us
    all_to_all x1, waiting for transfers between devices, local(): lax.all_to_all(by_head, 'hist', split_axis=0, concat_axis=0, tiled=True)  50.9 us
    gather x2, local copies, waits for them, and re-layouts, local(): jnp.take(incoming.reshape(req_count * capacity, tile_len, 2 * width), my_...  12.6 us
    slice x1, other arithmetic, local(): queries = projected[:, :, 2]  8.99 us
    all_to_all x1, starting transfers between devices, local(): lax.all_to_all(q_by_head, 'hist', split_axis=0, concat_axis=0, tiled=True)  7.65 us
    select_n x1, other arithmetic, local(): jnp.where(filled[:, None, None], outgoing, jnp.zeros((), kv_cache.dtype))  7.57 us
    all_to_all x1, starting transfers between devices, local(): lax.all_to_all(history_mine.reshape(hist_count, cand_rows, head_dim), 'hi...  7.47 us
  transfers between devices with their start and end apart: 4, of which 3 were waited for; matrix products, arithmetic and copies ran while one was open for 17% of the time, Pallas kernels for 0%

profile of v1, /device:TPU:9, one launch (start us, length us, event | category | flops | bytes accessed | tf_op | source)
XLA Modules:
  0.0 333.9 jit_solution(3960035367037564804)
XLA Ops:
  0.0 0.0 copy-start
  0.0 0.9 reshape.370
  0.9 0.4 dynamic-slice_reduce_fusion
  1.4 0.1 reshape.371
  1.5 0.1 broadcast_in_dim.118
  1.6 0.1 eq.98
  1.6 0.2 select_reduce_fusion
  1.9 0.1 fusion.20
  2.0 0.1 copy.66
  2.1 0.2 and_reduce_fusion
  2.3 0.1 reshape.372
  2.4 0.1 copy.65
  2.5 0.1 copy.64
  2.6 6.8 %gather_fusion = bf16[16,128,2048]{2,1,0:T(8,128)(2,1)} fusion(bf16[8,128,2048]{2,1,0:T(8,128)(2,1)} %param.10, s32[1024]{0:T(1024)S(1)} %pad_clamp_fusion.1), kind=kCustom, calls=%fused_computation | custom fusion | bytes 16777280 | tf_op jit(solution)/shard_map/jit(_take)/gather | solution.py:109
  9.4 7.6 %select_select_fusion = bf16[8,2,128,2048]{3,2,1,0:T(8,128)(2,1)} fusion(bf16[8,2,128,2048]{3,2,1,0:T(8,128)(2,1)} %bitcast.42, pred[8,2]{1,0:T(8,128)(4,1)S(1)} %copy.65, pred[8,2]{1,0:T(8,128)(4,1)S(1)} %copy.64), kind=kLoop, calls=%fused_computation.2 | loop fusion | flops 8388608 | bytes 16777248 | tf_op jit(solution)/shard_map/jit(_where)/select_n | solution.py:110
  17.0 0.0 copy-start.1
  17.0 5.7 %all-to-all-start.1 = ((bf16[8,2,128,2048]{3,2,1,0:T(8,128)(2,1)}), bf16[8,2,128,2048]{3,2,1,0:T(8,128)(2,1)}, u32[]{:S(2)}, u32[]{:S(2)}) async-start(bf16[8,2,128,2048]{3,2,1,0:T(8,128)(2,1)} %select_select_fusion), calls=%async_computation.1 | async-start | bytes 16777216 | tf_op jit(solution)/shard_map/all_to_all | solution.py:112
  22.6 0.0 copy-done.1
  22.6 0.1 convert_reduce_fusion
  22.8 0.3 fusion.12
  23.1 0.3 fusion.13
  23.3 7.2 %multiply_convert_fusion = bf16[256,4096]{1,0:T(8,128)(2,1)} fusion(bf16[256,1024]{1,0:T(8,128)(2,1)S(1)} %bitcast.51, bf16[1024,4096]{1,0:T(8,128)(2,1)} %param.11), kind=kOutput, calls=%fused_computation.4 | convolution fusion | flops 2152726528 | bytes 11010048 | tf_op jit(solution)/shard_map/dot_general | solution.py:125
  30.5 4.5 %reshape.367 = bf16[2,128,4,1024]{3,2,1,0:T(4,128)(2,1)} reshape(bf16[256,4096]{1,0:T(8,128)(2,1)} %multiply_convert_fusion) | data formatting | bytes 4194304 | tf_op jit(solution)/shard_map/reshape | solution.py:126
  35.0 9.0 %fusion.25 = (bf16[2,128,1,1024]{3,2,1,0:T(2,128)(2,1)}, f32[2,128,1,1024]{3,2,1,0:T(1,128)}, f32[2,128,1,1024]{3,2,1,0:T(1,128)}, bf16[2,128,1,1024]{3,2,1,0:T(2,128)(2,1)}) fusion(bf16[2,128,4,1024]{3,2,1,0:T(4,128)(2,1)} %reshape.367), kind=kLoop, calls=%fused_computation.67 | loop fusion | flops 524288 | bytes 5242880 | tf_op jit(solution)/shard_map/slice | solution.py:129
  44.0 2.4 copy.61
  46.4 1.0 copy.62
  47.4 0.1 compare_and_fusion.1
  47.5 67.9 %all-to-all-done.1 = bf16[8,2,128,2048]{3,2,1,0:T(8,128)(2,1)} async-done(((bf16[8,2,128,2048]{3,2,1,0:T(8,128)(2,1)}), bf16[8,2,128,2048]{3,2,1,0:T(8,128)(2,1)}, u32[]{:S(2)}, u32[]{:S(2)}) %all-to-all-start.1) | async-done | bytes 8388640 | tf_op jit(solution)/shard_map/all_to_all | solution.py:112
  115.4 7.6 %all-to-all-start = ((bf16[16,128,128]{2,1,0:T(8,128)(2,1)}), bf16[16,128,128]{2,1,0:T(8,128)(2,1)S(1)}, u32[]{:S(2)}, u32[]{:S(2)}) async-start(bf16[16,128,128]{2,1,0:T(8,128)(2,1)} %copy.62), calls=%async_computation | async-start | bytes 1048576 | tf_op jit(solution)/shard_map/all_to_all | solution.py:133
  123.1 0.1 broadcast_in_dim.121
  123.2 6.2 %gather_fusion.1 = bf16[8,128,2048]{2,1,0:T(8,128)(2,1)} fusion(bf16[16,128,2048]{2,1,0:T(8,128)(2,1)} %bitcast.7, s32[1024]{0:T(1024)S(1)} %pad_clamp_fusion), kind=kCustom, calls=%fused_computation.1 | custom fusion | bytes 8388640 | tf_op jit(solution)/shard_map/jit(_take)/gather | solution.py:116
  129.3 6.4 %copy.67 = bf16[8,128,2048]{1,2,0:T(8,128)(2,1)} copy(bf16[8,128,2048]{2,1,0:T(8,128)(2,1)} %gather_fusion.1) | data formatting | bytes 8388608 | tf_op jit(solution)/shard_map/jit(_take)/gather | solution.py:116
  135.8 4.6 %select_bitcast_fusion = bf16[2,8,4,128,256]{3,4,1,2,0:T(8,128)(2,1)} fusion(bf16[2,4,128,8,256]{2,4,3,1,0:T(8,128)(2,1)} %bitcast.44, pred[2,4]{1,0:T(4,128)(4,1)S(1)} %broadcast_in_dim.121), kind=kLoop, calls=%fused_computation.3 | loop fusion | flops 2097152 | bytes 8388616 | tf_op jit(solution)/shard_map/transpose | solution.py:122
  140.4 6.2 %copy.68 = bf16[2,8,4,128,256]{4,3,2,1,0:T(8,128)(2,1)} copy(bf16[2,8,4,128,256]{3,4,1,2,0:T(8,128)(2,1)} %select_bitcast_fusion) | data formatting | bytes 8388608 | tf_op jit(solution)/shard_map/transpose | solution.py:122
  146.6 0.0 all-to-all-done
  146.6 0.0 copy-start.2
  146.6 0.0 copy-start.6
  146.6 0.0 copy-start.3
  146.6 0.0 copy-start.4
  146.6 0.8 copy-done.2
  147.4 6.7 %all-to-all-start.2 = ((bf16[16,4,128,256]{3,2,1,0:T(8,128)(2,1)}), bf16[16,4,128,256]{3,2,1,0:T(8,128)(2,1)}, u32[]{:S(2)}, u32[]{:S(2)}) async-start(bf16[16,4,128,256]{3,2,1,0:T(8,128)(2,1)} %bitcast.43), calls=%async_computation.2 | async-start | bytes 8388608 | tf_op jit(solution)/shard_map/all_to_all | solution.py:123
  154.1 0.0 copy-done.6
  154.1 0.1 dynamic_slice.16
  154.2 0.0 copy-done.3
  154.2 0.0 copy-done.4
  154.2 0.2 select_reduce_fusion.2
  154.4 0.6 dynamic_slice.17.len_ref
  155.0 50.9 %all-to-all-done.2.kv_ref = bf16[16,4,128,256]{3,2,1,0:T(8,128)(2,1)} async-done(((bf16[16,4,128,256]{3,2,1,0:T(8,128)(2,1)}), bf16[16,4,128,256]{3,2,1,0:T(8,128)(2,1)}, u32[]{:S(2)}, u32[]{:S(2)}) %all-to-all-start.2) | async-done | bytes 4194336 | tf_op jit(solution)/shard_map/all_to_all | solution.py:123
  205.9 95.7 %shard_map.91 = f32[2048,128]{1,0:T(8,128)} custom-call(s32[1]{0:T(128)} %dynamic_slice.17.len_ref, bf16[2048,128]{1,0:T(8,128)(2,1)} %bitcast.50, bf16[16,4,128,256]{3,2,1,0:T(8,128)(2,1)} %all-to-all-done.2.kv_ref), custom_call_target="tpu_custom_call" | custom-call | tf_op jit(solution)/shard_map/pallas_call | solution.py:57
  301.5 0.0 copy-start.5
  301.5 7.5 %all-to-all-start.3 = ((f32[16,128,128]{2,1,0:T(8,128)}), f32[16,128,128]{2,1,0:T(8,128)}, u32[]{:S(2)}, u32[]{:S(2)}) async-start(f32[16,128,128]{2,1,0:T(8,128)} %bitcast.48), calls=%async_computation.3 | async-start | bytes 2097152 | tf_op jit(solution)/shard_map/all_to_all | solution.py:138
  309.0 2.5 copy_convert_fusion
  311.5 2.5 copy.73
  314.0 1.3 multiply_reduce_fusion.1
  315.4 0.0 copy-done.5
  315.4 0.1 divide_multiply_fusion
  315.5 0.1 copy.72
  315.6 0.1 broadcast_compare_fusion
  315.7 5.1 %all-to-all-done.3 = f32[16,128,128]{2,1,0:T(8,128)} async-done(((f32[16,128,128]{2,1,0:T(8,128)}), f32[16,128,128]{2,1,0:T(8,128)}, u32[]{:S(2)}, u32[]{:S(2)}) %all-to-all-start.3) | async-done | bytes 1048608 | tf_op jit(solution)/shard_map/all_to_all | solution.py:138
  320.8 5.1 %fusion.23 = (f32[2,128]{1,0:T(2,128)S(1)}, f32[2,128,8,128]{3,2,1,0:T(8,128)S(1)}) fusion(f32[2]{0:T(128)S(1)} %add_convert_fusion, f32[2,128,8,128]{3,2,1,0:T(8,128)} %bitcast.49, f32[2,128,8]{2,1,0:T(8,128)S(1)} %copy.72, f32[2,8,128,128]{3,2,1,0:T(8,128)} %bitcast.12), kind=kLoop, calls=%fused_computation.66 | loop fusion | flops 1048320 | bytes 3154952 | tf_op jit(solution)/shard_map/reduce_sum | solution.py:13
  325.9 1.2 reshape.377
  327.1 3.5 %multiply_reduce_fusion = f32[2,128]{1,0:T(2,128)S(1)} fusion(f32[2,128,8,128]{3,2,1,0:T(8,128)S(1)} %get-tuple-element.8, f32[2,128]{1,0:T(2,128)S(1)} %broadcast_multiply_fusion), kind=kLoop, calls=%fused_computation.22 | loop fusion | flops 786176 | bytes 1050624 | tf_op jit(solution)/shard_map/reduce_sum | solution.py:15
  330.6 0.0 copy-done
  330.6 3.3 fusion.7
  (15 shorter events, 0.1 us)
Async XLA Ops:
  0.0 330.6 %copy-start = (bf16[1024,1024]{1,0:T(8,128)(2,1)S(1)}, bf16[1024,1024]{1,0:T(8,128)(2,1)}, u32[]{:S(2)}) copy-start(bf16[1024,1024]{1,0:T(8,128)(2,1)} %param.12) | copy-start | bytes 6291460
  17.0 5.7 %copy-start.1 = (bf16[2,128,1024]{2,1,0:T(8,128)(2,1)S(1)}, bf16[2,128,1024]{2,1,0:T(8,128)(2,1)}, u32[]{:S(2)}) copy-start(bf16[2,128,1024]{2,1,0:T(8,128)(2,1)} %param.9) | copy-start | bytes 1572868
  17.0 98.4 %all-to-all-start.1 = ((bf16[8,2,128,2048]{3,2,1,0:T(8,128)(2,1)}), bf16[8,2,128,2048]{3,2,1,0:T(8,128)(2,1)}, u32[]{:S(2)}, u32[]{:S(2)}) async-start(bf16[8,2,128,2048]{3,2,1,0:T(8,128)(2,1)} %select_select_fusion), calls=%async_computation.1 | async-start | bytes 16777216 | tf_op jit(solution)/shard_map/all_to_all | solution.py:112
  115.4 31.2 %all-to-all-start = ((bf16[16,128,128]{2,1,0:T(8,128)(2,1)}), bf16[16,128,128]{2,1,0:T(8,128)(2,1)S(1)}, u32[]{:S(2)}, u32[]{:S(2)}) async-start(bf16[16,128,128]{2,1,0:T(8,128)(2,1)} %copy.62), calls=%async_computation | async-start | bytes 1048576 | tf_op jit(solution)/shard_map/all_to_all | solution.py:133
  146.6 0.8 copy-start.2
  146.6 7.5 %copy-start.6 = (s32[16]{0:T(128)S(1)}, s32[16]{0:T(128)}, u32[]{:S(2)}) copy-start(s32[16]{0:T(128)} %param.14) | copy-start | bytes 196
  146.6 7.6 %copy-start.3 = (s32[16]{0:T(128)S(1)}, s32[16]{0:T(128)}, u32[]{:S(2)}) copy-start(s32[16]{0:T(128)} %param.16) | copy-start | bytes 196
  146.6 7.6 %copy-start.4 = (s32[16]{0:T(128)S(1)}, s32[16]{0:T(128)}, u32[]{:S(2)}) copy-start(s32[16]{0:T(128)} %param.15) | copy-start | bytes 196
  147.4 58.5 %all-to-all-start.2 = ((bf16[16,4,128,256]{3,2,1,0:T(8,128)(2,1)}), bf16[16,4,128,256]{3,2,1,0:T(8,128)(2,1)}, u32[]{:S(2)}, u32[]{:S(2)}) async-start(bf16[16,4,128,256]{3,2,1,0:T(8,128)(2,1)} %bitcast.43), calls=%async_computation.2 | async-start | bytes 8388608 | tf_op jit(solution)/shard_map/all_to_all | solution.py:123
  301.5 13.8 %copy-start.5 = (f32[8]{0:T(128)S(1)}, f32[8]{0:T(128)}, u32[]{:S(2)}) copy-start(f32[8]{0:T(128)} %param.13) | copy-start | bytes 100
  301.5 19.3 %all-to-all-start.3 = ((f32[16,128,128]{2,1,0:T(8,128)}), f32[16,128,128]{2,1,0:T(8,128)}, u32[]{:S(2)}, u32[]{:S(2)}) async-start(f32[16,128,128]{2,1,0:T(8,128)} %bitcast.48), calls=%async_computation.3 | async-start | bytes 2097152 | tf_op jit(solution)/shard_map/all_to_all | solution.py:138

commit v2 on v1

--- a/solution.py
+++ b/solution.py
@@ -20,32 +20,33 @@
     return values * (0.5 + 0.5 * jnp.tanh(0.5 * values))
 
 
-def attend_kernel(len_ref, q_ref, kv_ref, o_ref, acc_ref, *, score_scale, chunk):
+def attend_kernel(len_ref, q_ref, kv_ref, o_ref, *, score_scale, chunk):
     length = len_ref[0]
     n_cls, n_tiles, tile_len, _ = kv_ref.shape
     head_dim = q_ref.shape[1]
+    span = n_tiles * tile_len
+    half_scale = 0.5 * score_scale
     o_ref[...] = jnp.zeros_like(o_ref)
 
     def one_class(c, carry):
-        for ci in range(q_ref.shape[0] // chunk):
-            rows = pl.ds(ci * chunk, chunk)
-            acc_ref[...] = jnp.zeros_like(acc_ref)
-            q_chunk = q_ref[rows, :]
-            for t in range(n_tiles):
-                remaining = length - (c + n_cls * t) * tile_len
+        key_index = lax.broadcasted_iota(jnp.int32, (1, span), 1)
+        position = (c + n_cls * (key_index // tile_len)) * tile_len + key_index % tile_len
+        live = position < length
 
-                @pl.when(remaining > 0)
-                def _():
-                    keys = kv_ref[c, t, :, pl.ds(0, head_dim)]
-                    values = kv_ref[c, t, :, pl.ds(head_dim, head_dim)]
-                    scores = lax.dot_general(
-                        q_chunk, keys, (((1,), (1,)), ((), ())), preferred_element_type=jnp.float32
-                    ) * score_scale
-                    token = lax.broadcasted_iota(jnp.int32, scores.shape, 1)
-                    weights = jnp.where(token < remaining, silu_tanh(scores), 0.0).astype(jnp.bfloat16)
-                    acc_ref[...] += jnp.dot(weights, values, preferred_element_type=jnp.float32)
+        @pl.when(c * tile_len < length)
+        def _():
+            keys = kv_ref[c, :, :, pl.ds(0, head_dim)].reshape(span, head_dim)
+            values = kv_ref[c, :, :, pl.ds(head_dim, head_dim)].reshape(span, head_dim)
+            for ci in range(q_ref.shape[0] // chunk):
+                rows = pl.ds(ci * chunk, chunk)
+                scores = lax.dot_general(
+                    q_ref[rows, :], keys, (((1,), (1,)), ((), ())), preferred_element_type=jnp.float32
+                )
+                half = scores * half_scale
+                weights = jnp.where(live, half + half * jnp.tanh(half), 0.0).astype(jnp.bfloat16)
+                part = jnp.dot(weights, values, preferred_element_type=jnp.float32)
+                o_ref[rows, :] += part.astype(jnp.bfloat16).astype(jnp.float32)
 
-            o_ref[rows, :] += acc_ref[...].astype(jnp.bfloat16).astype(jnp.float32)
         return carry
 
     lax.fori_loop(0, n_cls, one_class, 0)
@@ -63,7 +64,6 @@
             pl.BlockSpec(memory_space=pltpu.VMEM),
         ],
         out_specs=pl.BlockSpec(memory_space=pltpu.VMEM),
-        scratch_shapes=[pltpu.VMEM((chunk, head_dim), jnp.float32)],
     )(length, q_all, head_tiles)
 
 
@@ -105,21 +105,16 @@
         & (places[None, None, :] == jnp.arange(capacity)[None, :, None])
     )
     source_slot = jnp.sum(jnp.where(picked, local_slot[None, None, :], 0), axis=2).reshape(-1)
-    filled = jnp.any(picked, axis=2).reshape(-1)
-    outgoing = jnp.take(kv_cache, source_slot, axis=0)
-    outgoing = jnp.where(filled[:, None, None], outgoing, jnp.zeros((), kv_cache.dtype))
-    outgoing = outgoing.reshape(req_count, capacity, tile_len, 2 * width)
+    kv_by_head = kv_cache.reshape(slots_own, tile_len, heads, 2 * head_dim)
+    outgoing = jnp.take(kv_by_head, source_slot, axis=0).transpose(0, 2, 1, 3)
+    outgoing = outgoing.reshape(req_count, capacity, heads, tile_len, 2 * head_dim)
     incoming = lax.all_to_all(outgoing, "req", split_axis=0, concat_axis=0, tiled=True)
     first_entry = first_slot * per_hist
     my_owner = lax.dynamic_slice_in_dim(owners, first_entry, users_here * per_hist)
     my_place = lax.dynamic_slice_in_dim(places, first_entry, users_here * per_hist)
-    tiles = jnp.take(
-        incoming.reshape(req_count * capacity, tile_len, 2 * width),
-        my_owner * capacity + my_place,
-        axis=0,
-    )
-    tiles = tiles.reshape(users_here, per_hist, tile_len, heads, 2 * head_dim)
-    by_head = tiles.transpose(0, 3, 1, 2, 4).reshape(users_here * heads, per_hist, tile_len, 2 * head_dim)
+    picked_slot = (my_owner * capacity + my_place).reshape(users_here, per_hist)
+    tiles = incoming.reshape(req_count * capacity, heads, tile_len, 2 * head_dim)[picked_slot]
+    by_head = tiles.transpose(0, 2, 1, 3, 4).reshape(users_here * heads, per_hist, tile_len, 2 * head_dim)
     head_tiles = lax.all_to_all(by_head, "hist", split_axis=0, concat_axis=0, tiled=True)
     normed = layer_norm(cand_x.astype(jnp.float32)).astype(jnp.bfloat16)
     mixed_in = jnp.dot(normed.reshape(-1, width), w_uvqk, preferred_element_type=jnp.float32)

time: 335 us -> 274 us (0.82)
  the two profiles are of different devices: /device:TPU:9 before, /device:TPU:0 now
where the time goes in v2:
time: 274 us; the launch traced here: 273 us
  waiting for transfers between devices  130 us (47%)
  local copies, waits for them, and re-layouts  47.6 us (17%)
  other arithmetic  30.5 us (11%)
  starting transfers between devices  28.3 us (10%)
  Pallas kernels  25.9 us (9%)
  matrix products  10.5 us (4%)
    all_to_all x1, waiting for transfers between devices, local(): lax.all_to_all(outgoing, 'req', split_axis=0, concat_axis=0, tiled=True)  69.8 us
    all_to_all x1, waiting for transfers between devices, local(): lax.all_to_all(by_head, 'hist', split_axis=0, concat_axis=0, tiled=True)  53.6 us
    pallas_call x1, Pallas kernels, attend(): pl.pallas_call(functools.partial(attend_kernel, score_scale=score_scale,...  25.9 us
    select_n x1, local copies, waits for them, and re-layouts, local(): outgoing = jnp.take(kv_by_head, source_slot, axis=0).transpose(0, 2, 1, 3)  9.07 us
    slice x1, other arithmetic, local(): queries = projected[:, :, 2]  8.99 us
    all_to_all x1, starting transfers between devices, local(): lax.all_to_all(history_mine.reshape(hist_count, cand_rows, head_dim), 'hi...  8.19 us
    all_to_all x1, starting transfers between devices, local(): lax.all_to_all(q_by_head, 'hist', split_axis=0, concat_axis=0, tiled=True)  7.97 us
    select_n x2, other arithmetic, local(): outgoing = jnp.take(kv_by_head, source_slot, axis=0).transpose(0, 2, 1, 3)  7.47 us
  transfers between devices with their start and end apart: 4, of which 4 were waited for; matrix products, arithmetic and copies ran while one was open for 16% of the time, Pallas kernels for 0%

profile of v2, /device:TPU:0, one launch (start us, length us, event | category | flops | bytes accessed | tf_op | source)
XLA Modules:
  0.0 272.8 jit_solution(12890303815596922291)
XLA Ops:
  0.0 0.0 copy-start
  0.0 0.9 reshape.394
  0.9 0.4 dynamic-slice_reduce_fusion
  1.4 0.1 reshape.395
  1.5 0.1 broadcast_in_dim.93
  1.6 0.1 eq.97
  1.6 0.2 select_reduce_fusion
  1.9 0.1 select_reduce_fusion.1
  2.0 0.1 copy.62
  2.1 0.1 reshape.398
  2.2 0.1 reshape.396
  2.3 5.7 %copy.74 = bf16[128,8,8,256]{3,2,1,0:T(8,128)(2,1)} copy(bf16[128,8,8,256]{3,1,2,0:T(8,128)(2,1)} %bitcast.56) | data formatting | bytes 8388608
  7.9 6.8 %gather_fusion = bf16[16,128,8,256]{3,2,1,0:T(8,128)(2,1)} fusion(bf16[8,128,8,256]{3,2,1,0:T(8,128)(2,1)} %bitcast.50, s32[1024]{0:T(1024)S(1)} %pad_clamp_fusion.1), kind=kCustom, calls=%fused_computation | custom fusion | bytes 16777280 | tf_op jit(solution)/shard_map/jit(_take)/gather | solution.py:109
  14.8 7.5 %select_bitcast_fusion = bf16[16,8,128,256]{3,1,2,0:T(8,128)(2,1)} fusion(bf16[16,128,8,256]{3,2,1,0:T(8,128)(2,1)} %gather_fusion, pred[16]{0:T(512)(128)(4,1)S(1)} %compare_and_fusion), kind=kLoop, calls=%fused_computation.2 | loop fusion | flops 4194304 | bytes 16777232 | tf_op jit(solution)/shard_map/jit(_take)/select_n | solution.py:109
  22.3 9.1 %copy.64 = bf16[16,8,128,256]{3,2,1,0:T(8,128)(2,1)} copy(bf16[16,8,128,256]{3,1,2,0:T(8,128)(2,1)} %select_bitcast_fusion) | data formatting | bytes 16777216 | tf_op jit(solution)/shard_map/jit(_take)/select_n | solution.py:109
  31.3 0.0 copy-start.1
  31.3 5.1 %all-to-all-start.1 = ((bf16[8,2,8,128,256]{4,3,2,1,0:T(8,128)(2,1)}), bf16[8,2,8,128,256]{4,3,2,1,0:T(8,128)(2,1)}, u32[]{:S(2)}, u32[]{:S(2)}) async-start(bf16[8,2,8,128,256]{4,3,2,1,0:T(8,128)(2,1)} %bitcast.51), calls=%async_computation.1 | async-start | bytes 16777216 | tf_op jit(solution)/shard_map/all_to_all | solution.py:111
  36.4 0.0 copy-done.1
  36.4 0.1 convert_reduce_fusion
  36.6 0.3 fusion.12
  36.9 0.3 fusion.13
  37.2 7.2 %multiply_convert_fusion = bf16[256,4096]{1,0:T(8,128)(2,1)} fusion(bf16[256,1024]{1,0:T(8,128)(2,1)S(1)} %bitcast.61, bf16[1024,4096]{1,0:T(8,128)(2,1)} %param.11), kind=kOutput, calls=%fused_computation.3 | convolution fusion | flops 2152726528 | bytes 11010048 | tf_op jit(solution)/shard_map/dot_general | solution.py:120
  44.3 4.5 %reshape.391 = bf16[2,128,4,1024]{3,2,1,0:T(4,128)(2,1)} reshape(bf16[256,4096]{1,0:T(8,128)(2,1)} %multiply_convert_fusion) | data formatting | bytes 4194304 | tf_op jit(solution)/shard_map/reshape | solution.py:121
  48.8 9.0 %fusion.24 = (bf16[2,128,1,1024]{3,2,1,0:T(2,128)(2,1)}, f32[2,128,1,1024]{3,2,1,0:T(1,128)}, f32[2,128,1,1024]{3,2,1,0:T(1,128)}, bf16[2,128,1,1024]{3,2,1,0:T(2,128)(2,1)}) fusion(bf16[2,128,4,1024]{3,2,1,0:T(4,128)(2,1)} %reshape.391), kind=kLoop, calls=%fused_computation.64 | loop fusion | flops 524288 | bytes 5242880 | tf_op jit(solution)/shard_map/slice | solution.py:124
  57.8 2.4 copy.59
  60.2 1.0 copy.60
  61.3 69.8 %all-to-all-done.1 = bf16[8,2,8,128,256]{4,3,2,1,0:T(8,128)(2,1)} async-done(((bf16[8,2,8,128,256]{4,3,2,1,0:T(8,128)(2,1)}), bf16[8,2,8,128,256]{4,3,2,1,0:T(8,128)(2,1)}, u32[]{:S(2)}, u32[]{:S(2)}) %all-to-all-start.1) | async-done | bytes 8388640 | tf_op jit(solution)/shard_map/all_to_all | solution.py:111
  131.0 8.0 %all-to-all-start = ((bf16[16,128,128]{2,1,0:T(8,128)(2,1)}), bf16[16,128,128]{2,1,0:T(8,128)(2,1)S(1)}, u32[]{:S(2)}, u32[]{:S(2)}) async-start(bf16[16,128,128]{2,1,0:T(8,128)(2,1)} %copy.60), calls=%async_computation | async-start | bytes 1048576 | tf_op jit(solution)/shard_map/all_to_all | solution.py:128
  139.0 0.1 dynamic-slice_add_fusion
  139.1 0.1 reshape.401
  139.2 0.1 reshape.419
  139.3 6.2 %gather_fusion.1 = bf16[8,8,128,256]{3,2,1,0:T(8,128)(2,1)} fusion(bf16[16,8,128,256]{3,2,1,0:T(8,128)(2,1)} %bitcast.8, s32[1024]{0:T(1024)S(1)} %pad_clamp_fusion), kind=kCustom, calls=%fused_computation.1 | custom fusion | bytes 8388640 | tf_op jit(solution)/shard_map/gather | solution.py:116
  145.5 4.7 %copy.65 = bf16[2,8,4,128,256]{4,3,2,1,0:T(8,128)(2,1)} copy(bf16[2,8,4,128,256]{4,3,1,2,0:T(8,128)(2,1)} %bitcast.53) | data formatting | bytes 8388608 | tf_op jit(solution)/shard_map/transpose | solution.py:117
  150.1 0.2 all-to-all-done
  150.3 0.0 copy-start.2
  150.3 0.0 copy-start.6
  150.3 0.0 copy-start.3
  150.3 0.0 copy-start.4
  150.3 0.8 copy-done.2
  151.1 7.1 %all-to-all-start.2 = ((bf16[16,4,128,256]{3,2,1,0:T(8,128)(2,1)}), bf16[16,4,128,256]{3,2,1,0:T(8,128)(2,1)}, u32[]{:S(2)}, u32[]{:S(2)}) async-start(bf16[16,4,128,256]{3,2,1,0:T(8,128)(2,1)} %bitcast.52), calls=%async_computation.2 | async-start | bytes 8388608 | tf_op jit(solution)/shard_map/all_to_all | solution.py:118
  158.2 0.0 copy-done.6
  158.2 0.1 dynamic_slice.16
  158.3 0.0 copy-done.3
  158.3 0.0 copy-done.4
  158.3 0.2 select_reduce_fusion.3
  158.5 0.6 dynamic_slice.17.len_ref
  159.0 53.6 %all-to-all-done.2.kv_ref = bf16[16,4,128,256]{3,2,1,0:T(8,128)(2,1)} async-done(((bf16[16,4,128,256]{3,2,1,0:T(8,128)(2,1)}), bf16[16,4,128,256]{3,2,1,0:T(8,128)(2,1)}, u32[]{:S(2)}, u32[]{:S(2)}) %all-to-all-start.2) | async-done | bytes 4194336 | tf_op jit(solution)/shard_map/all_to_all | solution.py:118
  212.6 25.9 %shard_map.91 = f32[2048,128]{1,0:T(8,128)} custom-call(s32[1]{0:T(128)} %dynamic_slice.17.len_ref, bf16[2048,128]{1,0:T(8,128)(2,1)} %bitcast.60, bf16[16,4,128,256]{3,2,1,0:T(8,128)(2,1)} %all-to-all-done.2.kv_ref), custom_call_target="tpu_custom_call" | custom-call | tf_op jit(solution)/shard_map/pallas_call | solution.py:58
  238.5 0.0 copy-start.5
  238.5 8.2 %all-to-all-start.3 = ((f32[16,128,128]{2,1,0:T(8,128)}), f32[16,128,128]{2,1,0:T(8,128)}, u32[]{:S(2)}, u32[]{:S(2)}) async-start(f32[16,128,128]{2,1,0:T(8,128)} %bitcast.58), calls=%async_computation.3 | async-start | bytes 2097152 | tf_op jit(solution)/shard_map/all_to_all | solution.py:133
  246.7 2.5 copy_convert_fusion
  249.2 2.5 copy.70
  251.8 1.3 multiply_reduce_fusion.1
  253.1 0.0 copy-done.5
  253.1 0.1 divide_multiply_fusion
  253.2 0.1 copy.69
  253.4 0.1 broadcast_compare_fusion
  253.4 6.3 %all-to-all-done.3 = f32[16,128,128]{2,1,0:T(8,128)} async-done(((f32[16,128,128]{2,1,0:T(8,128)}), f32[16,128,128]{2,1,0:T(8,128)}, u32[]{:S(2)}, u32[]{:S(2)}) %all-to-all-start.3) | async-done | bytes 1048608 | tf_op jit(solution)/shard_map/all_to_all | solution.py:133
  259.7 5.1 %fusion.22 = (f32[2,128]{1,0:T(2,128)S(1)}, f32[2,128,8,128]{3,2,1,0:T(8,128)S(1)}) fusion(f32[2]{0:T(128)S(1)} %add_convert_fusion, f32[2,128,8,128]{3,2,1,0:T(8,128)} %bitcast.59, f32[2,128,8]{2,1,0:T(8,128)S(1)} %copy.69, f32[2,8,128,128]{3,2,1,0:T(8,128)} %bitcast.13), kind=kLoop, calls=%fused_computation.63 | loop fusion | flops 1048320 | bytes 3154952 | tf_op jit(solution)/shard_map/reduce_sum | solution.py:13
  264.8 1.2 reshape.405
  266.0 3.5 %multiply_reduce_fusion = f32[2,128]{1,0:T(2,128)S(1)} fusion(f32[2,128,8,128]{3,2,1,0:T(8,128)S(1)} %get-tuple-element.8, f32[2,128]{1,0:T(2,128)S(1)} %broadcast_multiply_fusion), kind=kLoop, calls=%fused_computation.21 | loop fusion | flops 786176 | bytes 1050624 | tf_op jit(solution)/shard_map/reduce_sum | solution.py:15
  269.5 0.0 copy-done
  269.5 3.3 %fusion.7 = bf16[2,128,1024]{2,1,0:T(8,128)(2,1)} fusion(bf16[1024,1024]{1,0:T(8,128)(2,1)S(1)} %copy-done, bf16[2,128,1024]{2,1,0:T(8,128)(2,1)} %param.9, f32[2,128,1,1024]{3,2,1,0:T(1,128)} %get-tuple-element.12, f32[2,128,1024]{2,1,0:T(8,128)} %reshape.405, f32[2,128]{1,0:T(2,128)S(1)} %add_rsqrt_fusion, f32[2,128]{1,0:T(2,128)S(1)} %broadcast_multiply_fusion, ...), kind=kOutput, calls=%fused_computation.10 | convolution fusion | flops 538968064 | bytes 5245184 | tf_op jit(solution)/shard_map/dot_general | solution.py:147
  (16 shorter events, 0.1 us)
Async XLA Ops:
  0.0 269.5 %copy-start = (bf16[1024,1024]{1,0:T(8,128)(2,1)S(1)}, bf16[1024,1024]{1,0:T(8,128)(2,1)}, u32[]{:S(2)}) copy-start(bf16[1024,1024]{1,0:T(8,128)(2,1)} %param.12) | copy-start | bytes 6291460
  31.3 5.1 %copy-start.1 = (bf16[2,128,1024]{2,1,0:T(8,128)(2,1)S(1)}, bf16[2,128,1024]{2,1,0:T(8,128)(2,1)}, u32[]{:S(2)}) copy-start(bf16[2,128,1024]{2,1,0:T(8,128)(2,1)} %param.9) | copy-start | bytes 1572868
  31.3 99.7 %all-to-all-start.1 = ((bf16[8,2,8,128,256]{4,3,2,1,0:T(8,128)(2,1)}), bf16[8,2,8,128,256]{4,3,2,1,0:T(8,128)(2,1)}, u32[]{:S(2)}, u32[]{:S(2)}) async-start(bf16[8,2,8,128,256]{4,3,2,1,0:T(8,128)(2,1)} %bitcast.51), calls=%async_computation.1 | async-start | bytes 16777216 | tf_op jit(solution)/shard_map/all_to_all | solution.py:111
  131.0 19.3 %all-to-all-start = ((bf16[16,128,128]{2,1,0:T(8,128)(2,1)}), bf16[16,128,128]{2,1,0:T(8,128)(2,1)S(1)}, u32[]{:S(2)}, u32[]{:S(2)}) async-start(bf16[16,128,128]{2,1,0:T(8,128)(2,1)} %copy.60), calls=%async_computation | async-start | bytes 1048576 | tf_op jit(solution)/shard_map/all_to_all | solution.py:128
  150.3 0.8 copy-start.2
  150.3 7.9 %copy-start.6 = (s32[16]{0:T(128)S(1)}, s32[16]{0:T(128)}, u32[]{:S(2)}) copy-start(s32[16]{0:T(128)} %param.14) | copy-start | bytes 196
  150.3 8.0 %copy-start.3 = (s32[16]{0:T(128)S(1)}, s32[16]{0:T(128)}, u32[]{:S(2)}) copy-start(s32[16]{0:T(128)} %param.16) | copy-start | bytes 196
  150.3 8.0 %copy-start.4 = (s32[16]{0:T(128)S(1)}, s32[16]{0:T(128)}, u32[]{:S(2)}) copy-start(s32[16]{0:T(128)} %param.15) | copy-start | bytes 196
  151.1 61.5 %all-to-all-start.2 = ((bf16[16,4,128,256]{3,2,1,0:T(8,128)(2,1)}), bf16[16,4,128,256]{3,2,1,0:T(8,128)(2,1)}, u32[]{:S(2)}, u32[]{:S(2)}) async-start(bf16[16,4,128,256]{3,2,1,0:T(8,128)(2,1)} %bitcast.52), calls=%async_computation.2 | async-start | bytes 8388608 | tf_op jit(solution)/shard_map/all_to_all | solution.py:118
  238.5 14.6 %copy-start.5 = (f32[8]{0:T(128)S(1)}, f32[8]{0:T(128)}, u32[]{:S(2)}) copy-start(f32[8]{0:T(128)} %param.13) | copy-start | bytes 100
  238.5 21.2 %all-to-all-start.3 = ((f32[16,128,128]{2,1,0:T(8,128)}), f32[16,128,128]{2,1,0:T(8,128)}, u32[]{:S(2)}, u32[]{:S(2)}) async-start(f32[16,128,128]{2,1,0:T(8,128)} %bitcast.58), calls=%async_computation.3 | async-start | bytes 2097152 | tf_op jit(solution)/shard_map/all_to_all | solution.py:133

commit v3 on v2

--- a/solution.py
+++ b/solution.py
@@ -20,12 +20,13 @@
     return values * (0.5 + 0.5 * jnp.tanh(0.5 * values))
 
 
-def attend_kernel(len_ref, q_ref, kv_ref, o_ref, *, score_scale, chunk):
+def attend_kernel(len_ref, packed_ref, o_ref, q_ref, *, span, tile_len, score_scale, chunk):
     length = len_ref[0]
-    n_cls, n_tiles, tile_len, _ = kv_ref.shape
-    head_dim = q_ref.shape[1]
-    span = n_tiles * tile_len
+    n_cls, _, head_dim = packed_ref.shape
+    block = q_ref.shape[0] // n_cls
     half_scale = 0.5 * score_scale
+    for b in range(n_cls):
+        q_ref[pl.ds(b * block, block), :] = packed_ref[b, pl.ds(2 * span, block), :]
     o_ref[...] = jnp.zeros_like(o_ref)
 
     def one_class(c, carry):
@@ -35,8 +36,8 @@
 
         @pl.when(c * tile_len < length)
         def _():
-            keys = kv_ref[c, :, :, pl.ds(0, head_dim)].reshape(span, head_dim)
-            values = kv_ref[c, :, :, pl.ds(head_dim, head_dim)].reshape(span, head_dim)
+            keys = packed_ref[c, pl.ds(0, span), :]
+            values = packed_ref[c, pl.ds(span, span), :]
             for ci in range(q_ref.shape[0] // chunk):
                 rows = pl.ds(ci * chunk, chunk)
                 scores = lax.dot_general(
@@ -52,19 +53,24 @@
     lax.fori_loop(0, n_cls, one_class, 0)
 
 
-def attend(length, q_all, head_tiles, score_scale):
-    rows, head_dim = q_all.shape
+def attend(length, packed, per_hist, tile_len, score_scale):
+    span = per_hist * tile_len
+    n_cls, packed_rows, head_dim = packed.shape
+    rows = n_cls * (packed_rows - 2 * span)
     chunk = 512
+    kernel = functools.partial(
+        attend_kernel, span=span, tile_len=tile_len, score_scale=score_scale, chunk=chunk
+    )
     return pl.pallas_call(
-        functools.partial(attend_kernel, score_scale=score_scale, chunk=chunk),
+        kernel,
         out_shape=jax.ShapeDtypeStruct((rows, head_dim), jnp.float32),
         in_specs=[
             pl.BlockSpec(memory_space=pltpu.SMEM),
             pl.BlockSpec(memory_space=pltpu.VMEM),
-            pl.BlockSpec(memory_space=pltpu.VMEM),
         ],
         out_specs=pl.BlockSpec(memory_space=pltpu.VMEM),
-    )(length, q_all, head_tiles)
+        scratch_shapes=[pltpu.VMEM((rows, head_dim), jnp.bfloat16)],
+    )(length, packed)
 
 
 def local(cand_x, kv_cache, w_uvqk, w_out, self_bias, user_rank, hist_len, cand_count, tile_slot):
@@ -105,17 +111,17 @@
         & (places[None, None, :] == jnp.arange(capacity)[None, :, None])
     )
     source_slot = jnp.sum(jnp.where(picked, local_slot[None, None, :], 0), axis=2).reshape(-1)
-    kv_by_head = kv_cache.reshape(slots_own, tile_len, heads, 2 * head_dim)
-    outgoing = jnp.take(kv_by_head, source_slot, axis=0).transpose(0, 2, 1, 3)
-    outgoing = outgoing.reshape(req_count, capacity, heads, tile_len, 2 * head_dim)
+    outgoing = kv_cache.at[source_slot].get(mode="promise_in_bounds")
+    outgoing = outgoing.reshape(req_count, capacity, tile_len, 2 * width)
     incoming = lax.all_to_all(outgoing, "req", split_axis=0, concat_axis=0, tiled=True)
     first_entry = first_slot * per_hist
     my_owner = lax.dynamic_slice_in_dim(owners, first_entry, users_here * per_hist)
     my_place = lax.dynamic_slice_in_dim(places, first_entry, users_here * per_hist)
-    picked_slot = (my_owner * capacity + my_place).reshape(users_here, per_hist)
-    tiles = incoming.reshape(req_count * capacity, heads, tile_len, 2 * head_dim)[picked_slot]
-    by_head = tiles.transpose(0, 2, 1, 3, 4).reshape(users_here * heads, per_hist, tile_len, 2 * head_dim)
-    head_tiles = lax.all_to_all(by_head, "hist", split_axis=0, concat_axis=0, tiled=True)
+    picked_slot = my_owner * capacity + my_place
+    tiles = incoming.reshape(req_count * capacity, tile_len, 2 * width)
+    tiles = tiles.at[picked_slot].get(mode="promise_in_bounds")
+    tiles = tiles.reshape(users_here, per_hist, tile_len, heads, 2, head_dim)
+    by_head = tiles.transpose(0, 3, 4, 1, 2, 5).reshape(users_here * heads, 2 * per_hist * tile_len, head_dim)
     normed = layer_norm(cand_x.astype(jnp.float32)).astype(jnp.bfloat16)
     mixed_in = jnp.dot(normed.reshape(-1, width), w_uvqk, preferred_element_type=jnp.float32)
     projected = jax.nn.silu(mixed_in).astype(jnp.bfloat16).reshape(users_here, cand_rows, 4, width)
@@ -125,11 +131,12 @@
     k_self = projected[:, :, 3]
     q_by_head = queries.reshape(users_here, cand_rows, heads, head_dim).transpose(0, 2, 1, 3)
     q_by_head = q_by_head.reshape(users_here * heads, cand_rows, head_dim)
-    q_all = lax.all_to_all(q_by_head, "hist", split_axis=0, concat_axis=0, tiled=True)
-    q_all = q_all.reshape(hist_count * cand_rows, head_dim)
+    packed = lax.all_to_all(
+        jnp.concatenate([by_head, q_by_head], axis=1), "hist", split_axis=0, concat_axis=0, tiled=True
+    )
     my_user = hist_index // heads
     my_length = lax.dynamic_slice_in_dim(lengths, my_user, 1)
-    history_mine = attend(my_length, q_all, head_tiles, score_scale)
+    history_mine = attend(my_length, packed, per_hist, tile_len, score_scale)
     history_back = lax.all_to_all(
         history_mine.reshape(hist_count, cand_rows, head_dim), "hist", split_axis=0, concat_axis=0, tiled=True
     )

time: 274 us -> 278 us (1.015)
  the two profiles are of different devices: /device:TPU:0 before, /device:TPU:8 now
where the time goes in v3:
time: 278 us; the launch traced here: 275 us
  waiting for transfers between devices  157 us (56%)
  local copies, waits for them, and re-layouts  39.1 us (14%)
  Pallas kernels  26.1 us (9%)
  other arithmetic  24.3 us (9%)
  starting transfers between devices  18 us (6%)
  matrix products  10.5 us (4%)
    all_to_all x1, waiting for transfers between devices, local(): lax.all_to_all(jnp.concatenate([by_head, q_by_head], axis=1), 'hist', spl...  72.3 us
    all_to_all x1, waiting for transfers between devices, local(): lax.all_to_all(outgoing, 'req', split_axis=0, concat_axis=0, tiled=True)  68.9 us
    pallas_call x1, Pallas kernels, attend(): pl.pallas_call(kernel, out_shape=jax.ShapeDtypeStruct((rows, head_dim), j...  26.1 us
    all_to_all x1, waiting for transfers between devices, local(): lax.all_to_all(history_mine.reshape(hist_count, cand_rows, head_dim), 'hi...  16.1 us
    gather x2, local copies, waits for them, and re-layouts, local(): tiles = tiles.at[picked_slot].get(mode='promise_in_bounds')  12.6 us
    slice x1, other arithmetic, local(): u_gate = projected[:, :, 0]  9.18 us
    all_to_all x1, starting transfers between devices, local(): lax.all_to_all(jnp.concatenate([by_head, q_by_head], axis=1), 'hist', spl...  8.14 us
    dot_general x1, matrix products, local(): jnp.dot(normed.reshape(-1, width), w_uvqk, preferred_element_type=jnp.flo...  7.15 us
  transfers between devices with their start and end apart: 3, of which 3 were waited for; matrix products, arithmetic and copies ran while one was open for 10% of the time, Pallas kernels for 0%

profile of v3, /device:TPU:8, one launch (start us, length us, event | category | flops | bytes accessed | tf_op | source)
XLA Modules:
  0.0 275.4 jit_solution(16711330917031381507)
XLA Ops:
  0.0 0.0 copy-start
  0.0 0.9 reshape.348
  0.9 0.4 dynamic-slice_reduce_fusion
  1.4 0.1 reshape.349
  1.5 0.1 broadcast_in_dim.86
  1.6 0.1 eq.97
  1.6 0.2 select_reduce_fusion
  1.9 0.1 select_reduce_fusion.1
  2.0 0.1 copy.38
  2.1 0.1 reshape.350
  2.2 6.8 %gather_fusion = bf16[16,128,2048]{2,1,0:T(8,128)(2,1)} fusion(bf16[8,128,2048]{2,1,0:T(8,128)(2,1)} %param.10, s32[1024]{0:T(1024)S(1)} %pad_clamp_fusion.1), kind=kCustom, calls=%fused_computation | custom fusion | bytes 16777280 | tf_op jit(solution)/shard_map/gather | solution.py:114
  9.0 0.0 copy-start.1
  9.0 5.3 %all-to-all-start = ((bf16[8,2,128,2048]{3,2,1,0:T(8,128)(2,1)}), bf16[8,2,128,2048]{3,2,1,0:T(8,128)(2,1)}, u32[]{:S(2)}, u32[]{:S(2)}) async-start(bf16[8,2,128,2048]{3,2,1,0:T(8,128)(2,1)} %bitcast.42), calls=%async_computation | async-start | bytes 16777216 | tf_op jit(solution)/shard_map/all_to_all | solution.py:116
  14.4 0.0 copy-done.1
  14.4 0.1 convert_reduce_fusion
  14.5 0.3 fusion.12
  14.8 0.3 fusion.13
  15.1 7.2 %multiply_convert_fusion = bf16[256,4096]{1,0:T(8,128)(2,1)} fusion(bf16[256,1024]{1,0:T(8,128)(2,1)S(1)} %bitcast.51, bf16[1024,4096]{1,0:T(8,128)(2,1)} %param.11), kind=kOutput, calls=%fused_computation.3 | convolution fusion | flops 2152726528 | bytes 11010048 | tf_op jit(solution)/shard_map/dot_general | solution.py:126
  22.3 4.5 %reshape.356 = bf16[2,128,4,1024]{3,2,1,0:T(4,128)(2,1)} reshape(bf16[256,4096]{1,0:T(8,128)(2,1)} %multiply_convert_fusion) | data formatting | bytes 4194304 | tf_op jit(solution)/shard_map/reshape | solution.py:127
  26.8 9.2 %fusion.25 = (bf16[2,128,1,1024]{3,2,1,0:T(2,128)(2,1)}, bf16[2,128,1,1024]{3,2,1,0:T(2,128)(2,1)}, f32[2,128,1,1024]{3,2,1,0:T(1,128)}, bf16[2,128,1,1024]{3,2,1,0:T(2,128)(2,1)}) fusion(bf16[2,128,4,1024]{3,2,1,0:T(4,128)(2,1)} %reshape.356), kind=kLoop, calls=%fused_computation.61 | loop fusion | flops 262144 | bytes 4718592 | tf_op jit(solution)/shard_map/slice | solution.py:128
  35.9 2.4 copy.48
  38.4 0.3 copy.42
  38.6 0.1 compare_select_fusion
  38.7 68.9 %all-to-all-done = bf16[8,2,128,2048]{3,2,1,0:T(8,128)(2,1)} async-done(((bf16[8,2,128,2048]{3,2,1,0:T(8,128)(2,1)}), bf16[8,2,128,2048]{3,2,1,0:T(8,128)(2,1)}, u32[]{:S(2)}, u32[]{:S(2)}) %all-to-all-start) | async-done | bytes 8388640 | tf_op jit(solution)/shard_map/all_to_all | solution.py:116
  107.7 6.2 %gather_fusion.1 = bf16[8,128,2048]{2,1,0:T(8,128)(2,1)} fusion(bf16[16,128,2048]{2,1,0:T(8,128)(2,1)} %bitcast.2, s32[1024]{0:T(1024)S(1)} %pad_clamp_fusion), kind=kCustom, calls=%fused_computation.1 | custom fusion | bytes 8388640 | tf_op jit(solution)/shard_map/gather | solution.py:122
  113.8 6.4 %copy.39 = bf16[8,128,2048]{1,2,0:T(8,128)(2,1)} copy(bf16[8,128,2048]{2,1,0:T(8,128)(2,1)} %gather_fusion.1) | data formatting | bytes 8388608 | tf_op jit(solution)/shard_map/gather | solution.py:122
  120.3 6.2 %copy.40 = bf16[2,8,2,4,128,128]{5,4,3,2,1,0:T(8,128)(2,1)} copy(bf16[2,8,2,4,128,128]{4,5,2,1,3,0:T(8,128)(2,1)} %bitcast.44) | data formatting | bytes 8388608 | tf_op jit(solution)/shard_map/transpose | solution.py:124
  126.5 4.8 %pad_maximum_fusion = bf16[16,1152,128]{2,1,0:T(8,128)(2,1)} fusion(bf16[16,128,128]{2,1,0:T(8,128)(2,1)S(1)} %bitcast.49, bf16[16,1024,128]{2,1,0:T(8,128)(2,1)} %bitcast.43), kind=kLoop, calls=%fused_computation.2 | loop fusion | flops 9437184 | bytes 9437184 | tf_op jit(solution)/shard_map/concatenate | solution.py:135
  131.3 0.0 copy-start.5
  131.3 0.0 copy-start.2
  131.3 0.0 copy-start.3
  131.3 8.1 %all-to-all-start.1 = ((bf16[16,1152,128]{2,1,0:T(8,128)(2,1)}), bf16[16,1152,128]{2,1,0:T(8,128)(2,1)}, u32[]{:S(2)}, u32[]{:S(2)}) async-start(bf16[16,1152,128]{2,1,0:T(8,128)(2,1)} %pad_maximum_fusion), calls=%async_computation.1 | async-start | bytes 9437184 | tf_op jit(solution)/shard_map/all_to_all | solution.py:134
  139.5 0.0 copy-done.5
  139.5 0.1 dynamic_slice.16
  139.6 0.0 copy-done.2
  139.6 0.0 copy-done.3
  139.6 0.2 select_reduce_fusion.3
  139.8 0.6 dynamic_slice.17.len_ref
  140.4 0.0 copy-start.4
  140.4 72.3 %all-to-all-done.1.packed_ref = bf16[16,1152,128]{2,1,0:T(8,128)(2,1)} async-done(((bf16[16,1152,128]{2,1,0:T(8,128)(2,1)}), bf16[16,1152,128]{2,1,0:T(8,128)(2,1)}, u32[]{:S(2)}, u32[]{:S(2)}) %all-to-all-start.1) | async-done | bytes 4718624 | tf_op jit(solution)/shard_map/all_to_all | solution.py:134
  212.6 26.1 %shard_map.91 = f32[2048,128]{1,0:T(8,128)} custom-call(s32[1]{0:T(128)} %dynamic_slice.17.len_ref, bf16[16,1152,128]{2,1,0:T(8,128)(2,1)} %all-to-all-done.1.packed_ref), custom_call_target="tpu_custom_call" | custom-call | tf_op jit(solution)/shard_map/pallas_call | solution.py:64
  238.7 4.5 %all-to-all-start.2 = ((f32[16,128,128]{2,1,0:T(8,128)}), f32[16,128,128]{2,1,0:T(8,128)}, u32[]{:S(2)}, u32[]{:S(2)}) async-start(f32[16,128,128]{2,1,0:T(8,128)} %bitcast.47), calls=%async_computation.2 | async-start | bytes 2097152 | tf_op jit(solution)/shard_map/all_to_all | solution.py:140
  243.2 2.4 copy.49
  245.6 0.2 fusion.15
  245.8 0.0 copy-done.4
  245.8 0.1 divide_multiply_fusion
  245.9 0.1 copy.45
  246.1 0.1 broadcast_compare_fusion
  246.1 16.1 %all-to-all-done.2 = f32[16,128,128]{2,1,0:T(8,128)} async-done(((f32[16,128,128]{2,1,0:T(8,128)}), f32[16,128,128]{2,1,0:T(8,128)}, u32[]{:S(2)}, u32[]{:S(2)}) %all-to-all-start.2) | async-done | bytes 1048608 | tf_op jit(solution)/shard_map/all_to_all | solution.py:140
  262.3 5.1 %fusion.23 = (f32[2,128]{1,0:T(2,128)S(1)}, f32[2,128,8,128]{3,2,1,0:T(8,128)S(1)}) fusion(f32[2]{0:T(128)S(1)} %add_convert_fusion, f32[2,128,8,128]{3,2,1,0:T(8,128)} %bitcast.48, f32[2,128,8]{2,1,0:T(8,128)S(1)} %copy.45, f32[2,8,128,128]{3,2,1,0:T(8,128)} %bitcast.11), kind=kLoop, calls=%fused_computation.60 | loop fusion | flops 1048320 | bytes 3154952 | tf_op jit(solution)/shard_map/reduce_sum | solution.py:13
  267.4 1.2 reshape.360
  268.5 3.5 %multiply_reduce_fusion = f32[2,128]{1,0:T(2,128)S(1)} fusion(f32[2,128,8,128]{3,2,1,0:T(8,128)S(1)} %get-tuple-element.8, f32[2,128]{1,0:T(2,128)S(1)} %broadcast_multiply_fusion), kind=kLoop, calls=%fused_computation.22 | loop fusion | flops 786176 | bytes 1050624 | tf_op jit(solution)/shard_map/reduce_sum | solution.py:15
  272.1 0.0 copy-done
  272.1 3.3 %fusion.7 = bf16[2,128,1024]{2,1,0:T(8,128)(2,1)} fusion(bf16[1024,1024]{1,0:T(8,128)(2,1)S(1)} %copy-done, bf16[2,128,1024]{2,1,0:T(8,128)(2,1)} %param.9, f32[2,128,1024]{2,1,0:T(8,128)} %reshape.360, bf16[2,128,1,1024]{3,2,1,0:T(2,128)(2,1)} %get-tuple-element.11, f32[2,128]{1,0:T(2,128)S(1)} %add_rsqrt_fusion, f32[2,128]{1,0:T(2,128)S(1)} %broadcast_multiply_fusion, ...), kind=kOutput, calls=%fused_computation.10 | convolution fusion | flops 539230208 | bytes 4720896 | tf_op jit(solution)/shard_map/dot_general | solution.py:154
  (14 shorter events, 0.1 us)
Async XLA Ops:
  0.0 272.1 %copy-start = (bf16[1024,1024]{1,0:T(8,128)(2,1)S(1)}, bf16[1024,1024]{1,0:T(8,128)(2,1)}, u32[]{:S(2)}) copy-start(bf16[1024,1024]{1,0:T(8,128)(2,1)} %param.12) | copy-start | bytes 6291460
  9.0 5.3 %copy-start.1 = (bf16[2,128,1024]{2,1,0:T(8,128)(2,1)S(1)}, bf16[2,128,1024]{2,1,0:T(8,128)(2,1)}, u32[]{:S(2)}) copy-start(bf16[2,128,1024]{2,1,0:T(8,128)(2,1)} %param.9) | copy-start | bytes 1572868
  9.0 98.6 %all-to-all-start = ((bf16[8,2,128,2048]{3,2,1,0:T(8,128)(2,1)}), bf16[8,2,128,2048]{3,2,1,0:T(8,128)(2,1)}, u32[]{:S(2)}, u32[]{:S(2)}) async-start(bf16[8,2,128,2048]{3,2,1,0:T(8,128)(2,1)} %bitcast.42), calls=%async_computation | async-start | bytes 16777216 | tf_op jit(solution)/shard_map/all_to_all | solution.py:116
  131.3 8.2 %copy-start.5 = (s32[16]{0:T(128)S(1)}, s32[16]{0:T(128)}, u32[]{:S(2)}) copy-start(s32[16]{0:T(128)} %param.14) | copy-start | bytes 196
  131.3 8.3 %copy-start.2 = (s32[16]{0:T(128)S(1)}, s32[16]{0:T(128)}, u32[]{:S(2)}) copy-start(s32[16]{0:T(128)} %param.16) | copy-start | bytes 196
  131.3 8.3 %copy-start.3 = (s32[16]{0:T(128)S(1)}, s32[16]{0:T(128)}, u32[]{:S(2)}) copy-start(s32[16]{0:T(128)} %param.15) | copy-start | bytes 196
  131.3 81.3 %all-to-all-start.1 = ((bf16[16,1152,128]{2,1,0:T(8,128)(2,1)}), bf16[16,1152,128]{2,1,0:T(8,128)(2,1)}, u32[]{:S(2)}, u32[]{:S(2)}) async-start(bf16[16,1152,128]{2,1,0:T(8,128)(2,1)} %pad_maximum_fusion), calls=%async_computation.1 | async-start | bytes 9437184 | tf_op jit(solution)/shard_map/all_to_all | solution.py:134
  140.4 105.5 %copy-start.4 = (f32[8]{0:T(128)S(1)}, f32[8]{0:T(128)}, u32[]{:S(2)}) copy-start(f32[8]{0:T(128)} %param.13) | copy-start | bytes 100
  238.7 23.6 %all-to-all-start.2 = ((f32[16,128,128]{2,1,0:T(8,128)}), f32[16,128,128]{2,1,0:T(8,128)}, u32[]{:S(2)}, u32[]{:S(2)}) async-start(f32[16,128,128]{2,1,0:T(8,128)} %bitcast.47), calls=%async_computation.2 | async-start | bytes 2097152 | tf_op jit(solution)/shard_map/all_to_all | solution.py:140

commit v4 on v3

--- a/solution.py
+++ b/solution.py
@@ -71,6 +71,68 @@
         out_specs=pl.BlockSpec(memory_space=pltpu.VMEM),
         scratch_shapes=[pltpu.VMEM((rows, head_dim), jnp.bfloat16)],
     )(length, packed)
+
+
+def pack_kernel(picked_ref, tiles_hbm, q_hbm, out_hbm, staged, in_sem, out_sem, q_sem, *, heads, per_hist):
+    users, cand_rows, width = q_hbm.shape
+    head_dim = width // heads
+    tile_len = tiles_hbm.shape[1]
+    span = per_hist * tile_len
+    n_in = users * per_hist
+    reads = []
+    for i in range(n_in):
+        read = pltpu.make_async_copy(tiles_hbm.at[picked_ref[i]], staged.at[i], in_sem.at[i])
+        read.start()
+        reads.append(read)
+    writes = []
+    for u in range(users):
+        for e in range(heads):
+            write = pltpu.make_async_copy(
+                q_hbm.at[u, :, pl.ds(e * head_dim, head_dim)],
+                out_hbm.at[u * heads + e, pl.ds(2 * span, cand_rows), :],
+                q_sem.at[u * heads + e],
+            )
+            write.start()
+            writes.append(write)
+    for i in range(n_in):
+        u, t = divmod(i, per_hist)
+        reads[i].wait()
+        for piece in range(2 * heads):
+            e, kv = divmod(piece, 2)
+            write = pltpu.make_async_copy(
+                staged.at[i, :, pl.ds(piece * head_dim, head_dim)],
+                out_hbm.at[u * heads + e, pl.ds(kv * span + t * tile_len, tile_len), :],
+                out_sem.at[i, piece],
+            )
+            write.start()
+            writes.append(write)
+    for write in writes:
+        write.wait()
+
+
+def pack_for_heads(picked_slot, tiles, queries, heads):
+    users, cand_rows, width = queries.shape
+    head_dim = width // heads
+    n_in = picked_slot.shape[0]
+    per_hist = n_in // users
+    tile_len = tiles.shape[1]
+    rows = 2 * per_hist * tile_len + cand_rows
+    return pl.pallas_call(
+        functools.partial(pack_kernel, heads=heads, per_hist=per_hist),
+        out_shape=jax.ShapeDtypeStruct((users * heads, rows, head_dim), tiles.dtype),
+        in_specs=[
+            pl.BlockSpec(memory_space=pltpu.SMEM),
+            pl.BlockSpec(memory_space=pl.ANY),
+            pl.BlockSpec(memory_space=pl.ANY),
+        ],
+        out_specs=pl.BlockSpec(memory_space=pl.ANY),
+        scratch_shapes=[
+            pltpu.VMEM((n_in, tile_len, tiles.shape[2]), tiles.dtype),
+            pltpu.SemaphoreType.DMA((n_in,)),
+            pltpu.SemaphoreType.DMA((n_in, 2 * heads)),
+            pltpu.SemaphoreType.DMA((users * heads,)),
+        ],
+    )(picked_slot, tiles, queries)
 
 
 def local(cand_x, kv_cache, w_uvqk, w_out, self_bias, user_rank, hist_len, cand_count, tile_slot):
@@ -117,11 +179,7 @@
     first_entry = first_slot * per_hist
     my_owner = lax.dynamic_slice_in_dim(owners, first_entry, users_here * per_hist)
     my_place = lax.dynamic_slice_in_dim(places, first_entry, users_here * per_hist)
-    picked_slot = my_owner * capacity + my_place
-    tiles = incoming.reshape(req_count * capacity, tile_len, 2 * width)
-    tiles = tiles.at[picked_slot].get(mode="promise_in_bounds")
-    tiles = tiles.reshape(users_here, per_hist, tile_len, heads, 2, head_dim)
-    by_head = tiles.transpose(0, 3, 4, 1, 2, 5).reshape(users_here * heads, 2 * per_hist * tile_len, head_dim)
+    picked_slot = (my_owner * capacity + my_place).astype(jnp.int32)
     normed = layer_norm(cand_x.astype(jnp.float32)).astype(jnp.bfloat16)
     mixed_in = jnp.dot(normed.reshape(-1, width), w_uvqk, preferred_element_type=jnp.float32)
     projected = jax.nn.silu(mixed_in).astype(jnp.bfloat16).reshape(users_here, cand_rows, 4, width)
@@ -129,11 +187,10 @@
     v_self = projected[:, :, 1]
     queries = projected[:, :, 2]
     k_self = projected[:, :, 3]
-    q_by_head = queries.reshape(users_here, cand_rows, heads, head_dim).transpose(0, 2, 1, 3)
-    q_by_head = q_by_head.reshape(users_here * heads, cand_rows, head_dim)
-    packed = lax.all_to_all(
-        jnp.concatenate([by_head, q_by_head], axis=1), "hist", split_axis=0, concat_axis=0, tiled=True
-    )
+    send = pack_for_heads(
+        picked_slot, incoming.reshape(req_count * capacity, tile_len, 2 * width), queries, heads
+    )
+    packed = lax.all_to_all(send, "hist", split_axis=0, concat_axis=0, tiled=True)
     my_user = hist_index // heads
     my_length = lax.dynamic_slice_in_dim(lengths, my_user, 1)
     history_mine = attend(my_length, packed, per_hist, tile_len, score_scale)

time: 278 us -> 272 us (0.978)
  local copies, waits for them, and re-layouts: 39.1 us -> 16.3 us
  starting transfers between devices: 18 us -> 32.8 us
  Pallas kernels: 26.1 us -> 33.1 us
  other arithmetic: 24.3 us -> 21.5 us
    pallas_call x0 -> x1, Pallas kernels: none -> 19.2 us  [pack_for_heads(): pl.pallas_call(functools.partial(pack_kernel, heads=heads, per_hist=per_h...]
    all_to_all x1, starting transfers between devices: 4.52 us -> 19.3 us  [local(): lax.all_to_all(history_mine.reshape(hist_count, cand_rows, head_dim), 'hi...]
    gather x2 -> x0, local copies, waits for them, and re-layouts: 12.6 us -> none  [local(): tiles = tiles.at[picked_slot].get(mode='promise_in_bounds')]
    pallas_call x1, Pallas kernels: 26.1 us -> 13.8 us  [attend(): pl.pallas_call(kernel, out_shape=jax.ShapeDtypeStruct((rows, head_dim), j...]
    transpose x2 -> x0, local copies, waits for them, and re-layouts: 6.53 us -> none  [the longest x1 6.25 us: local(): tiles.transpose(0, 3, 4, 1, 2, 5)]
    concatenate x1 -> x0, other arithmetic: 4.8 us -> none  [local(): jnp.concatenate([by_head, q_by_head], axis=1)]
    unnamed x14, local copies, waits for them, and re-layouts: 4.86 us -> 1.19 us
where the time goes in v4:
time: 272 us
  waiting for transfers between devices  157 us (58%)
  Pallas kernels  33.1 us (12%)
  starting transfers between devices  32.8 us (12%)
  other arithmetic  21.5 us (8%)
  local copies, waits for them, and re-layouts  16.3 us (6%)
  matrix products  10.5 us (4%)
    all_to_all x1, waiting for transfers between devices, local(): lax.all_to_all(send, 'hist', split_axis=0, concat_axis=0, tiled=True)  72.3 us
    all_to_all x1, waiting for transfers between devices, local(): lax.all_to_all(outgoing, 'req', split_axis=0, concat_axis=0, tiled=True)  70.6 us
    all_to_all x1, starting transfers between devices, local(): lax.all_to_all(history_mine.reshape(hist_count, cand_rows, head_dim), 'hi...  19.3 us
    pallas_call x1, Pallas kernels, pack_for_heads(): pl.pallas_call(functools.partial(pack_kernel, heads=heads, per_hist=per_h...  19.2 us
    all_to_all x1, waiting for transfers between devices, local(): lax.all_to_all(history_mine.reshape(hist_count, cand_rows, head_dim), 'hi...  14.6 us
    pallas_call x1, Pallas kernels, attend(): pl.pallas_call(kernel, out_shape=jax.ShapeDtypeStruct((rows, head_dim), j...  13.8 us
    slice x1, other arithmetic, local(): queries = projected[:, :, 2]  8.81 us
    all_to_all x1, starting transfers between devices, local(): lax.all_to_all(send, 'hist', split_axis=0, concat_axis=0, tiled=True)  8.15 us
  transfers between devices with their start and end apart: 3, of which 3 were waited for; matrix products, arithmetic and copies ran while one was open for 10% of the time, Pallas kernels for 0%

profile of v4, /device:TPU:8, one launch (start us, length us, event | category | flops | bytes accessed | tf_op | source)
XLA Modules:
  0.0 271.8 jit_solution(10857660495650661222)
XLA Ops:
  0.0 0.0 copy-start
  0.0 0.9 reshape.340
  0.9 0.4 dynamic-slice_reduce_fusion
  1.4 0.1 reshape.341
  1.5 0.1 broadcast_in_dim.83
  1.6 0.1 eq.98
  1.6 0.2 select_reduce_fusion
  1.9 0.1 select_reduce_fusion.1
  2.0 0.1 copy.28
  2.1 0.1 reshape.342
  2.2 6.8 %gather_fusion = bf16[16,128,2048]{2,1,0:T(8,128)(2,1)} fusion(bf16[8,128,2048]{2,1,0:T(8,128)(2,1)} %param.10, s32[1024]{0:T(1024)S(1)} %pad_clamp_fusion), kind=kCustom, calls=%fused_computation | custom fusion | bytes 16777280 | tf_op jit(solution)/shard_map/gather | solution.py:176
  9.0 0.0 copy-start.1
  9.0 5.3 %all-to-all-start = ((bf16[8,2,128,2048]{3,2,1,0:T(8,128)(2,1)}), bf16[8,2,128,2048]{3,2,1,0:T(8,128)(2,1)}, u32[]{:S(2)}, u32[]{:S(2)}) async-start(bf16[8,2,128,2048]{3,2,1,0:T(8,128)(2,1)} %bitcast.42), calls=%async_computation | async-start | bytes 16777216 | tf_op jit(solution)/shard_map/all_to_all | solution.py:178
  14.4 0.0 copy-done.1
  14.4 0.1 convert_reduce_fusion
  14.5 0.3 fusion.12
  14.8 0.3 fusion.13
  15.1 7.2 %multiply_convert_fusion = bf16[256,4096]{1,0:T(8,128)(2,1)} fusion(bf16[256,1024]{1,0:T(8,128)(2,1)S(1)} %bitcast.48, bf16[1024,4096]{1,0:T(8,128)(2,1)} %param.11), kind=kOutput, calls=%fused_computation.1 | convolution fusion | flops 2152726528 | bytes 11010048 | tf_op jit(solution)/shard_map/dot_general | solution.py:184
  22.3 4.5 %reshape.346 = bf16[2,128,4,1024]{3,2,1,0:T(4,128)(2,1)} reshape(bf16[256,4096]{1,0:T(8,128)(2,1)} %multiply_convert_fusion) | data formatting | bytes 4194304 | tf_op jit(solution)/shard_map/reshape | solution.py:185
  26.8 8.8 %fusion.24 = (bf16[2,128,1,1024]{3,2,1,0:T(2,128)(2,1)S(1)}, f32[2,128,1,1024]{3,2,1,0:T(1,128)}, f32[2,128,1,1024]{3,2,1,0:T(1,128)}, bf16[2,128,1,1024]{3,2,1,0:T(2,128)(2,1)}) fusion(bf16[2,128,4,1024]{3,2,1,0:T(4,128)(2,1)} %reshape.346), kind=kLoop, calls=%fused_computation.59 | loop fusion | flops 524288 | bytes 5242880 | tf_op jit(solution)/shard_map/slice | solution.py:188
  35.6 1.0 copy.46
  36.5 0.6 dynamic-slice_add_fusion.picked_ref
  37.1 70.6 %all-to-all-done = bf16[8,2,128,2048]{3,2,1,0:T(8,128)(2,1)} async-done(((bf16[8,2,128,2048]{3,2,1,0:T(8,128)(2,1)}), bf16[8,2,128,2048]{3,2,1,0:T(8,128)(2,1)}, u32[]{:S(2)}, u32[]{:S(2)}) %all-to-all-start) | async-done | bytes 8388640 | tf_op jit(solution)/shard_map/all_to_all | solution.py:178
  107.7 19.2 %shard_map.91 = bf16[16,1152,128]{2,1,0:T(8,128)(2,1)} custom-call(s32[8]{0:T(128)} %dynamic-slice_add_fusion.picked_ref, bf16[16,128,2048]{2,1,0:T(8,128)(2,1)} %bitcast.2.tiles_hbm, bf16[2,128,1024]{2,1,0:T(8,128)(2,1)} %bitcast.47), custom_call_target="tpu_custom_call" | custom-call | tf_op jit(solution)/shard_map/pallas_call | solution.py:120
  126.9 0.0 copy-start.5
  126.9 0.0 copy-start.2
  126.9 0.0 copy-start.3
  126.9 8.1 %all-to-all-start.1 = ((bf16[16,1152,128]{2,1,0:T(8,128)(2,1)}), bf16[16,1152,128]{2,1,0:T(8,128)(2,1)}, u32[]{:S(2)}, u32[]{:S(2)}) async-start(bf16[16,1152,128]{2,1,0:T(8,128)(2,1)} %shard_map.91), calls=%async_computation.1 | async-start | bytes 9437184 | tf_op jit(solution)/shard_map/all_to_all | solution.py:193
  135.1 0.0 copy-done.5
  135.1 0.1 dynamic_slice.16
  135.2 0.0 copy-done.2
  135.2 0.0 copy-done.3
  135.2 0.2 select_reduce_fusion.3
  135.4 0.6 dynamic_slice.17.len_ref
  136.0 72.3 %all-to-all-done.1.packed_ref = bf16[16,1152,128]{2,1,0:T(8,128)(2,1)} async-done(((bf16[16,1152,128]{2,1,0:T(8,128)(2,1)}), bf16[16,1152,128]{2,1,0:T(8,128)(2,1)}, u32[]{:S(2)}, u32[]{:S(2)}) %all-to-all-start.1) | async-done | bytes 4718624 | tf_op jit(solution)/shard_map/all_to_all | solution.py:193
  208.3 13.8 %shard_map.92 = f32[2048,128]{1,0:T(8,128)} custom-call(s32[1]{0:T(128)} %dynamic_slice.17.len_ref, bf16[16,1152,128]{2,1,0:T(8,128)(2,1)} %all-to-all-done.1.packed_ref), custom_call_target="tpu_custom_call" | custom-call | tf_op jit(solution)/shard_map/pallas_call | solution.py:64
  222.1 0.0 copy-start.4
  222.1 19.3 %all-to-all-start.2 = ((f32[16,128,128]{2,1,0:T(8,128)}), f32[16,128,128]{2,1,0:T(8,128)}, u32[]{:S(2)}, u32[]{:S(2)}) async-start(f32[16,128,128]{2,1,0:T(8,128)} %bitcast.45), calls=%async_computation.2 | async-start | bytes 2097152 | tf_op jit(solution)/shard_map/all_to_all | solution.py:197
  241.4 1.7 convert_multiply_fusion
  243.1 0.2 copy.38
  243.3 0.3 bitcast_reduce_fusion
  243.7 0.1 copy.32
  243.7 0.0 copy-done.4
  243.7 0.1 divide_multiply_fusion
  243.8 0.1 copy.33
  244.0 0.1 broadcast_compare_fusion
  244.1 14.6 %all-to-all-done.2 = f32[16,128,128]{2,1,0:T(8,128)} async-done(((f32[16,128,128]{2,1,0:T(8,128)}), f32[16,128,128]{2,1,0:T(8,128)}, u32[]{:S(2)}, u32[]{:S(2)}) %all-to-all-start.2) | async-done | bytes 1048608 | tf_op jit(solution)/shard_map/all_to_all | solution.py:197
  258.7 5.1 %fusion.22 = (f32[2,128]{1,0:T(2,128)S(1)}, f32[2,128,8,128]{3,2,1,0:T(8,128)S(1)}) fusion(f32[2]{0:T(128)S(1)} %add_convert_fusion, f32[2,128,8,128]{3,2,1,0:T(8,128)} %bitcast.46, f32[2,128,8]{2,1,0:T(8,128)S(1)} %copy.33, f32[2,8,128,128]{3,2,1,0:T(8,128)} %bitcast.6), kind=kLoop, calls=%fused_computation.58 | loop fusion | flops 1048320 | bytes 3154952 | tf_op jit(solution)/shard_map/reduce_sum | solution.py:13
  263.8 1.2 reshape.349
  265.0 3.5 %multiply_reduce_fusion = f32[2,128]{1,0:T(2,128)S(1)} fusion(f32[2,128,8,128]{3,2,1,0:T(8,128)S(1)} %get-tuple-element.8, f32[2,128]{1,0:T(2,128)S(1)} %broadcast_multiply_fusion), kind=kLoop, calls=%fused_computation.20 | loop fusion | flops 786176 | bytes 1050624 | tf_op jit(solution)/shard_map/reduce_sum | solution.py:15
  268.5 0.0 copy-done
  268.5 3.3 %fusion.7 = bf16[2,128,1024]{2,1,0:T(8,128)(2,1)} fusion(bf16[1024,1024]{1,0:T(8,128)(2,1)S(1)} %copy-done, bf16[2,128,1024]{2,1,0:T(8,128)(2,1)} %param.9, f32[2,128,1,1024]{3,2,1,0:T(1,128)} %get-tuple-element.13, f32[2,128,1024]{2,1,0:T(8,128)} %reshape.349, f32[2,128]{1,0:T(2,128)S(1)} %add_rsqrt_fusion, f32[2,128]{1,0:T(2,128)S(1)} %broadcast_multiply_fusion, ...), kind=kOutput, calls=%fused_computation.8 | convolution fusion | flops 538968064 | bytes 5245184 | tf_op jit(solution)/shard_map/dot_general | solution.py:211
  (13 shorter events, 0.1 us)
Async XLA Ops:
  0.0 268.5 %copy-start = (bf16[1024,1024]{1,0:T(8,128)(2,1)S(1)}, bf16[1024,1024]{1,0:T(8,128)(2,1)}, u32[]{:S(2)}) copy-start(bf16[1024,1024]{1,0:T(8,128)(2,1)} %param.12) | copy-start | bytes 6291460
  9.0 5.3 %copy-start.1 = (bf16[2,128,1024]{2,1,0:T(8,128)(2,1)S(1)}, bf16[2,128,1024]{2,1,0:T(8,128)(2,1)}, u32[]{:S(2)}) copy-start(bf16[2,128,1024]{2,1,0:T(8,128)(2,1)} %param.9) | copy-start | bytes 1572868
  9.0 98.6 %all-to-all-start = ((bf16[8,2,128,2048]{3,2,1,0:T(8,128)(2,1)}), bf16[8,2,128,2048]{3,2,1,0:T(8,128)(2,1)}, u32[]{:S(2)}, u32[]{:S(2)}) async-start(bf16[8,2,128,2048]{3,2,1,0:T(8,128)(2,1)} %bitcast.42), calls=%async_computation | async-start | bytes 16777216 | tf_op jit(solution)/shard_map/all_to_all | solution.py:178
  126.9 8.2 %copy-start.5 = (s32[16]{0:T(128)S(1)}, s32[16]{0:T(128)}, u32[]{:S(2)}) copy-start(s32[16]{0:T(128)} %param.14) | copy-start | bytes 196
  126.9 8.3 %copy-start.2 = (s32[16]{0:T(128)S(1)}, s32[16]{0:T(128)}, u32[]{:S(2)}) copy-start(s32[16]{0:T(128)} %param.16) | copy-start | bytes 196
  126.9 8.3 %copy-start.3 = (s32[16]{0:T(128)S(1)}, s32[16]{0:T(128)}, u32[]{:S(2)}) copy-start(s32[16]{0:T(128)} %param.15) | copy-start | bytes 196
  126.9 81.3 %all-to-all-start.1 = ((bf16[16,1152,128]{2,1,0:T(8,128)(2,1)}), bf16[16,1152,128]{2,1,0:T(8,128)(2,1)}, u32[]{:S(2)}, u32[]{:S(2)}) async-start(bf16[16,1152,128]{2,1,0:T(8,128)(2,1)} %shard_map.91), calls=%async_computation.1 | async-start | bytes 9437184 | tf_op jit(solution)/shard_map/all_to_all | solution.py:193
  222.1 21.6 %copy-start.4 = (f32[8]{0:T(128)S(1)}, f32[8]{0:T(128)}, u32[]{:S(2)}) copy-start(f32[8]{0:T(128)} %param.13) | copy-start | bytes 100
  222.1 36.6 %all-to-all-start.2 = ((f32[16,128,128]{2,1,0:T(8,128)}), f32[16,128,128]{2,1,0:T(8,128)}, u32[]{:S(2)}, u32[]{:S(2)}) async-start(f32[16,128,128]{2,1,0:T(8,128)} %bitcast.45), calls=%async_computation.2 | async-start | bytes 2097152 | tf_op jit(solution)/shard_map/all_to_all | solution.py:197

commit v5 on v4

--- a/solution.py
+++ b/solution.py
@@ -34,8 +34,7 @@
         position = (c + n_cls * (key_index // tile_len)) * tile_len + key_index % tile_len
         live = position < length
 
-        @pl.when(c * tile_len < length)
-        def _():
+        def add_class(masked):
             keys = packed_ref[c, pl.ds(0, span), :]
             values = packed_ref[c, pl.ds(span, span), :]
             for ci in range(q_ref.shape[0] // chunk):
@@ -44,9 +43,16 @@
                     q_ref[rows, :], keys, (((1,), (1,)), ((), ())), preferred_element_type=jnp.float32
                 )
                 half = scores * half_scale
-                weights = jnp.where(live, half + half * jnp.tanh(half), 0.0).astype(jnp.bfloat16)
-                part = jnp.dot(weights, values, preferred_element_type=jnp.float32)
+                weights = half + half * jnp.tanh(half)
+                if masked:
+                    weights = jnp.where(live, weights, 0.0)
+                part = jnp.dot(weights.astype(jnp.bfloat16), values, preferred_element_type=jnp.float32)
                 o_ref[rows, :] += part.astype(jnp.bfloat16).astype(jnp.float32)
+
+        last_start = (c + n_cls * (span // tile_len - 1)) * tile_len
+        whole = last_start + tile_len <= length
+        pl.when(whole)(lambda: add_class(False))
+        pl.when(jnp.logical_and(jnp.logical_not(whole), c * tile_len < length))(lambda: add_class(True))
 
         return carry
 
@@ -73,8 +79,8 @@
     )(length, packed)
 
 
-def pack_kernel(picked_ref, tiles_hbm, q_hbm, out_hbm, staged, in_sem, out_sem, q_sem, *, heads, per_hist):
-    users, cand_rows, width = q_hbm.shape
+def pack_kernel(picked_ref, tiles_hbm, q_ref, out_ref, staged, in_sem, *, heads, per_hist):
+    users, cand_rows, width = q_ref.shape
     head_dim = width // heads
     tile_len = tiles_hbm.shape[1]
     span = per_hist * tile_len
@@ -84,30 +90,17 @@
         read = pltpu.make_async_copy(tiles_hbm.at[picked_ref[i]], staged.at[i], in_sem.at[i])
         read.start()
         reads.append(read)
-    writes = []
     for u in range(users):
         for e in range(heads):
-            write = pltpu.make_async_copy(
-                q_hbm.at[u, :, pl.ds(e * head_dim, head_dim)],
-                out_hbm.at[u * heads + e, pl.ds(2 * span, cand_rows), :],
-                q_sem.at[u * heads + e],
-            )
-            write.start()
-            writes.append(write)
+            out_ref[u * heads + e, pl.ds(2 * span, cand_rows), :] = q_ref[u, :, pl.ds(e * head_dim, head_dim)]
     for i in range(n_in):
         u, t = divmod(i, per_hist)
         reads[i].wait()
         for piece in range(2 * heads):
             e, kv = divmod(piece, 2)
-            write = pltpu.make_async_copy(
-                staged.at[i, :, pl.ds(piece * head_dim, head_dim)],
-                out_hbm.at[u * heads + e, pl.ds(kv * span + t * tile_len, tile_len), :],
-                out_sem.at[i, piece],
-            )
-            write.start()
-            writes.append(write)
-    for write in writes:
-        write.wait()
+            out_ref[u * heads + e, pl.ds(kv * span + t * tile_len, tile_len), :] = staged[
+                i, :, pl.ds(piece * head_dim, head_dim)
+            ]
 
 
 def pack_for_heads(picked_slot, tiles, queries, heads):
@@ -123,14 +116,12 @@
         in_specs=[
             pl.BlockSpec(memory_space=pltpu.SMEM),
             pl.BlockSpec(memory_space=pl.ANY),
-            pl.BlockSpec(memory_space=pl.ANY),
+            pl.BlockSpec(memory_space=pltpu.VMEM),
         ],
-        out_specs=pl.BlockSpec(memory_space=pl.ANY),
+        out_specs=pl.BlockSpec(memory_space=pltpu.VMEM),
         scratch_shapes=[
             pltpu.VMEM((n_in, tile_len, tiles.shape[2]), tiles.dtype),
             pltpu.SemaphoreType.DMA((n_in,)),
-            pltpu.SemaphoreType.DMA((n_in, 2 * heads)),
-            pltpu.SemaphoreType.DMA((users * heads,)),
         ],
     )(picked_slot, tiles, queries)
 

time: 272 us -> 257 us (0.945)
  starting transfers between devices: 32.8 us -> 22 us
  waiting for transfers between devices: 157 us -> 153 us
    pallas_call x1, Pallas kernels: 19.2 us -> 5.51 us  [pack_for_heads(): pl.pallas_call(functools.partial(pack_kernel, heads=heads, per_hist=per_h...]
    pallas_call x1, Pallas kernels: 13.8 us -> 26.2 us  [attend(): pl.pallas_call(kernel, out_shape=jax.ShapeDtypeStruct((rows, head_dim), j...]
    all_to_all x1, starting transfers between devices: 19.3 us -> 8.46 us  [local(): lax.all_to_all(history_mine.reshape(hist_count, cand_rows, head_dim), 'hi...]
    all_to_all x1, waiting for transfers between devices: 14.6 us -> 10.3 us  [local(): lax.all_to_all(history_mine.reshape(hist_count, cand_rows, head_dim), 'hi...]
where the time goes in v5:
time: 257 us; the launch traced here: 255 us
  waiting for transfers between devices  153 us (60%)
  Pallas kernels  31.7 us (12%)
  starting transfers between devices  22 us (9%)
  other arithmetic  21.5 us (8%)
  local copies, waits for them, and re-layouts  16.3 us (6%)
  matrix products  10.5 us (4%)
    all_to_all x1, waiting for transfers between devices, local(): lax.all_to_all(send, 'hist', split_axis=0, concat_axis=0, tiled=True)  72.3 us
    all_to_all x1, waiting for transfers between devices, local(): lax.all_to_all(outgoing, 'req', split_axis=0, concat_axis=0, tiled=True)  70.6 us
    pallas_call x1, Pallas kernels, attend(): pl.pallas_call(kernel, out_shape=jax.ShapeDtypeStruct((rows, head_dim), j...  26.2 us
    all_to_all x1, waiting for transfers between devices, local(): lax.all_to_all(history_mine.reshape(hist_count, cand_rows, head_dim), 'hi...  10.3 us
    slice x1, other arithmetic, local(): queries = projected[:, :, 2]  8.81 us
    all_to_all x1, starting transfers between devices, local(): lax.all_to_all(history_mine.reshape(hist_count, cand_rows, head_dim), 'hi...  8.46 us
    all_to_all x1, starting transfers between devices, local(): lax.all_to_all(send, 'hist', split_axis=0, concat_axis=0, tiled=True)  8.15 us
    dot_general x1, matrix products, local(): jnp.dot(normed.reshape(-1, width), w_uvqk, preferred_element_type=jnp.flo...  7.15 us
  transfers between devices with their start and end apart: 3, of which 3 were waited for; matrix products, arithmetic and copies ran while one was open for 10% of the time, Pallas kernels for 0%

profile of v5, /device:TPU:8, one launch (start us, length us, event | category | flops | bytes accessed | tf_op | source)
XLA Modules:
  0.0 255.3 jit_solution(11108322386423571174)
XLA Ops:
  0.0 0.0 copy-start
  0.0 0.9 reshape.340
  0.9 0.4 dynamic-slice_reduce_fusion
  1.4 0.1 reshape.341
  1.5 0.1 broadcast_in_dim.83
  1.6 0.1 eq.98
  1.6 0.2 select_reduce_fusion
  1.9 0.1 select_reduce_fusion.1
  2.0 0.1 copy.28
  2.1 0.1 reshape.342
  2.2 6.8 %gather_fusion = bf16[16,128,2048]{2,1,0:T(8,128)(2,1)} fusion(bf16[8,128,2048]{2,1,0:T(8,128)(2,1)} %param.10, s32[1024]{0:T(1024)S(1)} %pad_clamp_fusion), kind=kCustom, calls=%fused_computation | custom fusion | bytes 16777280 | tf_op jit(solution)/shard_map/gather | solution.py:167
  9.0 0.0 copy-start.1
  9.0 5.4 %all-to-all-start = ((bf16[8,2,128,2048]{3,2,1,0:T(8,128)(2,1)}), bf16[8,2,128,2048]{3,2,1,0:T(8,128)(2,1)}, u32[]{:S(2)}, u32[]{:S(2)}) async-start(bf16[8,2,128,2048]{3,2,1,0:T(8,128)(2,1)} %bitcast.42), calls=%async_computation | async-start | bytes 16777216 | tf_op jit(solution)/shard_map/all_to_all | solution.py:169
  14.4 0.0 copy-done.1
  14.4 0.1 convert_reduce_fusion
  14.5 0.3 fusion.12
  14.8 0.3 fusion.13
  15.1 7.2 %multiply_convert_fusion = bf16[256,4096]{1,0:T(8,128)(2,1)} fusion(bf16[256,1024]{1,0:T(8,128)(2,1)S(1)} %bitcast.48, bf16[1024,4096]{1,0:T(8,128)(2,1)} %param.11), kind=kOutput, calls=%fused_computation.1 | convolution fusion | flops 2152726528 | bytes 11010048 | tf_op jit(solution)/shard_map/dot_general | solution.py:175
  22.3 4.5 %reshape.346 = bf16[2,128,4,1024]{3,2,1,0:T(4,128)(2,1)} reshape(bf16[256,4096]{1,0:T(8,128)(2,1)} %multiply_convert_fusion) | data formatting | bytes 4194304 | tf_op jit(solution)/shard_map/reshape | solution.py:176
  26.8 8.8 %fusion.24 = (bf16[2,128,1,1024]{3,2,1,0:T(2,128)(2,1)S(1)}, f32[2,128,1,1024]{3,2,1,0:T(1,128)}, f32[2,128,1,1024]{3,2,1,0:T(1,128)}, bf16[2,128,1,1024]{3,2,1,0:T(2,128)(2,1)}) fusion(bf16[2,128,4,1024]{3,2,1,0:T(4,128)(2,1)} %reshape.346), kind=kLoop, calls=%fused_computation.59 | loop fusion | flops 524288 | bytes 5242880 | tf_op jit(solution)/shard_map/slice | solution.py:179
  35.6 1.0 copy.46
  36.5 0.6 dynamic-slice_add_fusion.picked_ref
  37.1 70.6 %all-to-all-done = bf16[8,2,128,2048]{3,2,1,0:T(8,128)(2,1)} async-done(((bf16[8,2,128,2048]{3,2,1,0:T(8,128)(2,1)}), bf16[8,2,128,2048]{3,2,1,0:T(8,128)(2,1)}, u32[]{:S(2)}, u32[]{:S(2)}) %all-to-all-start) | async-done | bytes 8388640 | tf_op jit(solution)/shard_map/all_to_all | solution.py:169
  107.7 5.5 %shard_map.91 = bf16[16,1152,128]{2,1,0:T(8,128)(2,1)} custom-call(s32[8]{0:T(128)} %dynamic-slice_add_fusion.picked_ref, bf16[16,128,2048]{2,1,0:T(8,128)(2,1)} %bitcast.2.tiles_hbm, bf16[2,128,1024]{2,1,0:T(8,128)(2,1)} %bitcast.47), custom_call_target="tpu_custom_call" | custom-call | tf_op jit(solution)/shard_map/pallas_call | solution.py:113
  113.2 0.0 copy-start.5
  113.2 0.0 copy-start.2
  113.2 0.0 copy-start.3
  113.2 8.1 %all-to-all-start.1 = ((bf16[16,1152,128]{2,1,0:T(8,128)(2,1)}), bf16[16,1152,128]{2,1,0:T(8,128)(2,1)}, u32[]{:S(2)}, u32[]{:S(2)}) async-start(bf16[16,1152,128]{2,1,0:T(8,128)(2,1)} %shard_map.91), calls=%async_computation.1 | async-start | bytes 9437184 | tf_op jit(solution)/shard_map/all_to_all | solution.py:184
  121.4 0.0 copy-done.5
  121.4 0.1 dynamic_slice.16
  121.5 0.0 copy-done.2
  121.5 0.0 copy-done.3
  121.5 0.2 select_reduce_fusion.3
  121.7 0.6 dynamic_slice.17.len_ref
  122.3 72.3 %all-to-all-done.1.packed_ref = bf16[16,1152,128]{2,1,0:T(8,128)(2,1)} async-done(((bf16[16,1152,128]{2,1,0:T(8,128)(2,1)}), bf16[16,1152,128]{2,1,0:T(8,128)(2,1)}, u32[]{:S(2)}, u32[]{:S(2)}) %all-to-all-start.1) | async-done | bytes 4718624 | tf_op jit(solution)/shard_map/all_to_all | solution.py:184
  194.5 26.2 %shard_map.92 = f32[2048,128]{1,0:T(8,128)} custom-call(s32[1]{0:T(128)} %dynamic_slice.17.len_ref, bf16[16,1152,128]{2,1,0:T(8,128)(2,1)} %all-to-all-done.1.packed_ref), custom_call_target="tpu_custom_call" | custom-call | tf_op jit(solution)/shard_map/pallas_call | solution.py:70
  220.7 0.0 copy-start.4
  220.7 8.5 %all-to-all-start.2 = ((f32[16,128,128]{2,1,0:T(8,128)}), f32[16,128,128]{2,1,0:T(8,128)}, u32[]{:S(2)}, u32[]{:S(2)}) async-start(f32[16,128,128]{2,1,0:T(8,128)} %bitcast.45), calls=%async_computation.2 | async-start | bytes 2097152 | tf_op jit(solution)/shard_map/all_to_all | solution.py:188
  229.2 1.7 convert_multiply_fusion
  230.9 0.2 copy.38
  231.1 0.3 bitcast_reduce_fusion
  231.5 0.1 copy.32
  231.5 0.0 copy-done.4
  231.5 0.1 divide_multiply_fusion
  231.6 0.1 copy.33
  231.8 0.1 broadcast_compare_fusion
  231.9 10.3 %all-to-all-done.2 = f32[16,128,128]{2,1,0:T(8,128)} async-done(((f32[16,128,128]{2,1,0:T(8,128)}), f32[16,128,128]{2,1,0:T(8,128)}, u32[]{:S(2)}, u32[]{:S(2)}) %all-to-all-start.2) | async-done | bytes 1048608 | tf_op jit(solution)/shard_map/all_to_all | solution.py:188
  242.2 5.1 %fusion.22 = (f32[2,128]{1,0:T(2,128)S(1)}, f32[2,128,8,128]{3,2,1,0:T(8,128)S(1)}) fusion(f32[2]{0:T(128)S(1)} %add_convert_fusion, f32[2,128,8,128]{3,2,1,0:T(8,128)} %bitcast.46, f32[2,128,8]{2,1,0:T(8,128)S(1)} %copy.33, f32[2,8,128,128]{3,2,1,0:T(8,128)} %bitcast.6), kind=kLoop, calls=%fused_computation.58 | loop fusion | flops 1048320 | bytes 3154952 | tf_op jit(solution)/shard_map/reduce_sum | solution.py:13
  247.3 1.2 reshape.349
  248.4 3.5 %multiply_reduce_fusion = f32[2,128]{1,0:T(2,128)S(1)} fusion(f32[2,128,8,128]{3,2,1,0:T(8,128)S(1)} %get-tuple-element.8, f32[2,128]{1,0:T(2,128)S(1)} %broadcast_multiply_fusion), kind=kLoop, calls=%fused_computation.20 | loop fusion | flops 786176 | bytes 1050624 | tf_op jit(solution)/shard_map/reduce_sum | solution.py:15
  252.0 0.0 copy-done
  252.0 3.3 %fusion.7 = bf16[2,128,1024]{2,1,0:T(8,128)(2,1)} fusion(bf16[1024,1024]{1,0:T(8,128)(2,1)S(1)} %copy-done, bf16[2,128,1024]{2,1,0:T(8,128)(2,1)} %param.9, f32[2,128,1,1024]{3,2,1,0:T(1,128)} %get-tuple-element.13, f32[2,128,1024]{2,1,0:T(8,128)} %reshape.349, f32[2,128]{1,0:T(2,128)S(1)} %add_rsqrt_fusion, f32[2,128]{1,0:T(2,128)S(1)} %broadcast_multiply_fusion, ...), kind=kOutput, calls=%fused_computation.8 | convolution fusion | flops 538968064 | bytes 5245184 | tf_op jit(solution)/shard_map/dot_general | solution.py:202
  (13 shorter events, 0.1 us)
Async XLA Ops:
  0.0 252.0 %copy-start = (bf16[1024,1024]{1,0:T(8,128)(2,1)S(1)}, bf16[1024,1024]{1,0:T(8,128)(2,1)}, u32[]{:S(2)}) copy-start(bf16[1024,1024]{1,0:T(8,128)(2,1)} %param.12) | copy-start | bytes 6291460
  9.0 5.4 %copy-start.1 = (bf16[2,128,1024]{2,1,0:T(8,128)(2,1)S(1)}, bf16[2,128,1024]{2,1,0:T(8,128)(2,1)}, u32[]{:S(2)}) copy-start(bf16[2,128,1024]{2,1,0:T(8,128)(2,1)} %param.9) | copy-start | bytes 1572868
  9.0 98.7 %all-to-all-start = ((bf16[8,2,128,2048]{3,2,1,0:T(8,128)(2,1)}), bf16[8,2,128,2048]{3,2,1,0:T(8,128)(2,1)}, u32[]{:S(2)}, u32[]{:S(2)}) async-start(bf16[8,2,128,2048]{3,2,1,0:T(8,128)(2,1)} %bitcast.42), calls=%async_computation | async-start | bytes 16777216 | tf_op jit(solution)/shard_map/all_to_all | solution.py:169
  113.2 8.2 %copy-start.5 = (s32[16]{0:T(128)S(1)}, s32[16]{0:T(128)}, u32[]{:S(2)}) copy-start(s32[16]{0:T(128)} %param.14) | copy-start | bytes 196
  113.2 8.3 %copy-start.2 = (s32[16]{0:T(128)S(1)}, s32[16]{0:T(128)}, u32[]{:S(2)}) copy-start(s32[16]{0:T(128)} %param.16) | copy-start | bytes 196
  113.2 8.3 %copy-start.3 = (s32[16]{0:T(128)S(1)}, s32[16]{0:T(128)}, u32[]{:S(2)}) copy-start(s32[16]{0:T(128)} %param.15) | copy-start | bytes 196
  113.2 81.3 %all-to-all-start.1 = ((bf16[16,1152,128]{2,1,0:T(8,128)(2,1)}), bf16[16,1152,128]{2,1,0:T(8,128)(2,1)}, u32[]{:S(2)}, u32[]{:S(2)}) async-start(bf16[16,1152,128]{2,1,0:T(8,128)(2,1)} %shard_map.91), calls=%async_computation.1 | async-start | bytes 9437184 | tf_op jit(solution)/shard_map/all_to_all | solution.py:184
  220.7 10.8 %copy-start.4 = (f32[8]{0:T(128)S(1)}, f32[8]{0:T(128)}, u32[]{:S(2)}) copy-start(f32[8]{0:T(128)} %param.13) | copy-start | bytes 100
  220.7 21.4 %all-to-all-start.2 = ((f32[16,128,128]{2,1,0:T(8,128)}), f32[16,128,128]{2,1,0:T(8,128)}, u32[]{:S(2)}, u32[]{:S(2)}) async-start(f32[16,128,128]{2,1,0:T(8,128)} %bitcast.45), calls=%async_computation.2 | async-start | bytes 2097152 | tf_op jit(solution)/shard_map/all_to_all | solution.py:188

commit v6 on v5

--- a/solution.py
+++ b/solution.py
@@ -20,23 +20,83 @@
     return values * (0.5 + 0.5 * jnp.tanh(0.5 * values))
 
 
-def attend_kernel(len_ref, packed_ref, o_ref, q_ref, *, span, tile_len, score_scale, chunk):
+def req_a2a_kernel(send_ref, recv_ref, send_sem, recv_sem, local_sem, *, axis, other_axis):
+    n = send_ref.shape[0]
+    me = lax.axis_index(axis)
+    other = lax.axis_index(other_axis)
+    barrier = pltpu.get_barrier_semaphore()
+    for k in range(1, n):
+        peer = lax.rem(me + k, n)
+        pl.semaphore_signal(
+            barrier, inc=1, device_id={axis: peer, other_axis: other}, device_id_type=pl.DeviceIdType.MESH
+        )
+    pl.semaphore_wait(barrier, n - 1)
+    copies = []
+    for k in range(1, n):
+        peer = lax.rem(me + k, n)
+        copy = pltpu.make_async_remote_copy(
+            src_ref=send_ref.at[peer],
+            dst_ref=recv_ref.at[me],
+            send_sem=send_sem.at[k],
+            recv_sem=recv_sem.at[k],
+            device_id={axis: peer, other_axis: other},
+            device_id_type=pl.DeviceIdType.MESH,
+        )
+        copy.start()
+        copies.append(copy)
+    own = pltpu.make_async_copy(send_ref.at[me], recv_ref.at[me], local_sem)
+    own.start()
+    own.wait()
+    for copy in copies:
+        copy.wait_send()
+    for k in range(1, n):
+        src = lax.rem(me + n - k, n)
+        pltpu.make_async_remote_copy(
+            src_ref=send_ref.at[src],
+            dst_ref=recv_ref.at[src],
+            send_sem=send_sem.at[k],
+            recv_sem=recv_sem.at[k],
+            device_id={axis: src, other_axis: other},
+            device_id_type=pl.DeviceIdType.MESH,
+        ).wait_recv()
+
+
+def req_a2a(x, collective_id):
+    n = x.shape[0]
+    return pl.pallas_call(
+        functools.partial(req_a2a_kernel, axis="req", other_axis="hist"),
+        out_shape=jax.ShapeDtypeStruct(x.shape, x.dtype),
+        in_specs=[pl.BlockSpec(memory_space=pl.ANY)],
+        out_specs=pl.BlockSpec(memory_space=pl.ANY),
+        scratch_shapes=[
+            pltpu.SemaphoreType.DMA((n,)),
+            pltpu.SemaphoreType.DMA((n,)),
+            pltpu.SemaphoreType.DMA(()),
+        ],
+        compiler_params=pltpu.CompilerParams(collective_id=collective_id, has_side_effects=True),
+    )(x)
+
+
+def attend_kernel(
+    len_ref, kv_ref, qsrc_ref, o_ref, q_ref, *, n_tiles, sub, tile_len, offset, q_row, score_scale, chunk
+):
     length = len_ref[0]
-    n_cls, _, head_dim = packed_ref.shape
+    n_cls, _, head_dim = kv_ref.shape
+    span = n_tiles * sub
     block = q_ref.shape[0] // n_cls
     half_scale = 0.5 * score_scale
     for b in range(n_cls):
-        q_ref[pl.ds(b * block, block), :] = packed_ref[b, pl.ds(2 * span, block), :]
+        q_ref[pl.ds(b * block, block), :] = qsrc_ref[b, pl.ds(q_row, block), :]
     o_ref[...] = jnp.zeros_like(o_ref)
 
     def one_class(c, carry):
         key_index = lax.broadcasted_iota(jnp.int32, (1, span), 1)
-        position = (c + n_cls * (key_index // tile_len)) * tile_len + key_index % tile_len
+        position = (c + n_cls * (key_index // sub)) * tile_len + offset + key_index % sub
         live = position < length
 
         def add_class(masked):
-            keys = packed_ref[c, pl.ds(0, span), :]
-            values = packed_ref[c, pl.ds(span, span), :]
+            keys = kv_ref[c, pl.ds(0, span), :]
+            values = kv_ref[c, pl.ds(span, span), :]
             for ci in range(q_ref.shape[0] // chunk):
                 rows = pl.ds(ci * chunk, chunk)
                 scores = lax.dot_general(
@@ -46,26 +106,30 @@
                 weights = half + half * jnp.tanh(half)
                 if masked:
                     weights = jnp.where(live, weights, 0.0)
-                part = jnp.dot(weights.astype(jnp.bfloat16), values, preferred_element_type=jnp.float32)
-                o_ref[rows, :] += part.astype(jnp.bfloat16).astype(jnp.float32)
-
-        last_start = (c + n_cls * (span // tile_len - 1)) * tile_len
-        whole = last_start + tile_len <= length
+                o_ref[rows, :] += jnp.dot(weights.astype(jnp.bfloat16), values, preferred_element_type=jnp.float32)
+
+        last_key = (c + n_cls * (n_tiles - 1)) * tile_len + offset + sub
+        whole = last_key <= length
         pl.when(whole)(lambda: add_class(False))
-        pl.when(jnp.logical_and(jnp.logical_not(whole), c * tile_len < length))(lambda: add_class(True))
-
+        pl.when(jnp.logical_and(jnp.logical_not(whole), c * tile_len + offset < length))(lambda: add_class(True))
         return carry
 
     lax.fori_loop(0, n_cls, one_class, 0)
 
 
-def attend(length, packed, per_hist, tile_len, score_scale):
-    span = per_hist * tile_len
-    n_cls, packed_rows, head_dim = packed.shape
-    rows = n_cls * (packed_rows - 2 * span)
+def attend(length, kv_packed, q_packed, q_row, sub, tile_len, offset, score_scale):
+    n_cls, _, head_dim = q_packed.shape
+    rows = n_cls * (q_packed.shape[1] - q_row)
     chunk = 512
     kernel = functools.partial(
-        attend_kernel, span=span, tile_len=tile_len, score_scale=score_scale, chunk=chunk
+        attend_kernel,
+        n_tiles=q_row // (2 * sub),
+        sub=sub,
+        tile_len=tile_len,
+        offset=offset,
+        q_row=q_row,
+        score_scale=score_scale,
+        chunk=chunk,
     )
     return pl.pallas_call(
         kernel,
@@ -73,57 +137,61 @@
         in_specs=[
             pl.BlockSpec(memory_space=pltpu.SMEM),
             pl.BlockSpec(memory_space=pltpu.VMEM),
+            pl.BlockSpec(memory_space=pltpu.VMEM),
         ],
         out_specs=pl.BlockSpec(memory_space=pltpu.VMEM),
         scratch_shapes=[pltpu.VMEM((rows, head_dim), jnp.bfloat16)],
-    )(length, packed)
-
-
-def pack_kernel(picked_ref, tiles_hbm, q_ref, out_ref, staged, in_sem, *, heads, per_hist):
-    users, cand_rows, width = q_ref.shape
+    )(length, kv_packed, q_packed)
+
+
+def pack_kernel(picked_ref, tiles_hbm, *rest, heads, users, per_hist, with_q):
+    if with_q:
+        q_ref, out_ref, staged, in_sem = rest
+    else:
+        out_ref, staged, in_sem = rest
+    width = tiles_hbm.shape[2] // 2
     head_dim = width // heads
-    tile_len = tiles_hbm.shape[1]
-    span = per_hist * tile_len
+    sub = tiles_hbm.shape[1]
+    span = per_hist * sub
     n_in = users * per_hist
     reads = []
     for i in range(n_in):
         read = pltpu.make_async_copy(tiles_hbm.at[picked_ref[i]], staged.at[i], in_sem.at[i])
         read.start()
         reads.append(read)
-    for u in range(users):
-        for e in range(heads):
-            out_ref[u * heads + e, pl.ds(2 * span, cand_rows), :] = q_ref[u, :, pl.ds(e * head_dim, head_dim)]
+    if with_q:
+        cand_rows = q_ref.shape[1]
+        for u in range(users):
+            for e in range(heads):
+                out_ref[u * heads + e, pl.ds(2 * span, cand_rows), :] = q_ref[u, :, pl.ds(e * head_dim, head_dim)]
     for i in range(n_in):
         u, t = divmod(i, per_hist)
         reads[i].wait()
         for piece in range(2 * heads):
             e, kv = divmod(piece, 2)
-            out_ref[u * heads + e, pl.ds(kv * span + t * tile_len, tile_len), :] = staged[
+            out_ref[u * heads + e, pl.ds(kv * span + t * sub, sub), :] = staged[
                 i, :, pl.ds(piece * head_dim, head_dim)
             ]
 
 
-def pack_for_heads(picked_slot, tiles, queries, heads):
-    users, cand_rows, width = queries.shape
-    head_dim = width // heads
+def pack_for_heads(picked_slot, tiles, queries, users, heads):
     n_in = picked_slot.shape[0]
     per_hist = n_in // users
-    tile_len = tiles.shape[1]
-    rows = 2 * per_hist * tile_len + cand_rows
+    sub, wide = tiles.shape[1], tiles.shape[2]
+    head_dim = wide // (2 * heads)
+    rows = 2 * per_hist * sub + (0 if queries is None else queries.shape[1])
+    operands = [picked_slot, tiles] + ([] if queries is None else [queries])
     return pl.pallas_call(
-        functools.partial(pack_kernel, heads=heads, per_hist=per_hist),
+        functools.partial(pack_kernel, heads=heads, users=users, per_hist=per_hist, with_q=queries is not None),
         out_shape=jax.ShapeDtypeStruct((users * heads, rows, head_dim), tiles.dtype),
-        in_specs=[
-            pl.BlockSpec(memory_space=pltpu.SMEM),
-            pl.BlockSpec(memory_space=pl.ANY),
-            pl.BlockSpec(memory_space=pltpu.VMEM),
-        ],
+        in_specs=[pl.BlockSpec(memory_space=pltpu.SMEM), pl.BlockSpec(memory_space=pl.ANY)]
+        + ([] if queries is None else [pl.BlockSpec(memory_space=pltpu.VMEM)]),
         out_specs=pl.BlockSpec(memory_space=pltpu.VMEM),
         scratch_shapes=[
-            pltpu.VMEM((n_in, tile_len, tiles.shape[2]), tiles.dtype),
+            pltpu.VMEM((n_in, sub, wide), tiles.dtype),
             pltpu.SemaphoreType.DMA((n_in,)),
         ],
-    )(picked_slot, tiles, queries)
+    )(*operands)
 
 
 def local(cand_x, kv_cache, w_uvqk, w_out, self_bias, user_rank, hist_len, cand_count, tile_slot):
@@ -164,13 +232,17 @@
         & (places[None, None, :] == jnp.arange(capacity)[None, :, None])
     )
     source_slot = jnp.sum(jnp.where(picked, local_slot[None, None, :], 0), axis=2).reshape(-1)
-    outgoing = kv_cache.at[source_slot].get(mode="promise_in_bounds")
-    outgoing = outgoing.reshape(req_count, capacity, tile_len, 2 * width)
-    incoming = lax.all_to_all(outgoing, "req", split_axis=0, concat_axis=0, tiled=True)
     first_entry = first_slot * per_hist
     my_owner = lax.dynamic_slice_in_dim(owners, first_entry, users_here * per_hist)
     my_place = lax.dynamic_slice_in_dim(places, first_entry, users_here * per_hist)
     picked_slot = (my_owner * capacity + my_place).astype(jnp.int32)
+    sub = tile_len // 2
+    halves = []
+    for half in range(2):
+        kv_half = lax.slice_in_dim(kv_cache, half * sub, (half + 1) * sub, axis=1)
+        outgoing = kv_half.at[source_slot].get(mode="promise_in_bounds")
+        incoming = req_a2a(outgoing.reshape(req_count, capacity, sub, 2 * width), half)
+        halves.append(incoming.reshape(req_count * capacity, sub, 2 * width))
     normed = layer_norm(cand_x.astype(jnp.float32)).astype(jnp.bfloat16)
     mixed_in = jnp.dot(normed.reshape(-1, width), w_uvqk, preferred_element_type=jnp.float32)
     projected = jax.nn.silu(mixed_in).astype(jnp.bfloat16).reshape(users_here, cand_rows, 4, width)
@@ -178,13 +250,19 @@
     v_self = projected[:, :, 1]
     queries = projected[:, :, 2]
     k_self = projected[:, :, 3]
-    send = pack_for_heads(
-        picked_slot, incoming.reshape(req_count * capacity, tile_len, 2 * width), queries, heads
-    )
-    packed = lax.all_to_all(send, "hist", split_axis=0, concat_axis=0, tiled=True)
     my_user = hist_index // heads
     my_length = lax.dynamic_slice_in_dim(lengths, my_user, 1)
-    history_mine = attend(my_length, packed, per_hist, tile_len, score_scale)
+    q_row = 2 * per_hist * sub
+    packed_a = lax.all_to_all(
+        pack_for_heads(picked_slot, halves[0], queries, users_here, heads),
+        "hist", split_axis=0, concat_axis=0, tiled=True,
+    )
+    history_mine = attend(my_length, packed_a, packed_a, q_row, sub, tile_len, 0, score_scale)
+    packed_b = lax.all_to_all(
+        pack_for_heads(picked_slot, halves[1], None, users_here, heads),
+        "hist", split_axis=0, concat_axis=0, tiled=True,
+    )
+    history_mine = history_mine + attend(my_length, packed_b, packed_a, q_row, sub, tile_len, sub, score_scale)
     history_back = lax.all_to_all(
         history_mine.reshape(hist_count, cand_rows, head_dim), "hist", split_axis=0, concat_axis=0, tiled=True
     )

time: 257 us -> 246 us (0.957)
  the two profiles are of different devices: /device:TPU:8 before, /device:TPU:25 now
where the time goes in v6:
time: 246 us
  Pallas kernels  142 us (58%)
  other arithmetic  28.2 us (11%)
  waiting for transfers between devices  23.6 us (10%)
  local copies, waits for them, and re-layouts  21.9 us (9%)
  starting transfers between devices  18.8 us (8%)
  matrix products  10.5 us (4%)
    pallas_call x2, Pallas kernels, req_a2a(): pl.pallas_call(functools.partial(req_a2a_kernel, axis='req', other_axis='...  99.2 us
    pallas_call x2, Pallas kernels, attend(): pl.pallas_call(kernel, out_shape=jax.ShapeDtypeStruct((rows, head_dim), j...  35.2 us
    all_to_all x1, waiting for transfers between devices, local(): lax.all_to_all(history_mine.reshape(hist_count, cand_rows, head_dim), 'hi...  12.5 us
    all_to_all x1, waiting for transfers between devices, local(): lax.all_to_all(pack_for_heads(picked_slot, halves[1], None, users_here, h...  11.1 us
    slice x1, other arithmetic, local(): queries = projected[:, :, 2]  8.7 us
    gather x2, local copies, waits for them, and re-layouts, local(): outgoing = kv_half.at[source_slot].get(mode='promise_in_bounds')  8.7 us
    pallas_call x2, Pallas kernels, pack_for_heads(): pl.pallas_call(functools.partial(pack_kernel, heads=heads, users=users, p...  8.01 us
    all_to_all x1, starting transfers between devices, local(): lax.all_to_all(pack_for_heads(picked_slot, halves[0], queries, users_here...  7.65 us
  transfers between devices with their start and end apart: 3, of which 2 were waited for; matrix products, arithmetic and copies ran while one was open for 4% of the time, Pallas kernels for 29%

profile of v6, /device:TPU:25, one launch (start us, length us, event | category | flops | bytes accessed | tf_op | source)
XLA Modules:
  0.0 245.5 jit_solution(5028017923124182831)
XLA Ops:
  0.0 0.0 copy-start
  0.0 0.9 reshape.346
  0.9 0.4 dynamic-slice_reduce_fusion
  1.4 0.1 reshape.347
  1.5 1.2 convert_reduce_fusion
  2.7 1.3 fusion.12
  4.0 0.1 broadcast_in_dim.84
  4.1 0.1 eq.98
  4.2 0.2 select_reduce_fusion
  4.4 0.6 dynamic-slice_add_fusion.picked_ref
  5.0 0.1 select_reduce_fusion.1
  5.2 0.1 copy.28
  5.2 0.1 reshape.348
  5.4 1.3 fusion.13
  6.6 7.1 %multiply_convert_fusion = bf16[256,4096]{1,0:T(8,128)(2,1)} fusion(bf16[256,1024]{1,0:T(8,128)(2,1)S(1)} %bitcast.53, bf16[1024,4096]{1,0:T(8,128)(2,1)} %param.11), kind=kOutput, calls=%fused_computation.2 | convolution fusion | flops 2152726528 | bytes 11010048 | tf_op jit(solution)/shard_map/dot_general | solution.py:247
  13.8 4.5 %reshape.352 = bf16[2,128,4,1024]{3,2,1,0:T(4,128)(2,1)} reshape(bf16[256,4096]{1,0:T(8,128)(2,1)} %multiply_convert_fusion) | data formatting | bytes 4194304 | tf_op jit(solution)/shard_map/reshape | solution.py:248
  18.3 0.0 copy-start.1
  18.3 8.7 %fusion.25 = (bf16[2,128,1,1024]{3,2,1,0:T(2,128)(2,1)S(1)}, f32[2,128,1,1024]{3,2,1,0:T(1,128)}, f32[2,128,1,1024]{3,2,1,0:T(1,128)}, bf16[2,128,1,1024]{3,2,1,0:T(2,128)(2,1)}) fusion(bf16[2,128,4,1024]{3,2,1,0:T(4,128)(2,1)} %reshape.352), kind=kLoop, calls=%fused_computation.61 | loop fusion | flops 524288 | bytes 5242880 | tf_op jit(solution)/shard_map/slice | solution.py:251
  27.0 1.0 copy.46
  27.9 0.0 copy-done.1
  27.9 2.5 %fusion.24 = (bf16[8,64,2048]{2,1,0:T(8,128)(2,1)}, bf16[8,64,2048]{2,1,0:T(8,128)(2,1)}) fusion(bf16[8,128,2048]{2,1,0:T(8,128)(2,1)S(1)} %copy-done.1), kind=kLoop, calls=%fused_computation.60 | loop fusion | bytes 8388608 | tf_op jit(solution)/shard_map/slice | solution.py:242
  30.4 4.3 %gather_fusion = bf16[16,64,2048]{2,1,0:T(8,128)(2,1)} fusion(bf16[8,64,2048]{2,1,0:T(8,128)(2,1)} %get-tuple-element.12, s32[1024]{0:T(1024)S(1)} %pad_clamp_fusion), kind=kCustom, calls=%fused_computation | custom fusion | bytes 8388672 | tf_op jit(solution)/shard_map/gather | solution.py:243
  34.8 49.8 %shard_map.91 = bf16[8,2,64,2048]{3,2,1,0:T(8,128)(2,1)} custom-call(bf16[8,2,64,2048]{3,2,1,0:T(8,128)(2,1)} %bitcast.47), custom_call_target="tpu_custom_call" | custom-call | tf_op jit(solution)/shard_map/pallas_call | solution.py:66
  84.6 4.3 %shard_map.92 = bf16[16,640,128]{2,1,0:T(8,128)(2,1)} custom-call(s32[8]{0:T(128)} %dynamic-slice_add_fusion.picked_ref, bf16[16,64,2048]{2,1,0:T(8,128)(2,1)} %bitcast.44, bf16[2,128,1024]{2,1,0:T(8,128)(2,1)} %bitcast.52), custom_call_target="tpu_custom_call" | custom-call | tf_op jit(solution)/shard_map/pallas_call | solution.py:184
  88.8 7.7 %all-to-all-start = ((bf16[16,640,128]{2,1,0:T(8,128)(2,1)}), bf16[16,640,128]{2,1,0:T(8,128)(2,1)}, u32[]{:S(2)}, u32[]{:S(2)}) async-start(bf16[16,640,128]{2,1,0:T(8,128)(2,1)} %shard_map.92), calls=%async_computation | async-start | bytes 5242880 | tf_op jit(solution)/shard_map/all_to_all | solution.py:256
  96.5 4.4 %gather_fusion.1 = bf16[16,64,2048]{2,1,0:T(8,128)(2,1)} fusion(bf16[8,64,2048]{2,1,0:T(8,128)(2,1)} %get-tuple-element.11, s32[1024]{0:T(1024)S(1)} %pad_clamp_fusion), kind=kCustom, calls=%fused_computation.1 | custom fusion | bytes 8388672 | tf_op jit(solution)/shard_map/gather | solution.py:243
  100.9 49.4 %shard_map.94 = bf16[8,2,64,2048]{3,2,1,0:T(8,128)(2,1)} custom-call(bf16[8,2,64,2048]{3,2,1,0:T(8,128)(2,1)} %bitcast.45), custom_call_target="tpu_custom_call" | custom-call | tf_op jit(solution)/shard_map/pallas_call | solution.py:66
  150.3 0.0 copy-start.5
  150.3 0.0 copy-start.2
  150.3 0.0 copy-start.3
  150.3 3.7 %shard_map.95 = bf16[16,512,128]{2,1,0:T(8,128)(2,1)} custom-call(s32[8]{0:T(128)} %dynamic-slice_add_fusion.picked_ref, bf16[16,64,2048]{2,1,0:T(8,128)(2,1)} %bitcast.46), custom_call_target="tpu_custom_call" | custom-call | tf_op jit(solution)/shard_map/pallas_call | solution.py:184
  154.0 0.0 all-to-all-done.kv_ref.qsrc_ref
  154.1 6.7 %all-to-all-start.1 = ((bf16[16,512,128]{2,1,0:T(8,128)(2,1)}), bf16[16,512,128]{2,1,0:T(8,128)(2,1)}, u32[]{:S(2)}, u32[]{:S(2)}) async-start(bf16[16,512,128]{2,1,0:T(8,128)(2,1)} %shard_map.95), calls=%async_computation.1 | async-start | bytes 4194304 | tf_op jit(solution)/shard_map/all_to_all | solution.py:261
  160.8 0.0 copy-done.5
  160.8 0.1 dynamic_slice.16
  160.9 0.0 copy-done.2
  160.9 0.0 copy-done.3
  160.9 0.2 select_reduce_fusion.3
  161.0 0.6 dynamic_slice.17.len_ref
  161.6 17.7 %shard_map.93 = f32[2048,128]{1,0:T(8,128)} custom-call(s32[1]{0:T(128)} %dynamic_slice.17.len_ref, bf16[16,640,128]{2,1,0:T(8,128)(2,1)} %all-to-all-done.kv_ref.qsrc_ref, bf16[16,640,128]{2,1,0:T(8,128)(2,1)} %all-to-all-done.kv_ref.qsrc_ref), custom_call_target="tpu_custom_call" | custom-call | tf_op jit(solution)/shard_map/pallas_call | solution.py:134
  179.4 11.1 %all-to-all-done.1.kv_ref = bf16[16,512,128]{2,1,0:T(8,128)(2,1)} async-done(((bf16[16,512,128]{2,1,0:T(8,128)(2,1)}), bf16[16,512,128]{2,1,0:T(8,128)(2,1)}, u32[]{:S(2)}, u32[]{:S(2)}) %all-to-all-start.1) | async-done | bytes 2097184 | tf_op jit(solution)/shard_map/all_to_all | solution.py:261
  190.4 17.4 %shard_map.96 = f32[2048,128]{1,0:T(8,128)} custom-call(s32[1]{0:T(128)} %dynamic_slice.17.len_ref, bf16[16,512,128]{2,1,0:T(8,128)(2,1)} %all-to-all-done.1.kv_ref, bf16[16,640,128]{2,1,0:T(8,128)(2,1)} %all-to-all-done.kv_ref.qsrc_ref), custom_call_target="tpu_custom_call" | custom-call | tf_op jit(solution)/shard_map/pallas_call | solution.py:134
  207.9 2.7 %add.130 = f32[2048,128]{1,0:T(8,128)} add(f32[2048,128]{1,0:T(8,128)} %shard_map.93, f32[2048,128]{1,0:T(8,128)} %shard_map.96) | non-fusion elementwise | flops 262144 | bytes 3145728 | tf_op jit(solution)/shard_map/add | solution.py:265
  210.6 0.0 copy-start.4
  210.6 4.5 %all-to-all-start.2 = ((f32[16,128,128]{2,1,0:T(8,128)}), f32[16,128,128]{2,1,0:T(8,128)}, u32[]{:S(2)}, u32[]{:S(2)}) async-start(f32[16,128,128]{2,1,0:T(8,128)} %bitcast.48), calls=%async_computation.2 | async-start | bytes 2097152 | tf_op jit(solution)/shard_map/all_to_all | solution.py:266
  215.0 2.7 %convert_multiply_fusion = f32[2,128,1,1024]{3,1,0,2:T(8,128)} fusion(bf16[2,128,1,1024]{3,2,1,0:T(2,128)(2,1)} %get-tuple-element.16, bf16[2,128,1,1024]{3,2,1,0:T(2,128)(2,1)S(1)} %get-tuple-element.13), kind=kLoop, calls=%fused_computation.22 | loop fusion | flops 786432 | bytes 2097152 | tf_op jit(solution)/shard_map/mul | solution.py:273
  217.7 1.4 copy.38
  219.1 0.3 bitcast_reduce_fusion
  219.5 0.1 copy.32
  219.5 0.0 copy-done.4
  219.5 0.1 divide_multiply_fusion
  219.6 0.1 copy.33
  219.8 0.1 broadcast_compare_fusion
  219.9 12.5 %all-to-all-done.2 = f32[16,128,128]{2,1,0:T(8,128)} async-done(((f32[16,128,128]{2,1,0:T(8,128)}), f32[16,128,128]{2,1,0:T(8,128)}, u32[]{:S(2)}, u32[]{:S(2)}) %all-to-all-start.2) | async-done | bytes 1048608 | tf_op jit(solution)/shard_map/all_to_all | solution.py:266
  232.4 5.1 %fusion.22 = (f32[2,128]{1,0:T(2,128)S(1)}, f32[2,128,8,128]{3,2,1,0:T(8,128)S(1)}) fusion(f32[2]{0:T(128)S(1)} %add_convert_fusion, f32[2,128,8,128]{3,2,1,0:T(8,128)} %bitcast.51, f32[2,128,8]{2,1,0:T(8,128)S(1)} %copy.33, f32[2,8,128,128]{3,2,1,0:T(8,128)} %bitcast.8), kind=kLoop, calls=%fused_computation.59 | loop fusion | flops 1048320 | bytes 3154952 | tf_op jit(solution)/shard_map/reduce_sum | solution.py:13
  237.5 1.2 reshape.357
  238.7 3.5 %multiply_reduce_fusion = f32[2,128]{1,0:T(2,128)S(1)} fusion(f32[2,128,8,128]{3,2,1,0:T(8,128)S(1)} %get-tuple-element.8, f32[2,128]{1,0:T(2,128)S(1)} %broadcast_multiply_fusion), kind=kLoop, calls=%fused_computation.21 | loop fusion | flops 786176 | bytes 1050624 | tf_op jit(solution)/shard_map/reduce_sum | solution.py:15
  242.2 0.0 copy-done
  242.2 3.3 %fusion.7 = bf16[2,128,1024]{2,1,0:T(8,128)(2,1)} fusion(bf16[1024,1024]{1,0:T(8,128)(2,1)S(1)} %copy-done, bf16[2,128,1024]{2,1,0:T(8,128)(2,1)} %param.9, f32[2,128,1,1024]{3,2,1,0:T(1,128)} %get-tuple-element.15, f32[2,128,1024]{2,1,0:T(8,128)} %reshape.357, f32[2,128]{1,0:T(2,128)S(1)} %add_rsqrt_fusion, f32[2,128]{1,0:T(2,128)S(1)} %broadcast_multiply_fusion, ...), kind=kOutput, calls=%fused_computation.9 | convolution fusion | flops 538968064 | bytes 5245184 | tf_op jit(solution)/shard_map/dot_general | solution.py:280
  (13 shorter events, 0.1 us)
Async XLA Ops:
  0.0 242.2 %copy-start = (bf16[1024,1024]{1,0:T(8,128)(2,1)S(1)}, bf16[1024,1024]{1,0:T(8,128)(2,1)}, u32[]{:S(2)}) copy-start(bf16[1024,1024]{1,0:T(8,128)(2,1)} %param.12) | copy-start | bytes 6291460
  18.3 9.7 %copy-start.1 = (bf16[8,128,2048]{2,1,0:T(8,128)(2,1)S(1)}, bf16[8,128,2048]{2,1,0:T(8,128)(2,1)}, u32[]{:S(2)}) copy-start(bf16[8,128,2048]{2,1,0:T(8,128)(2,1)} %param.10) | copy-start | bytes 12582916
  88.8 65.2 %all-to-all-start = ((bf16[16,640,128]{2,1,0:T(8,128)(2,1)}), bf16[16,640,128]{2,1,0:T(8,128)(2,1)}, u32[]{:S(2)}, u32[]{:S(2)}) async-start(bf16[16,640,128]{2,1,0:T(8,128)(2,1)} %shard_map.92), calls=%async_computation | async-start | bytes 5242880 | tf_op jit(solution)/shard_map/all_to_all | solution.py:256
  150.3 10.5 %copy-start.5 = (s32[16]{0:T(128)S(1)}, s32[16]{0:T(128)}, u32[]{:S(2)}) copy-start(s32[16]{0:T(128)} %param.14) | copy-start | bytes 196
  150.3 10.6 %copy-start.2 = (s32[16]{0:T(128)S(1)}, s32[16]{0:T(128)}, u32[]{:S(2)}) copy-start(s32[16]{0:T(128)} %param.16) | copy-start | bytes 196
  150.3 10.6 %copy-start.3 = (s32[16]{0:T(128)S(1)}, s32[16]{0:T(128)}, u32[]{:S(2)}) copy-start(s32[16]{0:T(128)} %param.15) | copy-start | bytes 196
  154.1 36.4 %all-to-all-start.1 = ((bf16[16,512,128]{2,1,0:T(8,128)(2,1)}), bf16[16,512,128]{2,1,0:T(8,128)(2,1)}, u32[]{:S(2)}, u32[]{:S(2)}) async-start(bf16[16,512,128]{2,1,0:T(8,128)(2,1)} %shard_map.95), calls=%async_computation.1 | async-start | bytes 4194304 | tf_op jit(solution)/shard_map/all_to_all | solution.py:261
  210.6 9.0 %copy-start.4 = (f32[8]{0:T(128)S(1)}, f32[8]{0:T(128)}, u32[]{:S(2)}) copy-start(f32[8]{0:T(128)} %param.13) | copy-start | bytes 100
  210.6 21.8 %all-to-all-start.2 = ((f32[16,128,128]{2,1,0:T(8,128)}), f32[16,128,128]{2,1,0:T(8,128)}, u32[]{:S(2)}, u32[]{:S(2)}) async-start(f32[16,128,128]{2,1,0:T(8,128)} %bitcast.48), calls=%async_computation.2 | async-start | bytes 2097152 | tf_op jit(solution)/shard_map/all_to_all | solution.py:266

commit v7 on v6

--- a/solution.py
+++ b/solution.py
@@ -120,7 +120,7 @@
 def attend(length, kv_packed, q_packed, q_row, sub, tile_len, offset, score_scale):
     n_cls, _, head_dim = q_packed.shape
     rows = n_cls * (q_packed.shape[1] - q_row)
-    chunk = 512
+    chunk = 2048
     kernel = functools.partial(
         attend_kernel,
         n_tiles=q_row // (2 * sub),
@@ -241,7 +241,11 @@
     for half in range(2):
         kv_half = lax.slice_in_dim(kv_cache, half * sub, (half + 1) * sub, axis=1)
         outgoing = kv_half.at[source_slot].get(mode="promise_in_bounds")
-        incoming = req_a2a(outgoing.reshape(req_count, capacity, sub, 2 * width), half)
+        outgoing = outgoing.reshape(req_count, capacity, sub, 2 * width)
+        if half == 0:
+            incoming = lax.all_to_all(outgoing, "req", split_axis=0, concat_axis=0, tiled=True)
+        else:
+            incoming = req_a2a(outgoing, 0)
         halves.append(incoming.reshape(req_count * capacity, sub, 2 * width))
     normed = layer_norm(cand_x.astype(jnp.float32)).astype(jnp.bfloat16)
     mixed_in = jnp.dot(normed.reshape(-1, width), w_uvqk, preferred_element_type=jnp.float32)

time: 246 us -> 227 us (0.923)
  the two profiles are of different devices: /device:TPU:25 before, /device:TPU:8 now
where the time goes in v7:
time: 227 us; the launch traced here: 224 us
  Pallas kernels  73.6 us (32%)
  waiting for transfers between devices  53.6 us (24%)
  starting transfers between devices  35.9 us (16%)
  other arithmetic  25.5 us (11%)
  local copies, waits for them, and re-layouts  24.3 us (11%)
  matrix products  10.5 us (5%)
    pallas_call x1, Pallas kernels, req_a2a(): pl.pallas_call(functools.partial(req_a2a_kernel, axis='req', other_axis='...  47.5 us
    all_to_all x1, waiting for transfers between devices, local(): lax.all_to_all(outgoing, 'req', split_axis=0, concat_axis=0, tiled=True)  25.3 us
    all_to_all x1, waiting for transfers between devices, local(): lax.all_to_all(pack_for_heads(picked_slot, halves[1], None, users_here, h...  20.2 us
    pallas_call x2, Pallas kernels, attend(): pl.pallas_call(kernel, out_shape=jax.ShapeDtypeStruct((rows, head_dim), j...  18.1 us
    all_to_all x1, starting transfers between devices, local(): lax.all_to_all(history_mine.reshape(hist_count, cand_rows, head_dim), 'hi...  15.7 us
    slice x1, other arithmetic, local(): queries = projected[:, :, 2]  9.08 us
    gather x2, local copies, waits for them, and re-layouts, local(): outgoing = kv_half.at[source_slot].get(mode='promise_in_bounds')  8.75 us
    all_to_all x1, waiting for transfers between devices, local(): lax.all_to_all(history_mine.reshape(hist_count, cand_rows, head_dim), 'hi...  8.11 us
  transfers between devices with their start and end apart: 4, of which 3 were waited for; matrix products, arithmetic and copies ran while one was open for 15% of the time, Pallas kernels for 27%

profile of v7, /device:TPU:8, one launch (start us, length us, event | category | flops | bytes accessed | tf_op | source)
XLA Modules:
  0.0 223.5 jit_solution(442335759231880327)
XLA Ops:
  0.0 0.0 copy-start
  0.0 0.1 broadcast_in_dim.84
  0.1 0.1 eq.98
  0.2 0.9 reshape.346
  1.1 0.4 dynamic-slice_reduce_fusion
  1.5 0.1 reshape.347
  1.6 0.2 select_reduce_fusion
  1.8 0.1 select_reduce_fusion.1
  2.0 0.1 copy.28
  2.1 0.1 reshape.348
  2.2 4.8 %fusion.24 = (bf16[8,64,2048]{2,1,0:T(8,128)(2,1)}, bf16[8,64,2048]{2,1,0:T(8,128)(2,1)}) fusion(bf16[8,128,2048]{2,1,0:T(8,128)(2,1)} %param.10), kind=kLoop, calls=%fused_computation.60 | loop fusion | bytes 8388608 | tf_op jit(solution)/shard_map/slice | solution.py:242
  7.0 4.4 %gather_fusion = bf16[16,64,2048]{2,1,0:T(8,128)(2,1)} fusion(bf16[8,64,2048]{2,1,0:T(8,128)(2,1)} %get-tuple-element.12, s32[1024]{0:T(1024)S(1)} %pad_clamp_fusion), kind=kCustom, calls=%fused_computation | custom fusion | bytes 8388672 | tf_op jit(solution)/shard_map/gather | solution.py:243
  11.3 0.0 copy-start.1
  11.3 5.0 %all-to-all-start = ((bf16[8,2,64,2048]{3,2,1,0:T(8,128)(2,1)}), bf16[8,2,64,2048]{3,2,1,0:T(8,128)(2,1)}, u32[]{:S(2)}, u32[]{:S(2)}) async-start(bf16[8,2,64,2048]{3,2,1,0:T(8,128)(2,1)} %bitcast.44), calls=%async_computation | async-start | bytes 8388608 | tf_op jit(solution)/shard_map/all_to_all | solution.py:246
  16.4 0.0 copy-done.1
  16.4 0.1 convert_reduce_fusion
  16.6 0.3 fusion.12
  16.8 0.3 fusion.13
  17.1 7.2 %multiply_convert_fusion = bf16[256,4096]{1,0:T(8,128)(2,1)} fusion(bf16[256,1024]{1,0:T(8,128)(2,1)S(1)} %bitcast.52, bf16[1024,4096]{1,0:T(8,128)(2,1)} %param.11), kind=kOutput, calls=%fused_computation.2 | convolution fusion | flops 2152726528 | bytes 11010048 | tf_op jit(solution)/shard_map/dot_general | solution.py:251
  24.3 4.5 %reshape.352 = bf16[2,128,4,1024]{3,2,1,0:T(4,128)(2,1)} reshape(bf16[256,4096]{1,0:T(8,128)(2,1)} %multiply_convert_fusion) | data formatting | bytes 4194304 | tf_op jit(solution)/shard_map/reshape | solution.py:252
  28.8 9.1 %fusion.25 = (bf16[2,128,1,1024]{3,2,1,0:T(2,128)(2,1)S(1)}, f32[2,128,1,1024]{3,2,1,0:T(1,128)}, f32[2,128,1,1024]{3,2,1,0:T(1,128)}, bf16[2,128,1,1024]{3,2,1,0:T(2,128)(2,1)}) fusion(bf16[2,128,4,1024]{3,2,1,0:T(4,128)(2,1)} %reshape.352), kind=kLoop, calls=%fused_computation.61 | loop fusion | flops 524288 | bytes 5242880 | tf_op jit(solution)/shard_map/slice | solution.py:255
  37.9 1.0 copy.46
  38.8 0.6 dynamic-slice_add_fusion.picked_ref
  39.5 25.3 %all-to-all-done = bf16[8,2,64,2048]{3,2,1,0:T(8,128)(2,1)} async-done(((bf16[8,2,64,2048]{3,2,1,0:T(8,128)(2,1)}), bf16[8,2,64,2048]{3,2,1,0:T(8,128)(2,1)}, u32[]{:S(2)}, u32[]{:S(2)}) %all-to-all-start) | async-done | bytes 4194336 | tf_op jit(solution)/shard_map/all_to_all | solution.py:246
  64.7 4.3 %shard_map.91 = bf16[16,640,128]{2,1,0:T(8,128)(2,1)} custom-call(s32[8]{0:T(128)} %dynamic-slice_add_fusion.picked_ref, bf16[16,64,2048]{2,1,0:T(8,128)(2,1)} %bitcast.2.tiles_hbm, bf16[2,128,1024]{2,1,0:T(8,128)(2,1)} %bitcast.51), custom_call_target="tpu_custom_call" | custom-call | tf_op jit(solution)/shard_map/pallas_call | solution.py:184
  69.0 7.9 %all-to-all-start.1 = ((bf16[16,640,128]{2,1,0:T(8,128)(2,1)}), bf16[16,640,128]{2,1,0:T(8,128)(2,1)}, u32[]{:S(2)}, u32[]{:S(2)}) async-start(bf16[16,640,128]{2,1,0:T(8,128)(2,1)} %shard_map.91), calls=%async_computation.1 | async-start | bytes 5242880 | tf_op jit(solution)/shard_map/all_to_all | solution.py:260
  76.9 4.4 %gather_fusion.1 = bf16[16,64,2048]{2,1,0:T(8,128)(2,1)} fusion(bf16[8,64,2048]{2,1,0:T(8,128)(2,1)} %get-tuple-element.11, s32[1024]{0:T(1024)S(1)} %pad_clamp_fusion), kind=kCustom, calls=%fused_computation.1 | custom fusion | bytes 8388672 | tf_op jit(solution)/shard_map/gather | solution.py:243
  81.3 47.5 %shard_map.93 = bf16[8,2,64,2048]{3,2,1,0:T(8,128)(2,1)} custom-call(bf16[8,2,64,2048]{3,2,1,0:T(8,128)(2,1)} %bitcast.45), custom_call_target="tpu_custom_call" | custom-call | tf_op jit(solution)/shard_map/pallas_call | solution.py:66
  128.8 0.0 copy-start.5
  128.8 0.0 copy-start.2
  128.8 0.0 copy-start.3
  128.8 3.7 %shard_map.94 = bf16[16,512,128]{2,1,0:T(8,128)(2,1)} custom-call(s32[8]{0:T(128)} %dynamic-slice_add_fusion.picked_ref, bf16[16,64,2048]{2,1,0:T(8,128)(2,1)} %bitcast.46), custom_call_target="tpu_custom_call" | custom-call | tf_op jit(solution)/shard_map/pallas_call | solution.py:184
  132.6 0.0 all-to-all-done.1.kv_ref.qsrc_ref
  132.6 7.2 %all-to-all-start.2 = ((bf16[16,512,128]{2,1,0:T(8,128)(2,1)}), bf16[16,512,128]{2,1,0:T(8,128)(2,1)}, u32[]{:S(2)}, u32[]{:S(2)}) async-start(bf16[16,512,128]{2,1,0:T(8,128)(2,1)} %shard_map.94), calls=%async_computation.2 | async-start | bytes 4194304 | tf_op jit(solution)/shard_map/all_to_all | solution.py:265
  139.9 0.0 copy-done.5
  139.9 0.1 dynamic_slice.16
  139.9 0.0 copy-done.2
  139.9 0.0 copy-done.3
  139.9 0.2 select_reduce_fusion.3
  140.1 0.6 dynamic_slice.17.len_ref
  140.7 9.6 %shard_map.92 = f32[2048,128]{1,0:T(8,128)} custom-call(s32[1]{0:T(128)} %dynamic_slice.17.len_ref, bf16[16,640,128]{2,1,0:T(8,128)(2,1)} %all-to-all-done.1.kv_ref.qsrc_ref, bf16[16,640,128]{2,1,0:T(8,128)(2,1)} %all-to-all-done.1.kv_ref.qsrc_ref), custom_call_target="tpu_custom_call" | custom-call | tf_op jit(solution)/shard_map/pallas_call | solution.py:134
  150.3 20.2 %all-to-all-done.2.kv_ref = bf16[16,512,128]{2,1,0:T(8,128)(2,1)} async-done(((bf16[16,512,128]{2,1,0:T(8,128)(2,1)}), bf16[16,512,128]{2,1,0:T(8,128)(2,1)}, u32[]{:S(2)}, u32[]{:S(2)}) %all-to-all-start.2) | async-done | bytes 2097184 | tf_op jit(solution)/shard_map/all_to_all | solution.py:265
  170.5 8.5 %shard_map.95 = f32[2048,128]{1,0:T(8,128)} custom-call(s32[1]{0:T(128)} %dynamic_slice.17.len_ref, bf16[16,512,128]{2,1,0:T(8,128)(2,1)} %all-to-all-done.2.kv_ref, bf16[16,640,128]{2,1,0:T(8,128)(2,1)} %all-to-all-done.1.kv_ref.qsrc_ref), custom_call_target="tpu_custom_call" | custom-call | tf_op jit(solution)/shard_map/pallas_call | solution.py:134
  179.1 2.7 %add.130 = f32[2048,128]{1,0:T(8,128)} add(f32[2048,128]{1,0:T(8,128)} %shard_map.92, f32[2048,128]{1,0:T(8,128)} %shard_map.95) | non-fusion elementwise | flops 262144 | bytes 3145728 | tf_op jit(solution)/shard_map/add | solution.py:269
  181.7 0.0 copy-start.4
  181.7 15.7 %all-to-all-start.3 = ((f32[16,128,128]{2,1,0:T(8,128)}), f32[16,128,128]{2,1,0:T(8,128)}, u32[]{:S(2)}, u32[]{:S(2)}) async-start(f32[16,128,128]{2,1,0:T(8,128)} %bitcast.47), calls=%async_computation.3 | async-start | bytes 2097152 | tf_op jit(solution)/shard_map/all_to_all | solution.py:270
  197.5 2.7 %convert_multiply_fusion = f32[2,128,1,1024]{3,1,0,2:T(8,128)} fusion(bf16[2,128,1,1024]{3,2,1,0:T(2,128)(2,1)} %get-tuple-element.16, bf16[2,128,1,1024]{3,2,1,0:T(2,128)(2,1)S(1)} %get-tuple-element.13), kind=kLoop, calls=%fused_computation.22 | loop fusion | flops 786432 | bytes 2097152 | tf_op jit(solution)/shard_map/mul | solution.py:277
  200.1 1.4 copy.38
  201.6 0.3 bitcast_reduce_fusion
  201.9 0.1 copy.32
  202.0 0.0 copy-done.4
  202.0 0.1 divide_multiply_fusion
  202.1 0.1 copy.33
  202.2 0.1 broadcast_compare_fusion
  202.3 8.1 %all-to-all-done.3 = f32[16,128,128]{2,1,0:T(8,128)} async-done(((f32[16,128,128]{2,1,0:T(8,128)}), f32[16,128,128]{2,1,0:T(8,128)}, u32[]{:S(2)}, u32[]{:S(2)}) %all-to-all-start.3) | async-done | bytes 1048608 | tf_op jit(solution)/shard_map/all_to_all | solution.py:270
  210.4 5.1 %fusion.22 = (f32[2,128]{1,0:T(2,128)S(1)}, f32[2,128,8,128]{3,2,1,0:T(8,128)S(1)}) fusion(f32[2]{0:T(128)S(1)} %add_convert_fusion, f32[2,128,8,128]{3,2,1,0:T(8,128)} %bitcast.50, f32[2,128,8]{2,1,0:T(8,128)S(1)} %copy.33, f32[2,8,128,128]{3,2,1,0:T(8,128)} %bitcast.8), kind=kLoop, calls=%fused_computation.59 | loop fusion | flops 1048320 | bytes 3154952 | tf_op jit(solution)/shard_map/reduce_sum | solution.py:13
  215.5 1.2 reshape.357
  216.7 3.5 %multiply_reduce_fusion = f32[2,128]{1,0:T(2,128)S(1)} fusion(f32[2,128,8,128]{3,2,1,0:T(8,128)S(1)} %get-tuple-element.8, f32[2,128]{1,0:T(2,128)S(1)} %broadcast_multiply_fusion), kind=kLoop, calls=%fused_computation.21 | loop fusion | flops 786176 | bytes 1050624 | tf_op jit(solution)/shard_map/reduce_sum | solution.py:15
  220.2 0.0 copy-done
  220.2 3.3 %fusion.7 = bf16[2,128,1024]{2,1,0:T(8,128)(2,1)} fusion(bf16[1024,1024]{1,0:T(8,128)(2,1)S(1)} %copy-done, bf16[2,128,1024]{2,1,0:T(8,128)(2,1)} %param.9, f32[2,128,1,1024]{3,2,1,0:T(1,128)} %get-tuple-element.15, f32[2,128,1024]{2,1,0:T(8,128)} %reshape.357, f32[2,128]{1,0:T(2,128)S(1)} %add_rsqrt_fusion, f32[2,128]{1,0:T(2,128)S(1)} %broadcast_multiply_fusion, ...), kind=kOutput, calls=%fused_computation.9 | convolution fusion | flops 538968064 | bytes 5245184 | tf_op jit(solution)/shard_map/dot_general | solution.py:284
  (13 shorter events, 0.1 us)
Async XLA Ops:
  0.0 220.2 %copy-start = (bf16[1024,1024]{1,0:T(8,128)(2,1)S(1)}, bf16[1024,1024]{1,0:T(8,128)(2,1)}, u32[]{:S(2)}) copy-start(bf16[1024,1024]{1,0:T(8,128)(2,1)} %param.12) | copy-start | bytes 6291460
  11.3 5.1 %copy-start.1 = (bf16[2,128,1024]{2,1,0:T(8,128)(2,1)S(1)}, bf16[2,128,1024]{2,1,0:T(8,128)(2,1)}, u32[]{:S(2)}) copy-start(bf16[2,128,1024]{2,1,0:T(8,128)(2,1)} %param.9) | copy-start | bytes 1572868
  11.3 53.4 %all-to-all-start = ((bf16[8,2,64,2048]{3,2,1,0:T(8,128)(2,1)}), bf16[8,2,64,2048]{3,2,1,0:T(8,128)(2,1)}, u32[]{:S(2)}, u32[]{:S(2)}) async-start(bf16[8,2,64,2048]{3,2,1,0:T(8,128)(2,1)} %bitcast.44), calls=%async_computation | async-start | bytes 8388608 | tf_op jit(solution)/shard_map/all_to_all | solution.py:246
  69.0 63.6 %all-to-all-start.1 = ((bf16[16,640,128]{2,1,0:T(8,128)(2,1)}), bf16[16,640,128]{2,1,0:T(8,128)(2,1)}, u32[]{:S(2)}, u32[]{:S(2)}) async-start(bf16[16,640,128]{2,1,0:T(8,128)(2,1)} %shard_map.91), calls=%async_computation.1 | async-start | bytes 5242880 | tf_op jit(solution)/shard_map/all_to_all | solution.py:260
  128.8 11.1 %copy-start.5 = (s32[16]{0:T(128)S(1)}, s32[16]{0:T(128)}, u32[]{:S(2)}) copy-start(s32[16]{0:T(128)} %param.14) | copy-start | bytes 196
  128.8 11.2 %copy-start.2 = (s32[16]{0:T(128)S(1)}, s32[16]{0:T(128)}, u32[]{:S(2)}) copy-start(s32[16]{0:T(128)} %param.16) | copy-start | bytes 196
  128.8 11.1 %copy-start.3 = (s32[16]{0:T(128)S(1)}, s32[16]{0:T(128)}, u32[]{:S(2)}) copy-start(s32[16]{0:T(128)} %param.15) | copy-start | bytes 196
  132.6 38.0 %all-to-all-start.2 = ((bf16[16,512,128]{2,1,0:T(8,128)(2,1)}), bf16[16,512,128]{2,1,0:T(8,128)(2,1)}, u32[]{:S(2)}, u32[]{:S(2)}) async-start(bf16[16,512,128]{2,1,0:T(8,128)(2,1)} %shard_map.94), calls=%async_computation.2 | async-start | bytes 4194304 | tf_op jit(solution)/shard_map/all_to_all | solution.py:265
  181.7 20.2 %copy-start.4 = (f32[8]{0:T(128)S(1)}, f32[8]{0:T(128)}, u32[]{:S(2)}) copy-start(f32[8]{0:T(128)} %param.13) | copy-start | bytes 100
  181.7 28.7 %all-to-all-start.3 = ((f32[16,128,128]{2,1,0:T(8,128)}), f32[16,128,128]{2,1,0:T(8,128)}, u32[]{:S(2)}, u32[]{:S(2)}) async-start(f32[16,128,128]{2,1,0:T(8,128)} %bitcast.47), calls=%async_computation.3 | async-start | bytes 2097152 | tf_op jit(solution)/shard_map/all_to_all | solution.py:270

commit v8 on v7

--- a/solution.py
+++ b/solution.py
@@ -102,11 +102,11 @@
                 scores = lax.dot_general(
                     q_ref[rows, :], keys, (((1,), (1,)), ((), ())), preferred_element_type=jnp.float32
                 )
-                half = scores * half_scale
+                half = (scores * half_scale).astype(jnp.bfloat16)
                 weights = half + half * jnp.tanh(half)
                 if masked:
-                    weights = jnp.where(live, weights, 0.0)
-                o_ref[rows, :] += jnp.dot(weights.astype(jnp.bfloat16), values, preferred_element_type=jnp.float32)
+                    weights = jnp.where(live, weights, jnp.zeros_like(weights))
+                o_ref[rows, :] += jnp.dot(weights, values, preferred_element_type=jnp.float32)
 
         last_key = (c + n_cls * (n_tiles - 1)) * tile_len + offset + sub
         whole = last_key <= length

time: 227 us -> 229 us (level)
  Pallas kernels: 73.6 us -> 90.7 us
  starting transfers between devices: 35.9 us -> 27.2 us
  waiting for transfers between devices: 53.6 us -> 47.8 us
    pallas_call x2, Pallas kernels: 18.1 us -> 35.2 us  [attend(): pl.pallas_call(kernel, out_shape=jax.ShapeDtypeStruct((rows, head_dim), j...]
    all_to_all x1, starting transfers between devices: 15.7 us -> 6.93 us  [local(): lax.all_to_all(history_mine.reshape(hist_count, cand_rows, head_dim), 'hi...]
    all_to_all x1, waiting for transfers between devices: 20.2 us -> 12.1 us  [local(): lax.all_to_all(pack_for_heads(picked_slot, halves[1], None, users_here, h...]
    all_to_all x1, waiting for transfers between devices: 8.11 us -> 10.4 us  [local(): lax.all_to_all(history_mine.reshape(hist_count, cand_rows, head_dim), 'hi...]
  transfers between devices with their start and end apart: 4 -> 4, of which waited for: 3 -> 3; matrix products, arithmetic and copies ran while one was open for 15% -> 15% of each run, Pallas kernels for 27% -> 31%
where the time goes in v8:
time: 229 us; the launch traced here: 226 us
  Pallas kernels  90.7 us (40%)
  waiting for transfers between devices  47.8 us (21%)
  starting transfers between devices  27.2 us (12%)
  other arithmetic  25.5 us (11%)
  local copies, waits for them, and re-layouts  24.3 us (11%)
  matrix products  10.5 us (5%)
    pallas_call x1, Pallas kernels, req_a2a(): pl.pallas_call(functools.partial(req_a2a_kernel, axis='req', other_axis='...  47.5 us
    pallas_call x2, Pallas kernels, attend(): pl.pallas_call(kernel, out_shape=jax.ShapeDtypeStruct((rows, head_dim), j...  35.2 us
    all_to_all x1, waiting for transfers between devices, local(): lax.all_to_all(outgoing, 'req', split_axis=0, concat_axis=0, tiled=True)  25.3 us
    all_to_all x1, waiting for transfers between devices, local(): lax.all_to_all(pack_for_heads(picked_slot, halves[1], None, users_here, h...  12.1 us
    all_to_all x1, waiting for transfers between devices, local(): lax.all_to_all(history_mine.reshape(hist_count, cand_rows, head_dim), 'hi...  10.4 us
    slice x1, other arithmetic, local(): queries = projected[:, :, 2]  9.08 us
    gather x2, local copies, waits for them, and re-layouts, local(): outgoing = kv_half.at[source_slot].get(mode='promise_in_bounds')  8.75 us
    pallas_call x2, Pallas kernels, pack_for_heads(): pl.pallas_call(functools.partial(pack_kernel, heads=heads, users=users, p...  8.01 us
  transfers between devices with their start and end apart: 4, of which 3 were waited for; matrix products, arithmetic and copies ran while one was open for 15% of the time, Pallas kernels for 31%

profile of v8, /device:TPU:8, one launch (start us, length us, event | category | flops | bytes accessed | tf_op | source)
XLA Modules:
  0.0 226.0 jit_solution(9679422011672168115)
XLA Ops:
  0.0 0.0 copy-start
  0.0 0.1 broadcast_in_dim.84
  0.1 0.1 eq.98
  0.2 0.9 reshape.346
  1.1 0.4 dynamic-slice_reduce_fusion
  1.5 0.1 reshape.347
  1.6 0.2 select_reduce_fusion
  1.8 0.1 select_reduce_fusion.1
  2.0 0.1 copy.28
  2.1 0.1 reshape.348
  2.2 4.8 %fusion.24 = (bf16[8,64,2048]{2,1,0:T(8,128)(2,1)}, bf16[8,64,2048]{2,1,0:T(8,128)(2,1)}) fusion(bf16[8,128,2048]{2,1,0:T(8,128)(2,1)} %param.10), kind=kLoop, calls=%fused_computation.60 | loop fusion | bytes 8388608 | tf_op jit(solution)/shard_map/slice | solution.py:242
  7.0 4.4 %gather_fusion = bf16[16,64,2048]{2,1,0:T(8,128)(2,1)} fusion(bf16[8,64,2048]{2,1,0:T(8,128)(2,1)} %get-tuple-element.12, s32[1024]{0:T(1024)S(1)} %pad_clamp_fusion), kind=kCustom, calls=%fused_computation | custom fusion | bytes 8388672 | tf_op jit(solution)/shard_map/gather | solution.py:243
  11.3 0.0 copy-start.1
  11.3 5.0 %all-to-all-start = ((bf16[8,2,64,2048]{3,2,1,0:T(8,128)(2,1)}), bf16[8,2,64,2048]{3,2,1,0:T(8,128)(2,1)}, u32[]{:S(2)}, u32[]{:S(2)}) async-start(bf16[8,2,64,2048]{3,2,1,0:T(8,128)(2,1)} %bitcast.44), calls=%async_computation | async-start | bytes 8388608 | tf_op jit(solution)/shard_map/all_to_all | solution.py:246
  16.4 0.0 copy-done.1
  16.4 0.1 convert_reduce_fusion
  16.6 0.3 fusion.12
  16.8 0.3 fusion.13
  17.1 7.2 %multiply_convert_fusion = bf16[256,4096]{1,0:T(8,128)(2,1)} fusion(bf16[256,1024]{1,0:T(8,128)(2,1)S(1)} %bitcast.52, bf16[1024,4096]{1,0:T(8,128)(2,1)} %param.11), kind=kOutput, calls=%fused_computation.2 | convolution fusion | flops 2152726528 | bytes 11010048 | tf_op jit(solution)/shard_map/dot_general | solution.py:251
  24.3 4.5 %reshape.352 = bf16[2,128,4,1024]{3,2,1,0:T(4,128)(2,1)} reshape(bf16[256,4096]{1,0:T(8,128)(2,1)} %multiply_convert_fusion) | data formatting | bytes 4194304 | tf_op jit(solution)/shard_map/reshape | solution.py:252
  28.8 9.1 %fusion.25 = (bf16[2,128,1,1024]{3,2,1,0:T(2,128)(2,1)S(1)}, f32[2,128,1,1024]{3,2,1,0:T(1,128)}, f32[2,128,1,1024]{3,2,1,0:T(1,128)}, bf16[2,128,1,1024]{3,2,1,0:T(2,128)(2,1)}) fusion(bf16[2,128,4,1024]{3,2,1,0:T(4,128)(2,1)} %reshape.352), kind=kLoop, calls=%fused_computation.61 | loop fusion | flops 524288 | bytes 5242880 | tf_op jit(solution)/shard_map/slice | solution.py:255
  37.9 1.0 copy.46
  38.8 0.6 dynamic-slice_add_fusion.picked_ref
  39.5 25.3 %all-to-all-done = bf16[8,2,64,2048]{3,2,1,0:T(8,128)(2,1)} async-done(((bf16[8,2,64,2048]{3,2,1,0:T(8,128)(2,1)}), bf16[8,2,64,2048]{3,2,1,0:T(8,128)(2,1)}, u32[]{:S(2)}, u32[]{:S(2)}) %all-to-all-start) | async-done | bytes 4194336 | tf_op jit(solution)/shard_map/all_to_all | solution.py:246
  64.7 4.3 %shard_map.91 = bf16[16,640,128]{2,1,0:T(8,128)(2,1)} custom-call(s32[8]{0:T(128)} %dynamic-slice_add_fusion.picked_ref, bf16[16,64,2048]{2,1,0:T(8,128)(2,1)} %bitcast.2.tiles_hbm, bf16[2,128,1024]{2,1,0:T(8,128)(2,1)} %bitcast.51), custom_call_target="tpu_custom_call" | custom-call | tf_op jit(solution)/shard_map/pallas_call | solution.py:184
  69.0 7.9 %all-to-all-start.1 = ((bf16[16,640,128]{2,1,0:T(8,128)(2,1)}), bf16[16,640,128]{2,1,0:T(8,128)(2,1)}, u32[]{:S(2)}, u32[]{:S(2)}) async-start(bf16[16,640,128]{2,1,0:T(8,128)(2,1)} %shard_map.91), calls=%async_computation.1 | async-start | bytes 5242880 | tf_op jit(solution)/shard_map/all_to_all | solution.py:260
  76.9 4.4 %gather_fusion.1 = bf16[16,64,2048]{2,1,0:T(8,128)(2,1)} fusion(bf16[8,64,2048]{2,1,0:T(8,128)(2,1)} %get-tuple-element.11, s32[1024]{0:T(1024)S(1)} %pad_clamp_fusion), kind=kCustom, calls=%fused_computation.1 | custom fusion | bytes 8388672 | tf_op jit(solution)/shard_map/gather | solution.py:243
  81.3 47.5 %shard_map.93 = bf16[8,2,64,2048]{3,2,1,0:T(8,128)(2,1)} custom-call(bf16[8,2,64,2048]{3,2,1,0:T(8,128)(2,1)} %bitcast.45), custom_call_target="tpu_custom_call" | custom-call | tf_op jit(solution)/shard_map/pallas_call | solution.py:66
  128.8 0.0 copy-start.5
  128.8 0.0 copy-start.2
  128.8 0.0 copy-start.3
  128.8 3.7 %shard_map.94 = bf16[16,512,128]{2,1,0:T(8,128)(2,1)} custom-call(s32[8]{0:T(128)} %dynamic-slice_add_fusion.picked_ref, bf16[16,64,2048]{2,1,0:T(8,128)(2,1)} %bitcast.46), custom_call_target="tpu_custom_call" | custom-call | tf_op jit(solution)/shard_map/pallas_call | solution.py:184
  132.6 0.0 all-to-all-done.1.kv_ref.qsrc_ref
  132.6 7.2 %all-to-all-start.2 = ((bf16[16,512,128]{2,1,0:T(8,128)(2,1)}), bf16[16,512,128]{2,1,0:T(8,128)(2,1)}, u32[]{:S(2)}, u32[]{:S(2)}) async-start(bf16[16,512,128]{2,1,0:T(8,128)(2,1)} %shard_map.94), calls=%async_computation.2 | async-start | bytes 4194304 | tf_op jit(solution)/shard_map/all_to_all | solution.py:265
  139.9 0.0 copy-done.5
  139.9 0.1 dynamic_slice.16
  139.9 0.0 copy-done.2
  139.9 0.0 copy-done.3
  139.9 0.2 select_reduce_fusion.3
  140.1 0.6 dynamic_slice.17.len_ref
  140.7 17.7 %shard_map.92 = f32[2048,128]{1,0:T(8,128)} custom-call(s32[1]{0:T(128)} %dynamic_slice.17.len_ref, bf16[16,640,128]{2,1,0:T(8,128)(2,1)} %all-to-all-done.1.kv_ref.qsrc_ref, bf16[16,640,128]{2,1,0:T(8,128)(2,1)} %all-to-all-done.1.kv_ref.qsrc_ref), custom_call_target="tpu_custom_call" | custom-call | tf_op jit(solution)/shard_map/pallas_call | solution.py:134
  158.5 12.1 %all-to-all-done.2.kv_ref = bf16[16,512,128]{2,1,0:T(8,128)(2,1)} async-done(((bf16[16,512,128]{2,1,0:T(8,128)(2,1)}), bf16[16,512,128]{2,1,0:T(8,128)(2,1)}, u32[]{:S(2)}, u32[]{:S(2)}) %all-to-all-start.2) | async-done | bytes 2097184 | tf_op jit(solution)/shard_map/all_to_all | solution.py:265
  170.5 17.4 %shard_map.95 = f32[2048,128]{1,0:T(8,128)} custom-call(s32[1]{0:T(128)} %dynamic_slice.17.len_ref, bf16[16,512,128]{2,1,0:T(8,128)(2,1)} %all-to-all-done.2.kv_ref, bf16[16,640,128]{2,1,0:T(8,128)(2,1)} %all-to-all-done.1.kv_ref.qsrc_ref), custom_call_target="tpu_custom_call" | custom-call | tf_op jit(solution)/shard_map/pallas_call | solution.py:134
  188.0 2.7 %add.130 = f32[2048,128]{1,0:T(8,128)} add(f32[2048,128]{1,0:T(8,128)} %shard_map.92, f32[2048,128]{1,0:T(8,128)} %shard_map.95) | non-fusion elementwise | flops 262144 | bytes 3145728 | tf_op jit(solution)/shard_map/add | solution.py:269
  190.7 0.0 copy-start.4
  190.7 6.9 %all-to-all-start.3 = ((f32[16,128,128]{2,1,0:T(8,128)}), f32[16,128,128]{2,1,0:T(8,128)}, u32[]{:S(2)}, u32[]{:S(2)}) async-start(f32[16,128,128]{2,1,0:T(8,128)} %bitcast.47), calls=%async_computation.3 | async-start | bytes 2097152 | tf_op jit(solution)/shard_map/all_to_all | solution.py:270
  197.6 2.7 %convert_multiply_fusion = f32[2,128,1,1024]{3,1,0,2:T(8,128)} fusion(bf16[2,128,1,1024]{3,2,1,0:T(2,128)(2,1)} %get-tuple-element.16, bf16[2,128,1,1024]{3,2,1,0:T(2,128)(2,1)S(1)} %get-tuple-element.13), kind=kLoop, calls=%fused_computation.22 | loop fusion | flops 786432 | bytes 2097152 | tf_op jit(solution)/shard_map/mul | solution.py:277
  200.3 1.4 copy.38
  201.7 0.3 bitcast_reduce_fusion
  202.0 0.1 copy.32
  202.1 0.0 copy-done.4
  202.1 0.1 divide_multiply_fusion
  202.2 0.1 copy.33
  202.4 0.1 broadcast_compare_fusion
  202.4 10.4 %all-to-all-done.3 = f32[16,128,128]{2,1,0:T(8,128)} async-done(((f32[16,128,128]{2,1,0:T(8,128)}), f32[16,128,128]{2,1,0:T(8,128)}, u32[]{:S(2)}, u32[]{:S(2)}) %all-to-all-start.3) | async-done | bytes 1048608 | tf_op jit(solution)/shard_map/all_to_all | solution.py:270
  212.9 5.1 %fusion.22 = (f32[2,128]{1,0:T(2,128)S(1)}, f32[2,128,8,128]{3,2,1,0:T(8,128)S(1)}) fusion(f32[2]{0:T(128)S(1)} %add_convert_fusion, f32[2,128,8,128]{3,2,1,0:T(8,128)} %bitcast.50, f32[2,128,8]{2,1,0:T(8,128)S(1)} %copy.33, f32[2,8,128,128]{3,2,1,0:T(8,128)} %bitcast.8), kind=kLoop, calls=%fused_computation.59 | loop fusion | flops 1048320 | bytes 3154952 | tf_op jit(solution)/shard_map/reduce_sum | solution.py:13
  218.0 1.2 reshape.357
  219.2 3.5 %multiply_reduce_fusion = f32[2,128]{1,0:T(2,128)S(1)} fusion(f32[2,128,8,128]{3,2,1,0:T(8,128)S(1)} %get-tuple-element.8, f32[2,128]{1,0:T(2,128)S(1)} %broadcast_multiply_fusion), kind=kLoop, calls=%fused_computation.21 | loop fusion | flops 786176 | bytes 1050624 | tf_op jit(solution)/shard_map/reduce_sum | solution.py:15
  222.7 0.0 copy-done
  222.7 3.3 %fusion.7 = bf16[2,128,1024]{2,1,0:T(8,128)(2,1)} fusion(bf16[1024,1024]{1,0:T(8,128)(2,1)S(1)} %copy-done, bf16[2,128,1024]{2,1,0:T(8,128)(2,1)} %param.9, f32[2,128,1,1024]{3,2,1,0:T(1,128)} %get-tuple-element.15, f32[2,128,1024]{2,1,0:T(8,128)} %reshape.357, f32[2,128]{1,0:T(2,128)S(1)} %add_rsqrt_fusion, f32[2,128]{1,0:T(2,128)S(1)} %broadcast_multiply_fusion, ...), kind=kOutput, calls=%fused_computation.9 | convolution fusion | flops 538968064 | bytes 5245184 | tf_op jit(solution)/shard_map/dot_general | solution.py:284
  (13 shorter events, 0.1 us)
Async XLA Ops:
  0.0 222.7 %copy-start = (bf16[1024,1024]{1,0:T(8,128)(2,1)S(1)}, bf16[1024,1024]{1,0:T(8,128)(2,1)}, u32[]{:S(2)}) copy-start(bf16[1024,1024]{1,0:T(8,128)(2,1)} %param.12) | copy-start | bytes 6291460
  11.3 5.1 %copy-start.1 = (bf16[2,128,1024]{2,1,0:T(8,128)(2,1)S(1)}, bf16[2,128,1024]{2,1,0:T(8,128)(2,1)}, u32[]{:S(2)}) copy-start(bf16[2,128,1024]{2,1,0:T(8,128)(2,1)} %param.9) | copy-start | bytes 1572868
  11.3 53.4 %all-to-all-start = ((bf16[8,2,64,2048]{3,2,1,0:T(8,128)(2,1)}), bf16[8,2,64,2048]{3,2,1,0:T(8,128)(2,1)}, u32[]{:S(2)}, u32[]{:S(2)}) async-start(bf16[8,2,64,2048]{3,2,1,0:T(8,128)(2,1)} %bitcast.44), calls=%async_computation | async-start | bytes 8388608 | tf_op jit(solution)/shard_map/all_to_all | solution.py:246
  69.0 63.6 %all-to-all-start.1 = ((bf16[16,640,128]{2,1,0:T(8,128)(2,1)}), bf16[16,640,128]{2,1,0:T(8,128)(2,1)}, u32[]{:S(2)}, u32[]{:S(2)}) async-start(bf16[16,640,128]{2,1,0:T(8,128)(2,1)} %shard_map.91), calls=%async_computation.1 | async-start | bytes 5242880 | tf_op jit(solution)/shard_map/all_to_all | solution.py:260
  128.8 11.1 %copy-start.5 = (s32[16]{0:T(128)S(1)}, s32[16]{0:T(128)}, u32[]{:S(2)}) copy-start(s32[16]{0:T(128)} %param.14) | copy-start | bytes 196
  128.8 11.2 %copy-start.2 = (s32[16]{0:T(128)S(1)}, s32[16]{0:T(128)}, u32[]{:S(2)}) copy-start(s32[16]{0:T(128)} %param.16) | copy-start | bytes 196
  128.8 11.1 %copy-start.3 = (s32[16]{0:T(128)S(1)}, s32[16]{0:T(128)}, u32[]{:S(2)}) copy-start(s32[16]{0:T(128)} %param.15) | copy-start | bytes 196
  132.6 38.0 %all-to-all-start.2 = ((bf16[16,512,128]{2,1,0:T(8,128)(2,1)}), bf16[16,512,128]{2,1,0:T(8,128)(2,1)}, u32[]{:S(2)}, u32[]{:S(2)}) async-start(bf16[16,512,128]{2,1,0:T(8,128)(2,1)} %shard_map.94), calls=%async_computation.2 | async-start | bytes 4194304 | tf_op jit(solution)/shard_map/all_to_all | solution.py:265
  190.7 11.5 %copy-start.4 = (f32[8]{0:T(128)S(1)}, f32[8]{0:T(128)}, u32[]{:S(2)}) copy-start(f32[8]{0:T(128)} %param.13) | copy-start | bytes 100
  190.7 22.2 %all-to-all-start.3 = ((f32[16,128,128]{2,1,0:T(8,128)}), f32[16,128,128]{2,1,0:T(8,128)}, u32[]{:S(2)}, u32[]{:S(2)}) async-start(f32[16,128,128]{2,1,0:T(8,128)} %bitcast.47), calls=%async_computation.3 | async-start | bytes 2097152 | tf_op jit(solution)/shard_map/all_to_all | solution.py:270

commit v9 on v7

--- a/solution.py
+++ b/solution.py
@@ -194,6 +194,43 @@
     )(*operands)
 
 
+def finish_kernel(
+    bias_ref, len_ref, limit_ref, hist_ref, proj_ref, x_ref, w_ref, out_ref, att_ref, *, heads, score_scale
+):
+    users, rows, width = x_ref.shape
+    head_dim = width // heads
+    for u in range(users):
+        divisor = (len_ref[u] + 1).astype(jnp.float32)
+        for e in range(heads):
+            value = proj_ref[u, :, pl.ds(width + e * head_dim, head_dim)].astype(jnp.float32)
+            query = proj_ref[u, :, pl.ds(2 * width + e * head_dim, head_dim)].astype(jnp.float32)
+            key = proj_ref[u, :, pl.ds(3 * width + e * head_dim, head_dim)].astype(jnp.float32)
+            self_score = jnp.sum(query * key, axis=-1, keepdims=True) * score_scale + bias_ref[e]
+            own = self_score * (0.5 + 0.5 * jnp.tanh(0.5 * self_score)) * value
+            att_ref[:, pl.ds(e * head_dim, head_dim)] = (hist_ref[u * heads + e] + own) / divisor
+        attended = att_ref[...]
+        centred = attended - jnp.mean(attended, axis=-1, keepdims=True)
+        spread = jnp.mean(centred * centred, axis=-1, keepdims=True)
+        gate = proj_ref[u, :, pl.ds(0, width)].astype(jnp.float32)
+        gated = (centred * lax.rsqrt(spread + 1e-05) * gate).astype(jnp.bfloat16)
+        result = x_ref[u].astype(jnp.float32) + jnp.dot(gated, w_ref[...], preferred_element_type=jnp.float32)
+        row = lax.broadcasted_iota(jnp.int32, (rows, 1), 0)
+        out_ref[u] = jnp.where(row < limit_ref[u], result, 0.0).astype(out_ref.dtype)
+
+
+def finish(history_back, projected, cand_x, w_out, self_bias, lengths, row_limit, heads, score_scale):
+    users, rows, width = cand_x.shape
+    smem = pl.BlockSpec(memory_space=pltpu.SMEM)
+    vmem = pl.BlockSpec(memory_space=pltpu.VMEM)
+    return pl.pallas_call(
+        functools.partial(finish_kernel, heads=heads, score_scale=score_scale),
+        out_shape=jax.ShapeDtypeStruct(cand_x.shape, cand_x.dtype),
+        in_specs=[smem, smem, smem, vmem, vmem, vmem, vmem],
+        out_specs=vmem,
+        scratch_shapes=[pltpu.VMEM((rows, width), jnp.float32)],
+    )(self_bias, lengths, row_limit, history_back, projected, cand_x, w_out)
+
+
 def local(cand_x, kv_cache, w_uvqk, w_out, self_bias, user_rank, hist_len, cand_count, tile_slot):
     users_here, cand_rows, width = cand_x.shape
     heads = self_bias.shape[0]
@@ -270,22 +307,11 @@
     history_back = lax.all_to_all(
         history_mine.reshape(hist_count, cand_rows, head_dim), "hist", split_axis=0, concat_axis=0, tiled=True
     )
-    combined = history_back.reshape(users_here, heads, cand_rows, head_dim).transpose(0, 2, 1, 3)
-    query_wide = queries.astype(jnp.float32).reshape(users_here, cand_rows, heads, head_dim)
-    key_wide = k_self.astype(jnp.float32).reshape(users_here, cand_rows, heads, head_dim)
-    value_wide = v_self.astype(jnp.float32).reshape(users_here, cand_rows, heads, head_dim)
-    self_scores = jnp.sum(query_wide * key_wide, axis=-1) * score_scale + self_bias
-    own_term = jax.nn.silu(self_scores)[..., None] * value_wide
-    divisor = (lengths + 1).astype(jnp.float32)[:, None, None, None]
-    attended = (combined + own_term) / divisor
-    gated = (
-        layer_norm(attended.reshape(users_here, cand_rows, width)) * u_gate.astype(jnp.float32)
-    ).astype(jnp.bfloat16)
-    update = jnp.dot(gated.reshape(-1, width), w_out, preferred_element_type=jnp.float32)
-    result = cand_x.astype(jnp.float32) + update.reshape(users_here, cand_rows, width)
-    cand_index = hist_index * cand_rows + jnp.arange(cand_rows)
-    live_rows = cand_index[None, :] < live_counts[:, None]
-    return jnp.where(live_rows[:, :, None], result, 0.0).astype(jnp.bfloat16)
+    row_limit = (live_counts - hist_index * cand_rows).astype(jnp.int32)
+    return finish(
+        history_back, projected.reshape(users_here, cand_rows, 4 * width), cand_x, w_out, self_bias,
+        lengths.astype(jnp.int32), row_limit, heads, score_scale,
+    )
 
 
 def solution(mesh):

time: 227 us -> 218 us (0.960)
  Pallas kernels: 73.6 us -> 95.4 us
  other arithmetic: 25.5 us -> 4.74 us
  starting transfers between devices: 35.9 us -> 27 us
  waiting for transfers between devices: 53.6 us -> 61.4 us
  matrix products: 10.5 us -> 5.85 us
  local copies, waits for them, and re-layouts: 24.3 us -> 21.1 us
    pallas_call x2, Pallas kernels: 18.1 us -> 35 us  [attend(): pl.pallas_call(kernel, out_shape=jax.ShapeDtypeStruct((rows, head_dim), j...]
    all_to_all x1, waiting for transfers between devices: 25.3 us -> 34.4 us  [local(): lax.all_to_all(outgoing, 'req', split_axis=0, concat_axis=0, tiled=True)]
    slice x1 -> x0, other arithmetic: 9.08 us -> none  [local(): queries = projected[:, :, 2]]
    all_to_all x1, starting transfers between devices: 15.7 us -> 6.75 us  [local(): lax.all_to_all(history_mine.reshape(hist_count, cand_rows, head_dim), 'hi...]
    all_to_all x1, waiting for transfers between devices: 20.2 us -> 12.2 us  [local(): lax.all_to_all(pack_for_heads(picked_slot, halves[1], None, users_here, h...]
    all_to_all x1, waiting for transfers between devices: 8.11 us -> 14.8 us  [local(): lax.all_to_all(history_mine.reshape(hist_count, cand_rows, head_dim), 'hi...]
    reduce_sum x2 -> x1, other arithmetic: 5.25 us -> 0.15 us  [layer_norm(): mean_value = jnp.mean(values, axis=-1, keepdims=True)]
    pallas_call x0 -> x1, Pallas kernels: none -> 4.93 us  [finish(): pl.pallas_call(functools.partial(finish_kernel, heads=heads, score_scale=...]
  transfers between devices with their start and end apart: 4 -> 4, of which waited for: 3 -> 3; matrix products, arithmetic and copies ran while one was open for 15% -> 9% of each run, Pallas kernels for 27% -> 32%
where the time goes in v9:
time: 218 us; the launch traced here: 216 us
  Pallas kernels  95.4 us (44%)
  waiting for transfers between devices  61.4 us (28%)
  starting transfers between devices  27 us (12%)
  local copies, waits for them, and re-layouts  21.1 us (10%)
  matrix products  5.85 us (3%)
  other arithmetic  4.74 us (2%)
    pallas_call x1, Pallas kernels, req_a2a(): pl.pallas_call(functools.partial(req_a2a_kernel, axis='req', other_axis='...  47.5 us
    pallas_call x2, Pallas kernels, attend(): pl.pallas_call(kernel, out_shape=jax.ShapeDtypeStruct((rows, head_dim), j...  35 us
    all_to_all x1, waiting for transfers between devices, local(): lax.all_to_all(outgoing, 'req', split_axis=0, concat_axis=0, tiled=True)  34.4 us
    all_to_all x1, waiting for transfers between devices, local(): lax.all_to_all(history_mine.reshape(hist_count, cand_rows, head_dim), 'hi...  14.8 us
    all_to_all x1, waiting for transfers between devices, local(): lax.all_to_all(pack_for_heads(picked_slot, halves[1], None, users_here, h...  12.2 us
    pallas_call x2, Pallas kernels, pack_for_heads(): pl.pallas_call(functools.partial(pack_kernel, heads=heads, users=users, p...  7.99 us
    all_to_all x1, starting transfers between devices, local(): lax.all_to_all(pack_for_heads(picked_slot, halves[0], queries, users_here...  7.89 us
    all_to_all x1, starting transfers between devices, local(): lax.all_to_all(pack_for_heads(picked_slot, halves[1], None, users_here, h...  7.28 us
  transfers between devices with their start and end apart: 4, of which 3 were waited for; matrix products, arithmetic and copies ran while one was open for 9% of the time, Pallas kernels for 32%

profile of v9, /device:TPU:8, one launch (start us, length us, event | category | flops | bytes accessed | tf_op | source)
XLA Modules:
  0.0 215.7 jit_solution(9291781839097607882)
XLA Ops:
  0.0 0.8 reshape.248
  0.8 0.4 dynamic-slice_reduce_fusion
  1.2 0.1 reshape.249
  1.3 0.1 broadcast_in_dim.63
  1.4 0.1 eq.98
  1.5 0.2 select_reduce_fusion
  1.7 0.1 select_reduce_fusion.1
  1.9 0.1 copy.14
  1.9 0.1 reshape.250
  2.0 4.0 %fusion.7 = (bf16[8,64,2048]{2,1,0:T(8,128)(2,1)}, bf16[8,64,2048]{2,1,0:T(8,128)(2,1)S(1)}) fusion(bf16[8,128,2048]{2,1,0:T(8,128)(2,1)} %param.10), kind=kLoop, calls=%fused_computation.38 | loop fusion | bytes 8388608 | tf_op jit(solution)/shard_map/slice | solution.py:279
  6.0 2.8 %gather_fusion = bf16[16,64,2048]{2,1,0:T(8,128)(2,1)} fusion(bf16[8,64,2048]{2,1,0:T(8,128)(2,1)S(1)} %get-tuple-element.10, s32[1024]{0:T(1024)S(1)} %pad_clamp_fusion), kind=kCustom, calls=%fused_computation | custom fusion | bytes 8388672 | tf_op jit(solution)/shard_map/gather | solution.py:280
  8.8 0.0 copy-start.2
  8.8 5.0 %all-to-all-start = ((bf16[8,2,64,2048]{3,2,1,0:T(8,128)(2,1)}), bf16[8,2,64,2048]{3,2,1,0:T(8,128)(2,1)}, u32[]{:S(2)}, u32[]{:S(2)}) async-start(bf16[8,2,64,2048]{3,2,1,0:T(8,128)(2,1)} %bitcast.14), calls=%async_computation | async-start | bytes 8388608 | tf_op jit(solution)/shard_map/all_to_all | solution.py:283
  13.9 0.0 copy-done.2
  13.9 0.1 convert_reduce_fusion
  14.0 0.3 fusion.2
  14.3 0.3 fusion.3
  14.6 5.8 %multiply_convert_fusion = bf16[256,4096]{1,0:T(8,128)(2,1)S(1)} fusion(bf16[256,1024]{1,0:T(8,128)(2,1)S(1)} %bitcast.19, bf16[1024,4096]{1,0:T(8,128)(2,1)} %param.11), kind=kOutput, calls=%fused_computation.2 | convolution fusion | flops 2152726528 | bytes 11010048 | tf_op jit(solution)/shard_map/dot_general | solution.py:288
  20.4 0.0 copy-start.1
  20.5 3.0 %reshape.254 = bf16[2,128,4,1024]{3,2,1,0:T(4,128)(2,1)} reshape(bf16[256,4096]{1,0:T(8,128)(2,1)S(1)} %multiply_convert_fusion) | data formatting | bytes 4194304 | tf_op jit(solution)/shard_map/reshape | solution.py:289
  23.5 2.7 %slice.16 = bf16[2,128,1,1024]{3,2,1,0:T(2,128)(2,1)S(1)} slice(bf16[2,128,4,1024]{3,2,1,0:T(4,128)(2,1)} %reshape.254), slice={[0:2], [0:128], [2:3], [0:1024]} | slice | bytes 1048576 | tf_op jit(solution)/shard_map/slice | solution.py:292
  26.2 1.0 copy.19
  27.2 0.6 dynamic-slice_add_fusion.picked_ref
  27.8 34.4 %all-to-all-done = bf16[8,2,64,2048]{3,2,1,0:T(8,128)(2,1)} async-done(((bf16[8,2,64,2048]{3,2,1,0:T(8,128)(2,1)}), bf16[8,2,64,2048]{3,2,1,0:T(8,128)(2,1)}, u32[]{:S(2)}, u32[]{:S(2)}) %all-to-all-start) | async-done | bytes 4194336 | tf_op jit(solution)/shard_map/all_to_all | solution.py:283
  62.2 4.2 %shard_map.91 = bf16[16,640,128]{2,1,0:T(8,128)(2,1)} custom-call(s32[8]{0:T(128)} %dynamic-slice_add_fusion.picked_ref, bf16[16,64,2048]{2,1,0:T(8,128)(2,1)} %bitcast.2.tiles_hbm, bf16[2,128,1024]{2,1,0:T(8,128)(2,1)} %bitcast.18), custom_call_target="tpu_custom_call" | custom-call | tf_op jit(solution)/shard_map/pallas_call | solution.py:184
  66.4 0.0 copy-done.1
  66.5 7.9 %all-to-all-start.1 = ((bf16[16,640,128]{2,1,0:T(8,128)(2,1)}), bf16[16,640,128]{2,1,0:T(8,128)(2,1)S(1)}, u32[]{:S(2)}, u32[]{:S(2)}) async-start(bf16[16,640,128]{2,1,0:T(8,128)(2,1)} %shard_map.91), calls=%async_computation.1 | async-start | bytes 5242880 | tf_op jit(solution)/shard_map/all_to_all | solution.py:297
  74.4 4.4 %gather_fusion.1 = bf16[16,64,2048]{2,1,0:T(8,128)(2,1)} fusion(bf16[8,64,2048]{2,1,0:T(8,128)(2,1)} %get-tuple-element.9, s32[1024]{0:T(1024)S(1)} %pad_clamp_fusion), kind=kCustom, calls=%fused_computation.1 | custom fusion | bytes 8388672 | tf_op jit(solution)/shard_map/gather | solution.py:280
  78.7 47.5 %shard_map.93 = bf16[8,2,64,2048]{3,2,1,0:T(8,128)(2,1)} custom-call(bf16[8,2,64,2048]{3,2,1,0:T(8,128)(2,1)} %bitcast.15), custom_call_target="tpu_custom_call" | custom-call | tf_op jit(solution)/shard_map/pallas_call | solution.py:66
  126.2 0.0 copy-start.8
  126.2 0.0 copy-start.6
  126.2 0.0 copy-start.7
  126.2 3.7 %shard_map.94 = bf16[16,512,128]{2,1,0:T(8,128)(2,1)} custom-call(s32[8]{0:T(128)} %dynamic-slice_add_fusion.picked_ref, bf16[16,64,2048]{2,1,0:T(8,128)(2,1)} %bitcast.16), custom_call_target="tpu_custom_call" | custom-call | tf_op jit(solution)/shard_map/pallas_call | solution.py:184
  130.0 0.0 all-to-all-done.1.kv_ref.qsrc_ref
  130.0 0.0 copy-start
  130.0 7.3 %all-to-all-start.2 = ((bf16[16,512,128]{2,1,0:T(8,128)(2,1)}), bf16[16,512,128]{2,1,0:T(8,128)(2,1)}, u32[]{:S(2)}, u32[]{:S(2)}) async-start(bf16[16,512,128]{2,1,0:T(8,128)(2,1)} %shard_map.94), calls=%async_computation.2 | async-start | bytes 4194304 | tf_op jit(solution)/shard_map/all_to_all | solution.py:302
  137.3 0.0 copy-done.8
  137.3 0.1 dynamic_slice.16
  137.4 0.0 copy-done.6
  137.4 0.0 copy-done.7
  137.4 0.2 select_reduce_fusion.2
  137.6 0.0 copy-start.5
  137.6 0.6 dynamic_slice.17.len_ref
  138.2 0.0 copy-done
  138.2 17.6 %shard_map.92 = f32[2048,128]{1,0:T(8,128)} custom-call(s32[1]{0:T(128)} %dynamic_slice.17.len_ref, bf16[16,640,128]{2,1,0:T(8,128)(2,1)} %copy-done, bf16[16,640,128]{2,1,0:T(8,128)(2,1)} %copy-done), custom_call_target="tpu_custom_call" | custom-call | tf_op jit(solution)/shard_map/pallas_call | solution.py:134
  155.8 0.0 copy-start.3
  155.8 12.2 %all-to-all-done.2.kv_ref = bf16[16,512,128]{2,1,0:T(8,128)(2,1)} async-done(((bf16[16,512,128]{2,1,0:T(8,128)(2,1)}), bf16[16,512,128]{2,1,0:T(8,128)(2,1)}, u32[]{:S(2)}, u32[]{:S(2)}) %all-to-all-start.2) | async-done | bytes 2097184 | tf_op jit(solution)/shard_map/all_to_all | solution.py:302
  168.0 17.4 %shard_map.95 = f32[2048,128]{1,0:T(8,128)} custom-call(s32[1]{0:T(128)} %dynamic_slice.17.len_ref, bf16[16,512,128]{2,1,0:T(8,128)(2,1)} %all-to-all-done.2.kv_ref, bf16[16,640,128]{2,1,0:T(8,128)(2,1)} %copy-done), custom_call_target="tpu_custom_call" | custom-call | tf_op jit(solution)/shard_map/pallas_call | solution.py:134
  185.4 0.0 copy-done.5
  185.4 0.0 copy-done.3
  185.4 2.3 %add.81 = f32[2048,128]{1,0:T(8,128)} add(f32[2048,128]{1,0:T(8,128)S(1)} %copy-done.3, f32[2048,128]{1,0:T(8,128)} %shard_map.95) | non-fusion elementwise | flops 262144 | bytes 3145728 | tf_op jit(solution)/shard_map/add | solution.py:306
  187.7 6.7 %all-to-all-start.3 = ((f32[16,128,128]{2,1,0:T(8,128)}), f32[16,128,128]{2,1,0:T(8,128)S(1)}, u32[]{:S(2)}, u32[]{:S(2)}) async-start(f32[16,128,128]{2,1,0:T(8,128)} %bitcast.7), calls=%async_computation.3 | async-start | bytes 2097152 | tf_op jit(solution)/shard_map/all_to_all | solution.py:307
  194.5 0.5 broadcast_subtract_fusion.limit_ref
  195.0 14.8 %all-to-all-done.3.hist_ref = f32[16,128,128]{2,1,0:T(8,128)S(1)} async-done(((f32[16,128,128]{2,1,0:T(8,128)}), f32[16,128,128]{2,1,0:T(8,128)S(1)}, u32[]{:S(2)}, u32[]{:S(2)}) %all-to-all-start.3) | async-done | bytes 1048608 | tf_op jit(solution)/shard_map/all_to_all | solution.py:307
  209.8 0.0 copy-start.4
  209.8 1.0 copy-done.4
  210.8 4.9 %shard_map.96 = bf16[2,128,1024]{2,1,0:T(8,128)(2,1)} custom-call(f32[8]{0:T(128)} %bias_ref.1, s32[2]{0:T(128)} %copy-done.5, s32[2]{0:T(128)} %broadcast_subtract_fusion.limit_ref, f32[16,128,128]{2,1,0:T(8,128)} %copy-done.4, bf16[2,128,4096]{2,1,0:T(8,128)(2,1)} %bitcast.17, bf16[2,128,1024]{2,1,0:T(8,128)(2,1)} %x_ref.1, bf16[1024,1024]{1,0:T(8,128)(2,1)} %w_ref.1), custom_call_target="tpu_custom_call" | custom-call | tf_op jit(solution)/shard_map/pallas_call | solution.py:225
  (9 shorter events, 0.1 us)
Async XLA Ops:
  8.8 5.1 %copy-start.2 = (bf16[2,128,1024]{2,1,0:T(8,128)(2,1)S(1)}, bf16[2,128,1024]{2,1,0:T(8,128)(2,1)}, u32[]{:S(2)}) copy-start(bf16[2,128,1024]{2,1,0:T(8,128)(2,1)} %x_ref.1) | copy-start | bytes 1572868
  8.8 53.4 %all-to-all-start = ((bf16[8,2,64,2048]{3,2,1,0:T(8,128)(2,1)}), bf16[8,2,64,2048]{3,2,1,0:T(8,128)(2,1)}, u32[]{:S(2)}, u32[]{:S(2)}) async-start(bf16[8,2,64,2048]{3,2,1,0:T(8,128)(2,1)} %bitcast.14), calls=%async_computation | async-start | bytes 8388608 | tf_op jit(solution)/shard_map/all_to_all | solution.py:283
  20.4 46.0 %copy-start.1 = (bf16[256,4096]{1,0:T(8,128)(2,1)}, bf16[256,4096]{1,0:T(8,128)(2,1)S(1)}, u32[]{:S(2)}) copy-start(bf16[256,4096]{1,0:T(8,128)(2,1)S(1)} %multiply_convert_fusion) | copy-start | bytes 6291460
  66.5 63.5 %all-to-all-start.1 = ((bf16[16,640,128]{2,1,0:T(8,128)(2,1)}), bf16[16,640,128]{2,1,0:T(8,128)(2,1)S(1)}, u32[]{:S(2)}, u32[]{:S(2)}) async-start(bf16[16,640,128]{2,1,0:T(8,128)(2,1)} %shard_map.91), calls=%async_computation.1 | async-start | bytes 5242880 | tf_op jit(solution)/shard_map/all_to_all | solution.py:297
  126.2 11.1 %copy-start.8 = (s32[16]{0:T(128)S(1)}, s32[16]{0:T(128)}, u32[]{:S(2)}) copy-start(s32[16]{0:T(128)} %param.14) | copy-start | bytes 196
  126.2 11.2 %copy-start.6 = (s32[16]{0:T(128)S(1)}, s32[16]{0:T(128)}, u32[]{:S(2)}) copy-start(s32[16]{0:T(128)} %param.16) | copy-start | bytes 196
  126.2 11.2 %copy-start.7 = (s32[16]{0:T(128)S(1)}, s32[16]{0:T(128)}, u32[]{:S(2)}) copy-start(s32[16]{0:T(128)} %param.15) | copy-start | bytes 196
  130.0 8.2 %copy-start = (bf16[16,640,128]{2,1,0:T(8,128)(2,1)}, bf16[16,640,128]{2,1,0:T(8,128)(2,1)S(1)}, u32[]{:S(2)}) copy-start(bf16[16,640,128]{2,1,0:T(8,128)(2,1)S(1)} %all-to-all-done.1.kv_ref.qsrc_ref) | copy-start | bytes 7864324
  130.0 38.0 %all-to-all-start.2 = ((bf16[16,512,128]{2,1,0:T(8,128)(2,1)}), bf16[16,512,128]{2,1,0:T(8,128)(2,1)}, u32[]{:S(2)}, u32[]{:S(2)}) async-start(bf16[16,512,128]{2,1,0:T(8,128)(2,1)} %shard_map.94), calls=%async_computation.2 | async-start | bytes 4194304 | tf_op jit(solution)/shard_map/all_to_all | solution.py:302
  137.6 47.8 %copy-start.5 = (s32[2]{0:T(128)}, s32[2]{0:T(128)S(1)}, u32[]{:S(2)}) copy-start(s32[2]{0:T(128)S(1)} %get-tuple-element.6.len_ref) | copy-start | bytes 28
  155.8 29.7 %copy-start.3 = (f32[2048,128]{1,0:T(8,128)S(1)}, f32[2048,128]{1,0:T(8,128)}, u32[]{:S(2)}) copy-start(f32[2048,128]{1,0:T(8,128)} %shard_map.92) | copy-start | bytes 3145732
  187.7 22.1 %all-to-all-start.3 = ((f32[16,128,128]{2,1,0:T(8,128)}), f32[16,128,128]{2,1,0:T(8,128)S(1)}, u32[]{:S(2)}, u32[]{:S(2)}) async-start(f32[16,128,128]{2,1,0:T(8,128)} %bitcast.7), calls=%async_computation.3 | async-start | bytes 2097152 | tf_op jit(solution)/shard_map/all_to_all | solution.py:307
  209.8 1.0 copy-start.4

commit v10 on v9

--- a/solution.py
+++ b/solution.py
@@ -77,9 +77,12 @@
     )(x)
 
 
-def attend_kernel(
-    len_ref, kv_ref, qsrc_ref, o_ref, q_ref, *, n_tiles, sub, tile_len, offset, q_row, score_scale, chunk
-):
+def attend_kernel(len_ref, kv_ref, qsrc_ref, *rest, n_tiles, sub, tile_len, offset, q_row, score_scale, chunk):
+    if len(rest) == 3:
+        init_ref, o_ref, q_ref = rest
+    else:
+        init_ref = None
+        o_ref, q_ref = rest
     length = len_ref[0]
     n_cls, _, head_dim = kv_ref.shape
     span = n_tiles * sub
@@ -87,7 +90,10 @@
     half_scale = 0.5 * score_scale
     for b in range(n_cls):
         q_ref[pl.ds(b * block, block), :] = qsrc_ref[b, pl.ds(q_row, block), :]
-    o_ref[...] = jnp.zeros_like(o_ref)
+    if init_ref is None:
+        o_ref[...] = jnp.zeros_like(o_ref)
+    else:
+        o_ref[...] = init_ref[...]
 
     def one_class(c, carry):
         key_index = lax.broadcasted_iota(jnp.int32, (1, span), 1)
@@ -117,13 +123,13 @@
     lax.fori_loop(0, n_cls, one_class, 0)
 
 
-def attend(length, kv_packed, q_packed, q_row, sub, tile_len, offset, score_scale):
+def attend(length, kv_packed, q_packed, q_row, n_tiles, sub, tile_len, offset, score_scale, init=None):
     n_cls, _, head_dim = q_packed.shape
     rows = n_cls * (q_packed.shape[1] - q_row)
     chunk = 2048
     kernel = functools.partial(
         attend_kernel,
-        n_tiles=q_row // (2 * sub),
+        n_tiles=n_tiles,
         sub=sub,
         tile_len=tile_len,
         offset=offset,
@@ -134,14 +140,11 @@
     return pl.pallas_call(
         kernel,
         out_shape=jax.ShapeDtypeStruct((rows, head_dim), jnp.float32),
-        in_specs=[
-            pl.BlockSpec(memory_space=pltpu.SMEM),
-            pl.BlockSpec(memory_space=pltpu.VMEM),
-            pl.BlockSpec(memory_space=pltpu.VMEM),
-        ],
+        in_specs=[pl.BlockSpec(memory_space=pltpu.SMEM)]
+        + [pl.BlockSpec(memory_space=pltpu.VMEM)] * (2 if init is None else 3),
         out_specs=pl.BlockSpec(memory_space=pltpu.VMEM),
         scratch_shapes=[pltpu.VMEM((rows, head_dim), jnp.bfloat16)],
-    )(length, kv_packed, q_packed)
+    )(length, kv_packed, q_packed, *([] if init is None else [init]))
 
 
 def pack_kernel(picked_ref, tiles_hbm, *rest, heads, users, per_hist, with_q):
@@ -273,17 +276,18 @@
     my_owner = lax.dynamic_slice_in_dim(owners, first_entry, users_here * per_hist)
     my_place = lax.dynamic_slice_in_dim(places, first_entry, users_here * per_hist)
     picked_slot = (my_owner * capacity + my_place).astype(jnp.int32)
-    sub = tile_len // 2
+    first_len = tile_len - tile_len // 4
+    bounds = [(0, first_len), (first_len, tile_len)]
     halves = []
-    for half in range(2):
-        kv_half = lax.slice_in_dim(kv_cache, half * sub, (half + 1) * sub, axis=1)
+    for half, (lo, hi) in enumerate(bounds):
+        kv_half = lax.slice_in_dim(kv_cache, lo, hi, axis=1)
         outgoing = kv_half.at[source_slot].get(mode="promise_in_bounds")
-        outgoing = outgoing.reshape(req_count, capacity, sub, 2 * width)
+        outgoing = outgoing.reshape(req_count, capacity, hi - lo, 2 * width)
         if half == 0:
             incoming = lax.all_to_all(outgoing, "req", split_axis=0, concat_axis=0, tiled=True)
         else:
             incoming = req_a2a(outgoing, 0)
-        halves.append(incoming.reshape(req_count * capacity, sub, 2 * width))
+        halves.append(incoming.reshape(req_count * capacity, hi - lo, 2 * width))
     normed = layer_norm(cand_x.astype(jnp.float32)).astype(jnp.bfloat16)
     mixed_in = jnp.dot(normed.reshape(-1, width), w_uvqk, preferred_element_type=jnp.float32)
     projected = jax.nn.silu(mixed_in).astype(jnp.bfloat16).reshape(users_here, cand_rows, 4, width)
@@ -293,17 +297,20 @@
     k_self = projected[:, :, 3]
     my_user = hist_index // heads
     my_length = lax.dynamic_slice_in_dim(lengths, my_user, 1)
-    q_row = 2 * per_hist * sub
+    q_row = 2 * per_hist * first_len
     packed_a = lax.all_to_all(
         pack_for_heads(picked_slot, halves[0], queries, users_here, heads),
         "hist", split_axis=0, concat_axis=0, tiled=True,
     )
-    history_mine = attend(my_length, packed_a, packed_a, q_row, sub, tile_len, 0, score_scale)
+    history_mine = attend(my_length, packed_a, packed_a, q_row, per_hist, first_len, tile_len, 0, score_scale)
     packed_b = lax.all_to_all(
         pack_for_heads(picked_slot, halves[1], None, users_here, heads),
         "hist", split_axis=0, concat_axis=0, tiled=True,
     )
-    history_mine = history_mine + attend(my_length, packed_b, packed_a, q_row, sub, tile_len, sub, score_scale)
+    history_mine = attend(
+        my_length, packed_b, packed_a, q_row, per_hist, tile_len - first_len, tile_len, first_len, score_scale,
+        init=history_mine,
+    )
     history_back = lax.all_to_all(
         history_mine.reshape(hist_count, cand_rows, head_dim), "hist", split_axis=0, concat_axis=0, tiled=True
     )

time: 218 us -> 222 us (1.018)
  the two profiles are of different devices: /device:TPU:8 before, /device:TPU:0 now
where the time goes in v10:
time: 222 us
  waiting for transfers between devices  93 us (42%)
  Pallas kernels  58.8 us (26%)
  starting transfers between devices  44.6 us (20%)
  local copies, waits for them, and re-layouts  16.8 us (8%)
  matrix products  5.85 us (3%)
  other arithmetic  2.42 us (1%)
    all_to_all x1, waiting for transfers between devices, local(): lax.all_to_all(outgoing, 'req', split_axis=0, concat_axis=0, tiled=True)  58.2 us
    pallas_call x1, Pallas kernels, req_a2a(): pl.pallas_call(functools.partial(req_a2a_kernel, axis='req', other_axis='...  24.6 us
    all_to_all x1, starting transfers between devices, local(): lax.all_to_all(history_mine.reshape(hist_count, cand_rows, head_dim), 'hi...  21.6 us
    pallas_call x2, Pallas kernels, attend(): pl.pallas_call(kernel, out_shape=jax.ShapeDtypeStruct((rows, head_dim), j...  21.3 us
    all_to_all x1, waiting for transfers between devices, local(): lax.all_to_all(pack_for_heads(picked_slot, halves[0], queries, users_here...  18.7 us
    all_to_all x1, waiting for transfers between devices, local(): lax.all_to_all(history_mine.reshape(hist_count, cand_rows, head_dim), 'hi...  14.7 us
    all_to_all x1, starting transfers between devices, local(): lax.all_to_all(pack_for_heads(picked_slot, halves[1], None, users_here, h...  10 us
    all_to_all x1, starting transfers between devices, local(): lax.all_to_all(pack_for_heads(picked_slot, halves[0], queries, users_here...  8.15 us
  transfers between devices with their start and end apart: 4, of which 4 were waited for; matrix products, arithmetic and copies ran while one was open for 8% of the time, Pallas kernels for 19%

profile of v10, /device:TPU:0, one launch (start us, length us, event | category | flops | bytes accessed | tf_op | source)
XLA Modules:
  0.0 221.8 jit_solution(5348394571283552461)
XLA Ops:
  0.0 0.0 slice-start
  0.0 0.9 reshape.248
  0.9 0.4 dynamic-slice_reduce_fusion
  1.4 0.1 reshape.249
  1.5 0.1 broadcast_in_dim.63
  1.6 0.1 eq.98
  1.7 0.2 select_reduce_fusion
  1.9 0.1 select_reduce_fusion.1
  2.0 0.1 copy.14
  2.1 0.1 reshape.250
  2.2 0.0 slice-done
  2.2 3.6 %gather_fusion.1 = bf16[16,96,2048]{2,1,0:T(8,128)(2,1)} fusion(bf16[8,96,2048]{2,1,0:T(8,128)(2,1)S(1)} %slice-done, s32[1024]{0:T(1024)S(1)} %pad_clamp_fusion), kind=kCustom, calls=%fused_computation.1 | custom fusion | bytes 12582976 | tf_op jit(solution)/shard_map/gather | solution.py:284
  5.8 0.0 copy-start.1
  5.8 4.9 %all-to-all-start.1 = ((bf16[8,2,96,2048]{3,2,1,0:T(8,128)(2,1)}), bf16[8,2,96,2048]{3,2,1,0:T(8,128)(2,1)}, u32[]{:S(2)}, u32[]{:S(2)}) async-start(bf16[8,2,96,2048]{3,2,1,0:T(8,128)(2,1)} %bitcast.14), calls=%async_computation.1 | async-start | bytes 12582912 | tf_op jit(solution)/shard_map/all_to_all | solution.py:287
  10.7 0.0 copy-done.1
  10.7 0.1 convert_reduce_fusion
  10.9 0.3 fusion.2
  11.2 0.3 fusion.3
  11.4 5.8 %multiply_convert_fusion = bf16[256,4096]{1,0:T(8,128)(2,1)S(1)} fusion(bf16[256,1024]{1,0:T(8,128)(2,1)S(1)} %bitcast.20, bf16[1024,4096]{1,0:T(8,128)(2,1)} %param.11), kind=kOutput, calls=%fused_computation.2 | convolution fusion | flops 2152726528 | bytes 11010048 | tf_op jit(solution)/shard_map/dot_general | solution.py:292
  17.3 0.0 copy-start
  17.3 3.1 %reshape.256 = bf16[2,128,4,1024]{3,2,1,0:T(4,128)(2,1)} reshape(bf16[256,4096]{1,0:T(8,128)(2,1)S(1)} %multiply_convert_fusion) | data formatting | bytes 4194304 | tf_op jit(solution)/shard_map/reshape | solution.py:293
  20.4 2.7 %slice.16 = bf16[2,128,1,1024]{3,2,1,0:T(2,128)(2,1)S(1)} slice(bf16[2,128,4,1024]{3,2,1,0:T(4,128)(2,1)} %reshape.256), slice={[0:2], [0:128], [2:3], [0:1024]} | slice | bytes 1048576 | tf_op jit(solution)/shard_map/slice | solution.py:296
  23.1 1.0 copy.19
  24.0 0.6 dynamic-slice_add_fusion.picked_ref
  24.6 58.2 %all-to-all-done.1 = bf16[8,2,96,2048]{3,2,1,0:T(8,128)(2,1)} async-done(((bf16[8,2,96,2048]{3,2,1,0:T(8,128)(2,1)}), bf16[8,2,96,2048]{3,2,1,0:T(8,128)(2,1)}, u32[]{:S(2)}, u32[]{:S(2)}) %all-to-all-start.1) | async-done | bytes 6291488 | tf_op jit(solution)/shard_map/all_to_all | solution.py:287
  82.8 4.9 %shard_map.93 = bf16[16,896,128]{2,1,0:T(8,128)(2,1)} custom-call(s32[8]{0:T(128)} %dynamic-slice_add_fusion.picked_ref, bf16[16,96,2048]{2,1,0:T(8,128)(2,1)} %bitcast.4.tiles_hbm, bf16[2,128,1024]{2,1,0:T(8,128)(2,1)} %bitcast.19), custom_call_target="tpu_custom_call" | custom-call | tf_op jit(solution)/shard_map/pallas_call | solution.py:187
  87.7 0.0 copy-done
  87.8 0.0 slice-start.1
  87.8 8.1 %all-to-all-start.2 = ((bf16[16,896,128]{2,1,0:T(8,128)(2,1)}), bf16[16,896,128]{2,1,0:T(8,128)(2,1)}, u32[]{:S(2)}, u32[]{:S(2)}) async-start(bf16[16,896,128]{2,1,0:T(8,128)(2,1)} %shard_map.93), calls=%async_computation.2 | async-start | bytes 7340032 | tf_op jit(solution)/shard_map/all_to_all | solution.py:301
  95.9 0.0 slice-done.1
  95.9 2.0 gather_fusion
  97.9 0.0 copy-start.7
  97.9 0.0 copy-start.5
  97.9 0.0 copy-start.6
  97.9 24.6 %shard_map.91 = bf16[8,2,32,2048]{3,2,1,0:T(8,128)(2,1)} custom-call(bf16[8,2,32,2048]{3,2,1,0:T(8,128)(2,1)} %bitcast.16), custom_call_target="tpu_custom_call" | custom-call | tf_op jit(solution)/shard_map/pallas_call | solution.py:66
  122.6 3.1 %shard_map.92 = bf16[16,256,128]{2,1,0:T(8,128)(2,1)} custom-call(s32[8]{0:T(128)} %dynamic-slice_add_fusion.picked_ref, bf16[16,32,2048]{2,1,0:T(8,128)(2,1)} %bitcast.17), custom_call_target="tpu_custom_call" | custom-call | tf_op jit(solution)/shard_map/pallas_call | solution.py:187
  125.7 18.7 %all-to-all-done.2.kv_ref.qsrc_ref = bf16[16,896,128]{2,1,0:T(8,128)(2,1)} async-done(((bf16[16,896,128]{2,1,0:T(8,128)(2,1)}), bf16[16,896,128]{2,1,0:T(8,128)(2,1)}, u32[]{:S(2)}, u32[]{:S(2)}) %all-to-all-start.2) | async-done | bytes 3670048 | tf_op jit(solution)/shard_map/all_to_all | solution.py:301
  144.4 10.0 %all-to-all-start = ((bf16[16,256,128]{2,1,0:T(8,128)(2,1)}), bf16[16,256,128]{2,1,0:T(8,128)(2,1)S(1)}, u32[]{:S(2)}, u32[]{:S(2)}) async-start(bf16[16,256,128]{2,1,0:T(8,128)(2,1)} %shard_map.92), calls=%async_computation | async-start | bytes 2097152 | tf_op jit(solution)/shard_map/all_to_all | solution.py:306
  154.4 0.0 copy-done.7
  154.5 0.1 dynamic_slice.16
  154.5 0.0 copy-done.5
  154.5 0.0 copy-done.6
  154.5 0.2 select_reduce_fusion.2
  154.7 0.0 copy-start.4
  154.7 0.6 dynamic_slice.17.len_ref
  155.3 13.3 %shard_map.94.rest_0_ = f32[2048,128]{1,0:T(8,128)} custom-call(s32[1]{0:T(128)} %dynamic_slice.17.len_ref, bf16[16,896,128]{2,1,0:T(8,128)(2,1)} %all-to-all-done.2.kv_ref.qsrc_ref, bf16[16,896,128]{2,1,0:T(8,128)(2,1)} %all-to-all-done.2.kv_ref.qsrc_ref), custom_call_target="tpu_custom_call" | custom-call | tf_op jit(solution)/shard_map/pallas_call | solution.py:140
  168.7 0.0 copy-done.4
  168.7 1.4 all-to-all-done.kv_ref
  170.1 0.0 copy-start.2
  170.1 1.0 copy-done.2
  171.1 8.0 %shard_map.95 = f32[2048,128]{1,0:T(8,128)} custom-call(s32[1]{0:T(128)} %dynamic_slice.17.len_ref, bf16[16,256,128]{2,1,0:T(8,128)(2,1)} %copy-done.2, bf16[16,896,128]{2,1,0:T(8,128)(2,1)} %all-to-all-done.2.kv_ref.qsrc_ref, f32[2048,128]{1,0:T(8,128)} %shard_map.94.rest_0_), custom_call_target="tpu_custom_call" | custom-call | tf_op jit(solution)/shard_map/pallas_call | solution.py:140
  179.0 21.6 %all-to-all-start.3 = ((f32[16,128,128]{2,1,0:T(8,128)}), f32[16,128,128]{2,1,0:T(8,128)S(1)}, u32[]{:S(2)}, u32[]{:S(2)}) async-start(f32[16,128,128]{2,1,0:T(8,128)} %bitcast.18), calls=%async_computation.3 | async-start | bytes 2097152 | tf_op jit(solution)/shard_map/all_to_all | solution.py:314
  200.7 0.5 broadcast_subtract_fusion.limit_ref
  201.2 14.7 %all-to-all-done.3.hist_ref = f32[16,128,128]{2,1,0:T(8,128)S(1)} async-done(((f32[16,128,128]{2,1,0:T(8,128)}), f32[16,128,128]{2,1,0:T(8,128)S(1)}, u32[]{:S(2)}, u32[]{:S(2)}) %all-to-all-start.3) | async-done | bytes 1048608 | tf_op jit(solution)/shard_map/all_to_all | solution.py:314
  215.8 0.0 copy-start.3
  215.9 1.0 copy-done.3
  216.8 4.9 %shard_map.96 = bf16[2,128,1024]{2,1,0:T(8,128)(2,1)} custom-call(f32[8]{0:T(128)} %bias_ref.1, s32[2]{0:T(128)} %copy-done.4, s32[2]{0:T(128)} %broadcast_subtract_fusion.limit_ref, f32[16,128,128]{2,1,0:T(8,128)} %copy-done.3, bf16[2,128,4096]{2,1,0:T(8,128)(2,1)} %bitcast.15, bf16[2,128,1024]{2,1,0:T(8,128)(2,1)} %x_ref.1, bf16[1024,1024]{1,0:T(8,128)(2,1)} %w_ref.1), custom_call_target="tpu_custom_call" | custom-call | tf_op jit(solution)/shard_map/pallas_call | solution.py:228
  (9 shorter events, 0.1 us)
Async XLA Ops:
  0.0 2.2 slice-start
  5.8 4.9 %copy-start.1 = (bf16[2,128,1024]{2,1,0:T(8,128)(2,1)S(1)}, bf16[2,128,1024]{2,1,0:T(8,128)(2,1)}, u32[]{:S(2)}) copy-start(bf16[2,128,1024]{2,1,0:T(8,128)(2,1)} %x_ref.1) | copy-start | bytes 1572868
  5.8 77.0 %all-to-all-start.1 = ((bf16[8,2,96,2048]{3,2,1,0:T(8,128)(2,1)}), bf16[8,2,96,2048]{3,2,1,0:T(8,128)(2,1)}, u32[]{:S(2)}, u32[]{:S(2)}) async-start(bf16[8,2,96,2048]{3,2,1,0:T(8,128)(2,1)} %bitcast.14), calls=%async_computation.1 | async-start | bytes 12582912 | tf_op jit(solution)/shard_map/all_to_all | solution.py:287
  17.3 70.5 %copy-start = (bf16[256,4096]{1,0:T(8,128)(2,1)}, bf16[256,4096]{1,0:T(8,128)(2,1)S(1)}, u32[]{:S(2)}) copy-start(bf16[256,4096]{1,0:T(8,128)(2,1)S(1)} %multiply_convert_fusion) | copy-start | bytes 6291460
  87.8 8.2 %slice-start.1 = ((bf16[8,128,2048]{2,1,0:T(8,128)(2,1)}), bf16[8,32,2048]{2,1,0:T(8,128)(2,1)S(1)}, s32[]{:S(2)}) async-start(bf16[8,128,2048]{2,1,0:T(8,128)(2,1)} %param.10), calls=%async_computation.5 | async-start | bytes 2097152 | tf_op jit(solution)/shard_map/slice | solution.py:283
  87.8 56.6 %all-to-all-start.2 = ((bf16[16,896,128]{2,1,0:T(8,128)(2,1)}), bf16[16,896,128]{2,1,0:T(8,128)(2,1)}, u32[]{:S(2)}, u32[]{:S(2)}) async-start(bf16[16,896,128]{2,1,0:T(8,128)(2,1)} %shard_map.93), calls=%async_computation.2 | async-start | bytes 7340032 | tf_op jit(solution)/shard_map/all_to_all | solution.py:301
  97.9 56.5 %copy-start.7 = (s32[16]{0:T(128)S(1)}, s32[16]{0:T(128)}, u32[]{:S(2)}) copy-start(s32[16]{0:T(128)} %param.14) | copy-start | bytes 196
  97.9 56.6 %copy-start.5 = (s32[16]{0:T(128)S(1)}, s32[16]{0:T(128)}, u32[]{:S(2)}) copy-start(s32[16]{0:T(128)} %param.16) | copy-start | bytes 196
  97.9 56.6 %copy-start.6 = (s32[16]{0:T(128)S(1)}, s32[16]{0:T(128)}, u32[]{:S(2)}) copy-start(s32[16]{0:T(128)} %param.15) | copy-start | bytes 196
  144.4 25.6 %all-to-all-start = ((bf16[16,256,128]{2,1,0:T(8,128)(2,1)}), bf16[16,256,128]{2,1,0:T(8,128)(2,1)S(1)}, u32[]{:S(2)}, u32[]{:S(2)}) async-start(bf16[16,256,128]{2,1,0:T(8,128)(2,1)} %shard_map.92), calls=%async_computation | async-start | bytes 2097152 | tf_op jit(solution)/shard_map/all_to_all | solution.py:306
  154.7 13.9 %copy-start.4 = (s32[2]{0:T(128)}, s32[2]{0:T(128)S(1)}, u32[]{:S(2)}) copy-start(s32[2]{0:T(128)S(1)} %get-tuple-element.6.len_ref) | copy-start | bytes 28
  170.1 1.0 copy-start.2
  179.0 36.8 %all-to-all-start.3 = ((f32[16,128,128]{2,1,0:T(8,128)}), f32[16,128,128]{2,1,0:T(8,128)S(1)}, u32[]{:S(2)}, u32[]{:S(2)}) async-start(f32[16,128,128]{2,1,0:T(8,128)} %bitcast.18), calls=%async_computation.3 | async-start | bytes 2097152 | tf_op jit(solution)/shard_map/all_to_all | solution.py:314
  215.8 1.0 copy-start.3

commit v11 on v10

--- a/solution.py
+++ b/solution.py
@@ -210,7 +210,8 @@
             key = proj_ref[u, :, pl.ds(3 * width + e * head_dim, head_dim)].astype(jnp.float32)
             self_score = jnp.sum(query * key, axis=-1, keepdims=True) * score_scale + bias_ref[e]
             own = self_score * (0.5 + 0.5 * jnp.tanh(0.5 * self_score)) * value
-            att_ref[:, pl.ds(e * head_dim, head_dim)] = (hist_ref[u * heads + e] + own) / divisor
+            history = hist_ref[u * heads + e].astype(jnp.float32)
+            att_ref[:, pl.ds(e * head_dim, head_dim)] = (history + own) / divisor
         attended = att_ref[...]
         centred = attended - jnp.mean(attended, axis=-1, keepdims=True)
         spread = jnp.mean(centred * centred, axis=-1, keepdims=True)
@@ -276,18 +277,17 @@
     my_owner = lax.dynamic_slice_in_dim(owners, first_entry, users_here * per_hist)
     my_place = lax.dynamic_slice_in_dim(places, first_entry, users_here * per_hist)
     picked_slot = (my_owner * capacity + my_place).astype(jnp.int32)
-    first_len = tile_len - tile_len // 4
-    bounds = [(0, first_len), (first_len, tile_len)]
+    sub = tile_len // 2
     halves = []
-    for half, (lo, hi) in enumerate(bounds):
-        kv_half = lax.slice_in_dim(kv_cache, lo, hi, axis=1)
+    for half in range(2):
+        kv_half = lax.slice_in_dim(kv_cache, half * sub, (half + 1) * sub, axis=1)
         outgoing = kv_half.at[source_slot].get(mode="promise_in_bounds")
-        outgoing = outgoing.reshape(req_count, capacity, hi - lo, 2 * width)
+        outgoing = outgoing.reshape(req_count, capacity, sub, 2 * width)
         if half == 0:
             incoming = lax.all_to_all(outgoing, "req", split_axis=0, concat_axis=0, tiled=True)
         else:
             incoming = req_a2a(outgoing, 0)
-        halves.append(incoming.reshape(req_count * capacity, hi - lo, 2 * width))
+        halves.append(incoming.reshape(req_count * capacity, sub, 2 * width))
     normed = layer_norm(cand_x.astype(jnp.float32)).astype(jnp.bfloat16)
     mixed_in = jnp.dot(normed.reshape(-1, width), w_uvqk, preferred_element_type=jnp.float32)
     projected = jax.nn.silu(mixed_in).astype(jnp.bfloat16).reshape(users_here, cand_rows, 4, width)
@@ -297,20 +297,19 @@
     k_self = projected[:, :, 3]
     my_user = hist_index // heads
     my_length = lax.dynamic_slice_in_dim(lengths, my_user, 1)
-    q_row = 2 * per_hist * first_len
+    q_row = 2 * per_hist * sub
     packed_a = lax.all_to_all(
         pack_for_heads(picked_slot, halves[0], queries, users_here, heads),
         "hist", split_axis=0, concat_axis=0, tiled=True,
     )
-    history_mine = attend(my_length, packed_a, packed_a, q_row, per_hist, first_len, tile_len, 0, score_scale)
+    history_mine = attend(my_length, packed_a, packed_a, q_row, per_hist, sub, tile_len, 0, score_scale)
     packed_b = lax.all_to_all(
         pack_for_heads(picked_slot, halves[1], None, users_here, heads),
         "hist", split_axis=0, concat_axis=0, tiled=True,
     )
     history_mine = attend(
-        my_length, packed_b, packed_a, q_row, per_hist, tile_len - first_len, tile_len, first_len, score_scale,
-        init=history_mine,
-    )
+        my_length, packed_b, packed_a, q_row, per_hist, sub, tile_len, sub, score_scale, init=history_mine
+    ).astype(jnp.bfloat16)
     history_back = lax.all_to_all(
         history_mine.reshape(hist_count, cand_rows, head_dim), "hist", split_axis=0, concat_axis=0, tiled=True
     )

time: 222 us -> 210 us (0.946)
  the two profiles are of different devices: /device:TPU:0 before, /device:TPU:25 now
where the time goes in v11:
time: 210 us; the launch traced here: 209 us
  Pallas kernels  91.7 us (44%)
  waiting for transfers between devices  56.4 us (27%)
  starting transfers between devices  29.7 us (14%)
  local copies, waits for them, and re-layouts  20.9 us (10%)
  matrix products  5.85 us (3%)
  other arithmetic  4.51 us (2%)
    pallas_call x1, Pallas kernels, req_a2a(): pl.pallas_call(functools.partial(req_a2a_kernel, axis='req', other_axis='...  50.1 us
    all_to_all x1, waiting for transfers between devices, local(): lax.all_to_all(outgoing, 'req', split_axis=0, concat_axis=0, tiled=True)  33.3 us
    pallas_call x2, Pallas kernels, attend(): pl.pallas_call(kernel, out_shape=jax.ShapeDtypeStruct((rows, head_dim), j...  28.8 us
    all_to_all x1, waiting for transfers between devices, local(): lax.all_to_all(pack_for_heads(picked_slot, halves[1], None, users_here, h...  14.8 us
    all_to_all x1, starting transfers between devices, local(): lax.all_to_all(history_mine.reshape(hist_count, cand_rows, head_dim), 'hi...  9.97 us
    all_to_all x1, waiting for transfers between devices, local(): lax.all_to_all(history_mine.reshape(hist_count, cand_rows, head_dim), 'hi...  8.41 us
    pallas_call x2, Pallas kernels, pack_for_heads(): pl.pallas_call(functools.partial(pack_kernel, heads=heads, users=users, p...  7.99 us
    all_to_all x1, starting transfers between devices, local(): lax.all_to_all(pack_for_heads(picked_slot, halves[0], queries, users_here...  7.61 us
  transfers between devices with their start and end apart: 4, of which 3 were waited for; matrix products, arithmetic and copies ran while one was open for 9% of the time, Pallas kernels for 33%

profile of v11, /device:TPU:25, one launch (start us, length us, event | category | flops | bytes accessed | tf_op | source)
XLA Modules:
  0.0 209.4 jit_solution(8290869504502406692)
XLA Ops:
  0.0 0.1 broadcast_in_dim.63
  0.1 0.1 eq.98
  0.2 0.8 reshape.248
  1.0 0.4 dynamic-slice_reduce_fusion
  1.4 0.1 reshape.249
  1.5 4.0 %fusion.7 = (bf16[8,64,2048]{2,1,0:T(8,128)(2,1)S(1)}, bf16[8,64,2048]{2,1,0:T(8,128)(2,1)}) fusion(bf16[8,128,2048]{2,1,0:T(8,128)(2,1)} %param.10), kind=kLoop, calls=%fused_computation.38 | loop fusion | bytes 8388608 | tf_op jit(solution)/shard_map/slice | solution.py:283
  5.5 0.2 select_reduce_fusion
  5.7 0.1 select_reduce_fusion.1
  5.8 0.1 copy.14
  5.9 0.1 reshape.250
  6.0 2.8 %gather_fusion.1 = bf16[16,64,2048]{2,1,0:T(8,128)(2,1)} fusion(bf16[8,64,2048]{2,1,0:T(8,128)(2,1)S(1)} %get-tuple-element.9, s32[1024]{0:T(1024)S(1)} %pad_clamp_fusion), kind=kCustom, calls=%fused_computation.1 | custom fusion | bytes 8388672 | tf_op jit(solution)/shard_map/gather | solution.py:284
  8.8 0.0 copy-start.2
  8.8 5.1 %all-to-all-start.1 = ((bf16[8,2,64,2048]{3,2,1,0:T(8,128)(2,1)}), bf16[8,2,64,2048]{3,2,1,0:T(8,128)(2,1)}, u32[]{:S(2)}, u32[]{:S(2)}) async-start(bf16[8,2,64,2048]{3,2,1,0:T(8,128)(2,1)} %bitcast.14), calls=%async_computation.1 | async-start | bytes 8388608 | tf_op jit(solution)/shard_map/all_to_all | solution.py:287
  14.0 0.0 copy-done.2
  14.0 0.1 convert_reduce_fusion
  14.1 0.3 fusion.2
  14.4 0.3 fusion.3
  14.7 5.8 %multiply_convert_fusion = bf16[256,4096]{1,0:T(8,128)(2,1)S(1)} fusion(bf16[256,1024]{1,0:T(8,128)(2,1)S(1)} %bitcast.19, bf16[1024,4096]{1,0:T(8,128)(2,1)} %param.11), kind=kOutput, calls=%fused_computation.2 | convolution fusion | flops 2152726528 | bytes 11010048 | tf_op jit(solution)/shard_map/dot_general | solution.py:292
  20.5 0.0 copy-start.1
  20.5 3.0 %reshape.256 = bf16[2,128,4,1024]{3,2,1,0:T(4,128)(2,1)} reshape(bf16[256,4096]{1,0:T(8,128)(2,1)S(1)} %multiply_convert_fusion) | data formatting | bytes 4194304 | tf_op jit(solution)/shard_map/reshape | solution.py:293
  23.6 2.7 %slice.16 = bf16[2,128,1,1024]{3,2,1,0:T(2,128)(2,1)S(1)} slice(bf16[2,128,4,1024]{3,2,1,0:T(4,128)(2,1)} %reshape.256), slice={[0:2], [0:128], [2:3], [0:1024]} | slice | bytes 1048576 | tf_op jit(solution)/shard_map/slice | solution.py:296
  26.3 1.0 copy.19
  27.2 0.6 dynamic-slice_add_fusion.picked_ref
  27.9 33.3 %all-to-all-done.1 = bf16[8,2,64,2048]{3,2,1,0:T(8,128)(2,1)} async-done(((bf16[8,2,64,2048]{3,2,1,0:T(8,128)(2,1)}), bf16[8,2,64,2048]{3,2,1,0:T(8,128)(2,1)}, u32[]{:S(2)}, u32[]{:S(2)}) %all-to-all-start.1) | async-done | bytes 4194336 | tf_op jit(solution)/shard_map/all_to_all | solution.py:287
  61.2 4.2 %shard_map.93 = bf16[16,640,128]{2,1,0:T(8,128)(2,1)} custom-call(s32[8]{0:T(128)} %dynamic-slice_add_fusion.picked_ref, bf16[16,64,2048]{2,1,0:T(8,128)(2,1)} %bitcast.4.tiles_hbm, bf16[2,128,1024]{2,1,0:T(8,128)(2,1)} %bitcast.18), custom_call_target="tpu_custom_call" | custom-call | tf_op jit(solution)/shard_map/pallas_call | solution.py:187
  65.4 0.0 copy-done.1
  65.4 7.6 %all-to-all-start.2 = ((bf16[16,640,128]{2,1,0:T(8,128)(2,1)}), bf16[16,640,128]{2,1,0:T(8,128)(2,1)S(1)}, u32[]{:S(2)}, u32[]{:S(2)}) async-start(bf16[16,640,128]{2,1,0:T(8,128)(2,1)} %shard_map.93), calls=%async_computation.2 | async-start | bytes 5242880 | tf_op jit(solution)/shard_map/all_to_all | solution.py:301
  73.0 4.4 %gather_fusion = bf16[16,64,2048]{2,1,0:T(8,128)(2,1)} fusion(bf16[8,64,2048]{2,1,0:T(8,128)(2,1)} %get-tuple-element.10, s32[1024]{0:T(1024)S(1)} %pad_clamp_fusion), kind=kCustom, calls=%fused_computation | custom fusion | bytes 8388672 | tf_op jit(solution)/shard_map/gather | solution.py:284
  77.4 50.1 %shard_map.91 = bf16[8,2,64,2048]{3,2,1,0:T(8,128)(2,1)} custom-call(bf16[8,2,64,2048]{3,2,1,0:T(8,128)(2,1)} %bitcast.15), custom_call_target="tpu_custom_call" | custom-call | tf_op jit(solution)/shard_map/pallas_call | solution.py:66
  127.5 0.0 copy-start.7
  127.5 0.0 copy-start.5
  127.6 0.0 copy-start.6
  127.6 3.7 %shard_map.92 = bf16[16,512,128]{2,1,0:T(8,128)(2,1)} custom-call(s32[8]{0:T(128)} %dynamic-slice_add_fusion.picked_ref, bf16[16,64,2048]{2,1,0:T(8,128)(2,1)} %bitcast.16), custom_call_target="tpu_custom_call" | custom-call | tf_op jit(solution)/shard_map/pallas_call | solution.py:187
  131.3 0.0 all-to-all-done.2.kv_ref.qsrc_ref
  131.3 0.0 copy-start
  131.3 7.0 %all-to-all-start = ((bf16[16,512,128]{2,1,0:T(8,128)(2,1)}), bf16[16,512,128]{2,1,0:T(8,128)(2,1)}, u32[]{:S(2)}, u32[]{:S(2)}) async-start(bf16[16,512,128]{2,1,0:T(8,128)(2,1)} %shard_map.92), calls=%async_computation | async-start | bytes 4194304 | tf_op jit(solution)/shard_map/all_to_all | solution.py:306
  138.4 0.0 copy-done.7
  138.4 0.1 dynamic_slice.16
  138.5 0.0 copy-done.5
  138.5 0.0 copy-done.6
  138.5 0.2 select_reduce_fusion.2
  138.6 0.0 copy-start.4
  138.6 0.6 dynamic_slice.17.len_ref
  139.2 0.0 copy-done
  139.2 14.3 %shard_map.94.rest_0_ = f32[2048,128]{1,0:T(8,128)} custom-call(s32[1]{0:T(128)} %dynamic_slice.17.len_ref, bf16[16,640,128]{2,1,0:T(8,128)(2,1)} %copy-done, bf16[16,640,128]{2,1,0:T(8,128)(2,1)} %copy-done), custom_call_target="tpu_custom_call" | custom-call | tf_op jit(solution)/shard_map/pallas_call | solution.py:140
  153.6 14.8 %all-to-all-done.kv_ref = bf16[16,512,128]{2,1,0:T(8,128)(2,1)} async-done(((bf16[16,512,128]{2,1,0:T(8,128)(2,1)}), bf16[16,512,128]{2,1,0:T(8,128)(2,1)}, u32[]{:S(2)}, u32[]{:S(2)}) %all-to-all-start) | async-done | bytes 2097184 | tf_op jit(solution)/shard_map/all_to_all | solution.py:306
  168.3 14.4 %shard_map.95 = f32[2048,128]{1,0:T(8,128)} custom-call(s32[1]{0:T(128)} %dynamic_slice.17.len_ref, bf16[16,512,128]{2,1,0:T(8,128)(2,1)} %all-to-all-done.kv_ref, bf16[16,640,128]{2,1,0:T(8,128)(2,1)} %copy-done, f32[2048,128]{1,0:T(8,128)} %shard_map.94.rest_0_), custom_call_target="tpu_custom_call" | custom-call | tf_op jit(solution)/shard_map/pallas_call | solution.py:140
  182.8 0.0 copy-done.4
  182.8 2.1 convert_element_type.15
  184.8 10.0 %all-to-all-start.3 = ((bf16[16,128,128]{2,1,0:T(8,128)(2,1)}), bf16[16,128,128]{2,1,0:T(8,128)(2,1)S(1)}, u32[]{:S(2)}, u32[]{:S(2)}) async-start(bf16[16,128,128]{2,1,0:T(8,128)(2,1)} %bitcast.7), calls=%async_computation.3 | async-start | bytes 1048576 | tf_op jit(solution)/shard_map/all_to_all | solution.py:313
  194.8 0.5 broadcast_subtract_fusion.limit_ref
  195.4 8.4 %all-to-all-done.3.hist_ref = bf16[16,128,128]{2,1,0:T(8,128)(2,1)S(1)} async-done(((bf16[16,128,128]{2,1,0:T(8,128)(2,1)}), bf16[16,128,128]{2,1,0:T(8,128)(2,1)S(1)}, u32[]{:S(2)}, u32[]{:S(2)}) %all-to-all-start.3) | async-done | bytes 524320 | tf_op jit(solution)/shard_map/all_to_all | solution.py:313
  203.8 0.0 copy-start.3
  203.8 0.8 copy-done.3
  204.6 4.8 %shard_map.96 = bf16[2,128,1024]{2,1,0:T(8,128)(2,1)} custom-call(f32[8]{0:T(128)} %bias_ref.1, s32[2]{0:T(128)} %copy-done.4, s32[2]{0:T(128)} %broadcast_subtract_fusion.limit_ref, bf16[16,128,128]{2,1,0:T(8,128)(2,1)} %copy-done.3, bf16[2,128,4096]{2,1,0:T(8,128)(2,1)} %bitcast.17, bf16[2,128,1024]{2,1,0:T(8,128)(2,1)} %x_ref.1, bf16[1024,1024]{1,0:T(8,128)(2,1)} %w_ref.1), custom_call_target="tpu_custom_call" | custom-call | tf_op jit(solution)/shard_map/pallas_call | solution.py:229
  (9 shorter events, 0.1 us)
Async XLA Ops:
  8.8 5.1 %copy-start.2 = (bf16[2,128,1024]{2,1,0:T(8,128)(2,1)S(1)}, bf16[2,128,1024]{2,1,0:T(8,128)(2,1)}, u32[]{:S(2)}) copy-start(bf16[2,128,1024]{2,1,0:T(8,128)(2,1)} %x_ref.1) | copy-start | bytes 1572868
  8.8 52.3 %all-to-all-start.1 = ((bf16[8,2,64,2048]{3,2,1,0:T(8,128)(2,1)}), bf16[8,2,64,2048]{3,2,1,0:T(8,128)(2,1)}, u32[]{:S(2)}, u32[]{:S(2)}) async-start(bf16[8,2,64,2048]{3,2,1,0:T(8,128)(2,1)} %bitcast.14), calls=%async_computation.1 | async-start | bytes 8388608 | tf_op jit(solution)/shard_map/all_to_all | solution.py:287
  20.5 44.9 %copy-start.1 = (bf16[256,4096]{1,0:T(8,128)(2,1)}, bf16[256,4096]{1,0:T(8,128)(2,1)S(1)}, u32[]{:S(2)}) copy-start(bf16[256,4096]{1,0:T(8,128)(2,1)S(1)} %multiply_convert_fusion) | copy-start | bytes 6291460
  65.4 65.9 %all-to-all-start.2 = ((bf16[16,640,128]{2,1,0:T(8,128)(2,1)}), bf16[16,640,128]{2,1,0:T(8,128)(2,1)S(1)}, u32[]{:S(2)}, u32[]{:S(2)}) async-start(bf16[16,640,128]{2,1,0:T(8,128)(2,1)} %shard_map.93), calls=%async_computation.2 | async-start | bytes 5242880 | tf_op jit(solution)/shard_map/all_to_all | solution.py:301
  127.5 10.8 %copy-start.7 = (s32[16]{0:T(128)S(1)}, s32[16]{0:T(128)}, u32[]{:S(2)}) copy-start(s32[16]{0:T(128)} %param.14) | copy-start | bytes 196
  127.5 10.9 %copy-start.5 = (s32[16]{0:T(128)S(1)}, s32[16]{0:T(128)}, u32[]{:S(2)}) copy-start(s32[16]{0:T(128)} %param.16) | copy-start | bytes 196
  127.6 10.9 %copy-start.6 = (s32[16]{0:T(128)S(1)}, s32[16]{0:T(128)}, u32[]{:S(2)}) copy-start(s32[16]{0:T(128)} %param.15) | copy-start | bytes 196
  131.3 7.9 %copy-start = (bf16[16,640,128]{2,1,0:T(8,128)(2,1)}, bf16[16,640,128]{2,1,0:T(8,128)(2,1)S(1)}, u32[]{:S(2)}) copy-start(bf16[16,640,128]{2,1,0:T(8,128)(2,1)S(1)} %all-to-all-done.2.kv_ref.qsrc_ref) | copy-start | bytes 7864324
  131.3 37.0 %all-to-all-start = ((bf16[16,512,128]{2,1,0:T(8,128)(2,1)}), bf16[16,512,128]{2,1,0:T(8,128)(2,1)}, u32[]{:S(2)}, u32[]{:S(2)}) async-start(bf16[16,512,128]{2,1,0:T(8,128)(2,1)} %shard_map.92), calls=%async_computation | async-start | bytes 4194304 | tf_op jit(solution)/shard_map/all_to_all | solution.py:306
  138.6 44.1 %copy-start.4 = (s32[2]{0:T(128)}, s32[2]{0:T(128)S(1)}, u32[]{:S(2)}) copy-start(s32[2]{0:T(128)S(1)} %get-tuple-element.6.len_ref) | copy-start | bytes 28
  184.8 18.9 %all-to-all-start.3 = ((bf16[16,128,128]{2,1,0:T(8,128)(2,1)}), bf16[16,128,128]{2,1,0:T(8,128)(2,1)S(1)}, u32[]{:S(2)}, u32[]{:S(2)}) async-start(bf16[16,128,128]{2,1,0:T(8,128)(2,1)} %bitcast.7), calls=%async_computation.3 | async-start | bytes 1048576 | tf_op jit(solution)/shard_map/all_to_all | solution.py:313
  203.8 0.8 copy-start.3

commit v12 on v11

--- a/solution.py
+++ b/solution.py
@@ -278,19 +278,21 @@
     my_place = lax.dynamic_slice_in_dim(places, first_entry, users_here * per_hist)
     picked_slot = (my_owner * capacity + my_place).astype(jnp.int32)
     sub = tile_len // 2
-    halves = []
+    sending = []
     for half in range(2):
         kv_half = lax.slice_in_dim(kv_cache, half * sub, (half + 1) * sub, axis=1)
         outgoing = kv_half.at[source_slot].get(mode="promise_in_bounds")
-        outgoing = outgoing.reshape(req_count, capacity, sub, 2 * width)
-        if half == 0:
-            incoming = lax.all_to_all(outgoing, "req", split_axis=0, concat_axis=0, tiled=True)
-        else:
-            incoming = req_a2a(outgoing, 0)
-        halves.append(incoming.reshape(req_count * capacity, sub, 2 * width))
+        sending.append(outgoing.reshape(req_count, capacity, sub, 2 * width))
+    first_in = lax.all_to_all(sending[0], "req", split_axis=0, concat_axis=0, tiled=True)
     normed = layer_norm(cand_x.astype(jnp.float32)).astype(jnp.bfloat16)
     mixed_in = jnp.dot(normed.reshape(-1, width), w_uvqk, preferred_element_type=jnp.float32)
     projected = jax.nn.silu(mixed_in).astype(jnp.bfloat16).reshape(users_here, cand_rows, 4, width)
+    projected, second_out = lax.optimization_barrier((projected, sending[1]))
+    second_in = req_a2a(second_out, 0)
+    halves = [
+        first_in.reshape(req_count * capacity, sub, 2 * width),
+        second_in.reshape(req_count * capacity, sub, 2 * width),
+    ]
     u_gate = projected[:, :, 0]
     v_self = projected[:, :, 1]
     queries = projected[:, :, 2]

time: 210 us -> 208 us (level)
  the two profiles are of different devices: /device:TPU:25 before, /device:TPU:8 now
where the time goes in v12:
time: 208 us
  Pallas kernels  87.6 us (42%)
  waiting for transfers between devices  52.3 us (25%)
  starting transfers between devices  30.9 us (15%)
  local copies, waits for them, and re-layouts  25 us (12%)
  matrix products  7.25 us (3%)
  other arithmetic  4.44 us (2%)
    pallas_call x1, Pallas kernels, req_a2a(): pl.pallas_call(functools.partial(req_a2a_kernel, axis='req', other_axis='...  47.6 us
    all_to_all x1, waiting for transfers between devices, local(): lax.all_to_all(sending[0], 'req', split_axis=0, concat_axis=0, tiled=True)  27.5 us
    pallas_call x2, Pallas kernels, attend(): pl.pallas_call(kernel, out_shape=jax.ShapeDtypeStruct((rows, head_dim), j...  27.2 us
    all_to_all x1, waiting for transfers between devices, local(): lax.all_to_all(pack_for_heads(picked_slot, halves[1], None, users_here, h...  16.3 us
    all_to_all x1, starting transfers between devices, local(): lax.all_to_all(history_mine.reshape(hist_count, cand_rows, head_dim), 'hi...  10.8 us
    all_to_all x1, waiting for transfers between devices, local(): lax.all_to_all(history_mine.reshape(hist_count, cand_rows, head_dim), 'hi...  8.49 us
    pallas_call x2, Pallas kernels, pack_for_heads(): pl.pallas_call(functools.partial(pack_kernel, heads=heads, users=users, p...  8.01 us
    gather x2, local copies, waits for them, and re-layouts, local(): outgoing = kv_half.at[source_slot].get(mode='promise_in_bounds')  7.92 us
  transfers between devices with their start and end apart: 4, of which 3 were waited for; matrix products, arithmetic and copies ran while one was open for 12% of the time, Pallas kernels for 31%

profile of v12, /device:TPU:8, one launch (start us, length us, event | category | flops | bytes accessed | tf_op | source)
XLA Modules:
  0.0 207.7 jit_solution(4105319749165963319)
XLA Ops:
  0.0 0.1 broadcast_in_dim.63
  0.1 0.1 eq.98
  0.2 0.8 reshape.251
  1.0 0.4 dynamic-slice_reduce_fusion
  1.4 0.1 reshape.252
  1.5 4.0 %fusion.7 = (bf16[8,64,2048]{2,1,0:T(8,128)(2,1)S(1)}, bf16[8,64,2048]{2,1,0:T(8,128)(2,1)}) fusion(bf16[8,128,2048]{2,1,0:T(8,128)(2,1)} %param.10), kind=kLoop, calls=%fused_computation.38 | loop fusion | bytes 8388608 | tf_op jit(solution)/shard_map/slice | solution.py:283
  5.5 0.2 select_reduce_fusion
  5.7 0.1 select_reduce_fusion.1
  5.9 0.1 copy.15
  6.0 0.1 reshape.255
  6.1 2.8 %gather_fusion.1 = bf16[16,64,2048]{2,1,0:T(8,128)(2,1)} fusion(bf16[8,64,2048]{2,1,0:T(8,128)(2,1)S(1)} %get-tuple-element.13, s32[1024]{0:T(1024)S(1)} %pad_clamp_fusion), kind=kCustom, calls=%fused_computation.1 | custom fusion | bytes 8388672 | tf_op jit(solution)/shard_map/gather | solution.py:284
  8.8 0.0 copy-start.3
  8.8 5.0 %all-to-all-start.1 = ((bf16[8,2,64,2048]{3,2,1,0:T(8,128)(2,1)}), bf16[8,2,64,2048]{3,2,1,0:T(8,128)(2,1)}, u32[]{:S(2)}, u32[]{:S(2)}) async-start(bf16[8,2,64,2048]{3,2,1,0:T(8,128)(2,1)} %bitcast.12), calls=%async_computation.1 | async-start | bytes 8388608 | tf_op jit(solution)/shard_map/all_to_all | solution.py:286
  13.9 0.0 copy-done.3
  13.9 0.1 convert_reduce_fusion
  14.1 0.3 fusion.2
  14.3 0.3 fusion.3
  14.6 7.2 %multiply_convert_fusion = bf16[256,4096]{1,0:T(8,128)(2,1)} fusion(bf16[256,1024]{1,0:T(8,128)(2,1)S(1)} %bitcast.15, bf16[1024,4096]{1,0:T(8,128)(2,1)} %param.11), kind=kOutput, calls=%fused_computation.2 | convolution fusion | flops 2152726528 | bytes 11010048 | tf_op jit(solution)/shard_map/dot_general | solution.py:288
  21.9 3.3 %reshape.254 = bf16[2,128,4,1024]{3,2,1,0:T(4,128)(2,1)S(1)} reshape(bf16[256,4096]{1,0:T(8,128)(2,1)} %multiply_convert_fusion) | data formatting | bytes 4194304 | tf_op jit(solution)/shard_map/reshape | solution.py:289
  25.2 0.0 copy-start.1
  25.2 5.1 %gather_fusion = bf16[16,64,2048]{2,1,0:T(8,128)(2,1)} fusion(bf16[8,64,2048]{2,1,0:T(8,128)(2,1)} %get-tuple-element.14, s32[1024]{0:T(1024)S(1)} %pad_clamp_fusion), kind=kCustom, calls=%fused_computation | custom fusion | bytes 8388672 | tf_op jit(solution)/shard_map/gather | solution.py:284
  30.3 0.0 copy-done.1
  30.3 2.0 copy.16
  32.3 0.6 dynamic-slice_add_fusion.picked_ref
  32.9 1.9 slice_bitcast_fusion.rest_0_
  34.8 27.5 %all-to-all-done.1 = bf16[8,2,64,2048]{3,2,1,0:T(8,128)(2,1)} async-done(((bf16[8,2,64,2048]{3,2,1,0:T(8,128)(2,1)}), bf16[8,2,64,2048]{3,2,1,0:T(8,128)(2,1)}, u32[]{:S(2)}, u32[]{:S(2)}) %all-to-all-start.1) | async-done | bytes 4194336 | tf_op jit(solution)/shard_map/all_to_all | solution.py:286
  62.2 4.2 %shard_map.93 = bf16[16,640,128]{2,1,0:T(8,128)(2,1)} custom-call(s32[8]{0:T(128)} %dynamic-slice_add_fusion.picked_ref, bf16[16,64,2048]{2,1,0:T(8,128)(2,1)} %bitcast.5.tiles_hbm, bf16[2,128,1024]{2,1,0:T(8,128)(2,1)} %slice_bitcast_fusion.rest_0_), custom_call_target="tpu_custom_call" | custom-call | tf_op jit(solution)/shard_map/pallas_call | solution.py:187
  66.4 7.9 %all-to-all-start.2 = ((bf16[16,640,128]{2,1,0:T(8,128)(2,1)}), bf16[16,640,128]{2,1,0:T(8,128)(2,1)S(1)}, u32[]{:S(2)}, u32[]{:S(2)}) async-start(bf16[16,640,128]{2,1,0:T(8,128)(2,1)} %shard_map.93), calls=%async_computation.2 | async-start | bytes 5242880 | tf_op jit(solution)/shard_map/all_to_all | solution.py:303
  74.3 47.6 %shard_map.91 = bf16[8,2,64,2048]{3,2,1,0:T(8,128)(2,1)} custom-call(bf16[8,2,64,2048]{3,2,1,0:T(8,128)(2,1)} %bitcast.13), custom_call_target="tpu_custom_call" | custom-call | tf_op jit(solution)/shard_map/pallas_call | solution.py:66
  121.9 0.0 copy-start.8
  121.9 0.0 copy-start.6
  121.9 0.0 copy-start.7
  122.0 3.8 %shard_map.92 = bf16[16,512,128]{2,1,0:T(8,128)(2,1)} custom-call(s32[8]{0:T(128)} %dynamic-slice_add_fusion.picked_ref, bf16[16,64,2048]{2,1,0:T(8,128)(2,1)} %bitcast.14), custom_call_target="tpu_custom_call" | custom-call | tf_op jit(solution)/shard_map/pallas_call | solution.py:187
  125.8 0.0 all-to-all-done.2.kv_ref.qsrc_ref
  125.8 0.0 copy-start
  125.8 7.2 %all-to-all-start = ((bf16[16,512,128]{2,1,0:T(8,128)(2,1)}), bf16[16,512,128]{2,1,0:T(8,128)(2,1)}, u32[]{:S(2)}, u32[]{:S(2)}) async-start(bf16[16,512,128]{2,1,0:T(8,128)(2,1)} %shard_map.92), calls=%async_computation | async-start | bytes 4194304 | tf_op jit(solution)/shard_map/all_to_all | solution.py:308
  133.0 0.0 copy-done.8
  133.0 0.1 dynamic_slice.16
  133.1 0.0 copy-done.6
  133.1 0.0 copy-done.7
  133.1 0.2 select_reduce_fusion.2
  133.3 0.0 copy-start.5
  133.3 0.6 dynamic_slice.17.len_ref
  133.9 0.0 copy-done
  133.9 13.5 %shard_map.94.rest_0_ = f32[2048,128]{1,0:T(8,128)} custom-call(s32[1]{0:T(128)} %dynamic_slice.17.len_ref, bf16[16,640,128]{2,1,0:T(8,128)(2,1)} %copy-done, bf16[16,640,128]{2,1,0:T(8,128)(2,1)} %copy-done), custom_call_target="tpu_custom_call" | custom-call | tf_op jit(solution)/shard_map/pallas_call | solution.py:140
  147.4 0.0 copy-start.2
  147.4 16.3 %all-to-all-done.kv_ref = bf16[16,512,128]{2,1,0:T(8,128)(2,1)} async-done(((bf16[16,512,128]{2,1,0:T(8,128)(2,1)}), bf16[16,512,128]{2,1,0:T(8,128)(2,1)}, u32[]{:S(2)}, u32[]{:S(2)}) %all-to-all-start) | async-done | bytes 2097184 | tf_op jit(solution)/shard_map/all_to_all | solution.py:308
  163.7 13.7 %shard_map.95 = f32[2048,128]{1,0:T(8,128)} custom-call(s32[1]{0:T(128)} %dynamic_slice.17.len_ref, bf16[16,512,128]{2,1,0:T(8,128)(2,1)} %all-to-all-done.kv_ref, bf16[16,640,128]{2,1,0:T(8,128)(2,1)} %copy-done, f32[2048,128]{1,0:T(8,128)} %shard_map.94.rest_0_), custom_call_target="tpu_custom_call" | custom-call | tf_op jit(solution)/shard_map/pallas_call | solution.py:140
  177.4 0.0 copy-done.5
  177.4 2.1 convert_element_type.15
  179.4 10.8 %all-to-all-start.3 = ((bf16[16,128,128]{2,1,0:T(8,128)(2,1)}), bf16[16,128,128]{2,1,0:T(8,128)(2,1)S(1)}, u32[]{:S(2)}, u32[]{:S(2)}) async-start(bf16[16,128,128]{2,1,0:T(8,128)(2,1)} %bitcast.7), calls=%async_computation.3 | async-start | bytes 1048576 | tf_op jit(solution)/shard_map/all_to_all | solution.py:315
  190.2 0.0 copy-done.2
  190.3 2.8 %reshape.261.proj_ref = bf16[2,128,4096]{2,1,0:T(8,128)(2,1)} reshape(bf16[2,128,4,1024]{3,2,1,0:T(4,128)(2,1)S(1)} %copy-done.2) | data formatting | bytes 4194304 | tf_op jit(solution)/shard_map/reshape | solution.py:320
  193.1 0.5 broadcast_subtract_fusion.limit_ref
  193.6 8.5 %all-to-all-done.3.hist_ref = bf16[16,128,128]{2,1,0:T(8,128)(2,1)S(1)} async-done(((bf16[16,128,128]{2,1,0:T(8,128)(2,1)}), bf16[16,128,128]{2,1,0:T(8,128)(2,1)S(1)}, u32[]{:S(2)}, u32[]{:S(2)}) %all-to-all-start.3) | async-done | bytes 524320 | tf_op jit(solution)/shard_map/all_to_all | solution.py:315
  202.1 0.0 copy-start.4
  202.1 0.8 copy-done.4
  202.9 4.8 %shard_map.96 = bf16[2,128,1024]{2,1,0:T(8,128)(2,1)} custom-call(f32[8]{0:T(128)} %bias_ref.1, s32[2]{0:T(128)} %copy-done.5, s32[2]{0:T(128)} %broadcast_subtract_fusion.limit_ref, bf16[16,128,128]{2,1,0:T(8,128)(2,1)} %copy-done.4, bf16[2,128,4096]{2,1,0:T(8,128)(2,1)} %reshape.261.proj_ref, bf16[2,128,1024]{2,1,0:T(8,128)(2,1)} %x_ref.1, ...), custom_call_target="tpu_custom_call" | custom-call | tf_op jit(solution)/shard_map/pallas_call | solution.py:229
  (9 shorter events, 0.1 us)
Async XLA Ops:
  8.8 5.1 %copy-start.3 = (bf16[2,128,1024]{2,1,0:T(8,128)(2,1)S(1)}, bf16[2,128,1024]{2,1,0:T(8,128)(2,1)}, u32[]{:S(2)}) copy-start(bf16[2,128,1024]{2,1,0:T(8,128)(2,1)} %x_ref.1) | copy-start | bytes 1572868
  8.8 53.4 %all-to-all-start.1 = ((bf16[8,2,64,2048]{3,2,1,0:T(8,128)(2,1)}), bf16[8,2,64,2048]{3,2,1,0:T(8,128)(2,1)}, u32[]{:S(2)}, u32[]{:S(2)}) async-start(bf16[8,2,64,2048]{3,2,1,0:T(8,128)(2,1)} %bitcast.12), calls=%async_computation.1 | async-start | bytes 8388608 | tf_op jit(solution)/shard_map/all_to_all | solution.py:286
  25.2 5.2 %copy-start.1 = (bf16[2,128,4,1024]{3,2,1,0:T(4,128)(2,1)}, bf16[2,128,4,1024]{3,2,1,0:T(4,128)(2,1)S(1)}, u32[]{:S(2)}) copy-start(bf16[2,128,4,1024]{3,2,1,0:T(4,128)(2,1)S(1)} %reshape.254) | copy-start | bytes 6291460
  66.4 59.3 %all-to-all-start.2 = ((bf16[16,640,128]{2,1,0:T(8,128)(2,1)}), bf16[16,640,128]{2,1,0:T(8,128)(2,1)S(1)}, u32[]{:S(2)}, u32[]{:S(2)}) async-start(bf16[16,640,128]{2,1,0:T(8,128)(2,1)} %shard_map.93), calls=%async_computation.2 | async-start | bytes 5242880 | tf_op jit(solution)/shard_map/all_to_all | solution.py:303
  121.9 11.1 %copy-start.8 = (s32[16]{0:T(128)S(1)}, s32[16]{0:T(128)}, u32[]{:S(2)}) copy-start(s32[16]{0:T(128)} %param.14) | copy-start | bytes 196
  121.9 11.2 %copy-start.6 = (s32[16]{0:T(128)S(1)}, s32[16]{0:T(128)}, u32[]{:S(2)}) copy-start(s32[16]{0:T(128)} %param.16) | copy-start | bytes 196
  121.9 11.2 %copy-start.7 = (s32[16]{0:T(128)S(1)}, s32[16]{0:T(128)}, u32[]{:S(2)}) copy-start(s32[16]{0:T(128)} %param.15) | copy-start | bytes 196
  125.8 8.1 %copy-start = (bf16[16,640,128]{2,1,0:T(8,128)(2,1)}, bf16[16,640,128]{2,1,0:T(8,128)(2,1)S(1)}, u32[]{:S(2)}) copy-start(bf16[16,640,128]{2,1,0:T(8,128)(2,1)S(1)} %all-to-all-done.2.kv_ref.qsrc_ref) | copy-start | bytes 7864324
  125.8 37.9 %all-to-all-start = ((bf16[16,512,128]{2,1,0:T(8,128)(2,1)}), bf16[16,512,128]{2,1,0:T(8,128)(2,1)}, u32[]{:S(2)}, u32[]{:S(2)}) async-start(bf16[16,512,128]{2,1,0:T(8,128)(2,1)} %shard_map.92), calls=%async_computation | async-start | bytes 4194304 | tf_op jit(solution)/shard_map/all_to_all | solution.py:308
  133.3 44.1 %copy-start.5 = (s32[2]{0:T(128)}, s32[2]{0:T(128)S(1)}, u32[]{:S(2)}) copy-start(s32[2]{0:T(128)S(1)} %get-tuple-element.10.len_ref) | copy-start | bytes 28
  147.4 42.9 %copy-start.2 = (bf16[2,128,4,1024]{3,2,1,0:T(4,128)(2,1)S(1)}, bf16[2,128,4,1024]{3,2,1,0:T(4,128)(2,1)}, u32[]{:S(2)}) copy-start(bf16[2,128,4,1024]{3,2,1,0:T(4,128)(2,1)} %copy-done.1) | copy-start | bytes 6291460
  179.4 22.6 %all-to-all-start.3 = ((bf16[16,128,128]{2,1,0:T(8,128)(2,1)}), bf16[16,128,128]{2,1,0:T(8,128)(2,1)S(1)}, u32[]{:S(2)}, u32[]{:S(2)}) async-start(bf16[16,128,128]{2,1,0:T(8,128)(2,1)} %bitcast.7), calls=%async_computation.3 | async-start | bytes 1048576 | tf_op jit(solution)/shard_map/all_to_all | solution.py:315
  202.1 0.8 copy-start.4

commit v13 on v12

--- a/solution.py
+++ b/solution.py
@@ -78,10 +78,10 @@
 
 
 def attend_kernel(len_ref, kv_ref, qsrc_ref, *rest, n_tiles, sub, tile_len, offset, q_row, score_scale, chunk):
-    if len(rest) == 3:
-        init_ref, o_ref, q_ref = rest
+    if len(rest) == 4:
+        init_ref, out_ref, q_ref, o_ref = rest
     else:
-        init_ref = None
+        init_ref = out_ref = None
         o_ref, q_ref = rest
     length = len_ref[0]
     n_cls, _, head_dim = kv_ref.shape
@@ -121,6 +121,8 @@
         return carry
 
     lax.fori_loop(0, n_cls, one_class, 0)
+    if out_ref is not None:
+        out_ref[...] = o_ref[...].astype(out_ref.dtype)
 
 
 def attend(length, kv_packed, q_packed, q_row, n_tiles, sub, tile_len, offset, score_scale, init=None):
@@ -139,11 +141,12 @@
     )
     return pl.pallas_call(
         kernel,
-        out_shape=jax.ShapeDtypeStruct((rows, head_dim), jnp.float32),
+        out_shape=jax.ShapeDtypeStruct((rows, head_dim), jnp.float32 if init is None else jnp.bfloat16),
         in_specs=[pl.BlockSpec(memory_space=pltpu.SMEM)]
         + [pl.BlockSpec(memory_space=pltpu.VMEM)] * (2 if init is None else 3),
         out_specs=pl.BlockSpec(memory_space=pltpu.VMEM),
-        scratch_shapes=[pltpu.VMEM((rows, head_dim), jnp.bfloat16)],
+        scratch_shapes=[pltpu.VMEM((rows, head_dim), jnp.bfloat16)]
+        + ([] if init is None else [pltpu.VMEM((rows, head_dim), jnp.float32)]),
     )(length, kv_packed, q_packed, *([] if init is None else [init]))
 
 
@@ -286,17 +289,14 @@
     first_in = lax.all_to_all(sending[0], "req", split_axis=0, concat_axis=0, tiled=True)
     normed = layer_norm(cand_x.astype(jnp.float32)).astype(jnp.bfloat16)
     mixed_in = jnp.dot(normed.reshape(-1, width), w_uvqk, preferred_element_type=jnp.float32)
-    projected = jax.nn.silu(mixed_in).astype(jnp.bfloat16).reshape(users_here, cand_rows, 4, width)
+    projected = jax.nn.silu(mixed_in).astype(jnp.bfloat16).reshape(users_here, cand_rows, 4 * width)
     projected, second_out = lax.optimization_barrier((projected, sending[1]))
     second_in = req_a2a(second_out, 0)
     halves = [
         first_in.reshape(req_count * capacity, sub, 2 * width),
         second_in.reshape(req_count * capacity, sub, 2 * width),
     ]
-    u_gate = projected[:, :, 0]
-    v_self = projected[:, :, 1]
-    queries = projected[:, :, 2]
-    k_self = projected[:, :, 3]
+    queries = projected[:, :, 2 * width : 3 * width]
     my_user = hist_index // heads
     my_length = lax.dynamic_slice_in_dim(lengths, my_user, 1)
     q_row = 2 * per_hist * sub
@@ -311,13 +311,13 @@
     )
     history_mine = attend(
         my_length, packed_b, packed_a, q_row, per_hist, sub, tile_len, sub, score_scale, init=history_mine
-    ).astype(jnp.bfloat16)
+    )
     history_back = lax.all_to_all(
         history_mine.reshape(hist_count, cand_rows, head_dim), "hist", split_axis=0, concat_axis=0, tiled=True
     )
     row_limit = (live_counts - hist_index * cand_rows).astype(jnp.int32)
     return finish(
-        history_back, projected.reshape(users_here, cand_rows, 4 * width), cand_x, w_out, self_bias,
+        history_back, projected, cand_x, w_out, self_bias,
         lengths.astype(jnp.int32), row_limit, heads, score_scale,
     )
 

time: 208 us -> 207 us (level)
  waiting for transfers between devices: 52.3 us -> 66.9 us
  Pallas kernels: 87.6 us -> 76.7 us
  local copies, waits for them, and re-layouts: 25 us -> 16.5 us
  starting transfers between devices: 30.9 us -> 36.5 us
    pallas_call x2, Pallas kernels: 27.2 us -> 16.4 us  [attend(): pl.pallas_call(kernel, out_shape=jax.ShapeDtypeStruct((rows, head_dim), j...]
    all_to_all x1, waiting for transfers between devices: 27.5 us -> 36.2 us  [local(): lax.all_to_all(sending[0], 'req', split_axis=0, concat_axis=0, tiled=True)]
    reshape x2 -> x0, local copies, waits for them, and re-layouts: 6.13 us -> none  [the longest x1 3.32 us: local(): jax.nn.silu(mixed_in).astype(jnp.bfloat16)]
    all_to_all x1, starting transfers between devices: 10.8 us -> 16.5 us  [local(): lax.all_to_all(history_mine.reshape(hist_count, cand_rows, head_dim), 'hi...]
    all_to_all x1, waiting for transfers between devices: 16.3 us -> 21.2 us  [local(): lax.all_to_all(pack_for_heads(picked_slot, halves[1], None, users_here, h...]
  transfers between devices with their start and end apart: 4 -> 4, of which waited for: 3 -> 3; matrix products, arithmetic and copies ran while one was open for 12% -> 6% of each run, Pallas kernels for 31% -> 29%
where the time goes in v13:
time: 207 us; the launch traced here: 205 us
  Pallas kernels  76.7 us (37%)
  waiting for transfers between devices  66.9 us (32%)
  starting transfers between devices  36.5 us (18%)
  local copies, waits for them, and re-layouts  16.5 us (8%)
  matrix products  5.85 us (3%)
  other arithmetic  2.44 us (1%)
    pallas_call x1, Pallas kernels, req_a2a(): pl.pallas_call(functools.partial(req_a2a_kernel, axis='req', other_axis='...  47.6 us
    all_to_all x1, waiting for transfers between devices, local(): lax.all_to_all(sending[0], 'req', split_axis=0, concat_axis=0, tiled=True)  36.2 us
    all_to_all x1, waiting for transfers between devices, local(): lax.all_to_all(pack_for_heads(picked_slot, halves[1], None, users_here, h...  21.2 us
    all_to_all x1, starting transfers between devices, local(): lax.all_to_all(history_mine.reshape(hist_count, cand_rows, head_dim), 'hi...  16.5 us
    pallas_call x2, Pallas kernels, attend(): pl.pallas_call(kernel, out_shape=jax.ShapeDtypeStruct((rows, head_dim), j...  16.4 us
    all_to_all x1, waiting for transfers between devices, local(): lax.all_to_all(history_mine.reshape(hist_count, cand_rows, head_dim), 'hi...  9.49 us
    pallas_call x2, Pallas kernels, pack_for_heads(): pl.pallas_call(functools.partial(pack_kernel, heads=heads, users=users, p...  7.99 us
    all_to_all x1, starting transfers between devices, local(): lax.all_to_all(pack_for_heads(picked_slot, halves[0], queries, users_here...  7.89 us
  transfers between devices with their start and end apart: 4, of which 3 were waited for; matrix products, arithmetic and copies ran while one was open for 6% of the time, Pallas kernels for 29%

profile of v13, /device:TPU:8, one launch (start us, length us, event | category | flops | bytes accessed | tf_op | source)
XLA Modules:
  0.0 205.1 jit_solution(2883077017651288874)
XLA Ops:
  0.0 0.1 broadcast_in_dim.63
  0.1 0.1 eq.98
  0.2 0.8 reshape.248
  1.0 0.4 dynamic-slice_reduce_fusion
  1.4 0.1 reshape.249
  1.5 4.0 %fusion.7 = (bf16[8,64,2048]{2,1,0:T(8,128)(2,1)}, bf16[8,64,2048]{2,1,0:T(8,128)(2,1)S(1)}) fusion(bf16[8,128,2048]{2,1,0:T(8,128)(2,1)} %param.10), kind=kLoop, calls=%fused_computation.37 | loop fusion | bytes 8388608 | tf_op jit(solution)/shard_map/slice | solution.py:286
  5.5 0.2 select_reduce_fusion
  5.7 0.1 select_reduce_fusion.1
  5.9 0.1 copy.13
  6.0 0.1 reshape.252
  6.1 4.4 %gather_fusion.1 = bf16[16,64,2048]{2,1,0:T(8,128)(2,1)} fusion(bf16[8,64,2048]{2,1,0:T(8,128)(2,1)} %get-tuple-element.13, s32[1024]{0:T(1024)S(1)} %pad_clamp_fusion), kind=kCustom, calls=%fused_computation.1 | custom fusion | bytes 8388672 | tf_op jit(solution)/shard_map/gather | solution.py:287
  10.5 4.9 %all-to-all-start.1 = ((bf16[8,2,64,2048]{3,2,1,0:T(8,128)(2,1)}), bf16[8,2,64,2048]{3,2,1,0:T(8,128)(2,1)}, u32[]{:S(2)}, u32[]{:S(2)}) async-start(bf16[8,2,64,2048]{3,2,1,0:T(8,128)(2,1)} %bitcast.12), calls=%async_computation.1 | async-start | bytes 8388608 | tf_op jit(solution)/shard_map/all_to_all | solution.py:289
  15.4 0.0 copy-start.1
  15.4 2.7 %gather_fusion = bf16[16,64,2048]{2,1,0:T(8,128)(2,1)} fusion(bf16[8,64,2048]{2,1,0:T(8,128)(2,1)S(1)} %get-tuple-element.14, s32[1024]{0:T(1024)S(1)} %pad_clamp_fusion), kind=kCustom, calls=%fused_computation | custom fusion | bytes 8388672 | tf_op jit(solution)/shard_map/gather | solution.py:287
  18.1 0.0 copy-done.1
  18.1 0.1 convert_reduce_fusion
  18.3 0.3 fusion.2
  18.6 0.3 fusion.3
  18.8 5.8 %multiply_convert_fusion = bf16[256,4096]{1,0:T(8,128)(2,1)S(1)} fusion(bf16[256,1024]{1,0:T(8,128)(2,1)S(1)} %bitcast.17, bf16[1024,4096]{1,0:T(8,128)(2,1)} %param.11), kind=kOutput, calls=%fused_computation.2 | convolution fusion | flops 2152726528 | bytes 11010048 | tf_op jit(solution)/shard_map/dot_general | solution.py:291
  24.7 0.0 copy-start.2
  24.7 1.4 copy-done.2
  26.1 0.8 slice.11.rest_0_
  26.9 0.6 dynamic-slice_add_fusion.picked_ref
  27.5 36.2 %all-to-all-done.1 = bf16[8,2,64,2048]{3,2,1,0:T(8,128)(2,1)} async-done(((bf16[8,2,64,2048]{3,2,1,0:T(8,128)(2,1)}), bf16[8,2,64,2048]{3,2,1,0:T(8,128)(2,1)}, u32[]{:S(2)}, u32[]{:S(2)}) %all-to-all-start.1) | async-done | bytes 4194336 | tf_op jit(solution)/shard_map/all_to_all | solution.py:289
  63.7 4.2 %shard_map.93 = bf16[16,640,128]{2,1,0:T(8,128)(2,1)} custom-call(s32[8]{0:T(128)} %dynamic-slice_add_fusion.picked_ref, bf16[16,64,2048]{2,1,0:T(8,128)(2,1)} %bitcast.6.tiles_hbm, bf16[2,128,1024]{2,1,0:T(8,128)(2,1)} %slice.11.rest_0_), custom_call_target="tpu_custom_call" | custom-call | tf_op jit(solution)/shard_map/pallas_call | solution.py:190
  68.0 7.9 %all-to-all-start.2 = ((bf16[16,640,128]{2,1,0:T(8,128)(2,1)}), bf16[16,640,128]{2,1,0:T(8,128)(2,1)S(1)}, u32[]{:S(2)}, u32[]{:S(2)}) async-start(bf16[16,640,128]{2,1,0:T(8,128)(2,1)} %shard_map.93), calls=%async_computation.2 | async-start | bytes 5242880 | tf_op jit(solution)/shard_map/all_to_all | solution.py:303
  75.9 47.6 %shard_map.91 = bf16[8,2,64,2048]{3,2,1,0:T(8,128)(2,1)} custom-call(bf16[8,2,64,2048]{3,2,1,0:T(8,128)(2,1)} %bitcast.11), custom_call_target="tpu_custom_call" | custom-call | tf_op jit(solution)/shard_map/pallas_call | solution.py:66
  123.4 0.0 copy-start.7
  123.5 0.0 copy-start.5
  123.5 0.0 copy-start.6
  123.5 3.7 %shard_map.92 = bf16[16,512,128]{2,1,0:T(8,128)(2,1)} custom-call(s32[8]{0:T(128)} %dynamic-slice_add_fusion.picked_ref, bf16[16,64,2048]{2,1,0:T(8,128)(2,1)} %bitcast.13), custom_call_target="tpu_custom_call" | custom-call | tf_op jit(solution)/shard_map/pallas_call | solution.py:190
  127.2 0.0 all-to-all-done.2.kv_ref.qsrc_ref
  127.2 0.0 copy-start
  127.3 7.2 %all-to-all-start = ((bf16[16,512,128]{2,1,0:T(8,128)(2,1)}), bf16[16,512,128]{2,1,0:T(8,128)(2,1)}, u32[]{:S(2)}, u32[]{:S(2)}) async-start(bf16[16,512,128]{2,1,0:T(8,128)(2,1)} %shard_map.92), calls=%async_computation | async-start | bytes 4194304 | tf_op jit(solution)/shard_map/all_to_all | solution.py:308
  134.5 0.0 copy-done.7
  134.5 0.1 dynamic_slice.16
  134.6 0.0 copy-done.5
  134.6 0.0 copy-done.6
  134.6 0.2 select_reduce_fusion.2
  134.8 0.0 copy-start.4
  134.8 0.6 dynamic_slice.17.len_ref
  135.3 0.0 copy-done
  135.4 8.6 %shard_map.94.rest_0_ = f32[2048,128]{1,0:T(8,128)} custom-call(s32[1]{0:T(128)} %dynamic_slice.17.len_ref, bf16[16,640,128]{2,1,0:T(8,128)(2,1)} %copy-done, bf16[16,640,128]{2,1,0:T(8,128)(2,1)} %copy-done), custom_call_target="tpu_custom_call" | custom-call | tf_op jit(solution)/shard_map/pallas_call | solution.py:142
  144.0 21.2 %all-to-all-done.kv_ref = bf16[16,512,128]{2,1,0:T(8,128)(2,1)} async-done(((bf16[16,512,128]{2,1,0:T(8,128)(2,1)}), bf16[16,512,128]{2,1,0:T(8,128)(2,1)}, u32[]{:S(2)}, u32[]{:S(2)}) %all-to-all-start) | async-done | bytes 2097184 | tf_op jit(solution)/shard_map/all_to_all | solution.py:308
  165.2 7.8 %shard_map.95 = bf16[2048,128]{1,0:T(8,128)(2,1)} custom-call(s32[1]{0:T(128)} %dynamic_slice.17.len_ref, bf16[16,512,128]{2,1,0:T(8,128)(2,1)} %all-to-all-done.kv_ref, bf16[16,640,128]{2,1,0:T(8,128)(2,1)} %copy-done, f32[2048,128]{1,0:T(8,128)} %shard_map.94.rest_0_), custom_call_target="tpu_custom_call" | custom-call | tf_op jit(solution)/shard_map/pallas_call | solution.py:142
  172.9 0.0 copy-done.4
  172.9 16.5 %all-to-all-start.3 = ((bf16[16,128,128]{2,1,0:T(8,128)(2,1)}), bf16[16,128,128]{2,1,0:T(8,128)(2,1)S(1)}, u32[]{:S(2)}, u32[]{:S(2)}) async-start(bf16[16,128,128]{2,1,0:T(8,128)(2,1)} %bitcast.16), calls=%async_computation.3 | async-start | bytes 1048576 | tf_op jit(solution)/shard_map/all_to_all | solution.py:315
  189.4 0.6 broadcast_subtract_fusion.limit_ref
  190.0 9.5 %all-to-all-done.3.hist_ref = bf16[16,128,128]{2,1,0:T(8,128)(2,1)S(1)} async-done(((bf16[16,128,128]{2,1,0:T(8,128)(2,1)}), bf16[16,128,128]{2,1,0:T(8,128)(2,1)S(1)}, u32[]{:S(2)}, u32[]{:S(2)}) %all-to-all-start.3) | async-done | bytes 524320 | tf_op jit(solution)/shard_map/all_to_all | solution.py:315
  199.5 0.0 copy-start.3
  199.5 0.8 copy-done.3
  200.3 4.8 %shard_map.96 = bf16[2,128,1024]{2,1,0:T(8,128)(2,1)} custom-call(f32[8]{0:T(128)} %bias_ref.1, s32[2]{0:T(128)} %copy-done.4, s32[2]{0:T(128)} %broadcast_subtract_fusion.limit_ref, bf16[16,128,128]{2,1,0:T(8,128)(2,1)} %copy-done.3, bf16[2,128,4096]{2,1,0:T(8,128)(2,1)} %bitcast.15, bf16[2,128,1024]{2,1,0:T(8,128)(2,1)} %x_ref.1, bf16[1024,1024]{1,0:T(8,128)(2,1)} %w_ref.1), custom_call_target="tpu_custom_call" | custom-call | tf_op jit(solution)/shard_map/pallas_call | solution.py:232
  (9 shorter events, 0.1 us)
Async XLA Ops:
  10.5 53.2 %all-to-all-start.1 = ((bf16[8,2,64,2048]{3,2,1,0:T(8,128)(2,1)}), bf16[8,2,64,2048]{3,2,1,0:T(8,128)(2,1)}, u32[]{:S(2)}, u32[]{:S(2)}) async-start(bf16[8,2,64,2048]{3,2,1,0:T(8,128)(2,1)} %bitcast.12), calls=%async_computation.1 | async-start | bytes 8388608 | tf_op jit(solution)/shard_map/all_to_all | solution.py:289
  15.4 2.7 %copy-start.1 = (bf16[2,128,1024]{2,1,0:T(8,128)(2,1)S(1)}, bf16[2,128,1024]{2,1,0:T(8,128)(2,1)}, u32[]{:S(2)}) copy-start(bf16[2,128,1024]{2,1,0:T(8,128)(2,1)} %x_ref.1) | copy-start | bytes 1572868
  24.7 1.4 copy-start.2
  68.0 59.3 %all-to-all-start.2 = ((bf16[16,640,128]{2,1,0:T(8,128)(2,1)}), bf16[16,640,128]{2,1,0:T(8,128)(2,1)S(1)}, u32[]{:S(2)}, u32[]{:S(2)}) async-start(bf16[16,640,128]{2,1,0:T(8,128)(2,1)} %shard_map.93), calls=%async_computation.2 | async-start | bytes 5242880 | tf_op jit(solution)/shard_map/all_to_all | solution.py:303
  123.4 11.0 %copy-start.7 = (s32[16]{0:T(128)S(1)}, s32[16]{0:T(128)}, u32[]{:S(2)}) copy-start(s32[16]{0:T(128)} %param.14) | copy-start | bytes 196
  123.5 11.1 %copy-start.5 = (s32[16]{0:T(128)S(1)}, s32[16]{0:T(128)}, u32[]{:S(2)}) copy-start(s32[16]{0:T(128)} %param.16) | copy-start | bytes 196
  123.5 11.1 %copy-start.6 = (s32[16]{0:T(128)S(1)}, s32[16]{0:T(128)}, u32[]{:S(2)}) copy-start(s32[16]{0:T(128)} %param.15) | copy-start | bytes 196
  127.2 8.1 %copy-start = (bf16[16,640,128]{2,1,0:T(8,128)(2,1)}, bf16[16,640,128]{2,1,0:T(8,128)(2,1)S(1)}, u32[]{:S(2)}) copy-start(bf16[16,640,128]{2,1,0:T(8,128)(2,1)S(1)} %all-to-all-done.2.kv_ref.qsrc_ref) | copy-start | bytes 7864324
  127.3 37.9 %all-to-all-start = ((bf16[16,512,128]{2,1,0:T(8,128)(2,1)}), bf16[16,512,128]{2,1,0:T(8,128)(2,1)}, u32[]{:S(2)}, u32[]{:S(2)}) async-start(bf16[16,512,128]{2,1,0:T(8,128)(2,1)} %shard_map.92), calls=%async_computation | async-start | bytes 4194304 | tf_op jit(solution)/shard_map/all_to_all | solution.py:308
  134.8 38.2 %copy-start.4 = (s32[2]{0:T(128)}, s32[2]{0:T(128)S(1)}, u32[]{:S(2)}) copy-start(s32[2]{0:T(128)S(1)} %get-tuple-element.10.len_ref) | copy-start | bytes 28
  172.9 26.6 %all-to-all-start.3 = ((bf16[16,128,128]{2,1,0:T(8,128)(2,1)}), bf16[16,128,128]{2,1,0:T(8,128)(2,1)S(1)}, u32[]{:S(2)}, u32[]{:S(2)}) async-start(bf16[16,128,128]{2,1,0:T(8,128)(2,1)} %bitcast.16), calls=%async_computation.3 | async-start | bytes 1048576 | tf_op jit(solution)/shard_map/all_to_all | solution.py:315
  199.5 0.8 copy-start.3

commit v14 on v12

--- a/solution.py
+++ b/solution.py
@@ -280,8 +280,8 @@
     sub = tile_len // 2
     sending = []
     for half in range(2):
-        kv_half = lax.slice_in_dim(kv_cache, half * sub, (half + 1) * sub, axis=1)
-        outgoing = kv_half.at[source_slot].get(mode="promise_in_bounds")
+        kv_halves = kv_cache.reshape(slots_own, tile_len // sub, sub, 2 * width)
+        outgoing = kv_halves.at[source_slot, half].get(mode="promise_in_bounds")
         sending.append(outgoing.reshape(req_count, capacity, sub, 2 * width))
     first_in = lax.all_to_all(sending[0], "req", split_axis=0, concat_axis=0, tiled=True)
     normed = layer_norm(cand_x.astype(jnp.float32)).astype(jnp.bfloat16)

time: 208 us -> 205 us (0.986)
  Pallas kernels: 87.6 us -> 95.4 us
  starting transfers between devices: 30.9 us -> 24.8 us
  waiting for transfers between devices: 52.3 us -> 48.4 us
    pallas_call x2, Pallas kernels: 27.2 us -> 35 us  [attend(): pl.pallas_call(kernel, out_shape=jax.ShapeDtypeStruct((rows, head_dim), j...]
    all_to_all x1, starting transfers between devices: 10.8 us -> 4.63 us  [local(): lax.all_to_all(history_mine.reshape(hist_count, cand_rows, head_dim), 'hi...]
    slice x1 -> x0, local copies, waits for them, and re-layouts: 4.01 us -> none  [local(): kv_half = lax.slice_in_dim(kv_cache, half * sub, (half + 1) * sub, axis=1)]
    all_to_all x1, waiting for transfers between devices: 16.3 us -> 12.4 us  [local(): lax.all_to_all(pack_for_heads(picked_slot, halves[1], None, users_here, h...]
    gather x2, local copies, waits for them, and re-layouts: 7.92 us -> 10.7 us  [local(): outgoing = kv_halves.at[source_slot, half].get(mode='promise_in_bounds')]
  transfers between devices with their start and end apart: 4 -> 4, of which waited for: 3 -> 3; matrix products, arithmetic and copies ran while one was open for 12% -> 13% of each run, Pallas kernels for 31% -> 34%
where the time goes in v14:
time: 205 us; the launch traced here: 204 us
  Pallas kernels  95.4 us (47%)
  waiting for transfers between devices  48.4 us (24%)
  starting transfers between devices  24.8 us (12%)
  local copies, waits for them, and re-layouts  23.8 us (12%)
  matrix products  7.25 us (4%)
  other arithmetic  4.44 us (2%)
    pallas_call x1, Pallas kernels, req_a2a(): pl.pallas_call(functools.partial(req_a2a_kernel, axis='req', other_axis='...  47.6 us
    pallas_call x2, Pallas kernels, attend(): pl.pallas_call(kernel, out_shape=jax.ShapeDtypeStruct((rows, head_dim), j...  35 us
    all_to_all x1, waiting for transfers between devices, local(): lax.all_to_all(sending[0], 'req', split_axis=0, concat_axis=0, tiled=True)  26.9 us
    all_to_all x1, waiting for transfers between devices, local(): lax.all_to_all(pack_for_heads(picked_slot, halves[1], None, users_here, h...  12.4 us
    gather x2, local copies, waits for them, and re-layouts, local(): outgoing = kv_halves.at[source_slot, half].get(mode='promise_in_bounds')  10.7 us
    all_to_all x1, waiting for transfers between devices, local(): lax.all_to_all(history_mine.reshape(hist_count, cand_rows, head_dim), 'hi...  9.2 us
    pallas_call x2, Pallas kernels, pack_for_heads(): pl.pallas_call(functools.partial(pack_kernel, heads=heads, users=users, p...  8.01 us
    all_to_all x1, starting transfers between devices, local(): lax.all_to_all(pack_for_heads(picked_slot, halves[0], queries, users_here...  7.89 us
  transfers between devices with their start and end apart: 4, of which 3 were waited for; matrix products, arithmetic and copies ran while one was open for 13% of the time, Pallas kernels for 34%

profile of v14, /device:TPU:8, one launch (start us, length us, event | category | flops | bytes accessed | tf_op | source)
XLA Modules:
  0.0 204.3 jit_solution(18385752310423109422)
XLA Ops:
  0.0 0.1 broadcast_in_dim.63
  0.1 0.1 eq.98
  0.2 0.8 reshape.255
  1.0 0.4 dynamic-slice_reduce_fusion
  1.4 0.1 reshape.256
  1.5 0.2 select_reduce_fusion
  1.7 0.1 select_reduce_fusion.1
  1.9 0.1 copy.15
  1.9 0.1 reshape.260
  2.0 5.0 %gather_fusion.1 = bf16[16,64,2048]{2,1,0:T(8,128)(2,1)} fusion(bf16[8,2,64,2048]{3,2,1,0:T(8,128)(2,1)} %bitcast.15, s32[16]{0:T(128)S(1)} %get-tuple-element.13), kind=kCustom, calls=%fused_computation.1 | custom fusion | bytes 8388736 | tf_op jit(solution)/shard_map/gather | solution.py:284
  7.0 0.0 copy-start.3
  7.0 5.0 %all-to-all-start.1 = ((bf16[8,2,64,2048]{3,2,1,0:T(8,128)(2,1)}), bf16[8,2,64,2048]{3,2,1,0:T(8,128)(2,1)}, u32[]{:S(2)}, u32[]{:S(2)}) async-start(bf16[8,2,64,2048]{3,2,1,0:T(8,128)(2,1)} %bitcast.17), calls=%async_computation.1 | async-start | bytes 8388608 | tf_op jit(solution)/shard_map/all_to_all | solution.py:286
  12.1 0.0 copy-done.3
  12.1 0.1 convert_reduce_fusion
  12.2 0.3 fusion.2
  12.5 0.3 fusion.3
  12.8 7.2 %multiply_convert_fusion = bf16[256,4096]{1,0:T(8,128)(2,1)} fusion(bf16[256,1024]{1,0:T(8,128)(2,1)S(1)} %bitcast.20, bf16[1024,4096]{1,0:T(8,128)(2,1)} %param.11), kind=kOutput, calls=%fused_computation.2 | convolution fusion | flops 2152726528 | bytes 11010048 | tf_op jit(solution)/shard_map/dot_general | solution.py:288
  20.0 3.3 %reshape.258 = bf16[2,128,4,1024]{3,2,1,0:T(4,128)(2,1)S(1)} reshape(bf16[256,4096]{1,0:T(8,128)(2,1)} %multiply_convert_fusion) | data formatting | bytes 4194304 | tf_op jit(solution)/shard_map/reshape | solution.py:289
  23.4 0.0 copy-start.1
  23.4 5.7 %gather_fusion = bf16[16,64,2048]{2,1,0:T(8,128)(2,1)} fusion(bf16[8,2,64,2048]{3,2,1,0:T(8,128)(2,1)} %bitcast.16, s32[16]{0:T(128)S(1)} %get-tuple-element.14), kind=kCustom, calls=%fused_computation | custom fusion | bytes 8388736 | tf_op jit(solution)/shard_map/gather | solution.py:284
  29.1 0.0 copy-done.1
  29.1 2.0 copy.16
  31.1 0.6 dynamic-slice_add_fusion.picked_ref
  31.7 1.9 slice_bitcast_fusion.rest_0_
  33.5 26.9 %all-to-all-done.1 = bf16[8,2,64,2048]{3,2,1,0:T(8,128)(2,1)} async-done(((bf16[8,2,64,2048]{3,2,1,0:T(8,128)(2,1)}), bf16[8,2,64,2048]{3,2,1,0:T(8,128)(2,1)}, u32[]{:S(2)}, u32[]{:S(2)}) %all-to-all-start.1) | async-done | bytes 4194336 | tf_op jit(solution)/shard_map/all_to_all | solution.py:286
  60.4 4.2 %shard_map.93 = bf16[16,640,128]{2,1,0:T(8,128)(2,1)} custom-call(s32[8]{0:T(128)} %dynamic-slice_add_fusion.picked_ref, bf16[16,64,2048]{2,1,0:T(8,128)(2,1)} %bitcast.7.tiles_hbm, bf16[2,128,1024]{2,1,0:T(8,128)(2,1)} %slice_bitcast_fusion.rest_0_), custom_call_target="tpu_custom_call" | custom-call | tf_op jit(solution)/shard_map/pallas_call | solution.py:187
  64.6 7.9 %all-to-all-start.2 = ((bf16[16,640,128]{2,1,0:T(8,128)(2,1)}), bf16[16,640,128]{2,1,0:T(8,128)(2,1)S(1)}, u32[]{:S(2)}, u32[]{:S(2)}) async-start(bf16[16,640,128]{2,1,0:T(8,128)(2,1)} %shard_map.93), calls=%async_computation.2 | async-start | bytes 5242880 | tf_op jit(solution)/shard_map/all_to_all | solution.py:303
  72.5 47.6 %shard_map.91 = bf16[8,2,64,2048]{3,2,1,0:T(8,128)(2,1)} custom-call(bf16[8,2,64,2048]{3,2,1,0:T(8,128)(2,1)} %bitcast.18), custom_call_target="tpu_custom_call" | custom-call | tf_op jit(solution)/shard_map/pallas_call | solution.py:66
  120.1 0.0 copy-start.8
  120.1 0.0 copy-start.6
  120.1 0.0 copy-start.7
  120.1 3.8 %shard_map.92 = bf16[16,512,128]{2,1,0:T(8,128)(2,1)} custom-call(s32[8]{0:T(128)} %dynamic-slice_add_fusion.picked_ref, bf16[16,64,2048]{2,1,0:T(8,128)(2,1)} %bitcast.19), custom_call_target="tpu_custom_call" | custom-call | tf_op jit(solution)/shard_map/pallas_call | solution.py:187
  123.9 0.0 all-to-all-done.2.kv_ref.qsrc_ref
  124.0 0.0 copy-start
  124.0 7.2 %all-to-all-start = ((bf16[16,512,128]{2,1,0:T(8,128)(2,1)}), bf16[16,512,128]{2,1,0:T(8,128)(2,1)}, u32[]{:S(2)}, u32[]{:S(2)}) async-start(bf16[16,512,128]{2,1,0:T(8,128)(2,1)} %shard_map.92), calls=%async_computation | async-start | bytes 4194304 | tf_op jit(solution)/shard_map/all_to_all | solution.py:308
  131.2 0.0 copy-done.8
  131.2 0.1 dynamic_slice.16
  131.3 0.0 copy-done.6
  131.3 0.0 copy-done.7
  131.3 0.2 select_reduce_fusion.2
  131.5 0.0 copy-start.5
  131.5 0.6 dynamic_slice.17.len_ref
  132.0 0.0 copy-done
  132.1 17.5 %shard_map.94.rest_0_ = f32[2048,128]{1,0:T(8,128)} custom-call(s32[1]{0:T(128)} %dynamic_slice.17.len_ref, bf16[16,640,128]{2,1,0:T(8,128)(2,1)} %copy-done, bf16[16,640,128]{2,1,0:T(8,128)(2,1)} %copy-done), custom_call_target="tpu_custom_call" | custom-call | tf_op jit(solution)/shard_map/pallas_call | solution.py:140
  149.5 0.0 copy-start.2
  149.5 12.4 %all-to-all-done.kv_ref = bf16[16,512,128]{2,1,0:T(8,128)(2,1)} async-done(((bf16[16,512,128]{2,1,0:T(8,128)(2,1)}), bf16[16,512,128]{2,1,0:T(8,128)(2,1)}, u32[]{:S(2)}, u32[]{:S(2)}) %all-to-all-start) | async-done | bytes 2097184 | tf_op jit(solution)/shard_map/all_to_all | solution.py:308
  161.9 17.6 %shard_map.95 = f32[2048,128]{1,0:T(8,128)} custom-call(s32[1]{0:T(128)} %dynamic_slice.17.len_ref, bf16[16,512,128]{2,1,0:T(8,128)(2,1)} %all-to-all-done.kv_ref, bf16[16,640,128]{2,1,0:T(8,128)(2,1)} %copy-done, f32[2048,128]{1,0:T(8,128)} %shard_map.94.rest_0_), custom_call_target="tpu_custom_call" | custom-call | tf_op jit(solution)/shard_map/pallas_call | solution.py:140
  179.5 0.0 copy-done.5
  179.5 2.1 %convert_element_type.15 = bf16[2048,128]{1,0:T(8,128)(2,1)} convert(f32[2048,128]{1,0:T(8,128)} %shard_map.95) | non-fusion elementwise | flops 262144 | bytes 1572864 | tf_op jit(solution)/shard_map/convert_element_type | solution.py:314
  181.5 4.6 %all-to-all-start.3 = ((bf16[16,128,128]{2,1,0:T(8,128)(2,1)}), bf16[16,128,128]{2,1,0:T(8,128)(2,1)S(1)}, u32[]{:S(2)}, u32[]{:S(2)}) async-start(bf16[16,128,128]{2,1,0:T(8,128)(2,1)} %bitcast.9), calls=%async_computation.3 | async-start | bytes 1048576 | tf_op jit(solution)/shard_map/all_to_all | solution.py:315
  186.2 0.0 copy-done.2
  186.2 2.8 %reshape.266.proj_ref = bf16[2,128,4096]{2,1,0:T(8,128)(2,1)} reshape(bf16[2,128,4,1024]{3,2,1,0:T(4,128)(2,1)S(1)} %copy-done.2) | data formatting | bytes 4194304 | tf_op jit(solution)/shard_map/reshape | solution.py:320
  189.0 0.5 broadcast_subtract_fusion.limit_ref
  189.5 9.2 %all-to-all-done.3.hist_ref = bf16[16,128,128]{2,1,0:T(8,128)(2,1)S(1)} async-done(((bf16[16,128,128]{2,1,0:T(8,128)(2,1)}), bf16[16,128,128]{2,1,0:T(8,128)(2,1)S(1)}, u32[]{:S(2)}, u32[]{:S(2)}) %all-to-all-start.3) | async-done | bytes 524320 | tf_op jit(solution)/shard_map/all_to_all | solution.py:315
  198.7 0.0 copy-start.4
  198.7 0.8 copy-done.4
  199.5 4.8 %shard_map.96 = bf16[2,128,1024]{2,1,0:T(8,128)(2,1)} custom-call(f32[8]{0:T(128)} %bias_ref.1, s32[2]{0:T(128)} %copy-done.5, s32[2]{0:T(128)} %broadcast_subtract_fusion.limit_ref, bf16[16,128,128]{2,1,0:T(8,128)(2,1)} %copy-done.4, bf16[2,128,4096]{2,1,0:T(8,128)(2,1)} %reshape.266.proj_ref, bf16[2,128,1024]{2,1,0:T(8,128)(2,1)} %x_ref.1, ...), custom_call_target="tpu_custom_call" | custom-call | tf_op jit(solution)/shard_map/pallas_call | solution.py:229
  (8 shorter events, 0.1 us)
Async XLA Ops:
  7.0 5.1 %copy-start.3 = (bf16[2,128,1024]{2,1,0:T(8,128)(2,1)S(1)}, bf16[2,128,1024]{2,1,0:T(8,128)(2,1)}, u32[]{:S(2)}) copy-start(bf16[2,128,1024]{2,1,0:T(8,128)(2,1)} %x_ref.1) | copy-start | bytes 1572868
  7.0 53.4 %all-to-all-start.1 = ((bf16[8,2,64,2048]{3,2,1,0:T(8,128)(2,1)}), bf16[8,2,64,2048]{3,2,1,0:T(8,128)(2,1)}, u32[]{:S(2)}, u32[]{:S(2)}) async-start(bf16[8,2,64,2048]{3,2,1,0:T(8,128)(2,1)} %bitcast.17), calls=%async_computation.1 | async-start | bytes 8388608 | tf_op jit(solution)/shard_map/all_to_all | solution.py:286
  23.4 5.8 %copy-start.1 = (bf16[2,128,4,1024]{3,2,1,0:T(4,128)(2,1)}, bf16[2,128,4,1024]{3,2,1,0:T(4,128)(2,1)S(1)}, u32[]{:S(2)}) copy-start(bf16[2,128,4,1024]{3,2,1,0:T(4,128)(2,1)S(1)} %reshape.258) | copy-start | bytes 6291460
  64.6 59.3 %all-to-all-start.2 = ((bf16[16,640,128]{2,1,0:T(8,128)(2,1)}), bf16[16,640,128]{2,1,0:T(8,128)(2,1)S(1)}, u32[]{:S(2)}, u32[]{:S(2)}) async-start(bf16[16,640,128]{2,1,0:T(8,128)(2,1)} %shard_map.93), calls=%async_computation.2 | async-start | bytes 5242880 | tf_op jit(solution)/shard_map/all_to_all | solution.py:303
  120.1 11.1 %copy-start.8 = (s32[16]{0:T(128)S(1)}, s32[16]{0:T(128)}, u32[]{:S(2)}) copy-start(s32[16]{0:T(128)} %param.14) | copy-start | bytes 196
  120.1 11.2 %copy-start.6 = (s32[16]{0:T(128)S(1)}, s32[16]{0:T(128)}, u32[]{:S(2)}) copy-start(s32[16]{0:T(128)} %param.16) | copy-start | bytes 196
  120.1 11.2 %copy-start.7 = (s32[16]{0:T(128)S(1)}, s32[16]{0:T(128)}, u32[]{:S(2)}) copy-start(s32[16]{0:T(128)} %param.15) | copy-start | bytes 196
  124.0 8.1 %copy-start = (bf16[16,640,128]{2,1,0:T(8,128)(2,1)}, bf16[16,640,128]{2,1,0:T(8,128)(2,1)S(1)}, u32[]{:S(2)}) copy-start(bf16[16,640,128]{2,1,0:T(8,128)(2,1)S(1)} %all-to-all-done.2.kv_ref.qsrc_ref) | copy-start | bytes 7864324
  124.0 37.9 %all-to-all-start = ((bf16[16,512,128]{2,1,0:T(8,128)(2,1)}), bf16[16,512,128]{2,1,0:T(8,128)(2,1)}, u32[]{:S(2)}, u32[]{:S(2)}) async-start(bf16[16,512,128]{2,1,0:T(8,128)(2,1)} %shard_map.92), calls=%async_computation | async-start | bytes 4194304 | tf_op jit(solution)/shard_map/all_to_all | solution.py:308
  131.5 48.0 %copy-start.5 = (s32[2]{0:T(128)}, s32[2]{0:T(128)S(1)}, u32[]{:S(2)}) copy-start(s32[2]{0:T(128)S(1)} %get-tuple-element.10.len_ref) | copy-start | bytes 28
  149.5 36.7 %copy-start.2 = (bf16[2,128,4,1024]{3,2,1,0:T(4,128)(2,1)S(1)}, bf16[2,128,4,1024]{3,2,1,0:T(4,128)(2,1)}, u32[]{:S(2)}) copy-start(bf16[2,128,4,1024]{3,2,1,0:T(4,128)(2,1)} %copy-done.1) | copy-start | bytes 6291460
  181.5 17.2 %all-to-all-start.3 = ((bf16[16,128,128]{2,1,0:T(8,128)(2,1)}), bf16[16,128,128]{2,1,0:T(8,128)(2,1)S(1)}, u32[]{:S(2)}, u32[]{:S(2)}) async-start(bf16[16,128,128]{2,1,0:T(8,128)(2,1)} %bitcast.9), calls=%async_computation.3 | async-start | bytes 1048576 | tf_op jit(solution)/shard_map/all_to_all | solution.py:315
  198.7 0.8 copy-start.4

commit v15 on v12

--- a/solution.py
+++ b/solution.py
@@ -89,7 +89,7 @@
     block = q_ref.shape[0] // n_cls
     half_scale = 0.5 * score_scale
     for b in range(n_cls):
-        q_ref[pl.ds(b * block, block), :] = qsrc_ref[b, pl.ds(q_row, block), :]
+        q_ref[pl.ds(b * block, block), :] = qsrc_ref[b]
     if init_ref is None:
         o_ref[...] = jnp.zeros_like(o_ref)
     else:
@@ -139,9 +139,14 @@
     )
     return pl.pallas_call(
         kernel,
+        grid=(1,),
         out_shape=jax.ShapeDtypeStruct((rows, head_dim), jnp.float32),
-        in_specs=[pl.BlockSpec(memory_space=pltpu.SMEM)]
-        + [pl.BlockSpec(memory_space=pltpu.VMEM)] * (2 if init is None else 3),
+        in_specs=[
+            pl.BlockSpec(memory_space=pltpu.SMEM),
+            pl.BlockSpec(memory_space=pltpu.VMEM),
+            pl.BlockSpec((n_cls, rows // n_cls, head_dim), lambda i: (0, q_row // (rows // n_cls), 0)),
+        ]
+        + ([] if init is None else [pl.BlockSpec(memory_space=pltpu.VMEM)]),
         out_specs=pl.BlockSpec(memory_space=pltpu.VMEM),
         scratch_shapes=[pltpu.VMEM((rows, head_dim), jnp.bfloat16)],
     )(length, kv_packed, q_packed, *([] if init is None else [init]))

time: 208 us -> 208 us (level)
  no operation moved by 1% of the time
where the time goes in v15:
time: 208 us; the launch traced here: 207 us
  Pallas kernels  87.8 us (42%)
  waiting for transfers between devices  52.2 us (25%)
  starting transfers between devices  30.1 us (14%)
  local copies, waits for them, and re-layouts  25 us (12%)
  matrix products  7.25 us (3%)
  other arithmetic  4.44 us (2%)
    pallas_call x1, Pallas kernels, req_a2a(): pl.pallas_call(functools.partial(req_a2a_kernel, axis='req', other_axis='...  47.6 us
    all_to_all x1, waiting for transfers between devices, local(): lax.all_to_all(sending[0], 'req', split_axis=0, concat_axis=0, tiled=True)  27.5 us
    pallas_call x2, Pallas kernels, attend(): pl.pallas_call(kernel, grid=(1,), out_shape=jax.ShapeDtypeStruct((rows, h...  27.4 us
    all_to_all x1, waiting for transfers between devices, local(): lax.all_to_all(pack_for_heads(picked_slot, halves[1], None, users_here, h...  16.2 us
    all_to_all x1, starting transfers between devices, local(): lax.all_to_all(history_mine.reshape(hist_count, cand_rows, head_dim), 'hi...  10 us
    all_to_all x1, waiting for transfers between devices, local(): lax.all_to_all(history_mine.reshape(hist_count, cand_rows, head_dim), 'hi...  8.49 us
    pallas_call x2, Pallas kernels, pack_for_heads(): pl.pallas_call(functools.partial(pack_kernel, heads=heads, users=users, p...  8.01 us
    gather x2, local copies, waits for them, and re-layouts, local(): outgoing = kv_half.at[source_slot].get(mode='promise_in_bounds')  7.92 us
  transfers between devices with their start and end apart: 4, of which 3 were waited for; matrix products, arithmetic and copies ran while one was open for 12% of the time, Pallas kernels for 31%

profile of v15, /device:TPU:8, one launch (start us, length us, event | category | flops | bytes accessed | tf_op | source)
XLA Modules:
  0.0 207.0 jit_solution(4299682470537461758)
XLA Ops:
  0.0 0.1 broadcast_in_dim.63
  0.1 0.1 eq.98
  0.2 0.8 reshape.251
  1.0 0.4 dynamic-slice_reduce_fusion
  1.4 0.1 reshape.252
  1.5 4.0 %fusion.7 = (bf16[8,64,2048]{2,1,0:T(8,128)(2,1)S(1)}, bf16[8,64,2048]{2,1,0:T(8,128)(2,1)}) fusion(bf16[8,128,2048]{2,1,0:T(8,128)(2,1)} %param.10), kind=kLoop, calls=%fused_computation.38 | loop fusion | bytes 8388608 | tf_op jit(solution)/shard_map/slice | solution.py:288
  5.5 0.2 select_reduce_fusion
  5.7 0.1 select_reduce_fusion.1
  5.9 0.1 copy.15
  6.0 0.1 reshape.255
  6.1 2.8 %gather_fusion.1 = bf16[16,64,2048]{2,1,0:T(8,128)(2,1)} fusion(bf16[8,64,2048]{2,1,0:T(8,128)(2,1)S(1)} %get-tuple-element.13, s32[1024]{0:T(1024)S(1)} %pad_clamp_fusion), kind=kCustom, calls=%fused_computation.1 | custom fusion | bytes 8388672 | tf_op jit(solution)/shard_map/gather | solution.py:289
  8.8 0.0 copy-start.3
  8.8 5.0 %all-to-all-start.1 = ((bf16[8,2,64,2048]{3,2,1,0:T(8,128)(2,1)}), bf16[8,2,64,2048]{3,2,1,0:T(8,128)(2,1)}, u32[]{:S(2)}, u32[]{:S(2)}) async-start(bf16[8,2,64,2048]{3,2,1,0:T(8,128)(2,1)} %bitcast.12), calls=%async_computation.1 | async-start | bytes 8388608 | tf_op jit(solution)/shard_map/all_to_all | solution.py:291
  13.9 0.0 copy-done.3
  13.9 0.1 convert_reduce_fusion
  14.1 0.3 fusion.2
  14.3 0.3 fusion.3
  14.6 7.2 %multiply_convert_fusion = bf16[256,4096]{1,0:T(8,128)(2,1)} fusion(bf16[256,1024]{1,0:T(8,128)(2,1)S(1)} %bitcast.15, bf16[1024,4096]{1,0:T(8,128)(2,1)} %param.11), kind=kOutput, calls=%fused_computation.2 | convolution fusion | flops 2152726528 | bytes 11010048 | tf_op jit(solution)/shard_map/dot_general | solution.py:293
  21.9 3.3 %reshape.254 = bf16[2,128,4,1024]{3,2,1,0:T(4,128)(2,1)S(1)} reshape(bf16[256,4096]{1,0:T(8,128)(2,1)} %multiply_convert_fusion) | data formatting | bytes 4194304 | tf_op jit(solution)/shard_map/reshape | solution.py:294
  25.2 0.0 copy-start.1
  25.2 5.1 %gather_fusion = bf16[16,64,2048]{2,1,0:T(8,128)(2,1)} fusion(bf16[8,64,2048]{2,1,0:T(8,128)(2,1)} %get-tuple-element.14, s32[1024]{0:T(1024)S(1)} %pad_clamp_fusion), kind=kCustom, calls=%fused_computation | custom fusion | bytes 8388672 | tf_op jit(solution)/shard_map/gather | solution.py:289
  30.3 0.0 copy-done.1
  30.3 2.0 copy.16
  32.3 0.6 dynamic-slice_add_fusion.picked_ref
  32.9 1.9 slice_bitcast_fusion.rest_0_
  34.8 27.5 %all-to-all-done.1 = bf16[8,2,64,2048]{3,2,1,0:T(8,128)(2,1)} async-done(((bf16[8,2,64,2048]{3,2,1,0:T(8,128)(2,1)}), bf16[8,2,64,2048]{3,2,1,0:T(8,128)(2,1)}, u32[]{:S(2)}, u32[]{:S(2)}) %all-to-all-start.1) | async-done | bytes 4194336 | tf_op jit(solution)/shard_map/all_to_all | solution.py:291
  62.2 4.2 %shard_map.93 = bf16[16,640,128]{2,1,0:T(8,128)(2,1)} custom-call(s32[8]{0:T(128)} %dynamic-slice_add_fusion.picked_ref, bf16[16,64,2048]{2,1,0:T(8,128)(2,1)} %bitcast.5.tiles_hbm, bf16[2,128,1024]{2,1,0:T(8,128)(2,1)} %slice_bitcast_fusion.rest_0_), custom_call_target="tpu_custom_call" | custom-call | tf_op jit(solution)/shard_map/pallas_call | solution.py:192
  66.4 7.9 %all-to-all-start.2 = ((bf16[16,640,128]{2,1,0:T(8,128)(2,1)}), bf16[16,640,128]{2,1,0:T(8,128)(2,1)S(1)}, u32[]{:S(2)}, u32[]{:S(2)}) async-start(bf16[16,640,128]{2,1,0:T(8,128)(2,1)} %shard_map.93), calls=%async_computation.2 | async-start | bytes 5242880 | tf_op jit(solution)/shard_map/all_to_all | solution.py:308
  74.3 47.6 %shard_map.91 = bf16[8,2,64,2048]{3,2,1,0:T(8,128)(2,1)} custom-call(bf16[8,2,64,2048]{3,2,1,0:T(8,128)(2,1)} %bitcast.13), custom_call_target="tpu_custom_call" | custom-call | tf_op jit(solution)/shard_map/pallas_call | solution.py:66
  121.9 0.0 copy-start.8
  121.9 0.0 copy-start.6
  121.9 0.0 copy-start.7
  122.0 3.8 %shard_map.92 = bf16[16,512,128]{2,1,0:T(8,128)(2,1)} custom-call(s32[8]{0:T(128)} %dynamic-slice_add_fusion.picked_ref, bf16[16,64,2048]{2,1,0:T(8,128)(2,1)} %bitcast.14), custom_call_target="tpu_custom_call" | custom-call | tf_op jit(solution)/shard_map/pallas_call | solution.py:192
  125.8 0.0 all-to-all-done.2.kv_ref.qsrc_ref
  125.8 0.0 copy-start
  125.8 7.2 %all-to-all-start = ((bf16[16,512,128]{2,1,0:T(8,128)(2,1)}), bf16[16,512,128]{2,1,0:T(8,128)(2,1)}, u32[]{:S(2)}, u32[]{:S(2)}) async-start(bf16[16,512,128]{2,1,0:T(8,128)(2,1)} %shard_map.92), calls=%async_computation | async-start | bytes 4194304 | tf_op jit(solution)/shard_map/all_to_all | solution.py:313
  133.0 0.0 copy-done.8
  133.0 0.1 dynamic_slice.16
  133.1 0.0 copy-done.6
  133.1 0.0 copy-done.7
  133.1 0.2 select_reduce_fusion.2
  133.3 0.0 copy-start.5
  133.3 0.6 dynamic_slice.17.len_ref
  133.9 0.0 copy-done
  133.9 13.6 %shard_map.94.rest_0_ = f32[2048,128]{1,0:T(8,128)} custom-call(s32[1]{0:T(128)} %dynamic_slice.17.len_ref, bf16[16,640,128]{2,1,0:T(8,128)(2,1)} %copy-done, bf16[16,640,128]{2,1,0:T(8,128)(2,1)} %copy-done), custom_call_target="tpu_custom_call" | custom-call | tf_op jit(solution)/shard_map/pallas_call | solution.py:140
  147.5 0.0 copy-start.2
  147.5 16.2 %all-to-all-done.kv_ref = bf16[16,512,128]{2,1,0:T(8,128)(2,1)} async-done(((bf16[16,512,128]{2,1,0:T(8,128)(2,1)}), bf16[16,512,128]{2,1,0:T(8,128)(2,1)}, u32[]{:S(2)}, u32[]{:S(2)}) %all-to-all-start) | async-done | bytes 2097184 | tf_op jit(solution)/shard_map/all_to_all | solution.py:313
  163.7 13.8 %shard_map.95 = f32[2048,128]{1,0:T(8,128)} custom-call(s32[1]{0:T(128)} %dynamic_slice.17.len_ref, bf16[16,512,128]{2,1,0:T(8,128)(2,1)} %all-to-all-done.kv_ref, bf16[16,640,128]{2,1,0:T(8,128)(2,1)} %copy-done, f32[2048,128]{1,0:T(8,128)} %shard_map.94.rest_0_), custom_call_target="tpu_custom_call" | custom-call | tf_op jit(solution)/shard_map/pallas_call | solution.py:140
  177.5 0.0 copy-done.5
  177.5 2.1 convert_element_type.15
  179.6 10.0 %all-to-all-start.3 = ((bf16[16,128,128]{2,1,0:T(8,128)(2,1)}), bf16[16,128,128]{2,1,0:T(8,128)(2,1)S(1)}, u32[]{:S(2)}, u32[]{:S(2)}) async-start(bf16[16,128,128]{2,1,0:T(8,128)(2,1)} %bitcast.7), calls=%async_computation.3 | async-start | bytes 1048576 | tf_op jit(solution)/shard_map/all_to_all | solution.py:320
  189.6 0.0 copy-done.2
  189.6 2.8 %reshape.261.proj_ref = bf16[2,128,4096]{2,1,0:T(8,128)(2,1)} reshape(bf16[2,128,4,1024]{3,2,1,0:T(4,128)(2,1)S(1)} %copy-done.2) | data formatting | bytes 4194304 | tf_op jit(solution)/shard_map/reshape | solution.py:325
  192.4 0.5 broadcast_subtract_fusion.limit_ref
  193.0 8.5 %all-to-all-done.3.hist_ref = bf16[16,128,128]{2,1,0:T(8,128)(2,1)S(1)} async-done(((bf16[16,128,128]{2,1,0:T(8,128)(2,1)}), bf16[16,128,128]{2,1,0:T(8,128)(2,1)S(1)}, u32[]{:S(2)}, u32[]{:S(2)}) %all-to-all-start.3) | async-done | bytes 524320 | tf_op jit(solution)/shard_map/all_to_all | solution.py:320
  201.4 0.0 copy-start.4
  201.4 0.8 copy-done.4
  202.2 4.8 %shard_map.96 = bf16[2,128,1024]{2,1,0:T(8,128)(2,1)} custom-call(f32[8]{0:T(128)} %bias_ref.1, s32[2]{0:T(128)} %copy-done.5, s32[2]{0:T(128)} %broadcast_subtract_fusion.limit_ref, bf16[16,128,128]{2,1,0:T(8,128)(2,1)} %copy-done.4, bf16[2,128,4096]{2,1,0:T(8,128)(2,1)} %reshape.261.proj_ref, bf16[2,128,1024]{2,1,0:T(8,128)(2,1)} %x_ref.1, ...), custom_call_target="tpu_custom_call" | custom-call | tf_op jit(solution)/shard_map/pallas_call | solution.py:234
  (9 shorter events, 0.1 us)
Async XLA Ops:
  8.8 5.1 %copy-start.3 = (bf16[2,128,1024]{2,1,0:T(8,128)(2,1)S(1)}, bf16[2,128,1024]{2,1,0:T(8,128)(2,1)}, u32[]{:S(2)}) copy-start(bf16[2,128,1024]{2,1,0:T(8,128)(2,1)} %x_ref.1) | copy-start | bytes 1572868
  8.8 53.4 %all-to-all-start.1 = ((bf16[8,2,64,2048]{3,2,1,0:T(8,128)(2,1)}), bf16[8,2,64,2048]{3,2,1,0:T(8,128)(2,1)}, u32[]{:S(2)}, u32[]{:S(2)}) async-start(bf16[8,2,64,2048]{3,2,1,0:T(8,128)(2,1)} %bitcast.12), calls=%async_computation.1 | async-start | bytes 8388608 | tf_op jit(solution)/shard_map/all_to_all | solution.py:291
  25.2 5.2 %copy-start.1 = (bf16[2,128,4,1024]{3,2,1,0:T(4,128)(2,1)}, bf16[2,128,4,1024]{3,2,1,0:T(4,128)(2,1)S(1)}, u32[]{:S(2)}) copy-start(bf16[2,128,4,1024]{3,2,1,0:T(4,128)(2,1)S(1)} %reshape.254) | copy-start | bytes 6291460
  66.4 59.3 %all-to-all-start.2 = ((bf16[16,640,128]{2,1,0:T(8,128)(2,1)}), bf16[16,640,128]{2,1,0:T(8,128)(2,1)S(1)}, u32[]{:S(2)}, u32[]{:S(2)}) async-start(bf16[16,640,128]{2,1,0:T(8,128)(2,1)} %shard_map.93), calls=%async_computation.2 | async-start | bytes 5242880 | tf_op jit(solution)/shard_map/all_to_all | solution.py:308
  121.9 11.1 %copy-start.8 = (s32[16]{0:T(128)S(1)}, s32[16]{0:T(128)}, u32[]{:S(2)}) copy-start(s32[16]{0:T(128)} %param.14) | copy-start | bytes 196
  121.9 11.2 %copy-start.6 = (s32[16]{0:T(128)S(1)}, s32[16]{0:T(128)}, u32[]{:S(2)}) copy-start(s32[16]{0:T(128)} %param.16) | copy-start | bytes 196
  121.9 11.2 %copy-start.7 = (s32[16]{0:T(128)S(1)}, s32[16]{0:T(128)}, u32[]{:S(2)}) copy-start(s32[16]{0:T(128)} %param.15) | copy-start | bytes 196
  125.8 8.1 %copy-start = (bf16[16,640,128]{2,1,0:T(8,128)(2,1)}, bf16[16,640,128]{2,1,0:T(8,128)(2,1)S(1)}, u32[]{:S(2)}) copy-start(bf16[16,640,128]{2,1,0:T(8,128)(2,1)S(1)} %all-to-all-done.2.kv_ref.qsrc_ref) | copy-start | bytes 7864324
  125.8 37.9 %all-to-all-start = ((bf16[16,512,128]{2,1,0:T(8,128)(2,1)}), bf16[16,512,128]{2,1,0:T(8,128)(2,1)}, u32[]{:S(2)}, u32[]{:S(2)}) async-start(bf16[16,512,128]{2,1,0:T(8,128)(2,1)} %shard_map.92), calls=%async_computation | async-start | bytes 4194304 | tf_op jit(solution)/shard_map/all_to_all | solution.py:313
  133.3 44.3 %copy-start.5 = (s32[2]{0:T(128)}, s32[2]{0:T(128)S(1)}, u32[]{:S(2)}) copy-start(s32[2]{0:T(128)S(1)} %get-tuple-element.10.len_ref) | copy-start | bytes 28
  147.5 42.1 %copy-start.2 = (bf16[2,128,4,1024]{3,2,1,0:T(4,128)(2,1)S(1)}, bf16[2,128,4,1024]{3,2,1,0:T(4,128)(2,1)}, u32[]{:S(2)}) copy-start(bf16[2,128,4,1024]{3,2,1,0:T(4,128)(2,1)} %copy-done.1) | copy-start | bytes 6291460
  179.6 21.8 %all-to-all-start.3 = ((bf16[16,128,128]{2,1,0:T(8,128)(2,1)}), bf16[16,128,128]{2,1,0:T(8,128)(2,1)S(1)}, u32[]{:S(2)}, u32[]{:S(2)}) async-start(bf16[16,128,128]{2,1,0:T(8,128)(2,1)} %bitcast.7), calls=%async_computation.3 | async-start | bytes 1048576 | tf_op jit(solution)/shard_map/all_to_all | solution.py:320
  201.4 0.8 copy-start.4

commit v16 on v12

--- a/solution.py
+++ b/solution.py
@@ -200,37 +200,46 @@
 def finish_kernel(
     bias_ref, len_ref, limit_ref, hist_ref, proj_ref, x_ref, w_ref, out_ref, att_ref, *, heads, score_scale
 ):
-    users, rows, width = x_ref.shape
+    _, rows, width = x_ref.shape
     head_dim = width // heads
-    for u in range(users):
-        divisor = (len_ref[u] + 1).astype(jnp.float32)
-        for e in range(heads):
-            value = proj_ref[u, :, pl.ds(width + e * head_dim, head_dim)].astype(jnp.float32)
-            query = proj_ref[u, :, pl.ds(2 * width + e * head_dim, head_dim)].astype(jnp.float32)
-            key = proj_ref[u, :, pl.ds(3 * width + e * head_dim, head_dim)].astype(jnp.float32)
-            self_score = jnp.sum(query * key, axis=-1, keepdims=True) * score_scale + bias_ref[e]
-            own = self_score * (0.5 + 0.5 * jnp.tanh(0.5 * self_score)) * value
-            history = hist_ref[u * heads + e].astype(jnp.float32)
-            att_ref[:, pl.ds(e * head_dim, head_dim)] = (history + own) / divisor
-        attended = att_ref[...]
-        centred = attended - jnp.mean(attended, axis=-1, keepdims=True)
-        spread = jnp.mean(centred * centred, axis=-1, keepdims=True)
-        gate = proj_ref[u, :, pl.ds(0, width)].astype(jnp.float32)
-        gated = (centred * lax.rsqrt(spread + 1e-05) * gate).astype(jnp.bfloat16)
-        result = x_ref[u].astype(jnp.float32) + jnp.dot(gated, w_ref[...], preferred_element_type=jnp.float32)
-        row = lax.broadcasted_iota(jnp.int32, (rows, 1), 0)
-        out_ref[u] = jnp.where(row < limit_ref[u], result, 0.0).astype(out_ref.dtype)
+    u = pl.program_id(0)
+    divisor = (len_ref[u] + 1).astype(jnp.float32)
+    for e in range(heads):
+        value = proj_ref[0, :, pl.ds(width + e * head_dim, head_dim)].astype(jnp.float32)
+        query = proj_ref[0, :, pl.ds(2 * width + e * head_dim, head_dim)].astype(jnp.float32)
+        key = proj_ref[0, :, pl.ds(3 * width + e * head_dim, head_dim)].astype(jnp.float32)
+        self_score = jnp.sum(query * key, axis=-1, keepdims=True) * score_scale + bias_ref[e]
+        own = self_score * (0.5 + 0.5 * jnp.tanh(0.5 * self_score)) * value
+        history = hist_ref[e].astype(jnp.float32)
+        att_ref[:, pl.ds(e * head_dim, head_dim)] = (history + own) / divisor
+    attended = att_ref[...]
+    centred = attended - jnp.mean(attended, axis=-1, keepdims=True)
+    spread = jnp.mean(centred * centred, axis=-1, keepdims=True)
+    gate = proj_ref[0, :, pl.ds(0, width)].astype(jnp.float32)
+    gated = (centred * lax.rsqrt(spread + 1e-05) * gate).astype(jnp.bfloat16)
+    result = x_ref[0].astype(jnp.float32) + jnp.dot(gated, w_ref[...], preferred_element_type=jnp.float32)
+    row = lax.broadcasted_iota(jnp.int32, (rows, 1), 0)
+    out_ref[0] = jnp.where(row < limit_ref[u], result, 0.0).astype(out_ref.dtype)
 
 
 def finish(history_back, projected, cand_x, w_out, self_bias, lengths, row_limit, heads, score_scale):
     users, rows, width = cand_x.shape
+    head_dim = width // heads
     smem = pl.BlockSpec(memory_space=pltpu.SMEM)
-    vmem = pl.BlockSpec(memory_space=pltpu.VMEM)
     return pl.pallas_call(
         functools.partial(finish_kernel, heads=heads, score_scale=score_scale),
+        grid=(users,),
         out_shape=jax.ShapeDtypeStruct(cand_x.shape, cand_x.dtype),
-        in_specs=[smem, smem, smem, vmem, vmem, vmem, vmem],
-        out_specs=vmem,
+        in_specs=[
+            smem,
+            smem,
+            smem,
+            pl.BlockSpec((heads, rows, head_dim), lambda u: (u, 0, 0)),
+            pl.BlockSpec((1, rows, projected.shape[2]), lambda u: (u, 0, 0)),
+            pl.BlockSpec((1, rows, width), lambda u: (u, 0, 0)),
+            pl.BlockSpec((width, width), lambda u: (0, 0)),
+        ],
+        out_specs=pl.BlockSpec((1, rows, width), lambda u: (u, 0, 0)),
         scratch_shapes=[pltpu.VMEM((rows, width), jnp.float32)],
     )(self_bias, lengths, row_limit, history_back, projected, cand_x, w_out)
 

time: 208 us -> 209 us (level)
  Pallas kernels: 87.6 us -> 95.8 us
  waiting for transfers between devices: 52.3 us -> 48.2 us
  starting transfers between devices: 30.9 us -> 26.9 us
    pallas_call x2, Pallas kernels: 27.2 us -> 35.3 us  [attend(): pl.pallas_call(kernel, out_shape=jax.ShapeDtypeStruct((rows, head_dim), j...]
    all_to_all x1, starting transfers between devices: 10.8 us -> 6.76 us  [local(): lax.all_to_all(history_mine.reshape(hist_count, cand_rows, head_dim), 'hi...]
    all_to_all x1, waiting for transfers between devices: 16.3 us -> 12.3 us  [local(): lax.all_to_all(pack_for_heads(picked_slot, halves[1], None, users_here, h...]
  transfers between devices with their start and end apart: 4 -> 4, of which waited for: 3 -> 3; matrix products, arithmetic and copies ran while one was open for 12% -> 12% of each run, Pallas kernels for 31% -> 33%
where the time goes in v16:
time: 209 us; the launch traced here: 208 us
  Pallas kernels  95.8 us (46%)
  waiting for transfers between devices  48.2 us (23%)
  starting transfers between devices  26.9 us (13%)
  local copies, waits for them, and re-layouts  25 us (12%)
  matrix products  7.25 us (3%)
  other arithmetic  4.44 us (2%)
    pallas_call x1, Pallas kernels, req_a2a(): pl.pallas_call(functools.partial(req_a2a_kernel, axis='req', other_axis='...  47.6 us
    pallas_call x2, Pallas kernels, attend(): pl.pallas_call(kernel, out_shape=jax.ShapeDtypeStruct((rows, head_dim), j...  35.3 us
    all_to_all x1, waiting for transfers between devices, local(): lax.all_to_all(sending[0], 'req', split_axis=0, concat_axis=0, tiled=True)  27.5 us
    all_to_all x1, waiting for transfers between devices, local(): lax.all_to_all(pack_for_heads(picked_slot, halves[1], None, users_here, h...  12.3 us
    all_to_all x1, waiting for transfers between devices, local(): lax.all_to_all(history_mine.reshape(hist_count, cand_rows, head_dim), 'hi...  8.49 us
    pallas_call x2, Pallas kernels, pack_for_heads(): pl.pallas_call(functools.partial(pack_kernel, heads=heads, users=users, p...  8.01 us
    gather x2, local copies, waits for them, and re-layouts, local(): outgoing = kv_half.at[source_slot].get(mode='promise_in_bounds')  7.92 us
    all_to_all x1, starting transfers between devices, local(): lax.all_to_all(pack_for_heads(picked_slot, halves[0], queries, users_here...  7.89 us
  transfers between devices with their start and end apart: 4, of which 3 were waited for; matrix products, arithmetic and copies ran while one was open for 12% of the time, Pallas kernels for 33%

profile of v16, /device:TPU:8, one launch (start us, length us, event | category | flops | bytes accessed | tf_op | source)
XLA Modules:
  0.0 207.8 jit_solution(17084565010424222574)
XLA Ops:
  0.0 0.1 broadcast_in_dim.63
  0.1 0.1 eq.98
  0.2 0.8 reshape.251
  1.0 0.4 dynamic-slice_reduce_fusion
  1.4 0.1 reshape.252
  1.5 4.0 %fusion.7 = (bf16[8,64,2048]{2,1,0:T(8,128)(2,1)S(1)}, bf16[8,64,2048]{2,1,0:T(8,128)(2,1)}) fusion(bf16[8,128,2048]{2,1,0:T(8,128)(2,1)} %param.10), kind=kLoop, calls=%fused_computation.38 | loop fusion | bytes 8388608 | tf_op jit(solution)/shard_map/slice | solution.py:292
  5.5 0.2 select_reduce_fusion
  5.7 0.1 select_reduce_fusion.1
  5.9 0.1 copy.15
  6.0 0.1 reshape.255
  6.1 2.8 %gather_fusion.1 = bf16[16,64,2048]{2,1,0:T(8,128)(2,1)} fusion(bf16[8,64,2048]{2,1,0:T(8,128)(2,1)S(1)} %get-tuple-element.13, s32[1024]{0:T(1024)S(1)} %pad_clamp_fusion), kind=kCustom, calls=%fused_computation.1 | custom fusion | bytes 8388672 | tf_op jit(solution)/shard_map/gather | solution.py:293
  8.8 0.0 copy-start.3
  8.8 5.0 %all-to-all-start.1 = ((bf16[8,2,64,2048]{3,2,1,0:T(8,128)(2,1)}), bf16[8,2,64,2048]{3,2,1,0:T(8,128)(2,1)}, u32[]{:S(2)}, u32[]{:S(2)}) async-start(bf16[8,2,64,2048]{3,2,1,0:T(8,128)(2,1)} %bitcast.12), calls=%async_computation.1 | async-start | bytes 8388608 | tf_op jit(solution)/shard_map/all_to_all | solution.py:295
  13.9 0.0 copy-done.3
  13.9 0.1 convert_reduce_fusion
  14.1 0.3 fusion.2
  14.3 0.3 fusion.3
  14.6 7.2 %multiply_convert_fusion = bf16[256,4096]{1,0:T(8,128)(2,1)} fusion(bf16[256,1024]{1,0:T(8,128)(2,1)S(1)} %bitcast.15, bf16[1024,4096]{1,0:T(8,128)(2,1)} %param.11), kind=kOutput, calls=%fused_computation.2 | convolution fusion | flops 2152726528 | bytes 11010048 | tf_op jit(solution)/shard_map/dot_general | solution.py:297
  21.9 3.3 %reshape.254 = bf16[2,128,4,1024]{3,2,1,0:T(4,128)(2,1)S(1)} reshape(bf16[256,4096]{1,0:T(8,128)(2,1)} %multiply_convert_fusion) | data formatting | bytes 4194304 | tf_op jit(solution)/shard_map/reshape | solution.py:298
  25.2 0.0 copy-start.1
  25.2 5.1 %gather_fusion = bf16[16,64,2048]{2,1,0:T(8,128)(2,1)} fusion(bf16[8,64,2048]{2,1,0:T(8,128)(2,1)} %get-tuple-element.14, s32[1024]{0:T(1024)S(1)} %pad_clamp_fusion), kind=kCustom, calls=%fused_computation | custom fusion | bytes 8388672 | tf_op jit(solution)/shard_map/gather | solution.py:293
  30.3 0.0 copy-done.1
  30.3 2.0 copy.16
  32.3 0.6 dynamic-slice_add_fusion.picked_ref
  32.9 1.9 slice_bitcast_fusion.rest_0_
  34.8 27.5 %all-to-all-done.1 = bf16[8,2,64,2048]{3,2,1,0:T(8,128)(2,1)} async-done(((bf16[8,2,64,2048]{3,2,1,0:T(8,128)(2,1)}), bf16[8,2,64,2048]{3,2,1,0:T(8,128)(2,1)}, u32[]{:S(2)}, u32[]{:S(2)}) %all-to-all-start.1) | async-done | bytes 4194336 | tf_op jit(solution)/shard_map/all_to_all | solution.py:295
  62.2 4.2 %shard_map.93 = bf16[16,640,128]{2,1,0:T(8,128)(2,1)} custom-call(s32[8]{0:T(128)} %dynamic-slice_add_fusion.picked_ref, bf16[16,64,2048]{2,1,0:T(8,128)(2,1)} %bitcast.5.tiles_hbm, bf16[2,128,1024]{2,1,0:T(8,128)(2,1)} %slice_bitcast_fusion.rest_0_), custom_call_target="tpu_custom_call" | custom-call | tf_op jit(solution)/shard_map/pallas_call | solution.py:187
  66.4 7.9 %all-to-all-start.2 = ((bf16[16,640,128]{2,1,0:T(8,128)(2,1)}), bf16[16,640,128]{2,1,0:T(8,128)(2,1)S(1)}, u32[]{:S(2)}, u32[]{:S(2)}) async-start(bf16[16,640,128]{2,1,0:T(8,128)(2,1)} %shard_map.93), calls=%async_computation.2 | async-start | bytes 5242880 | tf_op jit(solution)/shard_map/all_to_all | solution.py:312
  74.3 47.6 %shard_map.91 = bf16[8,2,64,2048]{3,2,1,0:T(8,128)(2,1)} custom-call(bf16[8,2,64,2048]{3,2,1,0:T(8,128)(2,1)} %bitcast.13), custom_call_target="tpu_custom_call" | custom-call | tf_op jit(solution)/shard_map/pallas_call | solution.py:66
  121.9 0.0 copy-start.8
  121.9 0.0 copy-start.6
  121.9 0.0 copy-start.7
  122.0 3.8 %shard_map.92 = bf16[16,512,128]{2,1,0:T(8,128)(2,1)} custom-call(s32[8]{0:T(128)} %dynamic-slice_add_fusion.picked_ref, bf16[16,64,2048]{2,1,0:T(8,128)(2,1)} %bitcast.14), custom_call_target="tpu_custom_call" | custom-call | tf_op jit(solution)/shard_map/pallas_call | solution.py:187
  125.8 0.0 all-to-all-done.2.kv_ref.qsrc_ref
  125.8 0.0 copy-start
  125.8 7.2 %all-to-all-start = ((bf16[16,512,128]{2,1,0:T(8,128)(2,1)}), bf16[16,512,128]{2,1,0:T(8,128)(2,1)}, u32[]{:S(2)}, u32[]{:S(2)}) async-start(bf16[16,512,128]{2,1,0:T(8,128)(2,1)} %shard_map.92), calls=%async_computation | async-start | bytes 4194304 | tf_op jit(solution)/shard_map/all_to_all | solution.py:317
  133.0 0.0 copy-done.8
  133.0 0.1 dynamic_slice.16
  133.1 0.0 copy-done.6
  133.1 0.0 copy-done.7
  133.1 0.2 select_reduce_fusion.2
  133.3 0.0 copy-start.5
  133.3 0.6 dynamic_slice.17.len_ref
  133.9 0.0 copy-done
  133.9 17.6 %shard_map.94.rest_0_ = f32[2048,128]{1,0:T(8,128)} custom-call(s32[1]{0:T(128)} %dynamic_slice.17.len_ref, bf16[16,640,128]{2,1,0:T(8,128)(2,1)} %copy-done, bf16[16,640,128]{2,1,0:T(8,128)(2,1)} %copy-done), custom_call_target="tpu_custom_call" | custom-call | tf_op jit(solution)/shard_map/pallas_call | solution.py:140
  151.4 0.0 copy-start.2
  151.4 12.3 %all-to-all-done.kv_ref = bf16[16,512,128]{2,1,0:T(8,128)(2,1)} async-done(((bf16[16,512,128]{2,1,0:T(8,128)(2,1)}), bf16[16,512,128]{2,1,0:T(8,128)(2,1)}, u32[]{:S(2)}, u32[]{:S(2)}) %all-to-all-start) | async-done | bytes 2097184 | tf_op jit(solution)/shard_map/all_to_all | solution.py:317
  163.7 17.7 %shard_map.95 = f32[2048,128]{1,0:T(8,128)} custom-call(s32[1]{0:T(128)} %dynamic_slice.17.len_ref, bf16[16,512,128]{2,1,0:T(8,128)(2,1)} %all-to-all-done.kv_ref, bf16[16,640,128]{2,1,0:T(8,128)(2,1)} %copy-done, f32[2048,128]{1,0:T(8,128)} %shard_map.94.rest_0_), custom_call_target="tpu_custom_call" | custom-call | tf_op jit(solution)/shard_map/pallas_call | solution.py:140
  181.4 0.0 copy-done.5
  181.4 2.1 convert_element_type.15
  183.5 6.8 %all-to-all-start.3 = ((bf16[16,128,128]{2,1,0:T(8,128)(2,1)}), bf16[16,128,128]{2,1,0:T(8,128)(2,1)S(1)}, u32[]{:S(2)}, u32[]{:S(2)}) async-start(bf16[16,128,128]{2,1,0:T(8,128)(2,1)} %bitcast.7), calls=%async_computation.3 | async-start | bytes 1048576 | tf_op jit(solution)/shard_map/all_to_all | solution.py:324
  190.2 0.0 copy-done.2
  190.3 2.8 %reshape.261.proj_ref = bf16[2,128,4096]{2,1,0:T(8,128)(2,1)} reshape(bf16[2,128,4,1024]{3,2,1,0:T(4,128)(2,1)S(1)} %copy-done.2) | data formatting | bytes 4194304 | tf_op jit(solution)/shard_map/reshape | solution.py:329
  193.1 0.5 broadcast_subtract_fusion.limit_ref
  193.6 8.5 %all-to-all-done.3.hist_ref = bf16[16,128,128]{2,1,0:T(8,128)(2,1)S(1)} async-done(((bf16[16,128,128]{2,1,0:T(8,128)(2,1)}), bf16[16,128,128]{2,1,0:T(8,128)(2,1)S(1)}, u32[]{:S(2)}, u32[]{:S(2)}) %all-to-all-start.3) | async-done | bytes 524320 | tf_op jit(solution)/shard_map/all_to_all | solution.py:324
  202.1 0.0 copy-start.4
  202.1 0.8 copy-done.4
  202.9 4.9 %shard_map.96 = bf16[2,128,1024]{2,1,0:T(8,128)(2,1)} custom-call(f32[8]{0:T(128)} %bias_ref.1, s32[2]{0:T(128)} %copy-done.5, s32[2]{0:T(128)} %broadcast_subtract_fusion.limit_ref, bf16[16,128,128]{2,1,0:T(8,128)(2,1)} %copy-done.4, bf16[2,128,4096]{2,1,0:T(8,128)(2,1)} %reshape.261.proj_ref, bf16[2,128,1024]{2,1,0:T(8,128)(2,1)} %x_ref.1, ...), custom_call_target="tpu_custom_call" | custom-call | tf_op jit(solution)/shard_map/pallas_call | solution.py:229
  (9 shorter events, 0.1 us)
Async XLA Ops:
  8.8 5.1 %copy-start.3 = (bf16[2,128,1024]{2,1,0:T(8,128)(2,1)S(1)}, bf16[2,128,1024]{2,1,0:T(8,128)(2,1)}, u32[]{:S(2)}) copy-start(bf16[2,128,1024]{2,1,0:T(8,128)(2,1)} %x_ref.1) | copy-start | bytes 1572868
  8.8 53.4 %all-to-all-start.1 = ((bf16[8,2,64,2048]{3,2,1,0:T(8,128)(2,1)}), bf16[8,2,64,2048]{3,2,1,0:T(8,128)(2,1)}, u32[]{:S(2)}, u32[]{:S(2)}) async-start(bf16[8,2,64,2048]{3,2,1,0:T(8,128)(2,1)} %bitcast.12), calls=%async_computation.1 | async-start | bytes 8388608 | tf_op jit(solution)/shard_map/all_to_all | solution.py:295
  25.2 5.2 %copy-start.1 = (bf16[2,128,4,1024]{3,2,1,0:T(4,128)(2,1)}, bf16[2,128,4,1024]{3,2,1,0:T(4,128)(2,1)S(1)}, u32[]{:S(2)}) copy-start(bf16[2,128,4,1024]{3,2,1,0:T(4,128)(2,1)S(1)} %reshape.254) | copy-start | bytes 6291460
  66.4 59.3 %all-to-all-start.2 = ((bf16[16,640,128]{2,1,0:T(8,128)(2,1)}), bf16[16,640,128]{2,1,0:T(8,128)(2,1)S(1)}, u32[]{:S(2)}, u32[]{:S(2)}) async-start(bf16[16,640,128]{2,1,0:T(8,128)(2,1)} %shard_map.93), calls=%async_computation.2 | async-start | bytes 5242880 | tf_op jit(solution)/shard_map/all_to_all | solution.py:312
  121.9 11.1 %copy-start.8 = (s32[16]{0:T(128)S(1)}, s32[16]{0:T(128)}, u32[]{:S(2)}) copy-start(s32[16]{0:T(128)} %param.14) | copy-start | bytes 196
  121.9 11.2 %copy-start.6 = (s32[16]{0:T(128)S(1)}, s32[16]{0:T(128)}, u32[]{:S(2)}) copy-start(s32[16]{0:T(128)} %param.16) | copy-start | bytes 196
  121.9 11.2 %copy-start.7 = (s32[16]{0:T(128)S(1)}, s32[16]{0:T(128)}, u32[]{:S(2)}) copy-start(s32[16]{0:T(128)} %param.15) | copy-start | bytes 196
  125.8 8.1 %copy-start = (bf16[16,640,128]{2,1,0:T(8,128)(2,1)}, bf16[16,640,128]{2,1,0:T(8,128)(2,1)S(1)}, u32[]{:S(2)}) copy-start(bf16[16,640,128]{2,1,0:T(8,128)(2,1)S(1)} %all-to-all-done.2.kv_ref.qsrc_ref) | copy-start | bytes 7864324
  125.8 37.9 %all-to-all-start = ((bf16[16,512,128]{2,1,0:T(8,128)(2,1)}), bf16[16,512,128]{2,1,0:T(8,128)(2,1)}, u32[]{:S(2)}, u32[]{:S(2)}) async-start(bf16[16,512,128]{2,1,0:T(8,128)(2,1)} %shard_map.92), calls=%async_computation | async-start | bytes 4194304 | tf_op jit(solution)/shard_map/all_to_all | solution.py:317
  133.3 48.1 %copy-start.5 = (s32[2]{0:T(128)}, s32[2]{0:T(128)S(1)}, u32[]{:S(2)}) copy-start(s32[2]{0:T(128)S(1)} %get-tuple-element.10.len_ref) | copy-start | bytes 28
  151.4 38.8 %copy-start.2 = (bf16[2,128,4,1024]{3,2,1,0:T(4,128)(2,1)S(1)}, bf16[2,128,4,1024]{3,2,1,0:T(4,128)(2,1)}, u32[]{:S(2)}) copy-start(bf16[2,128,4,1024]{3,2,1,0:T(4,128)(2,1)} %copy-done.1) | copy-start | bytes 6291460
  183.5 18.6 %all-to-all-start.3 = ((bf16[16,128,128]{2,1,0:T(8,128)(2,1)}), bf16[16,128,128]{2,1,0:T(8,128)(2,1)S(1)}, u32[]{:S(2)}, u32[]{:S(2)}) async-start(bf16[16,128,128]{2,1,0:T(8,128)(2,1)} %bitcast.7), calls=%async_computation.3 | async-start | bytes 1048576 | tf_op jit(solution)/shard_map/all_to_all | solution.py:324
  202.1 0.8 copy-start.4

commit v17 on v12

--- a/solution.py
+++ b/solution.py
@@ -277,12 +277,13 @@
     my_owner = lax.dynamic_slice_in_dim(owners, first_entry, users_here * per_hist)
     my_place = lax.dynamic_slice_in_dim(places, first_entry, users_here * per_hist)
     picked_slot = (my_owner * capacity + my_place).astype(jnp.int32)
-    sub = tile_len // 2
+    first_len = tile_len * 5 // 8
+    bounds = [(0, first_len), (first_len, tile_len)]
     sending = []
-    for half in range(2):
-        kv_half = lax.slice_in_dim(kv_cache, half * sub, (half + 1) * sub, axis=1)
+    for lo, hi in bounds:
+        kv_half = lax.slice_in_dim(kv_cache, lo, hi, axis=1)
         outgoing = kv_half.at[source_slot].get(mode="promise_in_bounds")
-        sending.append(outgoing.reshape(req_count, capacity, sub, 2 * width))
+        sending.append(outgoing.reshape(req_count, capacity, hi - lo, 2 * width))
     first_in = lax.all_to_all(sending[0], "req", split_axis=0, concat_axis=0, tiled=True)
     normed = layer_norm(cand_x.astype(jnp.float32)).astype(jnp.bfloat16)
     mixed_in = jnp.dot(normed.reshape(-1, width), w_uvqk, preferred_element_type=jnp.float32)
@@ -290,8 +291,8 @@
     projected, second_out = lax.optimization_barrier((projected, sending[1]))
     second_in = req_a2a(second_out, 0)
     halves = [
-        first_in.reshape(req_count * capacity, sub, 2 * width),
-        second_in.reshape(req_count * capacity, sub, 2 * width),
+        first_in.reshape(req_count * capacity, first_len, 2 * width),
+        second_in.reshape(req_count * capacity, tile_len - first_len, 2 * width),
     ]
     u_gate = projected[:, :, 0]
     v_self = projected[:, :, 1]
@@ -299,18 +300,19 @@
     k_self = projected[:, :, 3]
     my_user = hist_index // heads
     my_length = lax.dynamic_slice_in_dim(lengths, my_user, 1)
-    q_row = 2 * per_hist * sub
+    q_row = 2 * per_hist * first_len
     packed_a = lax.all_to_all(
         pack_for_heads(picked_slot, halves[0], queries, users_here, heads),
         "hist", split_axis=0, concat_axis=0, tiled=True,
     )
-    history_mine = attend(my_length, packed_a, packed_a, q_row, per_hist, sub, tile_len, 0, score_scale)
+    history_mine = attend(my_length, packed_a, packed_a, q_row, per_hist, first_len, tile_len, 0, score_scale)
     packed_b = lax.all_to_all(
         pack_for_heads(picked_slot, halves[1], None, users_here, heads),
         "hist", split_axis=0, concat_axis=0, tiled=True,
     )
     history_mine = attend(
-        my_length, packed_b, packed_a, q_row, per_hist, sub, tile_len, sub, score_scale, init=history_mine
+        my_length, packed_b, packed_a, q_row, per_hist, tile_len - first_len, tile_len, first_len, score_scale,
+        init=history_mine,
     ).astype(jnp.bfloat16)
     history_back = lax.all_to_all(
         history_mine.reshape(hist_count, cand_rows, head_dim), "hist", split_axis=0, concat_axis=0, tiled=True

time: 208 us -> 202 us (0.971)
  the two profiles are of different devices: /device:TPU:8 before, /device:TPU:0 now
where the time goes in v17:
time: 202 us
  Pallas kernels  71.7 us (35%)
  waiting for transfers between devices  63.9 us (32%)
  starting transfers between devices  33.7 us (17%)
  local copies, waits for them, and re-layouts  20.4 us (10%)
  matrix products  7.16 us (4%)
  other arithmetic  4.41 us (2%)
    all_to_all x1, waiting for transfers between devices, local(): lax.all_to_all(sending[0], 'req', split_axis=0, concat_axis=0, tiled=True)  41.3 us
    pallas_call x1, Pallas kernels, req_a2a(): pl.pallas_call(functools.partial(req_a2a_kernel, axis='req', other_axis='...  36 us
    pallas_call x2, Pallas kernels, attend(): pl.pallas_call(kernel, out_shape=jax.ShapeDtypeStruct((rows, head_dim), j...  22.9 us
    all_to_all x1, starting transfers between devices, local(): lax.all_to_all(history_mine.reshape(hist_count, cand_rows, head_dim), 'hi...  15.1 us
    all_to_all x1, waiting for transfers between devices, local(): lax.all_to_all(pack_for_heads(picked_slot, halves[1], None, users_here, h...  11 us
    all_to_all x1, waiting for transfers between devices, local(): lax.all_to_all(history_mine.reshape(hist_count, cand_rows, head_dim), 'hi...  8.44 us
    pallas_call x2, Pallas kernels, pack_for_heads(): pl.pallas_call(functools.partial(pack_kernel, heads=heads, users=users, p...  7.99 us
    all_to_all x1, starting transfers between devices, local(): lax.all_to_all(pack_for_heads(picked_slot, halves[0], queries, users_here...  7.97 us
  transfers between devices with their start and end apart: 4, of which 4 were waited for; matrix products, arithmetic and copies ran while one was open for 11% of the time, Pallas kernels for 26%

profile of v17, /device:TPU:0, one launch (start us, length us, event | category | flops | bytes accessed | tf_op | source)
XLA Modules:
  0.0 201.6 jit_solution(17549843976463084326)
XLA Ops:
  0.0 0.0 slice-start
  0.0 0.1 broadcast_in_dim.63
  0.1 0.1 eq.98
  0.2 0.9 reshape.251
  1.1 0.4 dynamic-slice_reduce_fusion
  1.5 0.1 reshape.252
  1.6 0.2 select_reduce_fusion
  1.9 0.1 select_reduce_fusion.1
  2.0 0.1 copy.15
  2.1 0.1 reshape.255
  2.2 0.0 slice-done
  2.2 3.2 %gather_fusion.1 = bf16[16,80,2048]{2,1,0:T(8,128)(2,1)} fusion(bf16[8,80,2048]{2,1,0:T(8,128)(2,1)S(1)} %slice-done, s32[1024]{0:T(1024)S(1)} %pad_clamp_fusion), kind=kCustom, calls=%fused_computation.1 | custom fusion | bytes 10485824 | tf_op jit(solution)/shard_map/gather | solution.py:285
  5.4 4.6 %all-to-all-start.1 = ((bf16[8,2,80,2048]{3,2,1,0:T(8,128)(2,1)}), bf16[8,2,80,2048]{3,2,1,0:T(8,128)(2,1)}, u32[]{:S(2)}, u32[]{:S(2)}) async-start(bf16[8,2,80,2048]{3,2,1,0:T(8,128)(2,1)} %bitcast.12), calls=%async_computation.1 | async-start | bytes 10485760 | tf_op jit(solution)/shard_map/all_to_all | solution.py:287
  10.1 0.0 copy-start.2
  10.1 1.0 copy-done.2
  11.1 0.1 convert_reduce_fusion
  11.3 0.3 fusion.2
  11.6 0.3 fusion.3
  11.8 7.2 %multiply_convert_fusion = bf16[256,4096]{1,0:T(8,128)(2,1)} fusion(bf16[256,1024]{1,0:T(8,128)(2,1)S(1)} %bitcast.15, bf16[1024,4096]{1,0:T(8,128)(2,1)} %param.11), kind=kOutput, calls=%fused_computation.2 | convolution fusion | flops 2152726528 | bytes 11010048 | tf_op jit(solution)/shard_map/dot_general | solution.py:289
  19.0 0.0 slice-start.1
  19.0 4.6 %reshape.254 = bf16[2,128,4,1024]{3,2,1,0:T(4,128)(2,1)} reshape(bf16[256,4096]{1,0:T(8,128)(2,1)} %multiply_convert_fusion) | data formatting | bytes 4194304 | tf_op jit(solution)/shard_map/reshape | solution.py:290
  23.6 0.0 slice-done.1
  23.6 2.5 %gather_fusion = bf16[16,48,2048]{2,1,0:T(8,128)(2,1)} fusion(bf16[8,48,2048]{2,1,0:T(8,128)(2,1)S(1)} %slice-done.1, s32[1024]{0:T(1024)S(1)} %pad_clamp_fusion), kind=kCustom, calls=%fused_computation | custom fusion | bytes 6291520 | tf_op jit(solution)/shard_map/gather | solution.py:285
  26.1 2.2 %copy.16 = bf16[2,128,4,1024]{3,1,0,2:T(8,128)(2,1)S(1)} copy(bf16[2,128,4,1024]{3,2,1,0:T(4,128)(2,1)} %reshape.254) | data formatting | bytes 4194304 | tf_op jit(solution)/shard_map/optimization_barrier | solution.py:291
  28.3 0.6 dynamic-slice_add_fusion.picked_ref
  28.9 0.8 slice_bitcast_fusion.rest_0_
  29.7 41.3 %all-to-all-done.1 = bf16[8,2,80,2048]{3,2,1,0:T(8,128)(2,1)} async-done(((bf16[8,2,80,2048]{3,2,1,0:T(8,128)(2,1)}), bf16[8,2,80,2048]{3,2,1,0:T(8,128)(2,1)}, u32[]{:S(2)}, u32[]{:S(2)}) %all-to-all-start.1) | async-done | bytes 5242912 | tf_op jit(solution)/shard_map/all_to_all | solution.py:287
  71.0 4.5 %shard_map.93 = bf16[16,768,128]{2,1,0:T(8,128)(2,1)} custom-call(s32[8]{0:T(128)} %dynamic-slice_add_fusion.picked_ref, bf16[16,80,2048]{2,1,0:T(8,128)(2,1)} %bitcast.5.tiles_hbm, bf16[2,128,1024]{2,1,0:T(8,128)(2,1)} %slice_bitcast_fusion.rest_0_), custom_call_target="tpu_custom_call" | custom-call | tf_op jit(solution)/shard_map/pallas_call | solution.py:187
  75.5 8.0 %all-to-all-start.2 = ((bf16[16,768,128]{2,1,0:T(8,128)(2,1)}), bf16[16,768,128]{2,1,0:T(8,128)(2,1)S(1)}, u32[]{:S(2)}, u32[]{:S(2)}) async-start(bf16[16,768,128]{2,1,0:T(8,128)(2,1)} %shard_map.93), calls=%async_computation.2 | async-start | bytes 6291456 | tf_op jit(solution)/shard_map/all_to_all | solution.py:304
  83.5 36.0 %shard_map.91 = bf16[8,2,48,2048]{3,2,1,0:T(8,128)(2,1)} custom-call(bf16[8,2,48,2048]{3,2,1,0:T(8,128)(2,1)} %bitcast.13), custom_call_target="tpu_custom_call" | custom-call | tf_op jit(solution)/shard_map/pallas_call | solution.py:66
  119.5 0.0 copy-start.7
  119.5 0.0 copy-start.5
  119.5 0.0 copy-start.6
  119.5 3.5 %shard_map.92 = bf16[16,384,128]{2,1,0:T(8,128)(2,1)} custom-call(s32[8]{0:T(128)} %dynamic-slice_add_fusion.picked_ref, bf16[16,48,2048]{2,1,0:T(8,128)(2,1)} %bitcast.14), custom_call_target="tpu_custom_call" | custom-call | tf_op jit(solution)/shard_map/pallas_call | solution.py:187
  123.0 3.2 %all-to-all-done.2.kv_ref.qsrc_ref = bf16[16,768,128]{2,1,0:T(8,128)(2,1)S(1)} async-done(((bf16[16,768,128]{2,1,0:T(8,128)(2,1)}), bf16[16,768,128]{2,1,0:T(8,128)(2,1)S(1)}, u32[]{:S(2)}, u32[]{:S(2)}) %all-to-all-start.2) | async-done | bytes 3145760 | tf_op jit(solution)/shard_map/all_to_all | solution.py:304
  126.2 0.0 copy-start
  126.2 6.0 %all-to-all-start = ((bf16[16,384,128]{2,1,0:T(8,128)(2,1)}), bf16[16,384,128]{2,1,0:T(8,128)(2,1)}, u32[]{:S(2)}, u32[]{:S(2)}) async-start(bf16[16,384,128]{2,1,0:T(8,128)(2,1)} %shard_map.92), calls=%async_computation | async-start | bytes 3145728 | tf_op jit(solution)/shard_map/all_to_all | solution.py:309
  132.2 0.0 copy-done.7
  132.2 0.1 dynamic_slice.16
  132.3 0.0 copy-done.5
  132.3 0.0 copy-done.6
  132.3 0.2 select_reduce_fusion.2
  132.5 0.0 copy-start.4
  132.5 0.6 dynamic_slice.17.len_ref
  133.1 0.0 copy-done
  133.1 13.2 %shard_map.94.rest_0_ = f32[2048,128]{1,0:T(8,128)} custom-call(s32[1]{0:T(128)} %dynamic_slice.17.len_ref, bf16[16,768,128]{2,1,0:T(8,128)(2,1)} %copy-done, bf16[16,768,128]{2,1,0:T(8,128)(2,1)} %copy-done), custom_call_target="tpu_custom_call" | custom-call | tf_op jit(solution)/shard_map/pallas_call | solution.py:140
  146.3 0.0 copy-done.4
  146.3 0.0 copy-start.1
  146.3 11.0 %all-to-all-done.kv_ref = bf16[16,384,128]{2,1,0:T(8,128)(2,1)} async-done(((bf16[16,384,128]{2,1,0:T(8,128)(2,1)}), bf16[16,384,128]{2,1,0:T(8,128)(2,1)}, u32[]{:S(2)}, u32[]{:S(2)}) %all-to-all-start) | async-done | bytes 1572896 | tf_op jit(solution)/shard_map/all_to_all | solution.py:309
  157.3 9.7 %shard_map.95 = f32[2048,128]{1,0:T(8,128)} custom-call(s32[1]{0:T(128)} %dynamic_slice.17.len_ref, bf16[16,384,128]{2,1,0:T(8,128)(2,1)} %all-to-all-done.kv_ref, bf16[16,768,128]{2,1,0:T(8,128)(2,1)} %copy-done, f32[2048,128]{1,0:T(8,128)} %shard_map.94.rest_0_), custom_call_target="tpu_custom_call" | custom-call | tf_op jit(solution)/shard_map/pallas_call | solution.py:140
  167.0 2.1 %convert_element_type.15 = bf16[2048,128]{1,0:T(8,128)(2,1)} convert(f32[2048,128]{1,0:T(8,128)} %shard_map.95) | non-fusion elementwise | flops 262144 | bytes 1572864 | tf_op jit(solution)/shard_map/convert_element_type | solution.py:316
  169.1 15.1 %all-to-all-start.3 = ((bf16[16,128,128]{2,1,0:T(8,128)(2,1)}), bf16[16,128,128]{2,1,0:T(8,128)(2,1)S(1)}, u32[]{:S(2)}, u32[]{:S(2)}) async-start(bf16[16,128,128]{2,1,0:T(8,128)(2,1)} %bitcast.7), calls=%async_computation.3 | async-start | bytes 1048576 | tf_op jit(solution)/shard_map/all_to_all | solution.py:317
  184.2 0.0 copy-done.1
  184.2 2.8 %reshape.261.proj_ref = bf16[2,128,4096]{2,1,0:T(8,128)(2,1)} reshape(bf16[2,128,4,1024]{3,2,1,0:T(4,128)(2,1)S(1)} %copy-done.1) | data formatting | bytes 4194304 | tf_op jit(solution)/shard_map/reshape | solution.py:322
  187.0 0.5 broadcast_subtract_fusion.limit_ref
  187.5 8.4 %all-to-all-done.3.hist_ref = bf16[16,128,128]{2,1,0:T(8,128)(2,1)S(1)} async-done(((bf16[16,128,128]{2,1,0:T(8,128)(2,1)}), bf16[16,128,128]{2,1,0:T(8,128)(2,1)S(1)}, u32[]{:S(2)}, u32[]{:S(2)}) %all-to-all-start.3) | async-done | bytes 524320 | tf_op jit(solution)/shard_map/all_to_all | solution.py:317
  196.0 0.0 copy-start.3
  196.0 0.8 copy-done.3
  196.8 4.8 %shard_map.96 = bf16[2,128,1024]{2,1,0:T(8,128)(2,1)} custom-call(f32[8]{0:T(128)} %bias_ref.1, s32[2]{0:T(128)} %copy-done.4, s32[2]{0:T(128)} %broadcast_subtract_fusion.limit_ref, bf16[16,128,128]{2,1,0:T(8,128)(2,1)} %copy-done.3, bf16[2,128,4096]{2,1,0:T(8,128)(2,1)} %reshape.261.proj_ref, bf16[2,128,1024]{2,1,0:T(8,128)(2,1)} %x_ref.1, ...), custom_call_target="tpu_custom_call" | custom-call | tf_op jit(solution)/shard_map/pallas_call | solution.py:229
  (9 shorter events, 0.1 us)
Async XLA Ops:
  0.0 2.2 %slice-start = ((bf16[8,128,2048]{2,1,0:T(8,128)(2,1)}), bf16[8,80,2048]{2,1,0:T(8,128)(2,1)S(1)}, s32[]{:S(2)}) async-start(bf16[8,128,2048]{2,1,0:T(8,128)(2,1)} %param.10), calls=%async_computation.4 | async-start | bytes 5242880 | tf_op jit(solution)/shard_map/slice | solution.py:284
  5.4 65.6 %all-to-all-start.1 = ((bf16[8,2,80,2048]{3,2,1,0:T(8,128)(2,1)}), bf16[8,2,80,2048]{3,2,1,0:T(8,128)(2,1)}, u32[]{:S(2)}, u32[]{:S(2)}) async-start(bf16[8,2,80,2048]{3,2,1,0:T(8,128)(2,1)} %bitcast.12), calls=%async_computation.1 | async-start | bytes 10485760 | tf_op jit(solution)/shard_map/all_to_all | solution.py:287
  10.1 1.0 copy-start.2
  19.0 4.6 %slice-start.1 = ((bf16[8,128,2048]{2,1,0:T(8,128)(2,1)}), bf16[8,48,2048]{2,1,0:T(8,128)(2,1)S(1)}, s32[]{:S(2)}) async-start(bf16[8,128,2048]{2,1,0:T(8,128)(2,1)} %param.10), calls=%async_computation.5 | async-start | bytes 3145728 | tf_op jit(solution)/shard_map/slice | solution.py:284
  75.5 50.7 %all-to-all-start.2 = ((bf16[16,768,128]{2,1,0:T(8,128)(2,1)}), bf16[16,768,128]{2,1,0:T(8,128)(2,1)S(1)}, u32[]{:S(2)}, u32[]{:S(2)}) async-start(bf16[16,768,128]{2,1,0:T(8,128)(2,1)} %shard_map.93), calls=%async_computation.2 | async-start | bytes 6291456 | tf_op jit(solution)/shard_map/all_to_all | solution.py:304
  119.5 12.8 %copy-start.7 = (s32[16]{0:T(128)S(1)}, s32[16]{0:T(128)}, u32[]{:S(2)}) copy-start(s32[16]{0:T(128)} %param.14) | copy-start | bytes 196
  119.5 12.9 %copy-start.5 = (s32[16]{0:T(128)S(1)}, s32[16]{0:T(128)}, u32[]{:S(2)}) copy-start(s32[16]{0:T(128)} %param.16) | copy-start | bytes 196
  119.5 12.8 %copy-start.6 = (s32[16]{0:T(128)S(1)}, s32[16]{0:T(128)}, u32[]{:S(2)}) copy-start(s32[16]{0:T(128)} %param.15) | copy-start | bytes 196
  126.2 6.9 %copy-start = (bf16[16,768,128]{2,1,0:T(8,128)(2,1)}, bf16[16,768,128]{2,1,0:T(8,128)(2,1)S(1)}, u32[]{:S(2)}) copy-start(bf16[16,768,128]{2,1,0:T(8,128)(2,1)S(1)} %all-to-all-done.2.kv_ref.qsrc_ref) | copy-start | bytes 9437188
  126.2 31.0 %all-to-all-start = ((bf16[16,384,128]{2,1,0:T(8,128)(2,1)}), bf16[16,384,128]{2,1,0:T(8,128)(2,1)}, u32[]{:S(2)}, u32[]{:S(2)}) async-start(bf16[16,384,128]{2,1,0:T(8,128)(2,1)} %shard_map.92), calls=%async_computation | async-start | bytes 3145728 | tf_op jit(solution)/shard_map/all_to_all | solution.py:309
  132.5 13.8 %copy-start.4 = (s32[2]{0:T(128)}, s32[2]{0:T(128)S(1)}, u32[]{:S(2)}) copy-start(s32[2]{0:T(128)S(1)} %get-tuple-element.10.len_ref) | copy-start | bytes 28
  146.3 37.9 %copy-start.1 = (bf16[2,128,4,1024]{3,2,1,0:T(4,128)(2,1)S(1)}, bf16[2,128,4,1024]{3,2,1,0:T(4,128)(2,1)}, u32[]{:S(2)}) copy-start(bf16[2,128,4,1024]{3,2,1,0:T(4,128)(2,1)} %reshape.254) | copy-start | bytes 6291460
  169.1 26.9 %all-to-all-start.3 = ((bf16[16,128,128]{2,1,0:T(8,128)(2,1)}), bf16[16,128,128]{2,1,0:T(8,128)(2,1)S(1)}, u32[]{:S(2)}, u32[]{:S(2)}) async-start(bf16[16,128,128]{2,1,0:T(8,128)(2,1)} %bitcast.7), calls=%async_computation.3 | async-start | bytes 1048576 | tf_op jit(solution)/shard_map/all_to_all | solution.py:317
  196.0 0.8 copy-start.3

commit v18 on v17

--- a/solution.py
+++ b/solution.py
@@ -95,14 +95,19 @@
     else:
         o_ref[...] = init_ref[...]
 
-    def one_class(c, carry):
-        key_index = lax.broadcasted_iota(jnp.int32, (1, span), 1)
-        position = (c + n_cls * (key_index // sub)) * tile_len + offset + key_index % sub
+    group = 1 if span % 128 == 0 else 2
+
+    def one_class(g, carry):
+        c = g * group
+        key_index = lax.broadcasted_iota(jnp.int32, (1, group * span), 1)
+        cls = c + key_index // span
+        within = key_index % span
+        position = (cls + n_cls * (within // sub)) * tile_len + offset + within % sub
         live = position < length
 
         def add_class(masked):
-            keys = kv_ref[c, pl.ds(0, span), :]
-            values = kv_ref[c, pl.ds(span, span), :]
+            keys = jnp.concatenate([kv_ref[c + j, pl.ds(0, span), :] for j in range(group)], axis=0)
+            values = jnp.concatenate([kv_ref[c + j, pl.ds(span, span), :] for j in range(group)], axis=0)
             for ci in range(q_ref.shape[0] // chunk):
                 rows = pl.ds(ci * chunk, chunk)
                 scores = lax.dot_general(
@@ -114,13 +119,13 @@
                     weights = jnp.where(live, weights, 0.0)
                 o_ref[rows, :] += jnp.dot(weights.astype(jnp.bfloat16), values, preferred_element_type=jnp.float32)
 
-        last_key = (c + n_cls * (n_tiles - 1)) * tile_len + offset + sub
+        last_key = (c + group - 1 + n_cls * (n_tiles - 1)) * tile_len + offset + sub
         whole = last_key <= length
         pl.when(whole)(lambda: add_class(False))
         pl.when(jnp.logical_and(jnp.logical_not(whole), c * tile_len + offset < length))(lambda: add_class(True))
         return carry
 
-    lax.fori_loop(0, n_cls, one_class, 0)
+    lax.fori_loop(0, n_cls // group, one_class, 0)
 
 
 def attend(length, kv_packed, q_packed, q_row, n_tiles, sub, tile_len, offset, score_scale, init=None):

time: 202 us -> 193 us (0.955)
  the two profiles are of different devices: /device:TPU:0 before, /device:TPU:8 now
where the time goes in v18:
time: 193 us; the launch traced here: 191 us
  Pallas kernels  81.8 us (42%)
  waiting for transfers between devices  54.5 us (28%)
  starting transfers between devices  22.4 us (12%)
  local copies, waits for them, and re-layouts  20.4 us (11%)
  matrix products  7.16 us (4%)
  other arithmetic  4.41 us (2%)
    all_to_all x1, waiting for transfers between devices, local(): lax.all_to_all(sending[0], 'req', split_axis=0, concat_axis=0, tiled=True)  39.9 us
    pallas_call x1, Pallas kernels, req_a2a(): pl.pallas_call(functools.partial(req_a2a_kernel, axis='req', other_axis='...  36.3 us
    pallas_call x2, Pallas kernels, attend(): pl.pallas_call(kernel, out_shape=jax.ShapeDtypeStruct((rows, head_dim), j...  32.6 us
    pallas_call x2, Pallas kernels, pack_for_heads(): pl.pallas_call(functools.partial(pack_kernel, heads=heads, users=users, p...  7.99 us
    all_to_all x1, starting transfers between devices, local(): lax.all_to_all(pack_for_heads(picked_slot, halves[0], queries, users_here...  7.97 us
    dot_general x1, matrix products, local(): jnp.dot(normed.reshape(-1, width), w_uvqk, preferred_element_type=jnp.flo...  7.16 us
    all_to_all x1, waiting for transfers between devices, local(): lax.all_to_all(history_mine.reshape(hist_count, cand_rows, head_dim), 'hi...  6.76 us
    all_to_all x1, starting transfers between devices, local(): lax.all_to_all(pack_for_heads(picked_slot, halves[1], None, users_here, h...  5.97 us
  transfers between devices with their start and end apart: 4, of which 4 were waited for; matrix products, arithmetic and copies ran while one was open for 12% of the time, Pallas kernels for 31%

profile of v18, /device:TPU:8, one launch (start us, length us, event | category | flops | bytes accessed | tf_op | source)
XLA Modules:
  0.0 190.9 jit_solution(1865873909002870833)
XLA Ops:
  0.0 0.0 slice-start
  0.0 0.1 broadcast_in_dim.63
  0.1 0.1 eq.98
  0.2 0.9 reshape.251
  1.1 0.4 dynamic-slice_reduce_fusion
  1.5 0.1 reshape.252
  1.6 0.2 select_reduce_fusion
  1.9 0.1 select_reduce_fusion.1
  2.0 0.1 copy.15
  2.1 0.1 reshape.255
  2.2 0.0 slice-done
  2.2 3.2 %gather_fusion.1 = bf16[16,80,2048]{2,1,0:T(8,128)(2,1)} fusion(bf16[8,80,2048]{2,1,0:T(8,128)(2,1)S(1)} %slice-done, s32[1024]{0:T(1024)S(1)} %pad_clamp_fusion), kind=kCustom, calls=%fused_computation.1 | custom fusion | bytes 10485824 | tf_op jit(solution)/shard_map/gather | solution.py:290
  5.4 4.9 %all-to-all-start.1 = ((bf16[8,2,80,2048]{3,2,1,0:T(8,128)(2,1)}), bf16[8,2,80,2048]{3,2,1,0:T(8,128)(2,1)}, u32[]{:S(2)}, u32[]{:S(2)}) async-start(bf16[8,2,80,2048]{3,2,1,0:T(8,128)(2,1)} %bitcast.12), calls=%async_computation.1 | async-start | bytes 10485760 | tf_op jit(solution)/shard_map/all_to_all | solution.py:292
  10.3 0.0 copy-start.2
  10.3 1.0 copy-done.2
  11.4 0.1 convert_reduce_fusion
  11.5 0.3 fusion.2
  11.8 0.3 fusion.3
  12.1 7.2 %multiply_convert_fusion = bf16[256,4096]{1,0:T(8,128)(2,1)} fusion(bf16[256,1024]{1,0:T(8,128)(2,1)S(1)} %bitcast.15, bf16[1024,4096]{1,0:T(8,128)(2,1)} %param.11), kind=kOutput, calls=%fused_computation.2 | convolution fusion | flops 2152726528 | bytes 11010048 | tf_op jit(solution)/shard_map/dot_general | solution.py:294
  19.3 0.0 slice-start.1
  19.3 4.6 %reshape.254 = bf16[2,128,4,1024]{3,2,1,0:T(4,128)(2,1)} reshape(bf16[256,4096]{1,0:T(8,128)(2,1)} %multiply_convert_fusion) | data formatting | bytes 4194304 | tf_op jit(solution)/shard_map/reshape | solution.py:295
  23.9 0.0 slice-done.1
  23.9 2.5 %gather_fusion = bf16[16,48,2048]{2,1,0:T(8,128)(2,1)} fusion(bf16[8,48,2048]{2,1,0:T(8,128)(2,1)S(1)} %slice-done.1, s32[1024]{0:T(1024)S(1)} %pad_clamp_fusion), kind=kCustom, calls=%fused_computation | custom fusion | bytes 6291520 | tf_op jit(solution)/shard_map/gather | solution.py:290
  26.4 2.2 %copy.16 = bf16[2,128,4,1024]{3,1,0,2:T(8,128)(2,1)S(1)} copy(bf16[2,128,4,1024]{3,2,1,0:T(4,128)(2,1)} %reshape.254) | data formatting | bytes 4194304 | tf_op jit(solution)/shard_map/optimization_barrier | solution.py:296
  28.6 0.6 dynamic-slice_add_fusion.picked_ref
  29.2 0.8 slice_bitcast_fusion.rest_0_
  30.0 39.9 %all-to-all-done.1 = bf16[8,2,80,2048]{3,2,1,0:T(8,128)(2,1)} async-done(((bf16[8,2,80,2048]{3,2,1,0:T(8,128)(2,1)}), bf16[8,2,80,2048]{3,2,1,0:T(8,128)(2,1)}, u32[]{:S(2)}, u32[]{:S(2)}) %all-to-all-start.1) | async-done | bytes 5242912 | tf_op jit(solution)/shard_map/all_to_all | solution.py:292
  69.9 4.5 %shard_map.93 = bf16[16,768,128]{2,1,0:T(8,128)(2,1)} custom-call(s32[8]{0:T(128)} %dynamic-slice_add_fusion.picked_ref, bf16[16,80,2048]{2,1,0:T(8,128)(2,1)} %bitcast.5.tiles_hbm, bf16[2,128,1024]{2,1,0:T(8,128)(2,1)} %slice_bitcast_fusion.rest_0_), custom_call_target="tpu_custom_call" | custom-call | tf_op jit(solution)/shard_map/pallas_call | solution.py:192
  74.4 8.0 %all-to-all-start.2 = ((bf16[16,768,128]{2,1,0:T(8,128)(2,1)}), bf16[16,768,128]{2,1,0:T(8,128)(2,1)S(1)}, u32[]{:S(2)}, u32[]{:S(2)}) async-start(bf16[16,768,128]{2,1,0:T(8,128)(2,1)} %shard_map.93), calls=%async_computation.2 | async-start | bytes 6291456 | tf_op jit(solution)/shard_map/all_to_all | solution.py:309
  82.4 36.3 %shard_map.91 = bf16[8,2,48,2048]{3,2,1,0:T(8,128)(2,1)} custom-call(bf16[8,2,48,2048]{3,2,1,0:T(8,128)(2,1)} %bitcast.13), custom_call_target="tpu_custom_call" | custom-call | tf_op jit(solution)/shard_map/pallas_call | solution.py:66
  118.7 0.0 copy-start.7
  118.7 0.0 copy-start.5
  118.8 0.0 copy-start.6
  118.8 3.5 %shard_map.92 = bf16[16,384,128]{2,1,0:T(8,128)(2,1)} custom-call(s32[8]{0:T(128)} %dynamic-slice_add_fusion.picked_ref, bf16[16,48,2048]{2,1,0:T(8,128)(2,1)} %bitcast.14), custom_call_target="tpu_custom_call" | custom-call | tf_op jit(solution)/shard_map/pallas_call | solution.py:192
  122.3 2.9 %all-to-all-done.2.kv_ref.qsrc_ref = bf16[16,768,128]{2,1,0:T(8,128)(2,1)S(1)} async-done(((bf16[16,768,128]{2,1,0:T(8,128)(2,1)}), bf16[16,768,128]{2,1,0:T(8,128)(2,1)S(1)}, u32[]{:S(2)}, u32[]{:S(2)}) %all-to-all-start.2) | async-done | bytes 3145760 | tf_op jit(solution)/shard_map/all_to_all | solution.py:309
  125.2 0.0 copy-start
  125.2 6.0 %all-to-all-start = ((bf16[16,384,128]{2,1,0:T(8,128)(2,1)}), bf16[16,384,128]{2,1,0:T(8,128)(2,1)}, u32[]{:S(2)}, u32[]{:S(2)}) async-start(bf16[16,384,128]{2,1,0:T(8,128)(2,1)} %shard_map.92), calls=%async_computation | async-start | bytes 3145728 | tf_op jit(solution)/shard_map/all_to_all | solution.py:314
  131.2 0.0 copy-done.7
  131.2 0.1 dynamic_slice.16
  131.3 0.0 copy-done.5
  131.3 0.0 copy-done.6
  131.3 0.2 select_reduce_fusion.2
  131.4 0.0 copy-start.4
  131.4 0.6 dynamic_slice.17.len_ref
  132.0 0.0 copy-done
  132.0 18.7 %shard_map.94.rest_0_ = f32[2048,128]{1,0:T(8,128)} custom-call(s32[1]{0:T(128)} %dynamic_slice.17.len_ref, bf16[16,768,128]{2,1,0:T(8,128)(2,1)} %copy-done, bf16[16,768,128]{2,1,0:T(8,128)(2,1)} %copy-done), custom_call_target="tpu_custom_call" | custom-call | tf_op jit(solution)/shard_map/pallas_call | solution.py:145
  150.8 0.0 copy-done.4
  150.8 0.0 copy-start.1
  150.8 4.9 %all-to-all-done.kv_ref = bf16[16,384,128]{2,1,0:T(8,128)(2,1)} async-done(((bf16[16,384,128]{2,1,0:T(8,128)(2,1)}), bf16[16,384,128]{2,1,0:T(8,128)(2,1)}, u32[]{:S(2)}, u32[]{:S(2)}) %all-to-all-start) | async-done | bytes 1572896 | tf_op jit(solution)/shard_map/all_to_all | solution.py:314
  155.7 13.9 %shard_map.95 = f32[2048,128]{1,0:T(8,128)} custom-call(s32[1]{0:T(128)} %dynamic_slice.17.len_ref, bf16[16,384,128]{2,1,0:T(8,128)(2,1)} %all-to-all-done.kv_ref, bf16[16,768,128]{2,1,0:T(8,128)(2,1)} %copy-done, f32[2048,128]{1,0:T(8,128)} %shard_map.94.rest_0_), custom_call_target="tpu_custom_call" | custom-call | tf_op jit(solution)/shard_map/pallas_call | solution.py:145
  169.6 2.1 %convert_element_type.15 = bf16[2048,128]{1,0:T(8,128)(2,1)} convert(f32[2048,128]{1,0:T(8,128)} %shard_map.95) | non-fusion elementwise | flops 262144 | bytes 1572864 | tf_op jit(solution)/shard_map/convert_element_type | solution.py:321
  171.7 3.6 %all-to-all-start.3 = ((bf16[16,128,128]{2,1,0:T(8,128)(2,1)}), bf16[16,128,128]{2,1,0:T(8,128)(2,1)S(1)}, u32[]{:S(2)}, u32[]{:S(2)}) async-start(bf16[16,128,128]{2,1,0:T(8,128)(2,1)} %bitcast.7), calls=%async_computation.3 | async-start | bytes 1048576 | tf_op jit(solution)/shard_map/all_to_all | solution.py:322
  175.3 0.0 copy-done.1
  175.3 2.8 %reshape.261.proj_ref = bf16[2,128,4096]{2,1,0:T(8,128)(2,1)} reshape(bf16[2,128,4,1024]{3,2,1,0:T(4,128)(2,1)S(1)} %copy-done.1) | data formatting | bytes 4194304 | tf_op jit(solution)/shard_map/reshape | solution.py:327
  178.1 0.5 broadcast_subtract_fusion.limit_ref
  178.6 6.8 %all-to-all-done.3.hist_ref = bf16[16,128,128]{2,1,0:T(8,128)(2,1)S(1)} async-done(((bf16[16,128,128]{2,1,0:T(8,128)(2,1)}), bf16[16,128,128]{2,1,0:T(8,128)(2,1)S(1)}, u32[]{:S(2)}, u32[]{:S(2)}) %all-to-all-start.3) | async-done | bytes 524320 | tf_op jit(solution)/shard_map/all_to_all | solution.py:322
  185.3 0.0 copy-start.3
  185.3 0.8 copy-done.3
  186.1 4.8 %shard_map.96 = bf16[2,128,1024]{2,1,0:T(8,128)(2,1)} custom-call(f32[8]{0:T(128)} %bias_ref.1, s32[2]{0:T(128)} %copy-done.4, s32[2]{0:T(128)} %broadcast_subtract_fusion.limit_ref, bf16[16,128,128]{2,1,0:T(8,128)(2,1)} %copy-done.3, bf16[2,128,4096]{2,1,0:T(8,128)(2,1)} %reshape.261.proj_ref, bf16[2,128,1024]{2,1,0:T(8,128)(2,1)} %x_ref.1, ...), custom_call_target="tpu_custom_call" | custom-call | tf_op jit(solution)/shard_map/pallas_call | solution.py:234
  (9 shorter events, 0.1 us)
Async XLA Ops:
  0.0 2.2 %slice-start = ((bf16[8,128,2048]{2,1,0:T(8,128)(2,1)}), bf16[8,80,2048]{2,1,0:T(8,128)(2,1)S(1)}, s32[]{:S(2)}) async-start(bf16[8,128,2048]{2,1,0:T(8,128)(2,1)} %param.10), calls=%async_computation.4 | async-start | bytes 5242880 | tf_op jit(solution)/shard_map/slice | solution.py:289
  5.4 64.5 %all-to-all-start.1 = ((bf16[8,2,80,2048]{3,2,1,0:T(8,128)(2,1)}), bf16[8,2,80,2048]{3,2,1,0:T(8,128)(2,1)}, u32[]{:S(2)}, u32[]{:S(2)}) async-start(bf16[8,2,80,2048]{3,2,1,0:T(8,128)(2,1)} %bitcast.12), calls=%async_computation.1 | async-start | bytes 10485760 | tf_op jit(solution)/shard_map/all_to_all | solution.py:292
  10.3 1.0 copy-start.2
  19.3 4.6 %slice-start.1 = ((bf16[8,128,2048]{2,1,0:T(8,128)(2,1)}), bf16[8,48,2048]{2,1,0:T(8,128)(2,1)S(1)}, s32[]{:S(2)}) async-start(bf16[8,128,2048]{2,1,0:T(8,128)(2,1)} %param.10), calls=%async_computation.5 | async-start | bytes 3145728 | tf_op jit(solution)/shard_map/slice | solution.py:289
  74.4 50.8 %all-to-all-start.2 = ((bf16[16,768,128]{2,1,0:T(8,128)(2,1)}), bf16[16,768,128]{2,1,0:T(8,128)(2,1)S(1)}, u32[]{:S(2)}, u32[]{:S(2)}) async-start(bf16[16,768,128]{2,1,0:T(8,128)(2,1)} %shard_map.93), calls=%async_computation.2 | async-start | bytes 6291456 | tf_op jit(solution)/shard_map/all_to_all | solution.py:309
  118.7 12.4 %copy-start.7 = (s32[16]{0:T(128)S(1)}, s32[16]{0:T(128)}, u32[]{:S(2)}) copy-start(s32[16]{0:T(128)} %param.14) | copy-start | bytes 196
  118.7 12.5 %copy-start.5 = (s32[16]{0:T(128)S(1)}, s32[16]{0:T(128)}, u32[]{:S(2)}) copy-start(s32[16]{0:T(128)} %param.16) | copy-start | bytes 196
  118.8 12.5 %copy-start.6 = (s32[16]{0:T(128)S(1)}, s32[16]{0:T(128)}, u32[]{:S(2)}) copy-start(s32[16]{0:T(128)} %param.15) | copy-start | bytes 196
  125.2 6.9 %copy-start = (bf16[16,768,128]{2,1,0:T(8,128)(2,1)}, bf16[16,768,128]{2,1,0:T(8,128)(2,1)S(1)}, u32[]{:S(2)}) copy-start(bf16[16,768,128]{2,1,0:T(8,128)(2,1)S(1)} %all-to-all-done.2.kv_ref.qsrc_ref) | copy-start | bytes 9437188
  125.2 30.5 %all-to-all-start = ((bf16[16,384,128]{2,1,0:T(8,128)(2,1)}), bf16[16,384,128]{2,1,0:T(8,128)(2,1)}, u32[]{:S(2)}, u32[]{:S(2)}) async-start(bf16[16,384,128]{2,1,0:T(8,128)(2,1)} %shard_map.92), calls=%async_computation | async-start | bytes 3145728 | tf_op jit(solution)/shard_map/all_to_all | solution.py:314
  131.4 19.3 %copy-start.4 = (s32[2]{0:T(128)}, s32[2]{0:T(128)S(1)}, u32[]{:S(2)}) copy-start(s32[2]{0:T(128)S(1)} %get-tuple-element.10.len_ref) | copy-start | bytes 28
  150.8 24.5 %copy-start.1 = (bf16[2,128,4,1024]{3,2,1,0:T(4,128)(2,1)S(1)}, bf16[2,128,4,1024]{3,2,1,0:T(4,128)(2,1)}, u32[]{:S(2)}) copy-start(bf16[2,128,4,1024]{3,2,1,0:T(4,128)(2,1)} %reshape.254) | copy-start | bytes 6291460
  171.7 13.6 %all-to-all-start.3 = ((bf16[16,128,128]{2,1,0:T(8,128)(2,1)}), bf16[16,128,128]{2,1,0:T(8,128)(2,1)S(1)}, u32[]{:S(2)}, u32[]{:S(2)}) async-start(bf16[16,128,128]{2,1,0:T(8,128)(2,1)} %bitcast.7), calls=%async_computation.3 | async-start | bytes 1048576 | tf_op jit(solution)/shard_map/all_to_all | solution.py:322
  185.3 0.8 copy-start.3

commit v19 on v18

--- a/solution.py
+++ b/solution.py
@@ -78,10 +78,10 @@
 
 
 def attend_kernel(len_ref, kv_ref, qsrc_ref, *rest, n_tiles, sub, tile_len, offset, q_row, score_scale, chunk):
-    if len(rest) == 3:
-        init_ref, o_ref, q_ref = rest
+    if len(rest) == 4:
+        init_ref, out_ref, q_ref, o_ref = rest
     else:
-        init_ref = None
+        init_ref = out_ref = None
         o_ref, q_ref = rest
     length = len_ref[0]
     n_cls, _, head_dim = kv_ref.shape
@@ -126,6 +126,8 @@
         return carry
 
     lax.fori_loop(0, n_cls // group, one_class, 0)
+    if out_ref is not None:
+        out_ref[...] = o_ref[...].astype(out_ref.dtype)
 
 
 def attend(length, kv_packed, q_packed, q_row, n_tiles, sub, tile_len, offset, score_scale, init=None):
@@ -144,11 +146,12 @@
     )
     return pl.pallas_call(
         kernel,
-        out_shape=jax.ShapeDtypeStruct((rows, head_dim), jnp.float32),
+        out_shape=jax.ShapeDtypeStruct((rows, head_dim), jnp.float32 if init is None else jnp.bfloat16),
         in_specs=[pl.BlockSpec(memory_space=pltpu.SMEM)]
         + [pl.BlockSpec(memory_space=pltpu.VMEM)] * (2 if init is None else 3),
         out_specs=pl.BlockSpec(memory_space=pltpu.VMEM),
-        scratch_shapes=[pltpu.VMEM((rows, head_dim), jnp.bfloat16)],
+        scratch_shapes=[pltpu.VMEM((rows, head_dim), jnp.bfloat16)]
+        + ([] if init is None else [pltpu.VMEM((rows, head_dim), jnp.float32)]),
     )(length, kv_packed, q_packed, *([] if init is None else [init]))
 
 
@@ -318,7 +321,7 @@
     history_mine = attend(
         my_length, packed_b, packed_a, q_row, per_hist, tile_len - first_len, tile_len, first_len, score_scale,
         init=history_mine,
-    ).astype(jnp.bfloat16)
+    )
     history_back = lax.all_to_all(
         history_mine.reshape(hist_count, cand_rows, head_dim), "hist", split_axis=0, concat_axis=0, tiled=True
     )

time: 193 us -> 191 us (0.990)
  Pallas kernels: 81.8 us -> 78.8 us
  waiting for transfers between devices: 54.5 us -> 57.3 us
  other arithmetic: 4.41 us -> 2.34 us
    pallas_call x2, Pallas kernels: 32.6 us -> 29.7 us  [attend(): pl.pallas_call(kernel, out_shape=jax.ShapeDtypeStruct((rows, head_dim), j...]
    convert_element_type x1 -> x0, other arithmetic: 2.07 us -> none  [local(): history_mine = attend(my_length, packed_b, packed_a, q_row, per_hist, til...]
  transfers between devices with their start and end apart: 4 -> 4, of which waited for: 4 -> 4; matrix products, arithmetic and copies ran while one was open for 12% -> 12% of each run, Pallas kernels for 31% -> 30%
where the time goes in v19:
time: 191 us; the launch traced here: 189 us
  Pallas kernels  78.8 us (41%)
  waiting for transfers between devices  57.3 us (30%)
  starting transfers between devices  22.5 us (12%)
  local copies, waits for them, and re-layouts  20.5 us (11%)
  matrix products  7.16 us (4%)
  other arithmetic  2.34 us (1%)
    all_to_all x1, waiting for transfers between devices, local(): lax.all_to_all(sending[0], 'req', split_axis=0, concat_axis=0, tiled=True)  39.9 us
    pallas_call x1, Pallas kernels, req_a2a(): pl.pallas_call(functools.partial(req_a2a_kernel, axis='req', other_axis='...  36.3 us
    pallas_call x2, Pallas kernels, attend(): pl.pallas_call(kernel, out_shape=jax.ShapeDtypeStruct((rows, head_dim), j...  29.7 us
    pallas_call x2, Pallas kernels, pack_for_heads(): pl.pallas_call(functools.partial(pack_kernel, heads=heads, users=users, p...  7.99 us
    all_to_all x1, starting transfers between devices, local(): lax.all_to_all(pack_for_heads(picked_slot, halves[0], queries, users_here...  7.97 us
    all_to_all x1, waiting for transfers between devices, local(): lax.all_to_all(history_mine.reshape(hist_count, cand_rows, head_dim), 'hi...  7.9 us
    dot_general x1, matrix products, local(): jnp.dot(normed.reshape(-1, width), w_uvqk, preferred_element_type=jnp.flo...  7.16 us
    all_to_all x1, waiting for transfers between devices, local(): lax.all_to_all(pack_for_heads(picked_slot, halves[1], None, users_here, h...  6.57 us
  transfers between devices with their start and end apart: 4, of which 4 were waited for; matrix products, arithmetic and copies ran while one was open for 12% of the time, Pallas kernels for 30%

profile of v19, /device:TPU:8, one launch (start us, length us, event | category | flops | bytes accessed | tf_op | source)
XLA Modules:
  0.0 188.8 jit_solution(15920121224700859177)
XLA Ops:
  0.0 0.0 slice-start
  0.0 0.1 broadcast_in_dim.63
  0.1 0.1 eq.98
  0.2 0.9 reshape.251
  1.1 0.4 dynamic-slice_reduce_fusion
  1.5 0.1 reshape.252
  1.6 0.2 select_reduce_fusion
  1.9 0.1 select_reduce_fusion.1
  2.0 0.1 copy.15
  2.1 0.1 reshape.255
  2.2 0.0 slice-done
  2.2 3.2 %gather_fusion.1 = bf16[16,80,2048]{2,1,0:T(8,128)(2,1)} fusion(bf16[8,80,2048]{2,1,0:T(8,128)(2,1)S(1)} %slice-done, s32[1024]{0:T(1024)S(1)} %pad_clamp_fusion), kind=kCustom, calls=%fused_computation.1 | custom fusion | bytes 10485824 | tf_op jit(solution)/shard_map/gather | solution.py:293
  5.4 4.9 %all-to-all-start.1 = ((bf16[8,2,80,2048]{3,2,1,0:T(8,128)(2,1)}), bf16[8,2,80,2048]{3,2,1,0:T(8,128)(2,1)}, u32[]{:S(2)}, u32[]{:S(2)}) async-start(bf16[8,2,80,2048]{3,2,1,0:T(8,128)(2,1)} %bitcast.12), calls=%async_computation.1 | async-start | bytes 10485760 | tf_op jit(solution)/shard_map/all_to_all | solution.py:295
  10.3 0.0 copy-start.2
  10.3 1.0 copy-done.2
  11.4 0.1 convert_reduce_fusion
  11.5 0.3 fusion.2
  11.8 0.3 fusion.3
  12.1 7.2 %multiply_convert_fusion = bf16[256,4096]{1,0:T(8,128)(2,1)} fusion(bf16[256,1024]{1,0:T(8,128)(2,1)S(1)} %bitcast.16, bf16[1024,4096]{1,0:T(8,128)(2,1)} %param.11), kind=kOutput, calls=%fused_computation.2 | convolution fusion | flops 2152726528 | bytes 11010048 | tf_op jit(solution)/shard_map/dot_general | solution.py:297
  19.3 0.0 slice-start.1
  19.3 4.6 %reshape.254 = bf16[2,128,4,1024]{3,2,1,0:T(4,128)(2,1)} reshape(bf16[256,4096]{1,0:T(8,128)(2,1)} %multiply_convert_fusion) | data formatting | bytes 4194304 | tf_op jit(solution)/shard_map/reshape | solution.py:298
  23.9 0.0 slice-done.1
  23.9 2.5 %gather_fusion = bf16[16,48,2048]{2,1,0:T(8,128)(2,1)} fusion(bf16[8,48,2048]{2,1,0:T(8,128)(2,1)S(1)} %slice-done.1, s32[1024]{0:T(1024)S(1)} %pad_clamp_fusion), kind=kCustom, calls=%fused_computation | custom fusion | bytes 6291520 | tf_op jit(solution)/shard_map/gather | solution.py:293
  26.4 2.2 %copy.16 = bf16[2,128,4,1024]{3,1,0,2:T(8,128)(2,1)S(1)} copy(bf16[2,128,4,1024]{3,2,1,0:T(4,128)(2,1)} %reshape.254) | data formatting | bytes 4194304 | tf_op jit(solution)/shard_map/optimization_barrier | solution.py:299
  28.6 0.6 dynamic-slice_add_fusion.picked_ref
  29.2 0.8 slice_bitcast_fusion.rest_0_
  30.0 39.9 %all-to-all-done.1 = bf16[8,2,80,2048]{3,2,1,0:T(8,128)(2,1)} async-done(((bf16[8,2,80,2048]{3,2,1,0:T(8,128)(2,1)}), bf16[8,2,80,2048]{3,2,1,0:T(8,128)(2,1)}, u32[]{:S(2)}, u32[]{:S(2)}) %all-to-all-start.1) | async-done | bytes 5242912 | tf_op jit(solution)/shard_map/all_to_all | solution.py:295
  69.9 4.5 %shard_map.93 = bf16[16,768,128]{2,1,0:T(8,128)(2,1)} custom-call(s32[8]{0:T(128)} %dynamic-slice_add_fusion.picked_ref, bf16[16,80,2048]{2,1,0:T(8,128)(2,1)} %bitcast.5.tiles_hbm, bf16[2,128,1024]{2,1,0:T(8,128)(2,1)} %slice_bitcast_fusion.rest_0_), custom_call_target="tpu_custom_call" | custom-call | tf_op jit(solution)/shard_map/pallas_call | solution.py:195
  74.4 8.0 %all-to-all-start.2 = ((bf16[16,768,128]{2,1,0:T(8,128)(2,1)}), bf16[16,768,128]{2,1,0:T(8,128)(2,1)S(1)}, u32[]{:S(2)}, u32[]{:S(2)}) async-start(bf16[16,768,128]{2,1,0:T(8,128)(2,1)} %shard_map.93), calls=%async_computation.2 | async-start | bytes 6291456 | tf_op jit(solution)/shard_map/all_to_all | solution.py:312
  82.4 36.3 %shard_map.91 = bf16[8,2,48,2048]{3,2,1,0:T(8,128)(2,1)} custom-call(bf16[8,2,48,2048]{3,2,1,0:T(8,128)(2,1)} %bitcast.13), custom_call_target="tpu_custom_call" | custom-call | tf_op jit(solution)/shard_map/pallas_call | solution.py:66
  118.7 0.0 copy-start.7
  118.7 0.0 copy-start.5
  118.8 0.0 copy-start.6
  118.8 3.5 %shard_map.92 = bf16[16,384,128]{2,1,0:T(8,128)(2,1)} custom-call(s32[8]{0:T(128)} %dynamic-slice_add_fusion.picked_ref, bf16[16,48,2048]{2,1,0:T(8,128)(2,1)} %bitcast.14), custom_call_target="tpu_custom_call" | custom-call | tf_op jit(solution)/shard_map/pallas_call | solution.py:195
  122.3 2.9 %all-to-all-done.2.kv_ref.qsrc_ref = bf16[16,768,128]{2,1,0:T(8,128)(2,1)S(1)} async-done(((bf16[16,768,128]{2,1,0:T(8,128)(2,1)}), bf16[16,768,128]{2,1,0:T(8,128)(2,1)S(1)}, u32[]{:S(2)}, u32[]{:S(2)}) %all-to-all-start.2) | async-done | bytes 3145760 | tf_op jit(solution)/shard_map/all_to_all | solution.py:312
  125.2 0.0 copy-start
  125.2 6.0 %all-to-all-start = ((bf16[16,384,128]{2,1,0:T(8,128)(2,1)}), bf16[16,384,128]{2,1,0:T(8,128)(2,1)}, u32[]{:S(2)}, u32[]{:S(2)}) async-start(bf16[16,384,128]{2,1,0:T(8,128)(2,1)} %shard_map.92), calls=%async_computation | async-start | bytes 3145728 | tf_op jit(solution)/shard_map/all_to_all | solution.py:317
  131.2 0.0 copy-done.7
  131.2 0.1 dynamic_slice.16
  131.3 0.0 copy-done.5
  131.3 0.0 copy-done.6
  131.3 0.2 select_reduce_fusion.2
  131.4 0.0 copy-start.4
  131.4 0.7 dynamic_slice.17.len_ref
  132.1 0.0 copy-done
  132.1 17.0 %shard_map.94.rest_0_ = f32[2048,128]{1,0:T(8,128)} custom-call(s32[1]{0:T(128)} %dynamic_slice.17.len_ref, bf16[16,768,128]{2,1,0:T(8,128)(2,1)} %copy-done, bf16[16,768,128]{2,1,0:T(8,128)(2,1)} %copy-done), custom_call_target="tpu_custom_call" | custom-call | tf_op jit(solution)/shard_map/pallas_call | solution.py:147
  149.1 0.0 copy-done.4
  149.1 0.0 copy-start.1
  149.1 6.6 %all-to-all-done.kv_ref = bf16[16,384,128]{2,1,0:T(8,128)(2,1)} async-done(((bf16[16,384,128]{2,1,0:T(8,128)(2,1)}), bf16[16,384,128]{2,1,0:T(8,128)(2,1)}, u32[]{:S(2)}, u32[]{:S(2)}) %all-to-all-start) | async-done | bytes 1572896 | tf_op jit(solution)/shard_map/all_to_all | solution.py:317
  155.7 12.7 %shard_map.95 = bf16[2048,128]{1,0:T(8,128)(2,1)} custom-call(s32[1]{0:T(128)} %dynamic_slice.17.len_ref, bf16[16,384,128]{2,1,0:T(8,128)(2,1)} %all-to-all-done.kv_ref, bf16[16,768,128]{2,1,0:T(8,128)(2,1)} %copy-done, f32[2048,128]{1,0:T(8,128)} %shard_map.94.rest_0_), custom_call_target="tpu_custom_call" | custom-call | tf_op jit(solution)/shard_map/pallas_call | solution.py:147
  168.4 3.7 %all-to-all-start.3 = ((bf16[16,128,128]{2,1,0:T(8,128)(2,1)}), bf16[16,128,128]{2,1,0:T(8,128)(2,1)S(1)}, u32[]{:S(2)}, u32[]{:S(2)}) async-start(bf16[16,128,128]{2,1,0:T(8,128)(2,1)} %bitcast.15), calls=%async_computation.3 | async-start | bytes 1048576 | tf_op jit(solution)/shard_map/all_to_all | solution.py:325
  172.0 0.0 copy-done.1
  172.0 2.8 %reshape.261.proj_ref = bf16[2,128,4096]{2,1,0:T(8,128)(2,1)} reshape(bf16[2,128,4,1024]{3,2,1,0:T(4,128)(2,1)S(1)} %copy-done.1) | data formatting | bytes 4194304 | tf_op jit(solution)/shard_map/reshape | solution.py:330
  174.8 0.5 broadcast_subtract_fusion.limit_ref
  175.3 7.9 %all-to-all-done.3.hist_ref = bf16[16,128,128]{2,1,0:T(8,128)(2,1)S(1)} async-done(((bf16[16,128,128]{2,1,0:T(8,128)(2,1)}), bf16[16,128,128]{2,1,0:T(8,128)(2,1)S(1)}, u32[]{:S(2)}, u32[]{:S(2)}) %all-to-all-start.3) | async-done | bytes 524320 | tf_op jit(solution)/shard_map/all_to_all | solution.py:325
  183.2 0.0 copy-start.3
  183.2 0.8 copy-done.3
  184.0 4.8 %shard_map.96 = bf16[2,128,1024]{2,1,0:T(8,128)(2,1)} custom-call(f32[8]{0:T(128)} %bias_ref.1, s32[2]{0:T(128)} %copy-done.4, s32[2]{0:T(128)} %broadcast_subtract_fusion.limit_ref, bf16[16,128,128]{2,1,0:T(8,128)(2,1)} %copy-done.3, bf16[2,128,4096]{2,1,0:T(8,128)(2,1)} %reshape.261.proj_ref, bf16[2,128,1024]{2,1,0:T(8,128)(2,1)} %x_ref.1, ...), custom_call_target="tpu_custom_call" | custom-call | tf_op jit(solution)/shard_map/pallas_call | solution.py:237
  (9 shorter events, 0.1 us)
Async XLA Ops:
  0.0 2.2 %slice-start = ((bf16[8,128,2048]{2,1,0:T(8,128)(2,1)}), bf16[8,80,2048]{2,1,0:T(8,128)(2,1)S(1)}, s32[]{:S(2)}) async-start(bf16[8,128,2048]{2,1,0:T(8,128)(2,1)} %param.10), calls=%async_computation.4 | async-start | bytes 5242880 | tf_op jit(solution)/shard_map/slice | solution.py:292
  5.4 64.5 %all-to-all-start.1 = ((bf16[8,2,80,2048]{3,2,1,0:T(8,128)(2,1)}), bf16[8,2,80,2048]{3,2,1,0:T(8,128)(2,1)}, u32[]{:S(2)}, u32[]{:S(2)}) async-start(bf16[8,2,80,2048]{3,2,1,0:T(8,128)(2,1)} %bitcast.12), calls=%async_computation.1 | async-start | bytes 10485760 | tf_op jit(solution)/shard_map/all_to_all | solution.py:295
  10.3 1.0 copy-start.2
  19.3 4.6 %slice-start.1 = ((bf16[8,128,2048]{2,1,0:T(8,128)(2,1)}), bf16[8,48,2048]{2,1,0:T(8,128)(2,1)S(1)}, s32[]{:S(2)}) async-start(bf16[8,128,2048]{2,1,0:T(8,128)(2,1)} %param.10), calls=%async_computation.5 | async-start | bytes 3145728 | tf_op jit(solution)/shard_map/slice | solution.py:292
  74.4 50.8 %all-to-all-start.2 = ((bf16[16,768,128]{2,1,0:T(8,128)(2,1)}), bf16[16,768,128]{2,1,0:T(8,128)(2,1)S(1)}, u32[]{:S(2)}, u32[]{:S(2)}) async-start(bf16[16,768,128]{2,1,0:T(8,128)(2,1)} %shard_map.93), calls=%async_computation.2 | async-start | bytes 6291456 | tf_op jit(solution)/shard_map/all_to_all | solution.py:312
  118.7 12.4 %copy-start.7 = (s32[16]{0:T(128)S(1)}, s32[16]{0:T(128)}, u32[]{:S(2)}) copy-start(s32[16]{0:T(128)} %param.14) | copy-start | bytes 196
  118.7 12.5 %copy-start.5 = (s32[16]{0:T(128)S(1)}, s32[16]{0:T(128)}, u32[]{:S(2)}) copy-start(s32[16]{0:T(128)} %param.16) | copy-start | bytes 196
  118.8 12.5 %copy-start.6 = (s32[16]{0:T(128)S(1)}, s32[16]{0:T(128)}, u32[]{:S(2)}) copy-start(s32[16]{0:T(128)} %param.15) | copy-start | bytes 196
  125.2 6.9 %copy-start = (bf16[16,768,128]{2,1,0:T(8,128)(2,1)}, bf16[16,768,128]{2,1,0:T(8,128)(2,1)S(1)}, u32[]{:S(2)}) copy-start(bf16[16,768,128]{2,1,0:T(8,128)(2,1)S(1)} %all-to-all-done.2.kv_ref.qsrc_ref) | copy-start | bytes 9437188
  125.2 30.5 %all-to-all-start = ((bf16[16,384,128]{2,1,0:T(8,128)(2,1)}), bf16[16,384,128]{2,1,0:T(8,128)(2,1)}, u32[]{:S(2)}, u32[]{:S(2)}) async-start(bf16[16,384,128]{2,1,0:T(8,128)(2,1)} %shard_map.92), calls=%async_computation | async-start | bytes 3145728 | tf_op jit(solution)/shard_map/all_to_all | solution.py:317
  131.4 17.7 %copy-start.4 = (s32[2]{0:T(128)}, s32[2]{0:T(128)S(1)}, u32[]{:S(2)}) copy-start(s32[2]{0:T(128)S(1)} %get-tuple-element.10.len_ref) | copy-start | bytes 28
  149.1 22.9 %copy-start.1 = (bf16[2,128,4,1024]{3,2,1,0:T(4,128)(2,1)S(1)}, bf16[2,128,4,1024]{3,2,1,0:T(4,128)(2,1)}, u32[]{:S(2)}) copy-start(bf16[2,128,4,1024]{3,2,1,0:T(4,128)(2,1)} %reshape.254) | copy-start | bytes 6291460
  168.4 14.9 %all-to-all-start.3 = ((bf16[16,128,128]{2,1,0:T(8,128)(2,1)}), bf16[16,128,128]{2,1,0:T(8,128)(2,1)S(1)}, u32[]{:S(2)}, u32[]{:S(2)}) async-start(bf16[16,128,128]{2,1,0:T(8,128)(2,1)} %bitcast.15), calls=%async_computation.3 | async-start | bytes 1048576 | tf_op jit(solution)/shard_map/all_to_all | solution.py:325
  183.2 0.8 copy-start.3

commit v20 on v19

--- a/solution.py
+++ b/solution.py
@@ -95,7 +95,7 @@
     else:
         o_ref[...] = init_ref[...]
 
-    group = 1 if span % 128 == 0 else 2
+    group = 4 if 4 * span <= 1024 else (1 if span % 128 == 0 else 2)
 
     def one_class(g, carry):
         c = g * group

time: 191 us -> 189 us (0.990)
  waiting for transfers between devices: 57.3 us -> 54.6 us
  transfers between devices with their start and end apart: 4 -> 4, of which waited for: 4 -> 4; matrix products, arithmetic and copies ran while one was open for 12% -> 12% of each run, Pallas kernels for 30% -> 31%
where the time goes in v20:
time: 189 us; the launch traced here: 187 us
  Pallas kernels  80.2 us (42%)
  waiting for transfers between devices  54.6 us (29%)
  starting transfers between devices  22.4 us (12%)
  local copies, waits for them, and re-layouts  20.5 us (11%)
  matrix products  7.16 us (4%)
  other arithmetic  2.34 us (1%)
    all_to_all x1, waiting for transfers between devices, local(): lax.all_to_all(sending[0], 'req', split_axis=0, concat_axis=0, tiled=True)  39.9 us
    pallas_call x1, Pallas kernels, req_a2a(): pl.pallas_call(functools.partial(req_a2a_kernel, axis='req', other_axis='...  36.3 us
    pallas_call x2, Pallas kernels, attend(): pl.pallas_call(kernel, out_shape=jax.ShapeDtypeStruct((rows, head_dim), j...  31 us
    pallas_call x2, Pallas kernels, pack_for_heads(): pl.pallas_call(functools.partial(pack_kernel, heads=heads, users=users, p...  7.99 us
    all_to_all x1, starting transfers between devices, local(): lax.all_to_all(pack_for_heads(picked_slot, halves[0], queries, users_here...  7.97 us
    dot_general x1, matrix products, local(): jnp.dot(normed.reshape(-1, width), w_uvqk, preferred_element_type=jnp.flo...  7.16 us
    all_to_all x1, waiting for transfers between devices, local(): lax.all_to_all(history_mine.reshape(hist_count, cand_rows, head_dim), 'hi...  6.76 us
    all_to_all x1, starting transfers between devices, local(): lax.all_to_all(pack_for_heads(picked_slot, halves[1], None, users_here, h...  5.97 us
  transfers between devices with their start and end apart: 4, of which 4 were waited for; matrix products, arithmetic and copies ran while one was open for 12% of the time, Pallas kernels for 31%

profile of v20, /device:TPU:8, one launch (start us, length us, event | category | flops | bytes accessed | tf_op | source)
XLA Modules:
  0.0 187.4 jit_solution(2829967215148079142)
XLA Ops:
  0.0 0.0 slice-start
  0.0 0.1 broadcast_in_dim.63
  0.1 0.1 eq.98
  0.2 0.9 reshape.251
  1.1 0.4 dynamic-slice_reduce_fusion
  1.5 0.1 reshape.252
  1.6 0.2 select_reduce_fusion
  1.9 0.1 select_reduce_fusion.1
  2.0 0.1 copy.15
  2.1 0.1 reshape.255
  2.2 0.0 slice-done
  2.2 3.2 %gather_fusion.1 = bf16[16,80,2048]{2,1,0:T(8,128)(2,1)} fusion(bf16[8,80,2048]{2,1,0:T(8,128)(2,1)S(1)} %slice-done, s32[1024]{0:T(1024)S(1)} %pad_clamp_fusion), kind=kCustom, calls=%fused_computation.1 | custom fusion | bytes 10485824 | tf_op jit(solution)/shard_map/gather | solution.py:293
  5.4 4.9 %all-to-all-start.1 = ((bf16[8,2,80,2048]{3,2,1,0:T(8,128)(2,1)}), bf16[8,2,80,2048]{3,2,1,0:T(8,128)(2,1)}, u32[]{:S(2)}, u32[]{:S(2)}) async-start(bf16[8,2,80,2048]{3,2,1,0:T(8,128)(2,1)} %bitcast.12), calls=%async_computation.1 | async-start | bytes 10485760 | tf_op jit(solution)/shard_map/all_to_all | solution.py:295
  10.3 0.0 copy-start.2
  10.3 1.0 copy-done.2
  11.4 0.1 convert_reduce_fusion
  11.5 0.3 fusion.2
  11.8 0.3 fusion.3
  12.1 7.2 %multiply_convert_fusion = bf16[256,4096]{1,0:T(8,128)(2,1)} fusion(bf16[256,1024]{1,0:T(8,128)(2,1)S(1)} %bitcast.16, bf16[1024,4096]{1,0:T(8,128)(2,1)} %param.11), kind=kOutput, calls=%fused_computation.2 | convolution fusion | flops 2152726528 | bytes 11010048 | tf_op jit(solution)/shard_map/dot_general | solution.py:297
  19.3 0.0 slice-start.1
  19.3 4.6 %reshape.254 = bf16[2,128,4,1024]{3,2,1,0:T(4,128)(2,1)} reshape(bf16[256,4096]{1,0:T(8,128)(2,1)} %multiply_convert_fusion) | data formatting | bytes 4194304 | tf_op jit(solution)/shard_map/reshape | solution.py:298
  23.9 0.0 slice-done.1
  23.9 2.5 %gather_fusion = bf16[16,48,2048]{2,1,0:T(8,128)(2,1)} fusion(bf16[8,48,2048]{2,1,0:T(8,128)(2,1)S(1)} %slice-done.1, s32[1024]{0:T(1024)S(1)} %pad_clamp_fusion), kind=kCustom, calls=%fused_computation | custom fusion | bytes 6291520 | tf_op jit(solution)/shard_map/gather | solution.py:293
  26.4 2.2 %copy.16 = bf16[2,128,4,1024]{3,1,0,2:T(8,128)(2,1)S(1)} copy(bf16[2,128,4,1024]{3,2,1,0:T(4,128)(2,1)} %reshape.254) | data formatting | bytes 4194304 | tf_op jit(solution)/shard_map/optimization_barrier | solution.py:299
  28.6 0.6 dynamic-slice_add_fusion.picked_ref
  29.2 0.8 slice_bitcast_fusion.rest_0_
  30.0 39.9 %all-to-all-done.1 = bf16[8,2,80,2048]{3,2,1,0:T(8,128)(2,1)} async-done(((bf16[8,2,80,2048]{3,2,1,0:T(8,128)(2,1)}), bf16[8,2,80,2048]{3,2,1,0:T(8,128)(2,1)}, u32[]{:S(2)}, u32[]{:S(2)}) %all-to-all-start.1) | async-done | bytes 5242912 | tf_op jit(solution)/shard_map/all_to_all | solution.py:295
  69.9 4.5 %shard_map.93 = bf16[16,768,128]{2,1,0:T(8,128)(2,1)} custom-call(s32[8]{0:T(128)} %dynamic-slice_add_fusion.picked_ref, bf16[16,80,2048]{2,1,0:T(8,128)(2,1)} %bitcast.5.tiles_hbm, bf16[2,128,1024]{2,1,0:T(8,128)(2,1)} %slice_bitcast_fusion.rest_0_), custom_call_target="tpu_custom_call" | custom-call | tf_op jit(solution)/shard_map/pallas_call | solution.py:195
  74.4 8.0 %all-to-all-start.2 = ((bf16[16,768,128]{2,1,0:T(8,128)(2,1)}), bf16[16,768,128]{2,1,0:T(8,128)(2,1)S(1)}, u32[]{:S(2)}, u32[]{:S(2)}) async-start(bf16[16,768,128]{2,1,0:T(8,128)(2,1)} %shard_map.93), calls=%async_computation.2 | async-start | bytes 6291456 | tf_op jit(solution)/shard_map/all_to_all | solution.py:312
  82.4 36.3 %shard_map.91 = bf16[8,2,48,2048]{3,2,1,0:T(8,128)(2,1)} custom-call(bf16[8,2,48,2048]{3,2,1,0:T(8,128)(2,1)} %bitcast.13), custom_call_target="tpu_custom_call" | custom-call | tf_op jit(solution)/shard_map/pallas_call | solution.py:66
  118.7 0.0 copy-start.7
  118.7 0.0 copy-start.5
  118.8 0.0 copy-start.6
  118.8 3.5 %shard_map.92 = bf16[16,384,128]{2,1,0:T(8,128)(2,1)} custom-call(s32[8]{0:T(128)} %dynamic-slice_add_fusion.picked_ref, bf16[16,48,2048]{2,1,0:T(8,128)(2,1)} %bitcast.14), custom_call_target="tpu_custom_call" | custom-call | tf_op jit(solution)/shard_map/pallas_call | solution.py:195
  122.3 2.9 %all-to-all-done.2.kv_ref.qsrc_ref = bf16[16,768,128]{2,1,0:T(8,128)(2,1)S(1)} async-done(((bf16[16,768,128]{2,1,0:T(8,128)(2,1)}), bf16[16,768,128]{2,1,0:T(8,128)(2,1)S(1)}, u32[]{:S(2)}, u32[]{:S(2)}) %all-to-all-start.2) | async-done | bytes 3145760 | tf_op jit(solution)/shard_map/all_to_all | solution.py:312
  125.2 0.0 copy-start
  125.2 6.0 %all-to-all-start = ((bf16[16,384,128]{2,1,0:T(8,128)(2,1)}), bf16[16,384,128]{2,1,0:T(8,128)(2,1)}, u32[]{:S(2)}, u32[]{:S(2)}) async-start(bf16[16,384,128]{2,1,0:T(8,128)(2,1)} %shard_map.92), calls=%async_computation | async-start | bytes 3145728 | tf_op jit(solution)/shard_map/all_to_all | solution.py:317
  131.2 0.0 copy-done.7
  131.2 0.1 dynamic_slice.16
  131.3 0.0 copy-done.5
  131.3 0.0 copy-done.6
  131.3 0.2 select_reduce_fusion.2
  131.4 0.0 copy-start.4
  131.4 0.7 dynamic_slice.17.len_ref
  132.1 0.0 copy-done
  132.1 18.5 %shard_map.94.rest_0_ = f32[2048,128]{1,0:T(8,128)} custom-call(s32[1]{0:T(128)} %dynamic_slice.17.len_ref, bf16[16,768,128]{2,1,0:T(8,128)(2,1)} %copy-done, bf16[16,768,128]{2,1,0:T(8,128)(2,1)} %copy-done), custom_call_target="tpu_custom_call" | custom-call | tf_op jit(solution)/shard_map/pallas_call | solution.py:147
  150.6 0.0 copy-done.4
  150.6 0.0 copy-start.1
  150.6 5.1 %all-to-all-done.kv_ref = bf16[16,384,128]{2,1,0:T(8,128)(2,1)} async-done(((bf16[16,384,128]{2,1,0:T(8,128)(2,1)}), bf16[16,384,128]{2,1,0:T(8,128)(2,1)}, u32[]{:S(2)}, u32[]{:S(2)}) %all-to-all-start) | async-done | bytes 1572896 | tf_op jit(solution)/shard_map/all_to_all | solution.py:317
  155.7 12.5 %shard_map.95 = bf16[2048,128]{1,0:T(8,128)(2,1)} custom-call(s32[1]{0:T(128)} %dynamic_slice.17.len_ref, bf16[16,384,128]{2,1,0:T(8,128)(2,1)} %all-to-all-done.kv_ref, bf16[16,768,128]{2,1,0:T(8,128)(2,1)} %copy-done, f32[2048,128]{1,0:T(8,128)} %shard_map.94.rest_0_), custom_call_target="tpu_custom_call" | custom-call | tf_op jit(solution)/shard_map/pallas_call | solution.py:147
  168.2 3.6 %all-to-all-start.3 = ((bf16[16,128,128]{2,1,0:T(8,128)(2,1)}), bf16[16,128,128]{2,1,0:T(8,128)(2,1)S(1)}, u32[]{:S(2)}, u32[]{:S(2)}) async-start(bf16[16,128,128]{2,1,0:T(8,128)(2,1)} %bitcast.15), calls=%async_computation.3 | async-start | bytes 1048576 | tf_op jit(solution)/shard_map/all_to_all | solution.py:325
  171.8 0.0 copy-done.1
  171.8 2.8 %reshape.261.proj_ref = bf16[2,128,4096]{2,1,0:T(8,128)(2,1)} reshape(bf16[2,128,4,1024]{3,2,1,0:T(4,128)(2,1)S(1)} %copy-done.1) | data formatting | bytes 4194304 | tf_op jit(solution)/shard_map/reshape | solution.py:330
  174.6 0.5 broadcast_subtract_fusion.limit_ref
  175.1 6.8 %all-to-all-done.3.hist_ref = bf16[16,128,128]{2,1,0:T(8,128)(2,1)S(1)} async-done(((bf16[16,128,128]{2,1,0:T(8,128)(2,1)}), bf16[16,128,128]{2,1,0:T(8,128)(2,1)S(1)}, u32[]{:S(2)}, u32[]{:S(2)}) %all-to-all-start.3) | async-done | bytes 524320 | tf_op jit(solution)/shard_map/all_to_all | solution.py:325
  181.9 0.0 copy-start.3
  181.9 0.8 copy-done.3
  182.7 4.8 %shard_map.96 = bf16[2,128,1024]{2,1,0:T(8,128)(2,1)} custom-call(f32[8]{0:T(128)} %bias_ref.1, s32[2]{0:T(128)} %copy-done.4, s32[2]{0:T(128)} %broadcast_subtract_fusion.limit_ref, bf16[16,128,128]{2,1,0:T(8,128)(2,1)} %copy-done.3, bf16[2,128,4096]{2,1,0:T(8,128)(2,1)} %reshape.261.proj_ref, bf16[2,128,1024]{2,1,0:T(8,128)(2,1)} %x_ref.1, ...), custom_call_target="tpu_custom_call" | custom-call | tf_op jit(solution)/shard_map/pallas_call | solution.py:237
  (9 shorter events, 0.1 us)
Async XLA Ops:
  0.0 2.2 %slice-start = ((bf16[8,128,2048]{2,1,0:T(8,128)(2,1)}), bf16[8,80,2048]{2,1,0:T(8,128)(2,1)S(1)}, s32[]{:S(2)}) async-start(bf16[8,128,2048]{2,1,0:T(8,128)(2,1)} %param.10), calls=%async_computation.4 | async-start | bytes 5242880 | tf_op jit(solution)/shard_map/slice | solution.py:292
  5.4 64.5 %all-to-all-start.1 = ((bf16[8,2,80,2048]{3,2,1,0:T(8,128)(2,1)}), bf16[8,2,80,2048]{3,2,1,0:T(8,128)(2,1)}, u32[]{:S(2)}, u32[]{:S(2)}) async-start(bf16[8,2,80,2048]{3,2,1,0:T(8,128)(2,1)} %bitcast.12), calls=%async_computation.1 | async-start | bytes 10485760 | tf_op jit(solution)/shard_map/all_to_all | solution.py:295
  10.3 1.0 copy-start.2
  19.3 4.6 %slice-start.1 = ((bf16[8,128,2048]{2,1,0:T(8,128)(2,1)}), bf16[8,48,2048]{2,1,0:T(8,128)(2,1)S(1)}, s32[]{:S(2)}) async-start(bf16[8,128,2048]{2,1,0:T(8,128)(2,1)} %param.10), calls=%async_computation.5 | async-start | bytes 3145728 | tf_op jit(solution)/shard_map/slice | solution.py:292
  74.4 50.8 %all-to-all-start.2 = ((bf16[16,768,128]{2,1,0:T(8,128)(2,1)}), bf16[16,768,128]{2,1,0:T(8,128)(2,1)S(1)}, u32[]{:S(2)}, u32[]{:S(2)}) async-start(bf16[16,768,128]{2,1,0:T(8,128)(2,1)} %shard_map.93), calls=%async_computation.2 | async-start | bytes 6291456 | tf_op jit(solution)/shard_map/all_to_all | solution.py:312
  118.7 12.4 %copy-start.7 = (s32[16]{0:T(128)S(1)}, s32[16]{0:T(128)}, u32[]{:S(2)}) copy-start(s32[16]{0:T(128)} %param.14) | copy-start | bytes 196
  118.7 12.5 %copy-start.5 = (s32[16]{0:T(128)S(1)}, s32[16]{0:T(128)}, u32[]{:S(2)}) copy-start(s32[16]{0:T(128)} %param.16) | copy-start | bytes 196
  118.8 12.5 %copy-start.6 = (s32[16]{0:T(128)S(1)}, s32[16]{0:T(128)}, u32[]{:S(2)}) copy-start(s32[16]{0:T(128)} %param.15) | copy-start | bytes 196
  125.2 6.9 %copy-start = (bf16[16,768,128]{2,1,0:T(8,128)(2,1)}, bf16[16,768,128]{2,1,0:T(8,128)(2,1)S(1)}, u32[]{:S(2)}) copy-start(bf16[16,768,128]{2,1,0:T(8,128)(2,1)S(1)} %all-to-all-done.2.kv_ref.qsrc_ref) | copy-start | bytes 9437188
  125.2 30.5 %all-to-all-start = ((bf16[16,384,128]{2,1,0:T(8,128)(2,1)}), bf16[16,384,128]{2,1,0:T(8,128)(2,1)}, u32[]{:S(2)}, u32[]{:S(2)}) async-start(bf16[16,384,128]{2,1,0:T(8,128)(2,1)} %shard_map.92), calls=%async_computation | async-start | bytes 3145728 | tf_op jit(solution)/shard_map/all_to_all | solution.py:317
  131.4 19.2 %copy-start.4 = (s32[2]{0:T(128)}, s32[2]{0:T(128)S(1)}, u32[]{:S(2)}) copy-start(s32[2]{0:T(128)S(1)} %get-tuple-element.10.len_ref) | copy-start | bytes 28
  150.6 21.2 %copy-start.1 = (bf16[2,128,4,1024]{3,2,1,0:T(4,128)(2,1)S(1)}, bf16[2,128,4,1024]{3,2,1,0:T(4,128)(2,1)}, u32[]{:S(2)}) copy-start(bf16[2,128,4,1024]{3,2,1,0:T(4,128)(2,1)} %reshape.254) | copy-start | bytes 6291460
  168.2 13.6 %all-to-all-start.3 = ((bf16[16,128,128]{2,1,0:T(8,128)(2,1)}), bf16[16,128,128]{2,1,0:T(8,128)(2,1)S(1)}, u32[]{:S(2)}, u32[]{:S(2)}) async-start(bf16[16,128,128]{2,1,0:T(8,128)(2,1)} %bitcast.15), calls=%async_computation.3 | async-start | bytes 1048576 | tf_op jit(solution)/shard_map/all_to_all | solution.py:325
  181.9 0.8 copy-start.3

commit v21 on v20

--- a/solution.py
+++ b/solution.py
@@ -95,7 +95,7 @@
     else:
         o_ref[...] = init_ref[...]
 
-    group = 4 if 4 * span <= 1024 else (1 if span % 128 == 0 else 2)
+    group = 4 if 4 * span <= 1280 else (1 if span % 128 == 0 else 2)
 
     def one_class(g, carry):
         c = g * group

time: 189 us -> 192 us (1.016)
  the two profiles are of different devices: /device:TPU:8 before, /device:TPU:0 now
where the time goes in v21:
time: 192 us; the launch traced here: 191 us
  waiting for transfers between devices  68.2 us (36%)
  Pallas kernels  61.4 us (32%)
  starting transfers between devices  31.2 us (16%)
  local copies, waits for them, and re-layouts  20.5 us (11%)
  matrix products  7.16 us (4%)
  other arithmetic  2.34 us (1%)
    all_to_all x1, waiting for transfers between devices, local(): lax.all_to_all(sending[0], 'req', split_axis=0, concat_axis=0, tiled=True)  41.3 us
    pallas_call x1, Pallas kernels, req_a2a(): pl.pallas_call(functools.partial(req_a2a_kernel, axis='req', other_axis='...  36 us
    all_to_all x1, waiting for transfers between devices, local(): lax.all_to_all(pack_for_heads(picked_slot, halves[1], None, users_here, h...  15.9 us
    all_to_all x1, starting transfers between devices, local(): lax.all_to_all(history_mine.reshape(hist_count, cand_rows, head_dim), 'hi...  12.6 us
    pallas_call x2, Pallas kernels, attend(): pl.pallas_call(kernel, out_shape=jax.ShapeDtypeStruct((rows, head_dim), j...  12.6 us
    pallas_call x2, Pallas kernels, pack_for_heads(): pl.pallas_call(functools.partial(pack_kernel, heads=heads, users=users, p...  7.99 us
    all_to_all x1, starting transfers between devices, local(): lax.all_to_all(pack_for_heads(picked_slot, halves[0], queries, users_here...  7.97 us
    all_to_all x1, waiting for transfers between devices, local(): lax.all_to_all(history_mine.reshape(hist_count, cand_rows, head_dim), 'hi...  7.75 us
  transfers between devices with their start and end apart: 4, of which 4 were waited for; matrix products, arithmetic and copies ran while one was open for 12% of the time, Pallas kernels for 25%

profile of v21, /device:TPU:0, one launch (start us, length us, event | category | flops | bytes accessed | tf_op | source)
XLA Modules:
  0.0 191.0 jit_solution(2963351443242965291)
XLA Ops:
  0.0 0.0 slice-start
  0.0 0.1 broadcast_in_dim.63
  0.1 0.1 eq.98
  0.2 0.9 reshape.251
  1.1 0.4 dynamic-slice_reduce_fusion
  1.5 0.1 reshape.252
  1.6 0.2 select_reduce_fusion
  1.9 0.1 select_reduce_fusion.1
  2.0 0.1 copy.15
  2.1 0.1 reshape.255
  2.2 0.0 slice-done
  2.2 3.2 %gather_fusion.1 = bf16[16,80,2048]{2,1,0:T(8,128)(2,1)} fusion(bf16[8,80,2048]{2,1,0:T(8,128)(2,1)S(1)} %slice-done, s32[1024]{0:T(1024)S(1)} %pad_clamp_fusion), kind=kCustom, calls=%fused_computation.1 | custom fusion | bytes 10485824 | tf_op jit(solution)/shard_map/gather | solution.py:293
  5.4 4.6 %all-to-all-start.1 = ((bf16[8,2,80,2048]{3,2,1,0:T(8,128)(2,1)}), bf16[8,2,80,2048]{3,2,1,0:T(8,128)(2,1)}, u32[]{:S(2)}, u32[]{:S(2)}) async-start(bf16[8,2,80,2048]{3,2,1,0:T(8,128)(2,1)} %bitcast.12), calls=%async_computation.1 | async-start | bytes 10485760 | tf_op jit(solution)/shard_map/all_to_all | solution.py:295
  10.1 0.0 copy-start.2
  10.1 1.0 copy-done.2
  11.1 0.1 convert_reduce_fusion
  11.3 0.3 fusion.2
  11.6 0.3 fusion.3
  11.8 7.2 %multiply_convert_fusion = bf16[256,4096]{1,0:T(8,128)(2,1)} fusion(bf16[256,1024]{1,0:T(8,128)(2,1)S(1)} %bitcast.16, bf16[1024,4096]{1,0:T(8,128)(2,1)} %param.11), kind=kOutput, calls=%fused_computation.2 | convolution fusion | flops 2152726528 | bytes 11010048 | tf_op jit(solution)/shard_map/dot_general | solution.py:297
  19.0 0.0 slice-start.1
  19.0 4.6 %reshape.254 = bf16[2,128,4,1024]{3,2,1,0:T(4,128)(2,1)} reshape(bf16[256,4096]{1,0:T(8,128)(2,1)} %multiply_convert_fusion) | data formatting | bytes 4194304 | tf_op jit(solution)/shard_map/reshape | solution.py:298
  23.6 0.0 slice-done.1
  23.6 2.5 %gather_fusion = bf16[16,48,2048]{2,1,0:T(8,128)(2,1)} fusion(bf16[8,48,2048]{2,1,0:T(8,128)(2,1)S(1)} %slice-done.1, s32[1024]{0:T(1024)S(1)} %pad_clamp_fusion), kind=kCustom, calls=%fused_computation | custom fusion | bytes 6291520 | tf_op jit(solution)/shard_map/gather | solution.py:293
  26.1 2.2 %copy.16 = bf16[2,128,4,1024]{3,1,0,2:T(8,128)(2,1)S(1)} copy(bf16[2,128,4,1024]{3,2,1,0:T(4,128)(2,1)} %reshape.254) | data formatting | bytes 4194304 | tf_op jit(solution)/shard_map/optimization_barrier | solution.py:299
  28.3 0.6 dynamic-slice_add_fusion.picked_ref
  28.9 0.8 slice_bitcast_fusion.rest_0_
  29.7 41.3 %all-to-all-done.1 = bf16[8,2,80,2048]{3,2,1,0:T(8,128)(2,1)} async-done(((bf16[8,2,80,2048]{3,2,1,0:T(8,128)(2,1)}), bf16[8,2,80,2048]{3,2,1,0:T(8,128)(2,1)}, u32[]{:S(2)}, u32[]{:S(2)}) %all-to-all-start.1) | async-done | bytes 5242912 | tf_op jit(solution)/shard_map/all_to_all | solution.py:295
  71.0 4.5 %shard_map.93 = bf16[16,768,128]{2,1,0:T(8,128)(2,1)} custom-call(s32[8]{0:T(128)} %dynamic-slice_add_fusion.picked_ref, bf16[16,80,2048]{2,1,0:T(8,128)(2,1)} %bitcast.5.tiles_hbm, bf16[2,128,1024]{2,1,0:T(8,128)(2,1)} %slice_bitcast_fusion.rest_0_), custom_call_target="tpu_custom_call" | custom-call | tf_op jit(solution)/shard_map/pallas_call | solution.py:195
  75.5 8.0 %all-to-all-start.2 = ((bf16[16,768,128]{2,1,0:T(8,128)(2,1)}), bf16[16,768,128]{2,1,0:T(8,128)(2,1)S(1)}, u32[]{:S(2)}, u32[]{:S(2)}) async-start(bf16[16,768,128]{2,1,0:T(8,128)(2,1)} %shard_map.93), calls=%async_computation.2 | async-start | bytes 6291456 | tf_op jit(solution)/shard_map/all_to_all | solution.py:312
  83.5 36.0 %shard_map.91 = bf16[8,2,48,2048]{3,2,1,0:T(8,128)(2,1)} custom-call(bf16[8,2,48,2048]{3,2,1,0:T(8,128)(2,1)} %bitcast.13), custom_call_target="tpu_custom_call" | custom-call | tf_op jit(solution)/shard_map/pallas_call | solution.py:66
  119.5 0.0 copy-start.7
  119.5 0.0 copy-start.5
  119.5 0.0 copy-start.6
  119.5 3.5 %shard_map.92 = bf16[16,384,128]{2,1,0:T(8,128)(2,1)} custom-call(s32[8]{0:T(128)} %dynamic-slice_add_fusion.picked_ref, bf16[16,48,2048]{2,1,0:T(8,128)(2,1)} %bitcast.14), custom_call_target="tpu_custom_call" | custom-call | tf_op jit(solution)/shard_map/pallas_call | solution.py:195
  123.0 3.2 %all-to-all-done.2.kv_ref.qsrc_ref = bf16[16,768,128]{2,1,0:T(8,128)(2,1)S(1)} async-done(((bf16[16,768,128]{2,1,0:T(8,128)(2,1)}), bf16[16,768,128]{2,1,0:T(8,128)(2,1)S(1)}, u32[]{:S(2)}, u32[]{:S(2)}) %all-to-all-start.2) | async-done | bytes 3145760 | tf_op jit(solution)/shard_map/all_to_all | solution.py:312
  126.2 0.0 copy-start
  126.2 6.0 %all-to-all-start = ((bf16[16,384,128]{2,1,0:T(8,128)(2,1)}), bf16[16,384,128]{2,1,0:T(8,128)(2,1)}, u32[]{:S(2)}, u32[]{:S(2)}) async-start(bf16[16,384,128]{2,1,0:T(8,128)(2,1)} %shard_map.92), calls=%async_computation | async-start | bytes 3145728 | tf_op jit(solution)/shard_map/all_to_all | solution.py:317
  132.2 0.0 copy-done.7
  132.3 0.1 dynamic_slice.16
  132.3 0.0 copy-done.5
  132.3 0.0 copy-done.6
  132.3 0.2 select_reduce_fusion.2
  132.5 0.0 copy-start.4
  132.5 0.7 dynamic_slice.17.len_ref
  133.2 0.0 copy-done
  133.2 8.2 %shard_map.94.rest_0_ = f32[2048,128]{1,0:T(8,128)} custom-call(s32[1]{0:T(128)} %dynamic_slice.17.len_ref, bf16[16,768,128]{2,1,0:T(8,128)(2,1)} %copy-done, bf16[16,768,128]{2,1,0:T(8,128)(2,1)} %copy-done), custom_call_target="tpu_custom_call" | custom-call | tf_op jit(solution)/shard_map/pallas_call | solution.py:147
  141.4 0.0 copy-done.4
  141.4 0.0 copy-start.1
  141.4 15.9 %all-to-all-done.kv_ref = bf16[16,384,128]{2,1,0:T(8,128)(2,1)} async-done(((bf16[16,384,128]{2,1,0:T(8,128)(2,1)}), bf16[16,384,128]{2,1,0:T(8,128)(2,1)}, u32[]{:S(2)}, u32[]{:S(2)}) %all-to-all-start) | async-done | bytes 1572896 | tf_op jit(solution)/shard_map/all_to_all | solution.py:317
  157.3 4.4 %shard_map.95 = bf16[2048,128]{1,0:T(8,128)(2,1)} custom-call(s32[1]{0:T(128)} %dynamic_slice.17.len_ref, bf16[16,384,128]{2,1,0:T(8,128)(2,1)} %all-to-all-done.kv_ref, bf16[16,768,128]{2,1,0:T(8,128)(2,1)} %copy-done, f32[2048,128]{1,0:T(8,128)} %shard_map.94.rest_0_), custom_call_target="tpu_custom_call" | custom-call | tf_op jit(solution)/shard_map/pallas_call | solution.py:147
  161.7 12.6 %all-to-all-start.3 = ((bf16[16,128,128]{2,1,0:T(8,128)(2,1)}), bf16[16,128,128]{2,1,0:T(8,128)(2,1)S(1)}, u32[]{:S(2)}, u32[]{:S(2)}) async-start(bf16[16,128,128]{2,1,0:T(8,128)(2,1)} %bitcast.15), calls=%async_computation.3 | async-start | bytes 1048576 | tf_op jit(solution)/shard_map/all_to_all | solution.py:325
  174.4 0.0 copy-done.1
  174.4 2.8 %reshape.261.proj_ref = bf16[2,128,4096]{2,1,0:T(8,128)(2,1)} reshape(bf16[2,128,4,1024]{3,2,1,0:T(4,128)(2,1)S(1)} %copy-done.1) | data formatting | bytes 4194304 | tf_op jit(solution)/shard_map/reshape | solution.py:330
  177.2 0.5 broadcast_subtract_fusion.limit_ref
  177.7 7.7 %all-to-all-done.3.hist_ref = bf16[16,128,128]{2,1,0:T(8,128)(2,1)S(1)} async-done(((bf16[16,128,128]{2,1,0:T(8,128)(2,1)}), bf16[16,128,128]{2,1,0:T(8,128)(2,1)S(1)}, u32[]{:S(2)}, u32[]{:S(2)}) %all-to-all-start.3) | async-done | bytes 524320 | tf_op jit(solution)/shard_map/all_to_all | solution.py:325
  185.4 0.0 copy-start.3
  185.4 0.8 copy-done.3
  186.2 4.8 %shard_map.96 = bf16[2,128,1024]{2,1,0:T(8,128)(2,1)} custom-call(f32[8]{0:T(128)} %bias_ref.1, s32[2]{0:T(128)} %copy-done.4, s32[2]{0:T(128)} %broadcast_subtract_fusion.limit_ref, bf16[16,128,128]{2,1,0:T(8,128)(2,1)} %copy-done.3, bf16[2,128,4096]{2,1,0:T(8,128)(2,1)} %reshape.261.proj_ref, bf16[2,128,1024]{2,1,0:T(8,128)(2,1)} %x_ref.1, ...), custom_call_target="tpu_custom_call" | custom-call | tf_op jit(solution)/shard_map/pallas_call | solution.py:237
  (9 shorter events, 0.1 us)
Async XLA Ops:
  0.0 2.2 %slice-start = ((bf16[8,128,2048]{2,1,0:T(8,128)(2,1)}), bf16[8,80,2048]{2,1,0:T(8,128)(2,1)S(1)}, s32[]{:S(2)}) async-start(bf16[8,128,2048]{2,1,0:T(8,128)(2,1)} %param.10), calls=%async_computation.4 | async-start | bytes 5242880 | tf_op jit(solution)/shard_map/slice | solution.py:292
  5.4 65.6 %all-to-all-start.1 = ((bf16[8,2,80,2048]{3,2,1,0:T(8,128)(2,1)}), bf16[8,2,80,2048]{3,2,1,0:T(8,128)(2,1)}, u32[]{:S(2)}, u32[]{:S(2)}) async-start(bf16[8,2,80,2048]{3,2,1,0:T(8,128)(2,1)} %bitcast.12), calls=%async_computation.1 | async-start | bytes 10485760 | tf_op jit(solution)/shard_map/all_to_all | solution.py:295
  10.1 1.0 copy-start.2
  19.0 4.6 %slice-start.1 = ((bf16[8,128,2048]{2,1,0:T(8,128)(2,1)}), bf16[8,48,2048]{2,1,0:T(8,128)(2,1)S(1)}, s32[]{:S(2)}) async-start(bf16[8,128,2048]{2,1,0:T(8,128)(2,1)} %param.10), calls=%async_computation.5 | async-start | bytes 3145728 | tf_op jit(solution)/shard_map/slice | solution.py:292
  75.5 50.7 %all-to-all-start.2 = ((bf16[16,768,128]{2,1,0:T(8,128)(2,1)}), bf16[16,768,128]{2,1,0:T(8,128)(2,1)S(1)}, u32[]{:S(2)}, u32[]{:S(2)}) async-start(bf16[16,768,128]{2,1,0:T(8,128)(2,1)} %shard_map.93), calls=%async_computation.2 | async-start | bytes 6291456 | tf_op jit(solution)/shard_map/all_to_all | solution.py:312
  119.5 12.8 %copy-start.7 = (s32[16]{0:T(128)S(1)}, s32[16]{0:T(128)}, u32[]{:S(2)}) copy-start(s32[16]{0:T(128)} %param.14) | copy-start | bytes 196
  119.5 12.9 %copy-start.5 = (s32[16]{0:T(128)S(1)}, s32[16]{0:T(128)}, u32[]{:S(2)}) copy-start(s32[16]{0:T(128)} %param.16) | copy-start | bytes 196
  119.5 12.9 %copy-start.6 = (s32[16]{0:T(128)S(1)}, s32[16]{0:T(128)}, u32[]{:S(2)}) copy-start(s32[16]{0:T(128)} %param.15) | copy-start | bytes 196
  126.2 6.9 %copy-start = (bf16[16,768,128]{2,1,0:T(8,128)(2,1)}, bf16[16,768,128]{2,1,0:T(8,128)(2,1)S(1)}, u32[]{:S(2)}) copy-start(bf16[16,768,128]{2,1,0:T(8,128)(2,1)S(1)} %all-to-all-done.2.kv_ref.qsrc_ref) | copy-start | bytes 9437188
  126.2 31.0 %all-to-all-start = ((bf16[16,384,128]{2,1,0:T(8,128)(2,1)}), bf16[16,384,128]{2,1,0:T(8,128)(2,1)}, u32[]{:S(2)}, u32[]{:S(2)}) async-start(bf16[16,384,128]{2,1,0:T(8,128)(2,1)} %shard_map.92), calls=%async_computation | async-start | bytes 3145728 | tf_op jit(solution)/shard_map/all_to_all | solution.py:317
  132.5 8.8 %copy-start.4 = (s32[2]{0:T(128)}, s32[2]{0:T(128)S(1)}, u32[]{:S(2)}) copy-start(s32[2]{0:T(128)S(1)} %get-tuple-element.10.len_ref) | copy-start | bytes 28
  141.4 33.0 %copy-start.1 = (bf16[2,128,4,1024]{3,2,1,0:T(4,128)(2,1)S(1)}, bf16[2,128,4,1024]{3,2,1,0:T(4,128)(2,1)}, u32[]{:S(2)}) copy-start(bf16[2,128,4,1024]{3,2,1,0:T(4,128)(2,1)} %reshape.254) | copy-start | bytes 6291460
  161.7 23.7 %all-to-all-start.3 = ((bf16[16,128,128]{2,1,0:T(8,128)(2,1)}), bf16[16,128,128]{2,1,0:T(8,128)(2,1)S(1)}, u32[]{:S(2)}, u32[]{:S(2)}) async-start(bf16[16,128,128]{2,1,0:T(8,128)(2,1)} %bitcast.15), calls=%async_computation.3 | async-start | bytes 1048576 | tf_op jit(solution)/shard_map/all_to_all | solution.py:325
  185.4 0.8 copy-start.3

commit v22 on v21

--- a/solution.py
+++ b/solution.py
@@ -95,7 +95,7 @@
     else:
         o_ref[...] = init_ref[...]
 
-    group = 4 if 4 * span <= 1280 else (1 if span % 128 == 0 else 2)
+    group = 8 if 8 * span <= 1536 else (4 if 4 * span <= 1280 else (1 if span % 128 == 0 else 2))
 
     def one_class(g, carry):
         c = g * group

time: 192 us -> 191 us (level)
  the two profiles are of different devices: /device:TPU:0 before, /device:TPU:1 now
where the time goes in v22:
time: 191 us; the launch traced here: 189 us
  Pallas kernels  72.2 us (38%)
  waiting for transfers between devices  58.4 us (31%)
  starting transfers between devices  28.5 us (15%)
  local copies, waits for them, and re-layouts  20.5 us (11%)
  matrix products  7.16 us (4%)
  other arithmetic  2.34 us (1%)
    all_to_all x1, waiting for transfers between devices, local(): lax.all_to_all(sending[0], 'req', split_axis=0, concat_axis=0, tiled=True)  40.5 us
    pallas_call x1, Pallas kernels, req_a2a(): pl.pallas_call(functools.partial(req_a2a_kernel, axis='req', other_axis='...  39.5 us
    pallas_call x2, Pallas kernels, attend(): pl.pallas_call(kernel, out_shape=jax.ShapeDtypeStruct((rows, head_dim), j...  20 us
    all_to_all x1, waiting for transfers between devices, local(): lax.all_to_all(pack_for_heads(picked_slot, halves[1], None, users_here, h...  11.3 us
    all_to_all x1, starting transfers between devices, local(): lax.all_to_all(history_mine.reshape(hist_count, cand_rows, head_dim), 'hi...  8.15 us
    pallas_call x2, Pallas kernels, pack_for_heads(): pl.pallas_call(functools.partial(pack_kernel, heads=heads, users=users, p...  7.99 us
    all_to_all x1, starting transfers between devices, local(): lax.all_to_all(pack_for_heads(picked_slot, halves[0], queries, users_here...  7.69 us
    dot_general x1, matrix products, local(): jnp.dot(normed.reshape(-1, width), w_uvqk, preferred_element_type=jnp.flo...  7.16 us
  transfers between devices with their start and end apart: 4, of which 3 were waited for; matrix products, arithmetic and copies ran while one was open for 12% of the time, Pallas kernels for 29%

profile of v22, /device:TPU:1, one launch (start us, length us, event | category | flops | bytes accessed | tf_op | source)
XLA Modules:
  0.0 189.4 jit_solution(4174710550150138782)
XLA Ops:
  0.0 0.0 slice-start
  0.0 0.1 broadcast_in_dim.63
  0.1 0.1 eq.98
  0.2 0.9 reshape.251
  1.1 0.4 dynamic-slice_reduce_fusion
  1.5 0.1 reshape.252
  1.6 0.2 select_reduce_fusion
  1.9 0.1 select_reduce_fusion.1
  2.0 0.1 copy.15
  2.1 0.1 reshape.255
  2.2 0.0 slice-done
  2.2 3.2 %gather_fusion.1 = bf16[16,80,2048]{2,1,0:T(8,128)(2,1)} fusion(bf16[8,80,2048]{2,1,0:T(8,128)(2,1)S(1)} %slice-done, s32[1024]{0:T(1024)S(1)} %pad_clamp_fusion), kind=kCustom, calls=%fused_computation.1 | custom fusion | bytes 10485824 | tf_op jit(solution)/shard_map/gather | solution.py:293
  5.4 6.0 %all-to-all-start.1 = ((bf16[8,2,80,2048]{3,2,1,0:T(8,128)(2,1)}), bf16[8,2,80,2048]{3,2,1,0:T(8,128)(2,1)}, u32[]{:S(2)}, u32[]{:S(2)}) async-start(bf16[8,2,80,2048]{3,2,1,0:T(8,128)(2,1)} %bitcast.12), calls=%async_computation.1 | async-start | bytes 10485760 | tf_op jit(solution)/shard_map/all_to_all | solution.py:295
  11.4 0.0 copy-start.2
  11.4 1.0 copy-done.2
  12.4 0.1 convert_reduce_fusion
  12.6 0.3 fusion.2
  12.9 0.3 fusion.3
  13.2 7.2 %multiply_convert_fusion = bf16[256,4096]{1,0:T(8,128)(2,1)} fusion(bf16[256,1024]{1,0:T(8,128)(2,1)S(1)} %bitcast.16, bf16[1024,4096]{1,0:T(8,128)(2,1)} %param.11), kind=kOutput, calls=%fused_computation.2 | convolution fusion | flops 2152726528 | bytes 11010048 | tf_op jit(solution)/shard_map/dot_general | solution.py:297
  20.3 0.0 slice-start.1
  20.3 4.6 %reshape.254 = bf16[2,128,4,1024]{3,2,1,0:T(4,128)(2,1)} reshape(bf16[256,4096]{1,0:T(8,128)(2,1)} %multiply_convert_fusion) | data formatting | bytes 4194304 | tf_op jit(solution)/shard_map/reshape | solution.py:298
  24.9 0.0 slice-done.1
  24.9 2.5 %gather_fusion = bf16[16,48,2048]{2,1,0:T(8,128)(2,1)} fusion(bf16[8,48,2048]{2,1,0:T(8,128)(2,1)S(1)} %slice-done.1, s32[1024]{0:T(1024)S(1)} %pad_clamp_fusion), kind=kCustom, calls=%fused_computation | custom fusion | bytes 6291520 | tf_op jit(solution)/shard_map/gather | solution.py:293
  27.4 2.2 %copy.16 = bf16[2,128,4,1024]{3,1,0,2:T(8,128)(2,1)S(1)} copy(bf16[2,128,4,1024]{3,2,1,0:T(4,128)(2,1)} %reshape.254) | data formatting | bytes 4194304 | tf_op jit(solution)/shard_map/optimization_barrier | solution.py:299
  29.7 0.6 dynamic-slice_add_fusion.picked_ref
  30.2 0.8 slice_bitcast_fusion.rest_0_
  31.0 40.5 %all-to-all-done.1 = bf16[8,2,80,2048]{3,2,1,0:T(8,128)(2,1)} async-done(((bf16[8,2,80,2048]{3,2,1,0:T(8,128)(2,1)}), bf16[8,2,80,2048]{3,2,1,0:T(8,128)(2,1)}, u32[]{:S(2)}, u32[]{:S(2)}) %all-to-all-start.1) | async-done | bytes 5242912 | tf_op jit(solution)/shard_map/all_to_all | solution.py:295
  71.5 4.5 %shard_map.93 = bf16[16,768,128]{2,1,0:T(8,128)(2,1)} custom-call(s32[8]{0:T(128)} %dynamic-slice_add_fusion.picked_ref, bf16[16,80,2048]{2,1,0:T(8,128)(2,1)} %bitcast.5.tiles_hbm, bf16[2,128,1024]{2,1,0:T(8,128)(2,1)} %slice_bitcast_fusion.rest_0_), custom_call_target="tpu_custom_call" | custom-call | tf_op jit(solution)/shard_map/pallas_call | solution.py:195
  76.0 7.7 %all-to-all-start.2 = ((bf16[16,768,128]{2,1,0:T(8,128)(2,1)}), bf16[16,768,128]{2,1,0:T(8,128)(2,1)S(1)}, u32[]{:S(2)}, u32[]{:S(2)}) async-start(bf16[16,768,128]{2,1,0:T(8,128)(2,1)} %shard_map.93), calls=%async_computation.2 | async-start | bytes 6291456 | tf_op jit(solution)/shard_map/all_to_all | solution.py:312
  83.7 39.5 %shard_map.91 = bf16[8,2,48,2048]{3,2,1,0:T(8,128)(2,1)} custom-call(bf16[8,2,48,2048]{3,2,1,0:T(8,128)(2,1)} %bitcast.13), custom_call_target="tpu_custom_call" | custom-call | tf_op jit(solution)/shard_map/pallas_call | solution.py:66
  123.2 0.0 copy-start.7
  123.2 0.0 copy-start.5
  123.2 0.0 copy-start.6
  123.3 3.5 %shard_map.92 = bf16[16,384,128]{2,1,0:T(8,128)(2,1)} custom-call(s32[8]{0:T(128)} %dynamic-slice_add_fusion.picked_ref, bf16[16,48,2048]{2,1,0:T(8,128)(2,1)} %bitcast.14), custom_call_target="tpu_custom_call" | custom-call | tf_op jit(solution)/shard_map/pallas_call | solution.py:195
  126.8 0.0 all-to-all-done.2.kv_ref.qsrc_ref
  126.8 0.0 copy-start
  126.8 6.7 %all-to-all-start = ((bf16[16,384,128]{2,1,0:T(8,128)(2,1)}), bf16[16,384,128]{2,1,0:T(8,128)(2,1)}, u32[]{:S(2)}, u32[]{:S(2)}) async-start(bf16[16,384,128]{2,1,0:T(8,128)(2,1)} %shard_map.92), calls=%async_computation | async-start | bytes 3145728 | tf_op jit(solution)/shard_map/all_to_all | solution.py:317
  133.5 0.0 copy-done.7
  133.6 0.1 dynamic_slice.16
  133.6 0.0 copy-done.5
  133.6 0.0 copy-done.6
  133.6 0.2 select_reduce_fusion.2
  133.8 0.0 copy-start.4
  133.8 0.7 dynamic_slice.17.len_ref
  134.5 0.0 copy-done
  134.5 11.4 %shard_map.94.rest_0_ = f32[2048,128]{1,0:T(8,128)} custom-call(s32[1]{0:T(128)} %dynamic_slice.17.len_ref, bf16[16,768,128]{2,1,0:T(8,128)(2,1)} %copy-done, bf16[16,768,128]{2,1,0:T(8,128)(2,1)} %copy-done), custom_call_target="tpu_custom_call" | custom-call | tf_op jit(solution)/shard_map/pallas_call | solution.py:147
  145.9 0.0 copy-done.4
  145.9 0.0 copy-start.1
  145.9 11.3 %all-to-all-done.kv_ref = bf16[16,384,128]{2,1,0:T(8,128)(2,1)} async-done(((bf16[16,384,128]{2,1,0:T(8,128)(2,1)}), bf16[16,384,128]{2,1,0:T(8,128)(2,1)}, u32[]{:S(2)}, u32[]{:S(2)}) %all-to-all-start) | async-done | bytes 1572896 | tf_op jit(solution)/shard_map/all_to_all | solution.py:317
  157.3 8.5 %shard_map.95 = bf16[2048,128]{1,0:T(8,128)(2,1)} custom-call(s32[1]{0:T(128)} %dynamic_slice.17.len_ref, bf16[16,384,128]{2,1,0:T(8,128)(2,1)} %all-to-all-done.kv_ref, bf16[16,768,128]{2,1,0:T(8,128)(2,1)} %copy-done, f32[2048,128]{1,0:T(8,128)} %shard_map.94.rest_0_), custom_call_target="tpu_custom_call" | custom-call | tf_op jit(solution)/shard_map/pallas_call | solution.py:147
  165.8 8.1 %all-to-all-start.3 = ((bf16[16,128,128]{2,1,0:T(8,128)(2,1)}), bf16[16,128,128]{2,1,0:T(8,128)(2,1)S(1)}, u32[]{:S(2)}, u32[]{:S(2)}) async-start(bf16[16,128,128]{2,1,0:T(8,128)(2,1)} %bitcast.15), calls=%async_computation.3 | async-start | bytes 1048576 | tf_op jit(solution)/shard_map/all_to_all | solution.py:325
  173.9 0.0 copy-done.1
  174.0 2.8 %reshape.261.proj_ref = bf16[2,128,4096]{2,1,0:T(8,128)(2,1)} reshape(bf16[2,128,4,1024]{3,2,1,0:T(4,128)(2,1)S(1)} %copy-done.1) | data formatting | bytes 4194304 | tf_op jit(solution)/shard_map/reshape | solution.py:330
  176.7 0.5 broadcast_subtract_fusion.limit_ref
  177.2 6.5 %all-to-all-done.3.hist_ref = bf16[16,128,128]{2,1,0:T(8,128)(2,1)S(1)} async-done(((bf16[16,128,128]{2,1,0:T(8,128)(2,1)}), bf16[16,128,128]{2,1,0:T(8,128)(2,1)S(1)}, u32[]{:S(2)}, u32[]{:S(2)}) %all-to-all-start.3) | async-done | bytes 524320 | tf_op jit(solution)/shard_map/all_to_all | solution.py:325
  183.8 0.0 copy-start.3
  183.8 0.8 copy-done.3
  184.6 4.8 %shard_map.96 = bf16[2,128,1024]{2,1,0:T(8,128)(2,1)} custom-call(f32[8]{0:T(128)} %bias_ref.1, s32[2]{0:T(128)} %copy-done.4, s32[2]{0:T(128)} %broadcast_subtract_fusion.limit_ref, bf16[16,128,128]{2,1,0:T(8,128)(2,1)} %copy-done.3, bf16[2,128,4096]{2,1,0:T(8,128)(2,1)} %reshape.261.proj_ref, bf16[2,128,1024]{2,1,0:T(8,128)(2,1)} %x_ref.1, ...), custom_call_target="tpu_custom_call" | custom-call | tf_op jit(solution)/shard_map/pallas_call | solution.py:237
  (9 shorter events, 0.1 us)
Async XLA Ops:
  0.0 2.2 %slice-start = ((bf16[8,128,2048]{2,1,0:T(8,128)(2,1)}), bf16[8,80,2048]{2,1,0:T(8,128)(2,1)S(1)}, s32[]{:S(2)}) async-start(bf16[8,128,2048]{2,1,0:T(8,128)(2,1)} %param.10), calls=%async_computation.4 | async-start | bytes 5242880 | tf_op jit(solution)/shard_map/slice | solution.py:292
  5.4 66.1 %all-to-all-start.1 = ((bf16[8,2,80,2048]{3,2,1,0:T(8,128)(2,1)}), bf16[8,2,80,2048]{3,2,1,0:T(8,128)(2,1)}, u32[]{:S(2)}, u32[]{:S(2)}) async-start(bf16[8,2,80,2048]{3,2,1,0:T(8,128)(2,1)} %bitcast.12), calls=%async_computation.1 | async-start | bytes 10485760 | tf_op jit(solution)/shard_map/all_to_all | solution.py:295
  11.4 1.0 copy-start.2
  20.3 4.6 %slice-start.1 = ((bf16[8,128,2048]{2,1,0:T(8,128)(2,1)}), bf16[8,48,2048]{2,1,0:T(8,128)(2,1)S(1)}, s32[]{:S(2)}) async-start(bf16[8,128,2048]{2,1,0:T(8,128)(2,1)} %param.10), calls=%async_computation.5 | async-start | bytes 3145728 | tf_op jit(solution)/shard_map/slice | solution.py:292
  76.0 50.7 %all-to-all-start.2 = ((bf16[16,768,128]{2,1,0:T(8,128)(2,1)}), bf16[16,768,128]{2,1,0:T(8,128)(2,1)S(1)}, u32[]{:S(2)}, u32[]{:S(2)}) async-start(bf16[16,768,128]{2,1,0:T(8,128)(2,1)} %shard_map.93), calls=%async_computation.2 | async-start | bytes 6291456 | tf_op jit(solution)/shard_map/all_to_all | solution.py:312
  123.2 10.3 %copy-start.7 = (s32[16]{0:T(128)S(1)}, s32[16]{0:T(128)}, u32[]{:S(2)}) copy-start(s32[16]{0:T(128)} %param.14) | copy-start | bytes 196
  123.2 10.4 %copy-start.5 = (s32[16]{0:T(128)S(1)}, s32[16]{0:T(128)}, u32[]{:S(2)}) copy-start(s32[16]{0:T(128)} %param.16) | copy-start | bytes 196
  123.2 10.4 %copy-start.6 = (s32[16]{0:T(128)S(1)}, s32[16]{0:T(128)}, u32[]{:S(2)}) copy-start(s32[16]{0:T(128)} %param.15) | copy-start | bytes 196
  126.8 7.7 %copy-start = (bf16[16,768,128]{2,1,0:T(8,128)(2,1)}, bf16[16,768,128]{2,1,0:T(8,128)(2,1)S(1)}, u32[]{:S(2)}) copy-start(bf16[16,768,128]{2,1,0:T(8,128)(2,1)S(1)} %all-to-all-done.2.kv_ref.qsrc_ref) | copy-start | bytes 9437188
  126.8 30.5 %all-to-all-start = ((bf16[16,384,128]{2,1,0:T(8,128)(2,1)}), bf16[16,384,128]{2,1,0:T(8,128)(2,1)}, u32[]{:S(2)}, u32[]{:S(2)}) async-start(bf16[16,384,128]{2,1,0:T(8,128)(2,1)} %shard_map.92), calls=%async_computation | async-start | bytes 3145728 | tf_op jit(solution)/shard_map/all_to_all | solution.py:317
  133.8 12.1 %copy-start.4 = (s32[2]{0:T(128)}, s32[2]{0:T(128)S(1)}, u32[]{:S(2)}) copy-start(s32[2]{0:T(128)S(1)} %get-tuple-element.10.len_ref) | copy-start | bytes 28
  145.9 28.0 %copy-start.1 = (bf16[2,128,4,1024]{3,2,1,0:T(4,128)(2,1)S(1)}, bf16[2,128,4,1024]{3,2,1,0:T(4,128)(2,1)}, u32[]{:S(2)}) copy-start(bf16[2,128,4,1024]{3,2,1,0:T(4,128)(2,1)} %reshape.254) | copy-start | bytes 6291460
  165.8 18.0 %all-to-all-start.3 = ((bf16[16,128,128]{2,1,0:T(8,128)(2,1)}), bf16[16,128,128]{2,1,0:T(8,128)(2,1)S(1)}, u32[]{:S(2)}, u32[]{:S(2)}) async-start(bf16[16,128,128]{2,1,0:T(8,128)(2,1)} %bitcast.15), calls=%async_computation.3 | async-start | bytes 1048576 | tf_op jit(solution)/shard_map/all_to_all | solution.py:325
  183.8 0.8 copy-start.3

commit v23 on v22

--- a/solution.py
+++ b/solution.py
@@ -95,7 +95,7 @@
     else:
         o_ref[...] = init_ref[...]
 
-    group = 8 if 8 * span <= 1536 else (4 if 4 * span <= 1280 else (1 if span % 128 == 0 else 2))
+    group = 8 if 8 * span <= 2560 else (4 if 4 * span <= 1280 else (1 if span % 128 == 0 else 2))
 
     def one_class(g, carry):
         c = g * group

time: 191 us -> 191 us (level)
  the two profiles are of different devices: /device:TPU:1 before, /device:TPU:0 now
where the time goes in v23:
time: 191 us; the launch traced here: 190 us
  Pallas kernels  68.5 us (36%)
  waiting for transfers between devices  64.2 us (34%)
  starting transfers between devices  26.8 us (14%)
  local copies, waits for them, and re-layouts  20.5 us (11%)
  matrix products  7.16 us (4%)
  other arithmetic  2.34 us (1%)
    all_to_all x1, waiting for transfers between devices, local(): lax.all_to_all(sending[0], 'req', split_axis=0, concat_axis=0, tiled=True)  41.3 us
    pallas_call x1, Pallas kernels, req_a2a(): pl.pallas_call(functools.partial(req_a2a_kernel, axis='req', other_axis='...  36 us
    pallas_call x2, Pallas kernels, attend(): pl.pallas_call(kernel, out_shape=jax.ShapeDtypeStruct((rows, head_dim), j...  19.7 us
    all_to_all x1, waiting for transfers between devices, local(): lax.all_to_all(pack_for_heads(picked_slot, halves[1], None, users_here, h...  12.7 us
    all_to_all x1, starting transfers between devices, local(): lax.all_to_all(history_mine.reshape(hist_count, cand_rows, head_dim), 'hi...  8.19 us
    pallas_call x2, Pallas kernels, pack_for_heads(): pl.pallas_call(functools.partial(pack_kernel, heads=heads, users=users, p...  7.99 us
    all_to_all x1, starting transfers between devices, local(): lax.all_to_all(pack_for_heads(picked_slot, halves[0], queries, users_here...  7.97 us
    dot_general x1, matrix products, local(): jnp.dot(normed.reshape(-1, width), w_uvqk, preferred_element_type=jnp.flo...  7.16 us
  transfers between devices with their start and end apart: 4, of which 4 were waited for; matrix products, arithmetic and copies ran while one was open for 12% of the time, Pallas kernels for 27%

profile of v23, /device:TPU:0, one launch (start us, length us, event | category | flops | bytes accessed | tf_op | source)
XLA Modules:
  0.0 189.6 jit_solution(11352204711000926826)
XLA Ops:
  0.0 0.0 slice-start
  0.0 0.1 broadcast_in_dim.63
  0.1 0.1 eq.98
  0.2 0.9 reshape.251
  1.1 0.4 dynamic-slice_reduce_fusion
  1.5 0.1 reshape.252
  1.6 0.2 select_reduce_fusion
  1.9 0.1 select_reduce_fusion.1
  2.0 0.1 copy.15
  2.1 0.1 reshape.255
  2.2 0.0 slice-done
  2.2 3.2 %gather_fusion.1 = bf16[16,80,2048]{2,1,0:T(8,128)(2,1)} fusion(bf16[8,80,2048]{2,1,0:T(8,128)(2,1)S(1)} %slice-done, s32[1024]{0:T(1024)S(1)} %pad_clamp_fusion), kind=kCustom, calls=%fused_computation.1 | custom fusion | bytes 10485824 | tf_op jit(solution)/shard_map/gather | solution.py:293
  5.4 4.6 %all-to-all-start.1 = ((bf16[8,2,80,2048]{3,2,1,0:T(8,128)(2,1)}), bf16[8,2,80,2048]{3,2,1,0:T(8,128)(2,1)}, u32[]{:S(2)}, u32[]{:S(2)}) async-start(bf16[8,2,80,2048]{3,2,1,0:T(8,128)(2,1)} %bitcast.12), calls=%async_computation.1 | async-start | bytes 10485760 | tf_op jit(solution)/shard_map/all_to_all | solution.py:295
  10.1 0.0 copy-start.2
  10.1 1.0 copy-done.2
  11.1 0.1 convert_reduce_fusion
  11.3 0.3 fusion.2
  11.6 0.3 fusion.3
  11.8 7.2 %multiply_convert_fusion = bf16[256,4096]{1,0:T(8,128)(2,1)} fusion(bf16[256,1024]{1,0:T(8,128)(2,1)S(1)} %bitcast.16, bf16[1024,4096]{1,0:T(8,128)(2,1)} %param.11), kind=kOutput, calls=%fused_computation.2 | convolution fusion | flops 2152726528 | bytes 11010048 | tf_op jit(solution)/shard_map/dot_general | solution.py:297
  19.0 0.0 slice-start.1
  19.0 4.6 %reshape.254 = bf16[2,128,4,1024]{3,2,1,0:T(4,128)(2,1)} reshape(bf16[256,4096]{1,0:T(8,128)(2,1)} %multiply_convert_fusion) | data formatting | bytes 4194304 | tf_op jit(solution)/shard_map/reshape | solution.py:298
  23.6 0.0 slice-done.1
  23.6 2.5 %gather_fusion = bf16[16,48,2048]{2,1,0:T(8,128)(2,1)} fusion(bf16[8,48,2048]{2,1,0:T(8,128)(2,1)S(1)} %slice-done.1, s32[1024]{0:T(1024)S(1)} %pad_clamp_fusion), kind=kCustom, calls=%fused_computation | custom fusion | bytes 6291520 | tf_op jit(solution)/shard_map/gather | solution.py:293
  26.1 2.2 %copy.16 = bf16[2,128,4,1024]{3,1,0,2:T(8,128)(2,1)S(1)} copy(bf16[2,128,4,1024]{3,2,1,0:T(4,128)(2,1)} %reshape.254) | data formatting | bytes 4194304 | tf_op jit(solution)/shard_map/optimization_barrier | solution.py:299
  28.3 0.6 dynamic-slice_add_fusion.picked_ref
  28.9 0.8 slice_bitcast_fusion.rest_0_
  29.7 41.3 %all-to-all-done.1 = bf16[8,2,80,2048]{3,2,1,0:T(8,128)(2,1)} async-done(((bf16[8,2,80,2048]{3,2,1,0:T(8,128)(2,1)}), bf16[8,2,80,2048]{3,2,1,0:T(8,128)(2,1)}, u32[]{:S(2)}, u32[]{:S(2)}) %all-to-all-start.1) | async-done | bytes 5242912 | tf_op jit(solution)/shard_map/all_to_all | solution.py:295
  71.0 4.5 %shard_map.93 = bf16[16,768,128]{2,1,0:T(8,128)(2,1)} custom-call(s32[8]{0:T(128)} %dynamic-slice_add_fusion.picked_ref, bf16[16,80,2048]{2,1,0:T(8,128)(2,1)} %bitcast.5.tiles_hbm, bf16[2,128,1024]{2,1,0:T(8,128)(2,1)} %slice_bitcast_fusion.rest_0_), custom_call_target="tpu_custom_call" | custom-call | tf_op jit(solution)/shard_map/pallas_call | solution.py:195
  75.5 8.0 %all-to-all-start.2 = ((bf16[16,768,128]{2,1,0:T(8,128)(2,1)}), bf16[16,768,128]{2,1,0:T(8,128)(2,1)S(1)}, u32[]{:S(2)}, u32[]{:S(2)}) async-start(bf16[16,768,128]{2,1,0:T(8,128)(2,1)} %shard_map.93), calls=%async_computation.2 | async-start | bytes 6291456 | tf_op jit(solution)/shard_map/all_to_all | solution.py:312
  83.5 36.0 %shard_map.91 = bf16[8,2,48,2048]{3,2,1,0:T(8,128)(2,1)} custom-call(bf16[8,2,48,2048]{3,2,1,0:T(8,128)(2,1)} %bitcast.13), custom_call_target="tpu_custom_call" | custom-call | tf_op jit(solution)/shard_map/pallas_call | solution.py:66
  119.5 0.0 copy-start.7
  119.5 0.0 copy-start.5
  119.5 0.0 copy-start.6
  119.5 3.5 %shard_map.92 = bf16[16,384,128]{2,1,0:T(8,128)(2,1)} custom-call(s32[8]{0:T(128)} %dynamic-slice_add_fusion.picked_ref, bf16[16,48,2048]{2,1,0:T(8,128)(2,1)} %bitcast.14), custom_call_target="tpu_custom_call" | custom-call | tf_op jit(solution)/shard_map/pallas_call | solution.py:195
  123.0 3.2 %all-to-all-done.2.kv_ref.qsrc_ref = bf16[16,768,128]{2,1,0:T(8,128)(2,1)S(1)} async-done(((bf16[16,768,128]{2,1,0:T(8,128)(2,1)}), bf16[16,768,128]{2,1,0:T(8,128)(2,1)S(1)}, u32[]{:S(2)}, u32[]{:S(2)}) %all-to-all-start.2) | async-done | bytes 3145760 | tf_op jit(solution)/shard_map/all_to_all | solution.py:312
  126.2 0.0 copy-start
  126.2 6.0 %all-to-all-start = ((bf16[16,384,128]{2,1,0:T(8,128)(2,1)}), bf16[16,384,128]{2,1,0:T(8,128)(2,1)}, u32[]{:S(2)}, u32[]{:S(2)}) async-start(bf16[16,384,128]{2,1,0:T(8,128)(2,1)} %shard_map.92), calls=%async_computation | async-start | bytes 3145728 | tf_op jit(solution)/shard_map/all_to_all | solution.py:317
  132.2 0.0 copy-done.7
  132.2 0.1 dynamic_slice.16
  132.3 0.0 copy-done.5
  132.3 0.0 copy-done.6
  132.3 0.2 select_reduce_fusion.2
  132.5 0.0 copy-start.4
  132.5 0.7 dynamic_slice.17.len_ref
  133.2 0.0 copy-done
  133.2 11.4 %shard_map.94.rest_0_ = f32[2048,128]{1,0:T(8,128)} custom-call(s32[1]{0:T(128)} %dynamic_slice.17.len_ref, bf16[16,768,128]{2,1,0:T(8,128)(2,1)} %copy-done, bf16[16,768,128]{2,1,0:T(8,128)(2,1)} %copy-done), custom_call_target="tpu_custom_call" | custom-call | tf_op jit(solution)/shard_map/pallas_call | solution.py:147
  144.6 0.0 copy-done.4
  144.6 0.0 copy-start.1
  144.6 12.7 %all-to-all-done.kv_ref = bf16[16,384,128]{2,1,0:T(8,128)(2,1)} async-done(((bf16[16,384,128]{2,1,0:T(8,128)(2,1)}), bf16[16,384,128]{2,1,0:T(8,128)(2,1)}, u32[]{:S(2)}, u32[]{:S(2)}) %all-to-all-start) | async-done | bytes 1572896 | tf_op jit(solution)/shard_map/all_to_all | solution.py:317
  157.3 8.3 %shard_map.95 = bf16[2048,128]{1,0:T(8,128)(2,1)} custom-call(s32[1]{0:T(128)} %dynamic_slice.17.len_ref, bf16[16,384,128]{2,1,0:T(8,128)(2,1)} %all-to-all-done.kv_ref, bf16[16,768,128]{2,1,0:T(8,128)(2,1)} %copy-done, f32[2048,128]{1,0:T(8,128)} %shard_map.94.rest_0_), custom_call_target="tpu_custom_call" | custom-call | tf_op jit(solution)/shard_map/pallas_call | solution.py:147
  165.6 8.2 %all-to-all-start.3 = ((bf16[16,128,128]{2,1,0:T(8,128)(2,1)}), bf16[16,128,128]{2,1,0:T(8,128)(2,1)S(1)}, u32[]{:S(2)}, u32[]{:S(2)}) async-start(bf16[16,128,128]{2,1,0:T(8,128)(2,1)} %bitcast.15), calls=%async_computation.3 | async-start | bytes 1048576 | tf_op jit(solution)/shard_map/all_to_all | solution.py:325
  173.8 0.0 copy-done.1
  173.8 2.8 %reshape.261.proj_ref = bf16[2,128,4096]{2,1,0:T(8,128)(2,1)} reshape(bf16[2,128,4,1024]{3,2,1,0:T(4,128)(2,1)S(1)} %copy-done.1) | data formatting | bytes 4194304 | tf_op jit(solution)/shard_map/reshape | solution.py:330
  176.6 0.5 broadcast_subtract_fusion.limit_ref
  177.1 6.9 %all-to-all-done.3.hist_ref = bf16[16,128,128]{2,1,0:T(8,128)(2,1)S(1)} async-done(((bf16[16,128,128]{2,1,0:T(8,128)(2,1)}), bf16[16,128,128]{2,1,0:T(8,128)(2,1)S(1)}, u32[]{:S(2)}, u32[]{:S(2)}) %all-to-all-start.3) | async-done | bytes 524320 | tf_op jit(solution)/shard_map/all_to_all | solution.py:325
  184.0 0.0 copy-start.3
  184.0 0.8 copy-done.3
  184.8 4.8 %shard_map.96 = bf16[2,128,1024]{2,1,0:T(8,128)(2,1)} custom-call(f32[8]{0:T(128)} %bias_ref.1, s32[2]{0:T(128)} %copy-done.4, s32[2]{0:T(128)} %broadcast_subtract_fusion.limit_ref, bf16[16,128,128]{2,1,0:T(8,128)(2,1)} %copy-done.3, bf16[2,128,4096]{2,1,0:T(8,128)(2,1)} %reshape.261.proj_ref, bf16[2,128,1024]{2,1,0:T(8,128)(2,1)} %x_ref.1, ...), custom_call_target="tpu_custom_call" | custom-call | tf_op jit(solution)/shard_map/pallas_call | solution.py:237
  (9 shorter events, 0.1 us)
Async XLA Ops:
  0.0 2.2 %slice-start = ((bf16[8,128,2048]{2,1,0:T(8,128)(2,1)}), bf16[8,80,2048]{2,1,0:T(8,128)(2,1)S(1)}, s32[]{:S(2)}) async-start(bf16[8,128,2048]{2,1,0:T(8,128)(2,1)} %param.10), calls=%async_computation.4 | async-start | bytes 5242880 | tf_op jit(solution)/shard_map/slice | solution.py:292
  5.4 65.6 %all-to-all-start.1 = ((bf16[8,2,80,2048]{3,2,1,0:T(8,128)(2,1)}), bf16[8,2,80,2048]{3,2,1,0:T(8,128)(2,1)}, u32[]{:S(2)}, u32[]{:S(2)}) async-start(bf16[8,2,80,2048]{3,2,1,0:T(8,128)(2,1)} %bitcast.12), calls=%async_computation.1 | async-start | bytes 10485760 | tf_op jit(solution)/shard_map/all_to_all | solution.py:295
  10.1 1.0 copy-start.2
  19.0 4.6 %slice-start.1 = ((bf16[8,128,2048]{2,1,0:T(8,128)(2,1)}), bf16[8,48,2048]{2,1,0:T(8,128)(2,1)S(1)}, s32[]{:S(2)}) async-start(bf16[8,128,2048]{2,1,0:T(8,128)(2,1)} %param.10), calls=%async_computation.5 | async-start | bytes 3145728 | tf_op jit(solution)/shard_map/slice | solution.py:292
  75.5 50.7 %all-to-all-start.2 = ((bf16[16,768,128]{2,1,0:T(8,128)(2,1)}), bf16[16,768,128]{2,1,0:T(8,128)(2,1)S(1)}, u32[]{:S(2)}, u32[]{:S(2)}) async-start(bf16[16,768,128]{2,1,0:T(8,128)(2,1)} %shard_map.93), calls=%async_computation.2 | async-start | bytes 6291456 | tf_op jit(solution)/shard_map/all_to_all | solution.py:312
  119.5 12.8 %copy-start.7 = (s32[16]{0:T(128)S(1)}, s32[16]{0:T(128)}, u32[]{:S(2)}) copy-start(s32[16]{0:T(128)} %param.14) | copy-start | bytes 196
  119.5 12.9 %copy-start.5 = (s32[16]{0:T(128)S(1)}, s32[16]{0:T(128)}, u32[]{:S(2)}) copy-start(s32[16]{0:T(128)} %param.16) | copy-start | bytes 196
  119.5 12.8 %copy-start.6 = (s32[16]{0:T(128)S(1)}, s32[16]{0:T(128)}, u32[]{:S(2)}) copy-start(s32[16]{0:T(128)} %param.15) | copy-start | bytes 196
  126.2 6.9 %copy-start = (bf16[16,768,128]{2,1,0:T(8,128)(2,1)}, bf16[16,768,128]{2,1,0:T(8,128)(2,1)S(1)}, u32[]{:S(2)}) copy-start(bf16[16,768,128]{2,1,0:T(8,128)(2,1)S(1)} %all-to-all-done.2.kv_ref.qsrc_ref) | copy-start | bytes 9437188
  126.2 31.0 %all-to-all-start = ((bf16[16,384,128]{2,1,0:T(8,128)(2,1)}), bf16[16,384,128]{2,1,0:T(8,128)(2,1)}, u32[]{:S(2)}, u32[]{:S(2)}) async-start(bf16[16,384,128]{2,1,0:T(8,128)(2,1)} %shard_map.92), calls=%async_computation | async-start | bytes 3145728 | tf_op jit(solution)/shard_map/all_to_all | solution.py:317
  132.5 12.1 %copy-start.4 = (s32[2]{0:T(128)}, s32[2]{0:T(128)S(1)}, u32[]{:S(2)}) copy-start(s32[2]{0:T(128)S(1)} %get-tuple-element.10.len_ref) | copy-start | bytes 28
  144.6 29.2 %copy-start.1 = (bf16[2,128,4,1024]{3,2,1,0:T(4,128)(2,1)S(1)}, bf16[2,128,4,1024]{3,2,1,0:T(4,128)(2,1)}, u32[]{:S(2)}) copy-start(bf16[2,128,4,1024]{3,2,1,0:T(4,128)(2,1)} %reshape.254) | copy-start | bytes 6291460
  165.6 18.4 %all-to-all-start.3 = ((bf16[16,128,128]{2,1,0:T(8,128)(2,1)}), bf16[16,128,128]{2,1,0:T(8,128)(2,1)S(1)}, u32[]{:S(2)}, u32[]{:S(2)}) async-start(bf16[16,128,128]{2,1,0:T(8,128)(2,1)} %bitcast.15), calls=%async_computation.3 | async-start | bytes 1048576 | tf_op jit(solution)/shard_map/all_to_all | solution.py:325
  184.0 0.8 copy-start.3
